TPU v7x, 32 devices: a whole 2x2x4 slice. The times are simulated.
32 devices in a mesh: narrow: 2 (over y), wide: 16 (over z, x, core).
Axes of the slice: x: 2, y: 2, z: 4, core: 2. Of those that a mesh axis runs over, the one named last changes fastest.
Arguments:
- layer_input: bfloat16 [2, 2048, 2048], P('narrow', 'wide'), may hold values from -6 to 6
- lengths: int32 [2], P('narrow'), may hold values from 768 to 2048, as said below
- attn_gain: bfloat16 [2048], replicated, may hold values from 0.5 to 1.5
- w_query: bfloat16 [2048, 2048], P('wide'), may hold values from -0.125 to 0.125
- w_key: bfloat16 [2048, 2048], P('wide'), may hold values from -0.125 to 0.125
- w_value: bfloat16 [2048, 2048], P('wide'), may hold values from -0.125 to 0.125
- w_out: bfloat16 [2048, 2048], P('wide'), may hold values from -3 to 3
- mlp_gain: bfloat16 [2048], replicated, may hold values from 0.5 to 1.5
- w_gate: bfloat16 [8192, 2048], P('wide'), may hold values from -0.125 to 0.125
- w_up: bfloat16 [8192, 2048], P('wide'), may hold values from -0.125 to 0.125
- w_down: bfloat16 [8192, 2048], P('wide'), may hold values from -0.0625 to 0.0625
- cotangent: bfloat16 [2, 2048, 2048], P('narrow', 'wide'), may hold values from -8 to 8
Outputs:
- block_output: bfloat16 [2, 2048, 2048], P('narrow', 'wide')
- input_grad: float32 [2, 2048, 2048], P('narrow', 'wide')
- grad_attn_gain: float32 [2048], replicated
- grad_query: float32 [2048, 2048], P('wide')
- grad_key: float32 [2048, 2048], P('wide')
- grad_value: float32 [2048, 2048], P('wide')
- grad_out: float32 [2048, 2048], P('wide')
- grad_mlp_gain: float32 [2048], replicated
- grad_gate: float32 [8192, 2048], P('wide')
- grad_up: float32 [8192, 2048], P('wide')
- grad_down: float32 [8192, 2048], P('wide')
Inputs may be any that keep to these rules, and one draw needn't show every extreme that they name: `lengths`: valid positions of each sequence, counted from its start; in every draw one sequence fills all 2048 positions.
All inputs are finite; a program needn't handle non-finite values.
Results may differ from a plain program's by a relative error of at most 0.017.
Values may be sent and summed in bfloat16 or wider, within the bound.
No kernel may reach another device: no remote copies, remote signals or barrier semaphores. Data moves between devices by JAX's collectives and lax.ppermute only.
A program may use at most 768 MiB of HBM per device.

v0:
```python
import math

import jax
import jax.numpy as jnp
from jax import lax
from jax.sharding import PartitionSpec as P

HEAD_DIM = 64


EPSILON = 1e-05
THETA = 130000.0
NEGATIVE = -1e30


def contract_rows(left_side, right_side):
    return lax.dot_general(
        left_side, right_side, (((0,), (0,)), ((), ())), preferred_element_type=jnp.float32
    )


def contract_cols(left_side, right_side):
    return lax.dot_general(
        left_side, right_side, (((1,), (1,)), ((), ())), preferred_element_type=jnp.float32
    )


def split_heads(matrix):
    return matrix.reshape(matrix.shape[0], -1, HEAD_DIM)


def rotate(tensor):
    half_dim = tensor.shape[-1] // 2
    return jnp.concatenate([-tensor[..., half_dim:], tensor[..., :half_dim]], axis=-1)


def rotary_tables(positions):
    half_dim = HEAD_DIM // 2
    frequency = THETA ** (-jnp.arange(half_dim, dtype=jnp.float32) * 2.0 / HEAD_DIM)
    angles = positions.astype(jnp.float32)[:, None] * frequency[None, :]
    cosine_table = jnp.concatenate([jnp.cos(angles), jnp.cos(angles)], axis=-1)[:, None, :]
    sine_table = jnp.concatenate([jnp.sin(angles), jnp.sin(angles)], axis=-1)[:, None, :]
    return (cosine_table, sine_table)


def rms_factor(matrix):
    return lax.rsqrt(jnp.mean(matrix * matrix, axis=-1, keepdims=True) + EPSILON)


def norm_back(upstream, normed, gain_vec, factor):
    scaled = upstream * gain_vec
    return factor * (scaled - normed * jnp.mean(scaled * normed, axis=-1, keepdims=True))


def swiglu_back(hidden_back, gate_proj, up_proj):
    sigmoid_gate = jax.nn.sigmoid(gate_proj)
    gate_back = (
        hidden_back * up_proj * sigmoid_gate * (1.0 + gate_proj * (1.0 - sigmoid_gate))
    ).astype(jnp.bfloat16)
    up_back = (hidden_back * jax.nn.silu(gate_proj)).astype(jnp.bfloat16)
    return (gate_back, up_back)


def over_blocks(carried, arrays, needed, work):
    row_total = arrays[0].shape[0]
    block_size = math.gcd(row_total, 512)
    block_count = row_total // block_size
    stacked = tuple(
        (member.reshape((block_count, block_size) + member.shape[1:]) for member in arrays)
    )

    def advance(state_now, scan_item):
        block_start = scan_item[0] * block_size

        def run_block(state_in):
            return work(state_in, scan_item[1:], block_start)

        def keep_block(state_in):
            return state_in

        return (lax.cond(needed(block_start, block_size), run_block, keep_block, state_now), None)

    finished, unused = lax.scan(
        advance, carried, (jnp.arange(block_count, dtype=jnp.int32),) + stacked
    )
    return finished


def shards(
    layer_input,
    lengths,
    attn_gain,
    w_query,
    w_key,
    w_value,
    w_out,
    mlp_gain,
    w_gate,
    w_up,
    w_down,
    cotangent,
):
    local_rows = layer_input.shape[1]
    model_width = layer_input.shape[2]
    head_count = model_width // HEAD_DIM
    score_scale = HEAD_DIM ** (-0.5)
    length = lengths[0]
    first_pos = lax.axis_index("wide") * local_rows
    last_pos = first_pos + local_rows - 1
    positions = first_pos + jnp.arange(local_rows, dtype=jnp.int32)
    valid_rows = (positions < length).astype(jnp.float32)[:, None]
    cosine_table, sine_table = rotary_tables(positions)
    inputs = layer_input[0].astype(jnp.float32)
    gain_one = attn_gain.astype(jnp.float32)
    gain_two = mlp_gain.astype(jnp.float32)
    full_query, full_key, full_value, full_out = (
        lax.all_gather(w_query, "wide", axis=0, tiled=True),
        lax.all_gather(w_key, "wide", axis=0, tiled=True),
        lax.all_gather(w_value, "wide", axis=0, tiled=True),
        lax.all_gather(w_out, "wide", axis=0, tiled=True),
    )
    factor_one = rms_factor(inputs)
    normed_one = inputs * factor_one
    norm_one = (normed_one * gain_one).astype(jnp.bfloat16)
    query_lin = split_heads(jnp.dot(norm_one, full_query, preferred_element_type=jnp.float32))
    key_lin = split_heads(jnp.dot(norm_one, full_key, preferred_element_type=jnp.float32))
    query_rot = (query_lin * cosine_table + rotate(query_lin) * sine_table).astype(jnp.bfloat16)
    key_rot = (key_lin * cosine_table + rotate(key_lin) * sine_table).astype(jnp.bfloat16)
    value_heads = split_heads(
        jnp.dot(norm_one, full_value, preferred_element_type=jnp.float32)
    ).astype(jnp.bfloat16)
    key_flat = key_rot.reshape(local_rows, model_width)
    value_flat = value_heads.reshape(local_rows, model_width)

    def keys_needed(block_start, block_size):
        return (block_start <= last_pos) & (block_start < length)

    def queries_needed(block_start, block_size):
        return (block_start + block_size - 1 >= first_pos) & (first_pos < length)

    def key_mask(block_start, block_size):
        key_pos = block_start + jnp.arange(block_size, dtype=jnp.int32)
        return ((key_pos[None, :] <= positions[:, None]) & (key_pos[None, :] < length))[None]

    def forward_block(state_in, blocks, block_start):
        row_best, denominator, accumulated = state_in
        block_keys = split_heads(blocks[0])
        block_values = split_heads(blocks[1])
        allowed = key_mask(block_start, block_keys.shape[0])
        scores = (
            jnp.einsum("qhd,khd->hqk", query_rot, block_keys, preferred_element_type=jnp.float32)
            * score_scale
        )
        scores = jnp.where(allowed, scores, NEGATIVE)
        new_best = jnp.maximum(row_best, jnp.max(scores, axis=-1))
        weights_exp = jnp.where(allowed, jnp.exp(scores - new_best[:, :, None]), 0.0)
        shrink = jnp.exp(row_best - new_best)
        denominator = denominator * shrink + jnp.sum(weights_exp, axis=-1)
        update = jnp.einsum(
            "hqk,khd->qhd",
            weights_exp.astype(jnp.bfloat16),
            block_values,
            preferred_element_type=jnp.float32,
        )
        accumulated = accumulated * shrink.T[:, :, None] + update
        return (new_best, denominator, accumulated)

    forward_start = (
        jnp.full((head_count, local_rows), NEGATIVE, jnp.float32),
        jnp.zeros((head_count, local_rows), jnp.float32),
        jnp.zeros((local_rows, head_count, HEAD_DIM), jnp.float32),
    )
    row_best, denominator, accumulated = over_blocks(
        forward_start,
        (
            lax.all_gather(key_flat, "wide", axis=0, tiled=True),
            lax.all_gather(value_flat, "wide", axis=0, tiled=True),
        ),
        keys_needed,
        forward_block,
    )
    log_total = row_best + jnp.log(denominator)
    attention = (
        (accumulated / denominator.T[:, :, None])
        .reshape(local_rows, model_width)
        .astype(jnp.bfloat16)
    )
    residual = inputs + jnp.dot(attention, full_out, preferred_element_type=jnp.float32)
    factor_two = rms_factor(residual)
    normed_two = residual * factor_two
    norm_two = (normed_two * gain_two).astype(jnp.bfloat16)
    group_norm = lax.all_gather(norm_two, "wide", axis=0, tiled=True)
    gate_proj = contract_cols(group_norm, w_gate)
    up_proj = contract_cols(group_norm, w_up)
    hidden = (jax.nn.silu(gate_proj) * up_proj).astype(jnp.bfloat16)
    mlp_out = lax.psum_scatter(
        jnp.dot(hidden, w_down, preferred_element_type=jnp.float32),
        "wide",
        scatter_dimension=0,
        tiled=True,
    )
    block_output = (residual + mlp_out).astype(jnp.bfloat16)
    y_back = cotangent[0].astype(jnp.float32) * valid_rows
    mlp_back = y_back.astype(jnp.bfloat16)
    group_back = lax.all_gather(mlp_back, "wide", axis=0, tiled=True)
    hidden_back = contract_cols(group_back, w_down)
    gate_back, up_back = swiglu_back(hidden_back, gate_proj, up_proj)
    norm_two_back = lax.psum_scatter(
        jnp.dot(gate_back, w_gate, preferred_element_type=jnp.float32)
        + jnp.dot(up_back, w_up, preferred_element_type=jnp.float32),
        "wide",
        scatter_dimension=0,
        tiled=True,
    )
    gate_part = contract_rows(gate_back, group_norm)
    up_part = contract_rows(up_back, group_norm)
    down_part = contract_rows(hidden, group_back)
    residual_back = y_back + norm_back(norm_two_back, normed_two, gain_two, factor_two)
    gain_two_term = jnp.sum(norm_two_back * normed_two, axis=0)
    branch_back = residual_back.astype(jnp.bfloat16)
    attention_back = contract_cols(branch_back, full_out).astype(jnp.bfloat16)
    row_delta = jnp.sum(
        (attention_back.astype(jnp.float32) * attention.astype(jnp.float32)).reshape(
            local_rows, head_count, HEAD_DIM
        ),
        axis=-1,
    ).T
    back_heads = split_heads(attention_back)

    def query_grad_block(state_in, blocks, block_start):
        block_keys = split_heads(blocks[0])
        block_values = split_heads(blocks[1])
        allowed = key_mask(block_start, block_keys.shape[0])
        scores = (
            jnp.einsum("qhd,khd->hqk", query_rot, block_keys, preferred_element_type=jnp.float32)
            * score_scale
        )
        prob_block = jnp.where(allowed, jnp.exp(scores - log_total[:, :, None]), 0.0)
        pulled = jnp.einsum(
            "qhd,khd->hqk", back_heads, block_values, preferred_element_type=jnp.float32
        )
        score_back = (prob_block * (pulled - row_delta[:, :, None]) * score_scale).astype(
            jnp.bfloat16
        )
        return state_in + jnp.einsum(
            "hqk,khd->qhd", score_back, block_keys, preferred_element_type=jnp.float32
        )

    query_back = over_blocks(
        jnp.zeros((local_rows, head_count, HEAD_DIM), jnp.float32),
        (
            lax.all_gather(key_flat, "wide", axis=0, tiled=True),
            lax.all_gather(value_flat, "wide", axis=0, tiled=True),
        ),
        keys_needed,
        query_grad_block,
    )

    def key_grad_block(state_in, blocks, block_start):
        key_back, value_back = state_in
        block_query = split_heads(blocks[0].astype(jnp.bfloat16))
        block_back = split_heads(blocks[1].astype(jnp.bfloat16))
        block_size = block_query.shape[0]
        query_pos = block_start + jnp.arange(block_size, dtype=jnp.int32)
        allowed = ((positions[None, :] <= query_pos[:, None]) & (positions[None, :] < length))[None]
        scores = (
            jnp.einsum("qhd,khd->hqk", block_query, key_rot, preferred_element_type=jnp.float32)
            * score_scale
        )
        prob_block = jnp.where(allowed, jnp.exp(scores - blocks[2].T[:, :, None]), 0.0)
        value_back = value_back + jnp.einsum(
            "hqk,qhd->khd",
            prob_block.astype(jnp.bfloat16),
            block_back,
            preferred_element_type=jnp.float32,
        )
        pulled = jnp.einsum(
            "qhd,khd->hqk", block_back, value_heads, preferred_element_type=jnp.float32
        )
        score_back = (prob_block * (pulled - blocks[3].T[:, :, None]) * score_scale).astype(
            jnp.bfloat16
        )
        key_back = key_back + jnp.einsum(
            "hqk,qhd->khd", score_back, block_query, preferred_element_type=jnp.float32
        )
        return (key_back, value_back)

    query_wire = query_rot.reshape(local_rows, model_width).astype(jnp.float32)
    back_wire = attention_back.astype(jnp.float32)
    zero_heads = jnp.zeros((local_rows, head_count, HEAD_DIM), jnp.float32)
    key_back, value_back = over_blocks(
        (zero_heads, zero_heads),
        (
            lax.all_gather(query_wire, "wide", axis=0, tiled=True),
            lax.all_gather(back_wire, "wide", axis=0, tiled=True),
            lax.all_gather(log_total.T, "wide", axis=0, tiled=True),
            lax.all_gather(row_delta.T, "wide", axis=0, tiled=True),
        ),
        queries_needed,
        key_grad_block,
    )
    query_lin_back = (
        (query_back * cosine_table - rotate(query_back * sine_table))
        .reshape(local_rows, model_width)
        .astype(jnp.bfloat16)
    )
    key_lin_back = (
        (key_back * cosine_table - rotate(key_back * sine_table))
        .reshape(local_rows, model_width)
        .astype(jnp.bfloat16)
    )
    value_lin_back = value_back.reshape(local_rows, model_width).astype(jnp.bfloat16)
    norm_one_back = (
        contract_cols(query_lin_back, full_query)
        + contract_cols(key_lin_back, full_key)
        + contract_cols(value_lin_back, full_value)
    )
    input_back = residual_back + norm_back(norm_one_back, normed_one, gain_one, factor_one)
    gain_one_term = jnp.sum(norm_one_back * normed_one, axis=0)
    attention_part = lax.psum_scatter(
        jnp.concatenate(
            [
                contract_rows(norm_one, query_lin_back),
                contract_rows(norm_one, key_lin_back),
                contract_rows(norm_one, value_lin_back),
                contract_rows(attention, branch_back),
            ],
            axis=1,
        ),
        "wide",
        scatter_dimension=0,
        tiled=True,
    )
    gain_totals = lax.psum((gain_one_term, gain_two_term), ("narrow", "wide"))
    summed = lax.psum((attention_part, gate_part, up_part, down_part), "narrow")
    attention_sum = summed[0]
    return (
        block_output[None],
        input_back[None],
        gain_totals[0],
        attention_sum[:, :model_width],
        attention_sum[:, model_width : 2 * model_width],
        attention_sum[:, 2 * model_width : 3 * model_width],
        attention_sum[:, 3 * model_width :],
        gain_totals[1],
        summed[1],
        summed[2],
        summed[3],
    )


def solution(mesh):
    placed = (
        P("narrow", "wide", None),
        P("narrow"),
        P(),
        P("wide", None),
        P("wide", None),
        P("wide", None),
        P("wide", None),
        P(),
        P("wide", None),
        P("wide", None),
        P("wide", None),
        P("narrow", "wide", None),
    )
    return jax.shard_map(
        shards,
        mesh=mesh,
        in_specs=placed,
        out_specs=(
            P("narrow", "wide", None),
            P("narrow", "wide", None),
            P(),
            P("wide", None),
            P("wide", None),
            P("wide", None),
            P("wide", None),
            P(),
            P("wide", None),
            P("wide", None),
            P("wide", None),
        ),
        check_vma=False,
    )
```

profile of v0, /device:TPU:0, one launch (start us, length us, event | category | flops | bytes accessed | tf_op | source)
XLA Modules:
  0.0 2421.4 jit_solution(15811180874852004695)
XLA Ops:
  11.4 76.4 %all-gather.17.cloned.1.call-done = bf16[2048,2048]{1,0:T(8,128)(2,1)} async-done(((bf16[128,2048]{1,0:T(8,128)(2,1)}), bf16[2048,2048]{1,0:T(8,128)(2,1)}) %all-gather.17.cloned.1.call-update) | async-done | bytes 8388624 | tf_op jit(solution)/shard_map/all_gather | solution.py:119
  87.8 12.5 copy.64
  100.3 5.8 convolution_convert_fusion.1
  107.4 55.7 %all-gather.11.cloned.1.call-done = bf16[2048,2048]{1,0:T(8,128)(2,1)} async-done(((bf16[128,2048]{1,0:T(8,128)(2,1)}), bf16[2048,2048]{1,0:T(8,128)(2,1)}) %all-gather.11.cloned.1.call-update) | async-done | bytes 8388624 | tf_op jit(solution)/shard_map/all_gather | solution.py:118
  163.2 12.4 copy.61
  175.6 62.9 %all-gather.15.cloned.1.call-done = bf16[2048,2048]{1,0:T(8,128)(2,1)} async-done(((bf16[128,2048]{1,0:T(8,128)(2,1)}), bf16[2048,2048]{1,0:T(8,128)(2,1)}) %all-gather.15.cloned.1.call-update) | async-done | bytes 8388624 | tf_op jit(solution)/shard_map/all_gather | solution.py:117
  238.5 12.4 copy.63
  250.9 6.0 fusion.87
  263.9 50.4 %all-gather.19.cloned.1.call-done = bf16[2048,2048]{1,0:T(8,128)(2,1)} async-done(((bf16[128,2048]{1,0:T(8,128)(2,1)}), bf16[2048,2048]{1,0:T(8,128)(2,1)}) %all-gather.19.cloned.1.call-update) | async-done | bytes 8388624 | tf_op jit(solution)/shard_map/all_gather | solution.py:177
  314.3 11.6 copy.67
  325.9 64.2 %all-gather.13.cloned.1.call-done = bf16[2048,2048]{1,0:T(8,128)(2,1)} async-done(((bf16[128,2048]{1,0:T(8,128)(2,1)}), bf16[2048,2048]{1,0:T(8,128)(2,1)}) %all-gather.13.cloned.1.call-update) | async-done | bytes 8388624 | tf_op jit(solution)/shard_map/all_gather | solution.py:176
  390.0 11.5 copy.66
  402.7 18.2 while.47
  404.6 10.5 conditional.10
  423.0 42.2 %all-gather.21.cloned.1.call-done = bf16[2048,2048]{1,0:T(8,128)(2,1)} async-done(((bf16[128,2048]{1,0:T(8,128)(2,1)}), bf16[2048,2048]{1,0:T(8,128)(2,1)}) %all-gather.21.cloned.1.call-update) | async-done | bytes 8388624 | tf_op jit(solution)/shard_map/all_gather | solution.py:120
  465.2 4.9 multiply_reduce_fusion.2
  474.9 70.5 %all-gather.23.cloned.1.call-done = bf16[2048,2048]{1,0:T(8,128)(2,1)} async-done(((bf16[128,2048]{1,0:T(8,128)(2,1)}), bf16[2048,2048]{1,0:T(8,128)(2,1)}) %all-gather.23.cloned.1.call-update) | async-done | bytes 8388624 | tf_op jit(solution)/shard_map/all_gather | solution.py:192
  545.4 10.7 fusion.109
  556.1 6.7 fusion.108
  562.8 58.5 %all-gather.25.cloned.1.call-done = bf16[2048,2048]{1,0:T(8,128)(2,1)} async-done(((bf16[128,2048]{1,0:T(8,128)(2,1)}), bf16[2048,2048]{1,0:T(8,128)(2,1)}) %all-gather.25.cloned.1.call-update) | async-done | bytes 8388624 | tf_op jit(solution)/shard_map/all_gather | solution.py:205
  621.3 12.3 multiply_convert_fusion.6
  633.6 8.4 fusion.111
  642.0 11.8 convolution_add_fusion
  653.8 12.0 fusion.110
  668.2 162.5 %reduce-scatter.6.cloned.1.call-done = f32[128,2048]{1,0:T(8,128)} async-done(((f32[2048,2048]{1,0:T(8,128)}), f32[128,2048]{1,0:T(8,128)}) %reduce-scatter.6.cloned.1.call-update) | async-done | bytes 1048592 | tf_op jit(solution)/shard_map/reduce_scatter | solution.py:208
  832.9 179.4 %reduce-scatter.4.cloned.1.call-done = f32[128,2048]{1,0:T(8,128)} async-done(((f32[2048,2048]{1,0:T(8,128)}), f32[128,2048]{1,0:T(8,128)}) %reduce-scatter.4.cloned.1.call-update) | async-done | bytes 1048592 | tf_op jit(solution)/shard_map/reduce_scatter | solution.py:196
  1015.2 7.8 convert_multiply_fusion.2
  1023.1 65.9 %all-gather.27.cloned.1.call-done = bf16[2048,2048]{1,0:T(8,128)(2,1)} async-done(((bf16[128,2048]{1,0:T(8,128)(2,1)}), bf16[2048,2048]{1,0:T(8,128)(2,1)}) %all-gather.27.cloned.1.call-update) | async-done | bytes 8388624 | tf_op jit(solution)/shard_map/all_gather | solution.py:294
  1089.0 11.6 copy.74
  1100.7 20.8 all_gather.47
  1124.8 19.6 all_gather.49
  1146.3 26.4 %while.48 = (s32[]{:T(128)}, f32[128,32,64]{0,2,1:T(8,128)}, s32[4]{0:T(128)S(1)}, s32[]{:T(128)}, s32[]{:T(128)}, /*index=5*/bf16[4,512,2048]{1,2,0:T(8,128)(2,...) while((s32[]{:T(128)}, f32[128,32,64]{0,2,1:T(8,128)}, ...), condition=%wide.region_15.16_spmd.clone, body=%wide.region_12.15_spmd.clone.sunk | while | flops 820381312 | bytes 34774328 | solution.py:83
  1148.2 18.6 conditional.11
  1152.9 4.7 fusion.106
  1157.5 9.3 fusion.32
  1172.6 9.5 fusion.95
  1182.1 11.6 copy.76
  1195.9 116.0 %while.49 = (s32[]{:T(128)}, f32[128,32,64]{0,2,1:T(8,128)}, f32[128,32,64]{0,2,1:T(8,128)}, s32[4]{0:T(128)S(1)}, s32[]{:T(128)}, /*index=5*/pred[]{:T(512)}, s...) while((s32[]{:T(128)}, f32[128,32,64]{0,2,1:T(8,128)}, ...), condition=%wide.region_19.20_spmd.clone.clone, body=%wide.region_16.19_spmd.clone.clone.sunk | while | flops 1097466624 | bytes 47848052 | solution.py:83
  1197.3 27.6 %conditional.12 = ((f32[128,32,64]{0,2,1:T(8,128)}, f32[128,32,64]{0,2,1:T(8,128)})) conditional(s32[]{:T(128)} %convert_element_type.343, (f32[128,32,64]{0,2,1:T(8,128)}, f32[128,32,64]{0,2,1:T(8,128)}) %tuple.169, (s32[]{:T(128)}, s32[]{:T(128)}, s32[]{:T(128)}, bf16[4,512,2048]{1,2,0:T(8,128)(2,1)}, s32[]{:T(128)}, ...), branch_computations={%region_17.17_spmd, %region_18.18_spmd} | conditional | flops 1097466624 | bytes 47847212 | solution.py:81
  1202.9 4.6 fusion.107
  1207.5 11.0 fusion.52
  1218.5 6.4 fusion.53
  1226.2 27.6 %conditional.12 = ((f32[128,32,64]{0,2,1:T(8,128)}, f32[128,32,64]{0,2,1:T(8,128)})) conditional(s32[]{:T(128)} %convert_element_type.343, (f32[128,32,64]{0,2,1:T(8,128)}, f32[128,32,64]{0,2,1:T(8,128)}) %tuple.169, (s32[]{:T(128)}, s32[]{:T(128)}, s32[]{:T(128)}, bf16[4,512,2048]{1,2,0:T(8,128)(2,1)}, s32[]{:T(128)}, ...), branch_computations={%region_17.17_spmd, %region_18.18_spmd} | conditional | flops 1097466624 | bytes 47847212 | solution.py:81
  1231.7 4.6 fusion.107
  1236.4 11.0 fusion.52
  1247.4 6.4 fusion.53
  1255.0 27.6 %conditional.12 = ((f32[128,32,64]{0,2,1:T(8,128)}, f32[128,32,64]{0,2,1:T(8,128)})) conditional(s32[]{:T(128)} %convert_element_type.343, (f32[128,32,64]{0,2,1:T(8,128)}, f32[128,32,64]{0,2,1:T(8,128)}) %tuple.169, (s32[]{:T(128)}, s32[]{:T(128)}, s32[]{:T(128)}, bf16[4,512,2048]{1,2,0:T(8,128)(2,1)}, s32[]{:T(128)}, ...), branch_computations={%region_17.17_spmd, %region_18.18_spmd} | conditional | flops 1097466624 | bytes 47847212 | solution.py:81
  1265.2 11.0 fusion.52
  1276.2 6.4 fusion.53
  1283.9 27.6 %conditional.12 = ((f32[128,32,64]{0,2,1:T(8,128)}, f32[128,32,64]{0,2,1:T(8,128)})) conditional(s32[]{:T(128)} %convert_element_type.343, (f32[128,32,64]{0,2,1:T(8,128)}, f32[128,32,64]{0,2,1:T(8,128)}) %tuple.169, (s32[]{:T(128)}, s32[]{:T(128)}, s32[]{:T(128)}, bf16[4,512,2048]{1,2,0:T(8,128)(2,1)}, s32[]{:T(128)}, ...), branch_computations={%region_17.17_spmd, %region_18.18_spmd} | conditional | flops 1097466624 | bytes 47847212 | solution.py:81
  1294.1 11.0 fusion.52
  1305.0 6.4 fusion.53
  1319.7 8.3 fusion.89
  1328.0 8.2 fusion.91
  1336.2 39.9 %pad_maximum_fusion = f32[2048,8192]{0,1:T(8,128)} fusion(f32[2048,2048]{0,1:T(8,128)} %fusion.95, f32[2048,2048]{0,1:T(8,128)S(1)} %fusion.93, f32[2048,2048]{0,1:T(8,128)} %fusion.89, f32[2048,2048]{0,1:T(8,128)} %fusion.91), kind=kLoop, calls=%fused_computation.68 | loop fusion | flops 50331648 | bytes 134217728 | tf_op jit(solution)/shard_map/concatenate | solution.py:321
  1376.2 11.6 fusion.115
  1387.8 11.4 fusion.114
  1399.2 6.0 fusion.113
  1405.3 606.3 %reduce-scatter.8.cloned.1.call-done = f32[128,8192]{0,1:T(8,128)} async-done(((f32[2048,8192]{0,1:T(8,128)}), f32[128,8192]{0,1:T(8,128)}) %reduce-scatter.8.cloned.1.call-update) | async-done | bytes 4194320 | tf_op jit(solution)/shard_map/reduce_scatter | solution.py:320
  2011.6 6.4 fusion.112
  2018.0 7.5 convolution_add_fusion.2
  2028.7 39.0 %all-reduce = (f32[2048]{0:T(1024)}, f32[2048]{0:T(1024)}) all-reduce(f32[2048]{0:T(1024)S(1)} %get-tuple-element.985, f32[2048]{0:T(1024)S(1)} %copy-done.29), channel_id=1, replica_groups=mesh['narrow'=2,'wide'=16] {'narrow','wide'}, use_global_device_ids=true, to_apply=%region_22.23 | all-reduce | flops 4096 | bytes 32768 | tf_op jit(solution)/shard_map/psum | solution.py:334
  2069.0 326.6 %all-reduce.4.cloned.1.call-done = (f32[128,8192]{0,1:T(8,128)}, f32[512,2048]{1,0:T(8,128)}, f32[512,2048]{1,0:T(8,128)}, f32[512,2048]{1,0:T(8,128)}) async-done(((f32[128,8192]{0,1:T(8,128)}, f32[512,2048]{1,0:T(8,128)}, f32[512,2048]{1,0:T(8,128)}, f32[512,2048]{1,0:T(8,128)}), (f32[128,8192]{0,1:T(8,128)}, f32[512,2048]{1,0:T(8,128)}, f32[512,2048]{1,0:T(8,128)}, ...) | async-done | bytes 16777232 | tf_op jit(solution)/shard_map/psum | solution.py:335
  2405.5 5.0 copy.135
  (233 shorter events, 114.3 us)
Async XLA Ops:
  7.2 614.1 %copy-start = (bf16[512,2048]{1,0:T(8,128)(2,1)S(1)}, bf16[512,2048]{1,0:T(8,128)(2,1)}, u32[]{:S(2)}) copy-start(bf16[512,2048]{1,0:T(8,128)(2,1)} %param.34) | copy-start | bytes 6291460
  7.2 80.6 %all-gather.17.cloned.1.call-start = ((), (), s32[]{:S(2)}) async-start(), calls=%async_computation.6 | async-start | bytes 8912896 | tf_op jit(solution)/shard_map/all_gather | solution.py:119
  7.9 155.2 %all-gather.11.cloned.1.call-start = ((), (), s32[]{:S(2)}) async-start(), calls=%async_computation.3 | async-start | bytes 8912896 | tf_op jit(solution)/shard_map/all_gather | solution.py:118
  8.7 229.8 %all-gather.15.cloned.1.call-start = ((), (), s32[]{:S(2)}) async-start(), calls=%async_computation.5 | async-start | bytes 8912896 | tf_op jit(solution)/shard_map/all_gather | solution.py:117
  9.4 304.9 %all-gather.19.cloned.1.call-start = ((), (), s32[]{:S(2)}) async-start(), calls=%async_computation.7 | async-start | bytes 8912896 | tf_op jit(solution)/shard_map/all_gather | solution.py:177
  10.1 246.7 %copy-start.21 = (f32[2048]{0:T(1024)}, f32[2048]{0:T(1024)S(1)}, u32[]{:S(2)}) copy-start(f32[2048]{0:T(1024)S(1)} %convert_element_type.180) | copy-start | bytes 24580
  11.4 245.5 %copy-start.27 = (f32[128]{0:T(128)}, f32[128]{0:T(128)S(1)}, u32[]{:S(2)}) copy-start(f32[128]{0:T(128)S(1)} %add_rsqrt_fusion.1) | copy-start | bytes 1540
  87.8 12.5 copy-start.2
  106.1 69.4 %copy-start.19 = (bf16[128,32,64]{0,2,1:T(8,128)(2,1)}, bf16[128,32,64]{0,2,1:T(8,128)(2,1)S(1)}, u32[]{:S(2)}) copy-start(bf16[128,32,64]{0,2,1:T(8,128)(2,1)S(1)} %convolution_convert_fusion.1) | copy-start | bytes 1572868
  107.2 282.8 %all-gather.13.cloned.1.call-start = ((), (), s32[]{:S(2)}) async-start(), calls=%async_computation.4 | async-start | bytes 8912896 | tf_op jit(solution)/shard_map/all_gather | solution.py:176
  107.4 152.3 %copy-start.23 = (f32[128,64]{0,1:T(8,128)}, f32[128,64]{0,1:T(8,128)S(1)}, u32[]{:S(2)}) copy-start(f32[128,64]{0,1:T(8,128)S(1)} %get-tuple-element.1109) | copy-start | bytes 98308
  107.4 152.3 %copy-start.25 = (f32[128,64]{0,1:T(8,128)}, f32[128,64]{0,1:T(8,128)S(1)}, u32[]{:S(2)}) copy-start(f32[128,64]{0,1:T(8,128)S(1)} %get-tuple-element.1110) | copy-start | bytes 98308
  250.9 6.0 copy-start.4
  256.9 7.0 copy-start.30
  263.1 202.1 %all-gather.21.cloned.1.call-start = ((), (), s32[]{:S(2)}) async-start(), calls=%async_computation.8 | async-start | bytes 8912896 | tf_op jit(solution)/shard_map/all_gather | solution.py:120
  263.7 281.7 %all-gather.23.cloned.1.call-start = ((), (), s32[]{:S(2)}) async-start(), calls=%async_computation.9 | async-start | bytes 8912896 | tf_op jit(solution)/shard_map/all_gather | solution.py:192
  405.5 4.6 copy-start.14
  412.8 2.2 copy-start.15
  470.2 1.0 copy-start.6
  472.1 149.2 %all-gather.25.cloned.1.call-start = ((), (), s32[]{:S(2)}) async-start(), calls=%async_computation.11 | async-start | bytes 8912896 | tf_op jit(solution)/shard_map/all_gather | solution.py:205
  474.8 355.9 %reduce-scatter.6.cloned.1.call-start = ((), (), s32[]{:S(2)}) async-start(), calls=%async_computation.12 | async-start | bytes 17825792 | tf_op jit(solution)/shard_map/reduce_scatter | solution.py:208
  545.4 10.7 copy-start.31
  545.4 10.7 copy-start.32
  621.3 12.3 copy-start.33
  633.6 8.4 copy-start.34
  633.6 8.4 copy-start.16
  633.6 8.4 copy-start.18
  653.8 358.5 %reduce-scatter.4.cloned.1.call-start = ((), (), s32[]{:S(2)}) async-start(), calls=%async_computation.10 | async-start | bytes 17825792 | tf_op jit(solution)/shard_map/reduce_scatter | solution.py:196
  665.9 1.3 copy-start.10
  665.9 164.9 %copy-start.7 = (f32[128,2048]{1,0:T(8,128)S(1)}, f32[128,2048]{1,0:T(8,128)}, u32[]{:S(2)}) copy-start(f32[128,2048]{1,0:T(8,128)} %copy-done.6) | copy-start | bytes 3145732
  665.9 423.1 %all-gather.27.cloned.1.call-start = ((), (), s32[]{:S(2)}) async-start(), calls=%async_computation.13 | async-start | bytes 8912896 | tf_op jit(solution)/shard_map/all_gather | solution.py:294
  667.2 514.9 %all-gather.29.cloned.1.call-start = ((), (), s32[]{:S(2)}) async-start(), calls=%async_computation.14 | async-start | bytes 8912896 | tf_op jit(solution)/shard_map/all_gather | solution.py:295
  1015.2 85.4 %copy-start.8 = (f32[128,2048]{1,0:T(8,128)}, f32[128,2048]{1,0:T(8,128)S(1)}, u32[]{:S(2)}) copy-start(f32[128,2048]{1,0:T(8,128)S(1)} %get-tuple-element.1090) | copy-start | bytes 3145732
  1023.1 988.4 %reduce-scatter.8.cloned.1.call-start = ((), (), s32[]{:S(2)}) async-start(), calls=%async_computation.15 | async-start | bytes 71303168 | tf_op jit(solution)/shard_map/reduce_scatter | solution.py:320
  1089.0 33.1 %copy-start.11 = (bf16[128,2048]{1,0:T(8,128)(2,1)S(1)}, bf16[128,2048]{1,0:T(8,128)(2,1)}, u32[]{:S(2)}) copy-start(bf16[128,2048]{1,0:T(8,128)(2,1)} %get-tuple-element.1107) | copy-start | bytes 1572868
  1182.1 13.8 copy-start.5
  1182.1 13.8 copy-start.20
  1195.9 117.4 %copy-start.26 = (f32[128,64]{0,1:T(8,128)S(1)}, f32[128,64]{0,1:T(8,128)}, u32[]{:S(2)}) copy-start(f32[128,64]{0,1:T(8,128)} %copy-done.25) | copy-start | bytes 98308
  1311.8 3.4 copy-start.3
  1311.9 3.4 copy-start.22
  1311.9 3.4 copy-start.28
  1315.3 2.4 copy-start.24
  1376.2 1019.5 %all-reduce.4.cloned.1.call-start = ((), (), s32[]{:S(2)}) async-start(), calls=%async_computation.16 | async-start | bytes 33554432 | tf_op jit(solution)/shard_map/psum | solution.py:335
  1376.2 11.6 copy-start.17
  1376.2 23.0 slice-start.2
  1387.8 11.4 slice-start.3
  1387.8 11.4 copy-start.35
  2011.5 14.0 slice-start
  2018.0 7.5 slice-start.1
  2025.5 3.1 copy-start.29
  2025.6 42.1 %copy-start.9 = (f32[128,2048]{1,0:T(8,128)S(1)}, f32[128,2048]{1,0:T(8,128)}, u32[]{:S(2)}) copy-start(f32[128,2048]{1,0:T(8,128)} %copy-done.8) | copy-start | bytes 3145732
  2405.5 5.0 copy-start.13
  2405.5 7.1 copy-start.12
  2405.5 9.1 copy-start.1
Sparse Core Ops, SparseCore 0:
  10.2 77.5 all-gather.16
  90.0 73.1 all-gather.10
  165.3 73.1 all-gather.14
  241.1 73.1 all-gather.18
  316.8 73.1 all-gather.12
  392.0 73.1 all-gather.20
  472.2 73.1 all-gather.22
  548.1 73.1 all-gather.24
  653.9 176.8 reduce-scatter.5
  834.7 177.5 reduce-scatter.3
  1015.1 73.9 all-gather.26
  1091.1 76.0 all-gather.28
  1376.3 635.1 reduce-scatter.7
  2014.6 381.0 all-reduce.3
where the time goes:
time: 2430 us; the launch traced here: 2420 us
  waiting for transfers between devices  1820 us (75%)
  matrix products  270 us (11%)
  local copies, waits for them, and re-layouts  149 us (6%)
  blocking collectives  79.4 us (3%)
  other arithmetic  67.5 us (3%)
    reduce_scatter x1, waiting for transfers between devices, shards(): lax.psum_scatter(jnp.concatenate([contract_rows(norm_one, query_lin_back)...  606 us
    psum x1, waiting for transfers between devices, shards(): summed = lax.psum((attention_part, gate_part, up_part, down_part), 'narrow')  327 us
    reduce_scatter x1, waiting for transfers between devices, shards(): lax.psum_scatter(jnp.dot(hidden, w_down, preferred_element_type=jnp.float...  179 us
    reduce_scatter x1, waiting for transfers between devices, shards(): lax.psum_scatter(jnp.dot(gate_back, w_gate, preferred_element_type=jnp.fl...  163 us
    all_gather x1, waiting for transfers between devices, shards(): lax.all_gather(w_value, 'wide', axis=0, tiled=True)  76.4 us
    all_gather x1, waiting for transfers between devices, shards(): group_norm = lax.all_gather(norm_two, 'wide', axis=0, tiled=True)  70.5 us
    all_gather x1, waiting for transfers between devices, shards(): lax.all_gather(query_wire, 'wide', axis=0, tiled=True)  65.9 us
    all_gather x1, waiting for transfers between devices, shards(): lax.all_gather(key_flat, 'wide', axis=0, tiled=True)  64.2 us
  transfers between devices with their start and end apart: 14, of which 13 were waited for; matrix products, arithmetic and copies ran while one was open for 10% of the time, Pallas kernels for 0%

commit v1 on v0

v1 whole, which is shorter than its diff:
```python
import functools
import jax
import jax.numpy as jnp
from jax import lax
from jax.experimental import pallas as pl
from jax.experimental.pallas import tpu as pltpu
import numpy as np
from jax.sharding import PartitionSpec as P

HEAD_DIM = 64
NEGATIVE = -1e30
VMEM_LIMIT = 56 * 1024 * 1024


def dot_nt(a, b):
    return lax.dot_general(a, b, (((1,), (1,)), ((), ())), preferred_element_type=jnp.float32)


def dot_nn(a, b):
    return lax.dot_general(a, b, (((1,), (0,)), ((), ())), preferred_element_type=jnp.float32)


def half_turn(tensor):
    width = tensor.shape[-1]
    half_dim = HEAD_DIM // 2
    lane = lax.broadcasted_iota(jnp.int32, tensor.shape, 1)
    return jnp.where(
        lane % HEAD_DIM < half_dim,
        -pltpu.roll(tensor, width - half_dim, 1),
        pltpu.roll(tensor, half_dim, 1),
    )


def head_lanes(block, head):
    lane = lax.broadcasted_iota(jnp.int32, block.shape, 1)
    return jnp.where(lane // HEAD_DIM == head, block, jnp.zeros_like(block))


def forward_kernel(
    slot_ref, length_ref, lin_ref, cos_ref, sin_ref,
    att_ref, query_ref, key_ref, value_ref, log_ref,
    turned, attn_nat,
):
    rows = query_ref.shape[0]
    width = query_ref.shape[1]
    heads = width // HEAD_DIM
    slots = slot_ref.shape[0]
    shard = rows // slots
    length = length_ref[0]
    scale = HEAD_DIM ** (-0.5)

    @pl.loop(0, slots)
    def _(place):
        source = pl.ds(pl.multiple_of(slot_ref[place] * shard, shard), shard)
        target = pl.ds(pl.multiple_of(place * shard, shard), shard)
        cosine = cos_ref[target, :]
        sine = sin_ref[target, :]
        query_lin = lin_ref[source, 0:width]
        key_lin = lin_ref[source, width : 2 * width]
        value_lin = lin_ref[source, 2 * width : 3 * width]
        query = (query_lin * cosine + half_turn(query_lin) * sine).astype(jnp.bfloat16)
        query_ref[target, :] = (query.astype(jnp.float32) * scale).astype(jnp.bfloat16)
        key_ref[target, :] = (key_lin * cosine + half_turn(key_lin) * sine).astype(jnp.bfloat16)
        value_ref[target, :] = value_lin.astype(jnp.bfloat16)
        turned[:, target] = value_lin.T.astype(jnp.bfloat16)

    block_q = min(256, rows)
    block_k = min(512, rows)

    @pl.loop(0, rows // block_q)
    def _(i):
        q_first = pl.multiple_of(i * block_q, block_q)
        query = query_ref[pl.ds(q_first, block_q), :]
        parts = [head_lanes(query, h) for h in range(heads)]
        q_pos = q_first + lax.broadcasted_iota(jnp.int32, (1, block_q), 1)
        limit = jnp.minimum(q_pos, length - 1)
        full = jnp.minimum(q_first, length) // block_k
        stop = (jnp.minimum(q_first + block_q, length) + block_k - 1) // block_k

        def step(j, state, masked):
            k_first = pl.multiple_of(j * block_k, block_k)
            key = key_ref[pl.ds(k_first, block_k), :]
            out = []
            if masked:
                k_pos = k_first + lax.broadcasted_iota(jnp.int32, (block_k, block_q), 0)
                allowed = k_pos <= limit
            for h in range(heads):
                best, total, acc = state[3 * h : 3 * h + 3]
                scores = dot_nt(key, parts[h])
                if masked:
                    scores = jnp.where(allowed, scores, NEGATIVE)
                new_best = jnp.maximum(best, jnp.max(scores, axis=0, keepdims=True))
                weight = jnp.exp(scores - new_best)
                shrink = jnp.exp(best - new_best)
                total = total * shrink + jnp.sum(weight, axis=0, keepdims=True)
                value_t = turned[h * HEAD_DIM : (h + 1) * HEAD_DIM, pl.ds(k_first, block_k)]
                acc = acc * shrink + dot_nn(value_t, weight.astype(jnp.bfloat16))
                out += [new_best, total, acc]
            return tuple(out)

        state = ()
        for h in range(heads):
            state += (
                jnp.full((1, block_q), NEGATIVE, jnp.float32),
                jnp.zeros((1, block_q), jnp.float32),
                jnp.zeros((HEAD_DIM, block_q), jnp.float32),
            )
        state = lax.fori_loop(0, full, functools.partial(step, masked=False), state)
        state = lax.fori_loop(full, stop, functools.partial(step, masked=True), state)
        for h in range(heads):
            best, total, acc = state[3 * h : 3 * h + 3]
            log_ref[h : h + 1, pl.ds(q_first, block_q)] = best + jnp.log(total)
        joined = jnp.concatenate([state[3 * h + 2] / state[3 * h + 1] for h in range(heads)], axis=0)
        attn_nat[pl.ds(q_first, block_q), :] = joined.T.astype(jnp.bfloat16)

    @pl.loop(0, slots)
    def _(place):
        source = pl.ds(pl.multiple_of(slot_ref[place] * shard, shard), shard)
        target = pl.ds(pl.multiple_of(place * shard, shard), shard)
        att_ref[source, :] = attn_nat[target, :]


def attention_forward(slot_of, length, lin, cosine, sine):
    rows, width = cosine.shape
    vmem = pl.BlockSpec(memory_space=pltpu.VMEM)
    smem = pl.BlockSpec(memory_space=pltpu.SMEM)
    half = jax.ShapeDtypeStruct((rows, width), jnp.bfloat16)
    return pl.pallas_call(
        forward_kernel,
        out_shape=(half, half, half, half, jax.ShapeDtypeStruct((8, rows), jnp.float32)),
        in_specs=[smem, smem, vmem, vmem, vmem],
        out_specs=(vmem,) * 5,
        scratch_shapes=[
            pltpu.VMEM((width, rows), jnp.bfloat16),
            pltpu.VMEM((rows, width), jnp.bfloat16),
        ],
        compiler_params=pltpu.CompilerParams(vmem_limit_bytes=VMEM_LIMIT),
        cost_estimate=pl.CostEstimate(
            flops=4 * rows * rows * width, bytes_accessed=24 * rows * width, transcendentals=rows * rows
        ),
        name="attention_forward",
    )(slot_of, length, lin, cosine, sine)


def backward_kernel(
    slot_ref, length_ref, query_ref, key_ref, value_ref, att_ref, up_ref, log_ref, cos_ref, sin_ref,
    out_ref,
    key_t, up_nat, delta, key_acc, value_acc, query_acc,
):
    rows = query_ref.shape[0]
    width = query_ref.shape[1]
    heads = width // HEAD_DIM
    slots = slot_ref.shape[0]
    shard = rows // slots
    length = length_ref[0]
    scale = HEAD_DIM ** (-0.5)
    key_acc[...] = jnp.zeros_like(key_acc)
    value_acc[...] = jnp.zeros_like(value_acc)

    @pl.loop(0, slots)
    def _(place):
        source = pl.ds(pl.multiple_of(slot_ref[place] * shard, shard), shard)
        target = pl.ds(pl.multiple_of(place * shard, shard), shard)
        upstream = up_ref[source, :]
        up_nat[target, :] = upstream
        product = (upstream.astype(jnp.float32) * att_ref[source, :].astype(jnp.float32)).T
        for h in range(heads):
            delta[h : h + 1, target] = jnp.sum(
                product[h * HEAD_DIM : (h + 1) * HEAD_DIM, :], axis=0, keepdims=True
            )
        key_t[:, target] = key_ref[target, :].astype(jnp.float32).T.astype(jnp.bfloat16)

    block_q = min(256, rows)
    block_k = min(512, rows)

    @pl.loop(0, rows // block_q)
    def _(i):
        q_first = pl.multiple_of(i * block_q, block_q)
        here = pl.ds(q_first, block_q)
        query = query_ref[here, :]
        upstream = up_nat[here, :]
        q_parts = [head_lanes(query, h) for h in range(heads)]
        u_parts = [head_lanes(upstream, h) for h in range(heads)]
        logs = [log_ref[h : h + 1, here] for h in range(heads)]
        deltas = [delta[h : h + 1, here] for h in range(heads)]
        q_pos = q_first + lax.broadcasted_iota(jnp.int32, (1, block_q), 1)
        limit = jnp.minimum(q_pos, length - 1)
        full = jnp.minimum(q_first, length) // block_k
        stop = (jnp.minimum(q_first + block_q, length) + block_k - 1) // block_k

        def step(j, state, masked):
            k_first = pl.multiple_of(j * block_k, block_k)
            there = pl.ds(k_first, block_k)
            key = key_ref[there, :]
            value = value_ref[there, :]
            if masked:
                k_pos = k_first + lax.broadcasted_iota(jnp.int32, (block_k, block_q), 0)
                allowed = k_pos <= limit
            out = []
            key_add = None
            for h in range(heads):
                prob = jnp.exp(dot_nt(key, q_parts[h]) - logs[h])
                if masked:
                    prob = jnp.where(allowed, prob, 0.0)
                pulled = dot_nt(value, u_parts[h])
                score_back = (prob * (pulled - deltas[h])).astype(jnp.bfloat16)
                one = dot_nn(prob.astype(jnp.bfloat16), u_parts[h])
                two = dot_nn(score_back, q_parts[h])
                value_add = one if key_add is None else value_add + one
                key_add = two if key_add is None else key_add + two
                out.append(
                    state[h] + dot_nn(key_t[h * HEAD_DIM : (h + 1) * HEAD_DIM, there], score_back)
                )
            value_acc[there, :] += value_add
            key_acc[there, :] += key_add
            return tuple(out)

        state = tuple(jnp.zeros((HEAD_DIM, block_q), jnp.float32) for h in range(heads))
        state = lax.fori_loop(0, full, functools.partial(step, masked=False), state)
        state = lax.fori_loop(full, stop, functools.partial(step, masked=True), state)
        query_acc[here, :] = (jnp.concatenate(state, axis=0) * scale).T

    @pl.loop(0, slots)
    def _(place):
        source = pl.ds(pl.multiple_of(slot_ref[place] * shard, shard), shard)
        target = pl.ds(pl.multiple_of(place * shard, shard), shard)
        cosine = cos_ref[target, :]
        sine = sin_ref[target, :]
        for piece, held in enumerate((query_acc, key_acc)):
            grad = held[target, :]
            out_ref[source, piece * width : (piece + 1) * width] = (
                grad * cosine - half_turn(grad * sine)
            ).astype(jnp.bfloat16)
        out_ref[source, 2 * width : 3 * width] = value_acc[target, :].astype(jnp.bfloat16)


def attention_backward(slot_of, length, query, key, value, att, upstream, logs, cosine, sine):
    rows, width = query.shape
    vmem = pl.BlockSpec(memory_space=pltpu.VMEM)
    smem = pl.BlockSpec(memory_space=pltpu.SMEM)
    return pl.pallas_call(
        backward_kernel,
        out_shape=jax.ShapeDtypeStruct((rows, 3 * width), jnp.bfloat16),
        in_specs=[smem, smem] + [vmem] * 8,
        out_specs=vmem,
        scratch_shapes=[
            pltpu.VMEM((width, rows), jnp.bfloat16),
            pltpu.VMEM((rows, width), jnp.bfloat16),
            pltpu.VMEM((8, rows), jnp.float32),
            pltpu.VMEM((rows, width), jnp.float32),
            pltpu.VMEM((rows, width), jnp.float32),
            pltpu.VMEM((rows, width), jnp.float32),
        ],
        compiler_params=pltpu.CompilerParams(vmem_limit_bytes=VMEM_LIMIT),
        cost_estimate=pl.CostEstimate(
            flops=10 * rows * rows * width, bytes_accessed=36 * rows * width, transcendentals=rows * rows
        ),
        name="attention_backward",
    )(slot_of, length, query, key, value, att, upstream, logs, cosine, sine)


EPSILON = 1e-05
THETA = 130000.0


def contract_rows(left_side, right_side):
    return lax.dot_general(
        left_side, right_side, (((0,), (0,)), ((), ())), preferred_element_type=jnp.float32
    )


def rotary_tables(row_count, width):
    half_dim = HEAD_DIM // 2
    frequency = THETA ** (-jnp.arange(half_dim, dtype=jnp.float32) * 2.0 / HEAD_DIM)
    angles = jnp.arange(row_count, dtype=jnp.float32)[:, None] * frequency[None, :]
    copies = width // half_dim
    return (jnp.tile(jnp.cos(angles), (1, copies)), jnp.tile(jnp.sin(angles), (1, copies)))


def rms_factor(matrix):
    return lax.rsqrt(jnp.mean(matrix * matrix, axis=-1, keepdims=True) + EPSILON)


def norm_back(upstream, normed, gain_vec, factor):
    scaled = upstream * gain_vec
    return factor * (scaled - normed * jnp.mean(scaled * normed, axis=-1, keepdims=True))


def swiglu_back(hidden_back, gate_proj, up_proj):
    sigmoid_gate = jax.nn.sigmoid(gate_proj)
    gate_back = hidden_back * up_proj * sigmoid_gate * (1.0 + gate_proj * (1.0 - sigmoid_gate))
    up_back = hidden_back * jax.nn.silu(gate_proj)
    return (gate_back.astype(jnp.bfloat16), up_back.astype(jnp.bfloat16))


class Ring:
    def __init__(self, size):
        self.size = size
        self.pairs = size // 2
        self.reach = self.pairs // 2
        columns = self.pairs // 2
        self.order = [2 * a for a in range(columns)] + [2 * a + 1 for a in reversed(range(columns))]
        self.ahead = []
        self.behind = []
        for place, pair in enumerate(self.order):
            following = self.order[(place + 1) % self.pairs]
            for lane in range(2):
                self.ahead.append((2 * pair + lane, 2 * following + lane))
                self.behind.append((2 * following + lane, 2 * pair + lane))
        self.across = [(device, device ^ 1) for device in range(size)]

    def slots(self):
        offsets = [(0, 0), (0, 1)]
        for step in range(1, self.reach):
            offsets += [(-step, 0), (step, 0), (-step, 1), (step, 1)]
        offsets += [(self.reach, 0), (self.reach, 1)]
        table = np.zeros((self.size, self.size), np.int32)
        for device in range(self.size):
            place = self.order.index(device // 2)
            for slot, (offset, flip) in enumerate(offsets):
                pair = self.order[(place + offset) % self.pairs]
                table[device, 2 * pair + (device % 2 ^ flip)] = slot
        return table

    def forward(self, array):
        return lax.ppermute(array, "wide", self.ahead)

    def backward(self, array):
        return lax.ppermute(array, "wide", self.behind)

    def twin(self, array):
        return lax.ppermute(array, "wide", self.across)

    def gather(self, rows):
        groups = [[rows, self.twin(rows)]]
        ahead = behind = rows
        middle = rows.shape[0] // 2
        for step in range(1, self.reach + 1):
            if step == self.reach:
                ahead, behind = ahead[:middle], behind[middle:]
            ahead, behind = self.forward(ahead), self.backward(behind)
            groups.append([ahead, behind, self.twin(ahead), self.twin(behind)])
        return [jnp.concatenate(group, axis=0) for group in groups]

    def scatter(self, make):
        sums = [None] * (self.reach + 1)
        down = up = None
        for step in range(self.reach, -1, -1):
            mine, other = make(step)
            total = mine + self.twin(other.astype(jnp.bfloat16)).astype(jnp.float32)
            count = total.shape[0] // 2
            if step == 0:
                return total + down.astype(jnp.float32) + up.astype(jnp.float32)
            low, high = total[:count], total[count:]
            if step == self.reach - 1:
                middle = count // 2
                low = jnp.concatenate([low[:middle] + down.astype(jnp.float32), low[middle:]], axis=0)
                high = jnp.concatenate([high[:middle], high[middle:] + up.astype(jnp.float32)], axis=0)
            elif step < self.reach - 1:
                low = low + down.astype(jnp.float32)
                high = high + up.astype(jnp.float32)
            down = self.backward(low.astype(jnp.bfloat16))
            up = self.forward(high.astype(jnp.bfloat16))

    def total(self, array):
        array = array + lax.ppermute(array, "narrow", [(0, 1), (1, 0)])
        bit = 1
        while bit < self.size:
            array = array + lax.ppermute(array, "wide", [(i, i ^ bit) for i in range(self.size)])
            bit *= 2
        return array


def both_sequences(part):
    part = lax.optimization_barrier(part.astype(jnp.bfloat16))
    return part.astype(jnp.float32) + lax.ppermute(part, "narrow", [(0, 1), (1, 0)]).astype(
        jnp.float32
    )


def halves(array):
    middle = array.shape[0] // 2
    return array[:middle], array[middle:]


def shards(
    ring,
    layer_input,
    lengths,
    attn_gain,
    w_query,
    w_key,
    w_value,
    w_out,
    mlp_gain,
    w_gate,
    w_up,
    w_down,
    cotangent,
):
    size = ring.size
    local_rows = layer_input.shape[1]
    model_width = layer_input.shape[2]
    row_count = local_rows * size
    own_width = model_width // size
    width = max(own_width, 2 * HEAD_DIM)
    sharing = width // own_width
    device = lax.axis_index("wide")
    member = device % sharing
    slot_of = lax.dynamic_index_in_dim(jnp.asarray(ring.slots()), device, keepdims=False)

    def own_columns(array):
        if sharing == 1:
            return array
        runs = array.reshape(array.shape[0], -1, sharing, own_width)
        return lax.dynamic_index_in_dim(runs, member, axis=2, keepdims=False).reshape(
            array.shape[0], -1
        )

    positions = device * local_rows + jnp.arange(local_rows, dtype=jnp.int32)
    valid_rows = (positions < lengths[0]).astype(jnp.float32)[:, None]
    cosine, sine = rotary_tables(row_count, width)
    inputs = layer_input[0].astype(jnp.float32)
    gain_one = attn_gain.astype(jnp.float32)
    gain_two = mlp_gain.astype(jnp.float32)
    y_back = cotangent[0].astype(jnp.float32) * valid_rows
    mlp_back = y_back.astype(jnp.bfloat16)

    blocks = jnp.concatenate(
        [w.reshape(own_width, -1, width) for w in (w_query, w_key, w_value)], axis=-1
    ).transpose(1, 0, 2)
    blocks = jnp.repeat(blocks, sharing, axis=0)
    w_heads = lax.all_to_all(blocks, "wide", 0, 0, tiled=True).reshape(model_width, 3 * width)
    w_out_heads = w_out
    if sharing > 1:
        near = [list(range(a, a + sharing)) for a in range(0, size, sharing)]
        w_out_heads = lax.all_gather(w_out, "wide", axis=0, tiled=True, axis_index_groups=near)

    factor_one = rms_factor(inputs)
    normed_one = inputs * factor_one
    norm_one = (normed_one * gain_one).astype(jnp.bfloat16)
    group_one = ring.gather(norm_one)
    lin = jnp.concatenate([dot_nn(rows, w_heads) for rows in group_one], axis=0)
    heads_attention, query, key, value, logs = attention_forward(
        slot_of, lengths, lin, cosine, sine
    )
    attention = own_columns(heads_attention)
    starts = [0]
    for rows in group_one:
        starts.append(starts[-1] + rows.shape[0])

    def group_of(array, step):
        return array[starts[step] : starts[step + 1]]

    def residual_part(step):
        mine, other = halves(group_of(attention, step))
        return dot_nn(mine, w_out), dot_nn(other, w_out)

    residual = inputs + ring.scatter(residual_part)
    factor_two = rms_factor(residual)
    normed_two = residual * factor_two
    norm_two = (normed_two * gain_two).astype(jnp.bfloat16)
    group_back = ring.gather(mlp_back)
    group_two = ring.gather(norm_two)
    w_both = jnp.concatenate([w_gate, w_up], axis=0)
    units = w_gate.shape[0]
    hidden = []
    both_back = []
    for rows, back in zip(group_two, group_back):
        both = dot_nt(rows, w_both)
        gate_proj, up_proj = both[:, :units], both[:, units:]
        hidden.append((jax.nn.silu(gate_proj) * up_proj).astype(jnp.bfloat16))
        both_back.append(
            jnp.concatenate(swiglu_back(dot_nt(back, w_down), gate_proj, up_proj), axis=1)
        )

    def pull_part(step):
        mine, other = halves(both_back[step])
        return dot_nn(mine, w_both), dot_nn(other, w_both)

    def mlp_part(step):
        mine, other = halves(hidden[step])
        return dot_nn(mine, w_down), dot_nn(other, w_down)

    norm_two_back = ring.scatter(pull_part)
    residual_back = y_back + norm_back(norm_two_back, normed_two, gain_two, factor_two)
    gain_two_term = jnp.sum(norm_two_back * normed_two, axis=0)
    branch_back = residual_back.astype(jnp.bfloat16)
    group_branch = ring.gather(branch_back)
    upstream = jnp.concatenate(
        [dot_nt(rows, w_out_heads).astype(jnp.bfloat16) for rows in group_branch], axis=0
    )
    mlp_out = ring.scatter(mlp_part)
    block_output = (residual + mlp_out).astype(jnp.bfloat16)

    all_two = jnp.concatenate(group_two, axis=0)
    both_sum = both_sequences(contract_rows(jnp.concatenate(both_back, axis=0), all_two))
    down_sum = both_sequences(
        contract_rows(jnp.concatenate(hidden, axis=0), jnp.concatenate(group_back, axis=0))
    )
    out_sum = both_sequences(contract_rows(attention, jnp.concatenate(group_branch, axis=0)))

    lin_back = own_columns(
        attention_backward(
            slot_of, lengths, query, key, value, heads_attention, upstream, logs, cosine, sine
        )
    )
    w_own = own_columns(w_heads)

    def input_part(step):
        mine, other = halves(group_of(lin_back, step))
        return dot_nt(mine, w_own), dot_nt(other, w_own)

    heads_part = contract_rows(jnp.concatenate(group_one, axis=0), lin_back)
    gain_one_term = jnp.sum(heads_part * w_own.astype(jnp.float32), axis=1) / gain_one
    gain_totals = ring.total(jnp.stack([gain_one_term, gain_two_term]))
    heads_sum = both_sequences(heads_part).astype(jnp.bfloat16).reshape(size, own_width, 3 * own_width)
    heads_sum = lax.all_to_all(heads_sum, "wide", 0, 0, tiled=True).astype(jnp.float32)
    attention_sums = [
        heads_sum[:, :, piece * own_width : (piece + 1) * own_width]
        .transpose(1, 0, 2)
        .reshape(own_width, model_width)
        for piece in range(3)
    ]
    norm_one_back = ring.scatter(input_part)
    input_back = residual_back + norm_back(norm_one_back, normed_one, gain_one, factor_one)
    return (
        block_output[None],
        input_back[None],
        gain_totals[0],
        attention_sums[0],
        attention_sums[1],
        attention_sums[2],
        out_sum,
        gain_totals[1],
        both_sum[:units],
        both_sum[units:],
        down_sum,
    )


def solution(mesh):
    placed = (
        P("narrow", "wide", None),
        P("narrow"),
        P(),
        P("wide", None),
        P("wide", None),
        P("wide", None),
        P("wide", None),
        P(),
        P("wide", None),
        P("wide", None),
        P("wide", None),
        P("narrow", "wide", None),
    )
    return jax.shard_map(
        functools.partial(shards, Ring(mesh.shape["wide"])),
        mesh=mesh,
        in_specs=placed,
        out_specs=(
            P("narrow", "wide", None),
            P("narrow", "wide", None),
            P(),
            P("wide", None),
            P("wide", None),
            P("wide", None),
            P("wide", None),
            P(),
            P("wide", None),
            P("wide", None),
            P("wide", None),
        ),
        check_vma=False,
    )
```

time: 2430 us -> 692 us (0.28)
  waiting for transfers between devices: 1820 us -> 243 us
  matrix products: 270 us -> 115 us
  starting transfers between devices: 0.92 us -> 127 us
  blocking collectives: 79.4 us -> 0 us
  Pallas kernels: 0 us -> 54.5 us
  local copies, waits for them, and re-layouts: 149 us -> 96.4 us
  other arithmetic: 67.5 us -> 38.2 us
    reduce_scatter x3 -> x0, waiting for transfers between devices: 948 us -> none  [the longest x1 606 us: shards(): lax.psum_scatter(jnp.concatenate([contract_rows(norm_one, query_lin_back)...]
    all_gather x10 -> x0, waiting for transfers between devices: 547 us -> none  [the longest x1 76.4 us: shards(): lax.all_gather(w_value, 'wide', axis=0, tiled=True)]
    psum x1 -> x0, waiting for transfers between devices: 327 us -> none  [shards(): summed = lax.psum((attention_part, gate_part, up_part, down_part), 'narrow')]
    ppermute x0 -> x129, waiting for transfers between devices: none -> 243 us  [the longest x32 119 us: backward(): return lax.ppermute(array, 'wide', self.behind)]
    dot_general x30 -> x60, matrix products: 213 us -> 85.3 us  [the longest x25 48.5 us: dot_nt(): lax.dot_general(a, b, (((1,), (1,)), ((), ())), preferred_element_type=jn...]
    ppermute x0 -> x129, starting transfers between devices: none -> 116 us  [the longest x32 55.4 us: forward(): return lax.ppermute(array, 'wide', self.ahead)]
    pallas_call x0 -> x2, Pallas kernels: none -> 54.5 us  [the longest x1 27.4 us: attention_forward(): pl.pallas_call(forward_kernel, out_shape=(half, half, half, half, jax.Sha...]
    all_gather x2 -> x0, blocking collectives: 40.4 us -> none  [the longest x1 20.8 us: shards(): lax.all_gather(log_total.T, 'wide', axis=0, tiled=True)]
  transfers between devices with their start and end apart: 14 -> 131, of which waited for: 13 -> 41; matrix products, arithmetic and copies ran while one was open for 10% -> 32% of each run, Pallas kernels for 0% -> 4%
where the time goes in v1:
time: 692 us; the launch traced here: 678 us
  waiting for transfers between devices  243 us (35%)
  starting transfers between devices  127 us (18%)
  matrix products  115 us (17%)
  local copies, waits for them, and re-layouts  96.4 us (14%)
  Pallas kernels  54.5 us (8%)
  other arithmetic  38.2 us (6%)
    ppermute x32, waiting for transfers between devices, backward(): return lax.ppermute(array, 'wide', self.behind)  119 us
    unnamed x201, local copies, waits for them, and re-layouts  72.6 us
    ppermute x32, waiting for transfers between devices, forward(): return lax.ppermute(array, 'wide', self.ahead)  67.4 us
    ppermute x32, starting transfers between devices, forward(): return lax.ppermute(array, 'wide', self.ahead)  55.4 us
    ppermute x4, waiting for transfers between devices, both_sequences(): lax.ppermute(part, 'narrow', [(0, 1), (1, 0)]).astype(jnp.float32)  53.5 us
    dot_general x25, matrix products, dot_nt(): lax.dot_general(a, b, (((1,), (1,)), ((), ())), preferred_element_type=jn...  48.5 us
    ppermute x32, starting transfers between devices, backward(): return lax.ppermute(array, 'wide', self.behind)  41.2 us
    dot_general x35, matrix products, dot_nn(): lax.dot_general(a, b, (((1,), (0,)), ((), ())), preferred_element_type=jn...  36.7 us
  transfers between devices with their start and end apart: 131, of which 41 were waited for; matrix products, arithmetic and copies ran while one was open for 32% of the time, Pallas kernels for 4%

profile of v1, /device:TPU:0, one launch (start us, length us, event | category | flops | bytes accessed | tf_op | source)
XLA Modules:
  0.0 677.8 jit_solution(8583149230969567646)
XLA Ops:
  5.0 2.9 collective-permute-start.2
  16.6 2.3 maximum_bitcast_fusion
  18.9 6.4 all-to-all-start
  26.4 3.2 constant_dynamic-update-slice_fusion.1
  31.8 2.5 copy.57.sin_ref
  35.4 2.5 copy.56.cos_ref
  37.9 3.2 constant_dynamic-update-slice_fusion
  58.4 10.3 %collective-permute-done.6 = bf16[128,2048]{1,0:T(8,128)(2,1)S(1)} collective-permute-done((bf16[128,2048]{1,0:T(8,128)(2,1)}, bf16[128,2048]{1,0:T(8,128)(2,1)S(1)}, u32[]{:S(2)}, u32[]{:S(2)}) %collective-permute-start.6) | collective-permute-done | bytes 524320 | tf_op jit(solution)/shard_map/ppermute | solution.py:329
  68.7 10.5 %collective-permute-start.67 = (bf16[128,2048]{1,0:T(8,128)(2,1)}, bf16[128,2048]{1,0:T(8,128)(2,1)S(1)}, u32[]{:S(2)}, u32[]{:S(2)}) collective-permute-start(bf16[128,2048]{1,0:T(8,128)(2,1)} %collective-permute-done.62), channel_id=1, source_target_pairs={{0,4},{1,5},{4,8},{5,9},{8,12},{9,13},{12,14},{13,15},{14,10},{15,... | collective-permute-start | bytes 1572872 | tf_op jit(solution)/shard_map/ppermute | solution.py:326
  83.3 7.2 %collective-permute-start.9 = (bf16[128,2048]{1,0:T(8,128)(2,1)S(1)}, bf16[128,2048]{1,0:T(8,128)(2,1)S(1)}, u32[]{:S(2)}, u32[]{:S(2)}) collective-permute-start(bf16[128,2048]{1,0:T(8,128)(2,1)S(1)} %collective-permute-done.5), channel_id=1, source_target_pairs={{0,4},{1,5},{4,8},{5,9},{8,12},{9,13},{12,14},{13,15},{14,10},{15,... | collective-permute-start | bytes 1572872 | tf_op jit(solution)/shard_map/ppermute | solution.py:326
  94.6 7.1 %collective-permute-start.72 = (bf16[128,2048]{1,0:T(8,128)(2,1)S(1)}, bf16[128,2048]{1,0:T(8,128)(2,1)S(1)}, u32[]{:S(2)}, u32[]{:S(2)}) collective-permute-start(bf16[128,2048]{1,0:T(8,128)(2,1)S(1)} %collective-permute-done.67), channel_id=1, source_target_pairs={{0,4},{1,5},{4,8},{5,9},{8,12},{9,13},{12,14},{13,15},{14,10},{15,... | collective-permute-start | bytes 1572872 | tf_op jit(solution)/shard_map/ppermute | solution.py:326
  103.6 9.3 %collective-permute-start.13 = (bf16[64,2048]{1,0:T(8,128)(2,1)S(1)}, bf16[64,2048]{1,0:T(8,128)(2,1)}, u32[]{:S(2)}, u32[]{:S(2)}) collective-permute-start(bf16[64,2048]{1,0:T(8,128)(2,1)S(1)} %slice.490), channel_id=1, source_target_pairs={{0,4},{1,5},{4,8},{5,9},{8,12},{9,13},{12,14},{13,15},{14,10},{15,... | collective-permute-start | bytes 786440 | tf_op jit(solution)/shard_map/ppermute | solution.py:326
  128.8 2.5 fusion.143
  131.4 3.1 fusion.138
  134.6 2.8 fusion.133
  137.5 2.7 fusion.128
  140.2 2.5 fusion.146.lin_ref
  144.3 27.4 %attention_forward.1 = (bf16[2048,128]{1,0:T(8,128)(2,1)}, bf16[2048,128]{1,0:T(8,128)(2,1)}, bf16[2048,128]{1,0:T(8,128)(2,1)}, bf16[2048,128]{1,0:T(8,128)(2,1)}, f32[8,2048]{1,0:T(8,128)}) custom-call(s32[16]{0:T(128)} %dynamic-slice_bitcast_fusion.slot_ref, s32[1]{0:T(128)} %copy.226.length_ref, f32[2048,384]{1,0:T(8,128)} %copy-done.63, ...), custom_call_target="tpu_custom_call" | custom-call | flops 2147483648 | bytes 6291456 | tf_op jit(solution)/shard_map/attention_forward/pallas_call | solution.py:128
  179.9 6.3 collective-permute-done.22
  190.7 10.3 %collective-permute-done.27 = bf16[128,2048]{1,0:T(8,128)(2,1)S(1)} collective-permute-done((bf16[128,2048]{1,0:T(8,128)(2,1)S(1)}, bf16[128,2048]{1,0:T(8,128)(2,1)S(1)}, u32[]{:S(2)}, u32[]{:S(2)}) %collective-permute-start.27) | collective-permute-done | bytes 524320 | tf_op jit(solution)/shard_map/ppermute | solution.py:326
  204.7 9.3 %collective-permute-done.24 = bf16[128,2048]{1,0:T(8,128)(2,1)S(1)} collective-permute-done((bf16[128,2048]{1,0:T(8,128)(2,1)S(1)}, bf16[128,2048]{1,0:T(8,128)(2,1)S(1)}, u32[]{:S(2)}, u32[]{:S(2)}) %collective-permute-start.24) | collective-permute-done | bytes 524320 | tf_op jit(solution)/shard_map/ppermute | solution.py:329
  221.1 5.3 collective-permute-done.25
  237.4 9.8 %collective-permute-done.33 = bf16[128,2048]{1,0:T(8,128)(2,1)S(1)} collective-permute-done((bf16[128,2048]{1,0:T(8,128)(2,1)S(1)}, bf16[128,2048]{1,0:T(8,128)(2,1)S(1)}, u32[]{:S(2)}, u32[]{:S(2)}) %collective-permute-start.33) | collective-permute-done | bytes 524320 | tf_op jit(solution)/shard_map/ppermute | solution.py:329
  255.5 2.4 fusion.24
  262.2 2.8 multiply_convert_fusion.4
  270.4 3.1 collective-permute-done.43
  275.7 2.4 fusion.32
  281.3 6.6 collective-permute-done.42
  298.5 6.5 collective-permute-done.47
  305.7 2.4 fusion.40
  313.3 8.6 %convolution_convert_fusion.1 = bf16[512,2048]{1,0:T(8,128)(2,1)S(1)} fusion(bf16[2048,512]{1,0:T(8,128)(2,1)S(1)} %copy-done.56, bf16[2048,2048]{1,0:T(8,128)(2,1)} %constant_dynamic-update-slice_fusion.61), kind=kOutput, calls=%fused_computation.5 | convolution fusion | flops 4296015872 | bytes 12582912 | tf_op jit(solution)/shard_map/dot_general | solution.py:267
  344.1 4.2 collective-permute-done.52
  351.1 4.7 collective-permute-done.82
  359.5 9.2 %collective-permute-done.57 = bf16[128,2048]{1,0:T(8,128)(2,1)S(1)} collective-permute-done((bf16[128,2048]{1,0:T(8,128)(2,1)S(1)}, bf16[128,2048]{1,0:T(8,128)(2,1)S(1)}, u32[]{:S(2)}, u32[]{:S(2)}) %collective-permute-start.57) | collective-permute-done | bytes 524320 | tf_op jit(solution)/shard_map/ppermute | solution.py:326
  371.0 9.6 %collective-permute-done.87 = bf16[128,2048]{1,0:T(8,128)(2,1)S(1)} collective-permute-done((bf16[128,2048]{1,0:T(8,128)(2,1)S(1)}, bf16[128,2048]{1,0:T(8,128)(2,1)S(1)}, u32[]{:S(2)}, u32[]{:S(2)}) %collective-permute-start.87) | collective-permute-done | bytes 524320 | tf_op jit(solution)/shard_map/ppermute | solution.py:326
  383.5 9.2 %collective-permute-done.54 = bf16[128,2048]{1,0:T(8,128)(2,1)S(1)} collective-permute-done((bf16[128,2048]{1,0:T(8,128)(2,1)S(1)}, bf16[128,2048]{1,0:T(8,128)(2,1)S(1)}, u32[]{:S(2)}, u32[]{:S(2)}) %collective-permute-start.54) | collective-permute-done | bytes 524320 | tf_op jit(solution)/shard_map/ppermute | solution.py:329
  395.1 9.7 %collective-permute-done.84 = bf16[128,2048]{1,0:T(8,128)(2,1)S(1)} collective-permute-done((bf16[128,2048]{1,0:T(8,128)(2,1)S(1)}, bf16[128,2048]{1,0:T(8,128)(2,1)S(1)}, u32[]{:S(2)}, u32[]{:S(2)}) %collective-permute-start.84) | collective-permute-done | bytes 524320 | tf_op jit(solution)/shard_map/ppermute | solution.py:329
  409.3 11.7 %convolution_convert_fusion = bf16[1024,2048]{1,0:T(8,128)(2,1)S(1)} fusion(bf16[2048,1024]{1,0:T(8,128)(2,1)S(1)} %copy-done.54, bf16[2048,2048]{1,0:T(8,128)(2,1)} %constant_dynamic-update-slice_fusion.38), kind=kOutput, calls=%fused_computation.2 | convolution fusion | flops 8592031744 | bytes 16777216 | tf_op jit(solution)/shard_map/dot_general | solution.py:267
  422.1 3.6 collective-permute-done.85
  431.9 2.8 convert_add_fusion.1
  434.7 5.5 collective-permute-done.92
  443.3 8.8 %collective-permute-done.96 = bf16[128,2048]{1,0:T(8,128)(2,1)S(1)} collective-permute-done((bf16[128,2048]{1,0:T(8,128)(2,1)S(1)}, bf16[128,2048]{1,0:T(8,128)(2,1)S(1)}, u32[]{:S(2)}, u32[]{:S(2)}) %collective-permute-start.96) | collective-permute-done | bytes 524320 | tf_op jit(solution)/shard_map/ppermute | solution.py:329
  454.1 2.4 collective-permute-done.95
  458.8 48.3 %collective-permute-done.127 = bf16[1024,2048]{1,0:T(8,128)(2,1)} collective-permute-done((bf16[1024,2048]{1,0:T(8,128)(2,1)S(1)}, bf16[1024,2048]{1,0:T(8,128)(2,1)}, u32[]{:S(2)}, u32[]{:S(2)}) %collective-permute-start.127) | collective-permute-done | bytes 4194336 | tf_op jit(solution)/shard_map/ppermute | solution.py:376
  507.1 5.4 convert_add_fusion
  512.5 4.0 fusion.401
  520.3 2.4 fusion.161
  530.1 27.1 %attention_backward.1 = bf16[2048,384]{1,0:T(8,128)(2,1)} custom-call(s32[16]{0:T(128)} %dynamic-slice_bitcast_fusion.slot_ref, s32[1]{0:T(128)} %copy.226.length_ref, bf16[2048,128]{1,0:T(8,128)(2,1)} %get-tuple-element.17.query_ref, bf16[2048,128]{1,0:T(8,128)(2,1)} %get-tuple-element.18.key_ref, bf16[2048,128]{1,0:T(8,128)(2,1)} %get-tuple-element.19.value_ref, ...), custom_call_target="tpu_custom_call" | custom-call | flops 5368709120 | bytes 9437184 | tf_op jit(solution)/shard_map/attention_backward/pallas_call | solution.py:241
  557.1 8.0 %fusion.402 = (bf16[2048,384]{0,1:T(8,128)(2,1)S(1)}, f32[2048]{0:T(1024)S(1)}) fusion(bf16[2048,2048]{1,0:T(8,128)(2,1)} %constant_dynamic-update-slice_fusion.2, bf16[2048,384]{1,0:T(8,128)(2,1)} %attention_backward.1, bf16[16,128,384]{1,2,0:T(8,128)(2,1)} %all-to-all-done), kind=kOutput, calls=%fused_computation.552 | convolution fusion | flops 3224369152 | bytes 13115392 | tf_op jit(solution)/shard_map/dot_general | solution.py:267
  577.6 3.1 convolution_convert_fusion.4
  587.3 3.7 collective-permute-done.112
  593.4 2.7 convolution_convert_fusion.16
  598.8 5.0 collective-permute-done.117
  607.9 5.2 collective-permute-done.125
  615.9 4.7 all-to-all-start.1
  620.6 2.5 convert_add_fusion.4
  623.1 6.9 %collective-permute-done.118 = bf16[128,2048]{1,0:T(8,128)(2,1)} collective-permute-done((bf16[128,2048]{1,0:T(8,128)(2,1)}, bf16[128,2048]{1,0:T(8,128)(2,1)}, u32[]{:S(2)}, u32[]{:S(2)}) %collective-permute-start.118) | collective-permute-done | bytes 524320 | tf_op jit(solution)/shard_map/ppermute | solution.py:326
  636.5 23.6 %collective-permute-done.115 = bf16[128,2048]{1,0:T(8,128)(2,1)S(1)} collective-permute-done((bf16[128,2048]{1,0:T(8,128)(2,1)S(1)}, bf16[128,2048]{1,0:T(8,128)(2,1)S(1)}, u32[]{:S(2)}, u32[]{:S(2)}) %collective-permute-start.115) | collective-permute-done | bytes 524320 | tf_op jit(solution)/shard_map/ppermute | solution.py:329
  661.7 2.2 fusion.173
  664.0 2.6 fusion.177
  666.6 3.1 fusion.403
  669.7 2.5 copy.69
  672.3 2.5 copy.68
  674.8 2.5 copy.67
  (553 shorter events, 240.3 us)
Async XLA Ops:
  5.0 36.1 %collective-permute-start.2 = (bf16[128,2048]{1,0:T(8,128)(2,1)}, bf16[128,2048]{1,0:T(8,128)(2,1)}, u32[]{:S(2)}, u32[]{:S(2)}) collective-permute-start(bf16[128,2048]{1,0:T(8,128)(2,1)} %get-tuple-element.52), channel_id=1, source_target_pairs={{4,0},{5,1},{8,4},{9,5},{12,8},{13,9},{14,12},{15,13},{10,14},{11,... | collective-permute-start | bytes 1572872 | tf_op jit(solution)/shard_map/ppermute | solution.py:329
  7.9 37.2 %collective-permute-start.1 = (bf16[128,2048]{1,0:T(8,128)(2,1)}, bf16[128,2048]{1,0:T(8,128)(2,1)}, u32[]{:S(2)}, u32[]{:S(2)}) collective-permute-start(bf16[128,2048]{1,0:T(8,128)(2,1)} %get-tuple-element.52), channel_id=1, source_target_pairs={{0,4},{1,5},{4,8},{5,9},{8,12},{9,13},{12,14},{13,15},{14,10},{15,... | collective-permute-start | bytes 1572872 | tf_op jit(solution)/shard_map/ppermute | solution.py:326
  8.0 33.5 %collective-permute-start = (bf16[128,2048]{1,0:T(8,128)(2,1)}, bf16[128,2048]{1,0:T(8,128)(2,1)}, u32[]{:S(2)}, u32[]{:S(2)}) collective-permute-start(bf16[128,2048]{1,0:T(8,128)(2,1)} %get-tuple-element.52), channel_id=1, source_target_pairs={{0,1},{1,0},{2,3},{3,2},{4,5},{5,4},{6,7},{7,6},{8,9},{9,8},{10,11... | collective-permute-start | bytes 1572872 | tf_op jit(solution)/shard_map/ppermute | solution.py:332
  10.9 39.3 %collective-permute-start.63 = (bf16[128,2048]{1,0:T(8,128)(2,1)}, bf16[128,2048]{1,0:T(8,128)(2,1)}, u32[]{:S(2)}, u32[]{:S(2)}) collective-permute-start(bf16[128,2048]{1,0:T(8,128)(2,1)} %get-tuple-element.35), channel_id=1, source_target_pairs={{4,0},{5,1},{8,4},{9,5},{12,8},{13,9},{14,12},{15,13},{10,14},{11,... | collective-permute-start | bytes 1572872 | tf_op jit(solution)/shard_map/ppermute | solution.py:329
  12.8 37.7 %collective-permute-start.62 = (bf16[128,2048]{1,0:T(8,128)(2,1)}, bf16[128,2048]{1,0:T(8,128)(2,1)}, u32[]{:S(2)}, u32[]{:S(2)}) collective-permute-start(bf16[128,2048]{1,0:T(8,128)(2,1)} %get-tuple-element.35), channel_id=1, source_target_pairs={{0,4},{1,5},{4,8},{5,9},{8,12},{9,13},{12,14},{13,15},{14,10},{15,... | collective-permute-start | bytes 1572872 | tf_op jit(solution)/shard_map/ppermute | solution.py:326
  18.9 109.9 %all-to-all-start = ((bf16[16,128,384]{1,2,0:T(8,128)(2,1)}), bf16[16,128,384]{1,2,0:T(8,128)(2,1)}, u32[]{:S(2)}, u32[]{:S(2)}) async-start(bf16[16,128,384]{1,2,0:T(8,128)(2,1)} %maximum_bitcast_fusion), calls=%async_computation | async-start | bytes 3145728 | tf_op jit(solution)/shard_map/all_to_all | solution.py:433
  41.5 27.2 %collective-permute-start.6 = (bf16[128,2048]{1,0:T(8,128)(2,1)}, bf16[128,2048]{1,0:T(8,128)(2,1)S(1)}, u32[]{:S(2)}, u32[]{:S(2)}) collective-permute-start(bf16[128,2048]{1,0:T(8,128)(2,1)} %collective-permute-done.2), channel_id=1, source_target_pairs={{4,0},{5,1},{8,4},{9,5},{12,8},{13,9},{14,12},{15,13},{10,14},{11,... | collective-permute-start | bytes 1572872 | tf_op jit(solution)/shard_map/ppermute | solution.py:329
  50.2 29.0 %collective-permute-start.5 = (bf16[128,2048]{1,0:T(8,128)(2,1)}, bf16[128,2048]{1,0:T(8,128)(2,1)S(1)}, u32[]{:S(2)}, u32[]{:S(2)}) collective-permute-start(bf16[128,2048]{1,0:T(8,128)(2,1)} %collective-permute-done.1), channel_id=1, source_target_pairs={{0,4},{1,5},{4,8},{5,9},{8,12},{9,13},{12,14},{13,15},{14,10},{15,... | collective-permute-start | bytes 1572872 | tf_op jit(solution)/shard_map/ppermute | solution.py:326
  50.6 32.7 %collective-permute-start.68 = (bf16[128,2048]{1,0:T(8,128)(2,1)}, bf16[128,2048]{1,0:T(8,128)(2,1)S(1)}, u32[]{:S(2)}, u32[]{:S(2)}) collective-permute-start(bf16[128,2048]{1,0:T(8,128)(2,1)} %collective-permute-done.63), channel_id=1, source_target_pairs={{4,0},{5,1},{8,4},{9,5},{12,8},{13,9},{14,12},{15,13},{10,14},{11,... | collective-permute-start | bytes 1572872 | tf_op jit(solution)/shard_map/ppermute | solution.py:329
  56.1 25.9 %collective-permute-start.65 = (bf16[128,2048]{1,0:T(8,128)(2,1)}, bf16[128,2048]{1,0:T(8,128)(2,1)S(1)}, u32[]{:S(2)}, u32[]{:S(2)}) collective-permute-start(bf16[128,2048]{1,0:T(8,128)(2,1)} %collective-permute-done.63), channel_id=1, source_target_pairs={{0,1},{1,0},{2,3},{3,2},{4,5},{5,4},{6,7},{7,6},{8,9},{9,8},{10,11... | collective-permute-start | bytes 1572872 | tf_op jit(solution)/shard_map/ppermute | solution.py:332
  57.0 24.1 %collective-permute-start.64 = (bf16[128,2048]{1,0:T(8,128)(2,1)}, bf16[128,2048]{1,0:T(8,128)(2,1)S(1)}, u32[]{:S(2)}, u32[]{:S(2)}) collective-permute-start(bf16[128,2048]{1,0:T(8,128)(2,1)} %collective-permute-done.62), channel_id=1, source_target_pairs={{0,1},{1,0},{2,3},{3,2},{4,5},{5,4},{6,7},{7,6},{8,9},{9,8},{10,11... | collective-permute-start | bytes 1572872 | tf_op jit(solution)/shard_map/ppermute | solution.py:332
  68.7 21.8 %collective-permute-start.67 = (bf16[128,2048]{1,0:T(8,128)(2,1)}, bf16[128,2048]{1,0:T(8,128)(2,1)S(1)}, u32[]{:S(2)}, u32[]{:S(2)}) collective-permute-start(bf16[128,2048]{1,0:T(8,128)(2,1)} %collective-permute-done.62), channel_id=1, source_target_pairs={{0,4},{1,5},{4,8},{5,9},{8,12},{9,13},{12,14},{13,15},{14,10},{15,... | collective-permute-start | bytes 1572872 | tf_op jit(solution)/shard_map/ppermute | solution.py:326
  79.2 15.3 %collective-permute-start.10 = (bf16[128,2048]{1,0:T(8,128)(2,1)S(1)}, bf16[128,2048]{1,0:T(8,128)(2,1)S(1)}, u32[]{:S(2)}, u32[]{:S(2)}) collective-permute-start(bf16[128,2048]{1,0:T(8,128)(2,1)S(1)} %collective-permute-done.6), channel_id=1, source_target_pairs={{4,0},{5,1},{8,4},{9,5},{12,8},{13,9},{14,12},{15,13},{10,14},{11,... | collective-permute-start | bytes 1572872 | tf_op jit(solution)/shard_map/ppermute | solution.py:329
  83.3 18.5 %collective-permute-start.9 = (bf16[128,2048]{1,0:T(8,128)(2,1)S(1)}, bf16[128,2048]{1,0:T(8,128)(2,1)S(1)}, u32[]{:S(2)}, u32[]{:S(2)}) collective-permute-start(bf16[128,2048]{1,0:T(8,128)(2,1)S(1)} %collective-permute-done.5), channel_id=1, source_target_pairs={{0,4},{1,5},{4,8},{5,9},{8,12},{9,13},{12,14},{13,15},{14,10},{15,... | collective-permute-start | bytes 1572872 | tf_op jit(solution)/shard_map/ppermute | solution.py:326
  92.2 21.8 %collective-permute-start.70 = (bf16[128,2048]{1,0:T(8,128)(2,1)S(1)}, bf16[128,2048]{1,0:T(8,128)(2,1)S(1)}, u32[]{:S(2)}, u32[]{:S(2)}) collective-permute-start(bf16[128,2048]{1,0:T(8,128)(2,1)S(1)} %collective-permute-done.68), channel_id=1, source_target_pairs={{0,1},{1,0},{2,3},{3,2},{4,5},{5,4},{6,7},{7,6},{8,9},{9,8},{10,11... | collective-permute-start | bytes 1572872 | tf_op jit(solution)/shard_map/ppermute | solution.py:332
  93.2 19.8 %collective-permute-start.69 = (bf16[128,2048]{1,0:T(8,128)(2,1)S(1)}, bf16[128,2048]{1,0:T(8,128)(2,1)S(1)}, u32[]{:S(2)}, u32[]{:S(2)}) collective-permute-start(bf16[128,2048]{1,0:T(8,128)(2,1)S(1)} %collective-permute-done.67), channel_id=1, source_target_pairs={{0,1},{1,0},{2,3},{3,2},{4,5},{5,4},{6,7},{7,6},{8,9},{9,8},{10,11... | collective-permute-start | bytes 1572872 | tf_op jit(solution)/shard_map/ppermute | solution.py:332
  94.6 20.4 %collective-permute-start.72 = (bf16[128,2048]{1,0:T(8,128)(2,1)S(1)}, bf16[128,2048]{1,0:T(8,128)(2,1)S(1)}, u32[]{:S(2)}, u32[]{:S(2)}) collective-permute-start(bf16[128,2048]{1,0:T(8,128)(2,1)S(1)} %collective-permute-done.67), channel_id=1, source_target_pairs={{0,4},{1,5},{4,8},{5,9},{8,12},{9,13},{12,14},{13,15},{14,10},{15,... | collective-permute-start | bytes 1572872 | tf_op jit(solution)/shard_map/ppermute | solution.py:326
  101.7 19.3 %collective-permute-start.14 = (bf16[64,2048]{1,0:T(8,128)(2,1)S(1)}, bf16[64,2048]{1,0:T(8,128)(2,1)}, u32[]{:S(2)}, u32[]{:S(2)}) collective-permute-start(bf16[64,2048]{1,0:T(8,128)(2,1)S(1)} %slice.491), channel_id=1, source_target_pairs={{4,0},{5,1},{8,4},{9,5},{12,8},{13,9},{14,12},{15,13},{10,14},{11,... | collective-permute-start | bytes 786440 | tf_op jit(solution)/shard_map/ppermute | solution.py:329
  103.6 17.9 %collective-permute-start.13 = (bf16[64,2048]{1,0:T(8,128)(2,1)S(1)}, bf16[64,2048]{1,0:T(8,128)(2,1)}, u32[]{:S(2)}, u32[]{:S(2)}) collective-permute-start(bf16[64,2048]{1,0:T(8,128)(2,1)S(1)} %slice.490), channel_id=1, source_target_pairs={{0,4},{1,5},{4,8},{5,9},{8,12},{9,13},{12,14},{13,15},{14,10},{15,... | collective-permute-start | bytes 786440 | tf_op jit(solution)/shard_map/ppermute | solution.py:326
  121.5 18.6 %collective-permute-start.16 = (bf16[64,2048]{1,0:T(8,128)(2,1)}, bf16[64,2048]{1,0:T(8,128)(2,1)}, u32[]{:S(2)}, u32[]{:S(2)}) collective-permute-start(bf16[64,2048]{1,0:T(8,128)(2,1)} %collective-permute-done.14), channel_id=1, source_target_pairs={{0,1},{1,0},{2,3},{3,2},{4,5},{5,4},{6,7},{7,6},{8,9},{9,8},{10,11... | collective-permute-start | bytes 786440 | tf_op jit(solution)/shard_map/ppermute | solution.py:332
  125.0 15.2 %collective-permute-start.15 = (bf16[64,2048]{1,0:T(8,128)(2,1)}, bf16[64,2048]{1,0:T(8,128)(2,1)}, u32[]{:S(2)}, u32[]{:S(2)}) collective-permute-start(bf16[64,2048]{1,0:T(8,128)(2,1)} %collective-permute-done.13), channel_id=1, source_target_pairs={{0,1},{1,0},{2,3},{3,2},{4,5},{5,4},{6,7},{7,6},{8,9},{9,8},{10,11... | collective-permute-start | bytes 786440 | tf_op jit(solution)/shard_map/ppermute | solution.py:332
  125.8 105.4 %collective-permute-start.80 = (bf16[64,2048]{1,0:T(8,128)(2,1)S(1)}, bf16[64,2048]{1,0:T(8,128)(2,1)}, u32[]{:S(2)}, u32[]{:S(2)}) collective-permute-start(bf16[64,2048]{1,0:T(8,128)(2,1)S(1)} %collective-permute-done.78), channel_id=1, source_target_pairs={{0,1},{1,0},{2,3},{3,2},{4,5},{5,4},{6,7},{7,6},{8,9},{9,8},{10,11... | collective-permute-start | bytes 786440 | tf_op jit(solution)/shard_map/ppermute | solution.py:332
  125.8 103.7 %collective-permute-start.79 = (bf16[64,2048]{1,0:T(8,128)(2,1)}, bf16[64,2048]{1,0:T(8,128)(2,1)}, u32[]{:S(2)}, u32[]{:S(2)}) collective-permute-start(bf16[64,2048]{1,0:T(8,128)(2,1)} %collective-permute-done.77), channel_id=1, source_target_pairs={{0,1},{1,0},{2,3},{3,2},{4,5},{5,4},{6,7},{7,6},{8,9},{9,8},{10,11... | collective-permute-start | bytes 786440 | tf_op jit(solution)/shard_map/ppermute | solution.py:332
  190.2 14.0 %collective-permute-start.18 = (bf16[256,2048]{1,0:T(8,128)(2,1)S(1)}, bf16[256,2048]{1,0:T(8,128)(2,1)S(1)}, u32[]{:S(2)}, u32[]{:S(2)}) collective-permute-start(bf16[256,2048]{1,0:T(8,128)(2,1)S(1)} %convolution_convert_fusion.10), channel_id=1, source_target_pairs={{0,1},{1,0},{2,3},{3,2},{4,5},{5,4},{6,7},{7,6},{8,9},{9,8},{10,11... | collective-permute-start | bytes 3145736 | tf_op jit(solution)/shard_map/ppermute | solution.py:332
  204.2 16.9 %collective-permute-start.17 = (bf16[128,2048]{1,0:T(8,128)(2,1)S(1)}, bf16[128,2048]{1,0:T(8,128)(2,1)S(1)}, u32[]{:S(2)}, u32[]{:S(2)}) collective-permute-start(bf16[128,2048]{1,0:T(8,128)(2,1)S(1)} %convolution_convert_fusion.22), channel_id=1, source_target_pairs={{0,1},{1,0},{2,3},{3,2},{4,5},{5,4},{6,7},{7,6},{8,9},{9,8},{10,11... | collective-permute-start | bytes 1572872 | tf_op jit(solution)/shard_map/ppermute | solution.py:332
  232.9 14.3 %collective-permute-start.33 = (bf16[128,2048]{1,0:T(8,128)(2,1)S(1)}, bf16[128,2048]{1,0:T(8,128)(2,1)S(1)}, u32[]{:S(2)}, u32[]{:S(2)}) collective-permute-start(bf16[128,2048]{1,0:T(8,128)(2,1)S(1)} %get-tuple-element.47), channel_id=1, source_target_pairs={{4,0},{5,1},{8,4},{9,5},{12,8},{13,9},{14,12},{15,13},{10,14},{11,... | collective-permute-start | bytes 1572872 | tf_op jit(solution)/shard_map/ppermute | solution.py:329
  234.2 17.0 %collective-permute-start.32 = (bf16[128,2048]{1,0:T(8,128)(2,1)S(1)}, bf16[128,2048]{1,0:T(8,128)(2,1)S(1)}, u32[]{:S(2)}, u32[]{:S(2)}) collective-permute-start(bf16[128,2048]{1,0:T(8,128)(2,1)S(1)} %get-tuple-element.47), channel_id=1, source_target_pairs={{0,4},{1,5},{4,8},{5,9},{8,12},{9,13},{12,14},{13,15},{14,10},{15,... | collective-permute-start | bytes 1572872 | tf_op jit(solution)/shard_map/ppermute | solution.py:326
  237.4 169.8 %collective-permute-start.31 = (bf16[128,2048]{1,0:T(8,128)(2,1)S(1)}, bf16[128,2048]{1,0:T(8,128)(2,1)S(1)}, u32[]{:S(2)}, u32[]{:S(2)}) collective-permute-start(bf16[128,2048]{1,0:T(8,128)(2,1)S(1)} %convolution_convert_fusion.20), channel_id=1, source_target_pairs={{0,1},{1,0},{2,3},{3,2},{4,5},{5,4},{6,7},{7,6},{8,9},{9,8},{10,11... | collective-permute-start | bytes 1572872 | tf_op jit(solution)/shard_map/ppermute | solution.py:332
  247.2 13.6 %collective-permute-start.38 = (bf16[128,2048]{1,0:T(8,128)(2,1)S(1)}, bf16[128,2048]{1,0:T(8,128)(2,1)S(1)}, u32[]{:S(2)}, u32[]{:S(2)}) collective-permute-start(bf16[128,2048]{1,0:T(8,128)(2,1)S(1)} %collective-permute-done.33), channel_id=1, source_target_pairs={{4,0},{5,1},{8,4},{9,5},{12,8},{13,9},{14,12},{15,13},{10,14},{11,... | collective-permute-start | bytes 1572872 | tf_op jit(solution)/shard_map/ppermute | solution.py:329
  251.2 14.4 %collective-permute-start.37 = (bf16[128,2048]{1,0:T(8,128)(2,1)S(1)}, bf16[128,2048]{1,0:T(8,128)(2,1)S(1)}, u32[]{:S(2)}, u32[]{:S(2)}) collective-permute-start(bf16[128,2048]{1,0:T(8,128)(2,1)S(1)} %collective-permute-done.32), channel_id=1, source_target_pairs={{0,4},{1,5},{4,8},{5,9},{8,12},{9,13},{12,14},{13,15},{14,10},{15,... | collective-permute-start | bytes 1572872 | tf_op jit(solution)/shard_map/ppermute | solution.py:326
  259.1 37.7 %collective-permute-start.36 = (bf16[256,2048]{1,0:T(8,128)(2,1)S(1)}, bf16[256,2048]{1,0:T(8,128)(2,1)S(1)}, u32[]{:S(2)}, u32[]{:S(2)}) collective-permute-start(bf16[256,2048]{1,0:T(8,128)(2,1)S(1)} %convolution_convert_fusion.7), channel_id=1, source_target_pairs={{0,1},{1,0},{2,3},{3,2},{4,5},{5,4},{6,7},{7,6},{8,9},{9,8},{10,11... | collective-permute-start | bytes 3145736 | tf_op jit(solution)/shard_map/ppermute | solution.py:332
  273.5 21.6 %collective-permute-start.66 = (bf16[256,2048]{1,0:T(8,128)(2,1)S(1)}, bf16[256,2048]{1,0:T(8,128)(2,1)S(1)}, u32[]{:S(2)}, u32[]{:S(2)}) collective-permute-start(bf16[256,2048]{1,0:T(8,128)(2,1)S(1)} %convolution_convert_fusion.13), channel_id=1, source_target_pairs={{0,1},{1,0},{2,3},{3,2},{4,5},{5,4},{6,7},{7,6},{8,9},{9,8},{10,11... | collective-permute-start | bytes 3145736 | tf_op jit(solution)/shard_map/ppermute | solution.py:332
  273.5 14.4 %collective-permute-start.42 = (bf16[128,2048]{1,0:T(8,128)(2,1)S(1)}, bf16[128,2048]{1,0:T(8,128)(2,1)S(1)}, u32[]{:S(2)}, u32[]{:S(2)}) collective-permute-start(bf16[128,2048]{1,0:T(8,128)(2,1)S(1)} %collective-permute-done.37), channel_id=1, source_target_pairs={{0,4},{1,5},{4,8},{5,9},{8,12},{9,13},{12,14},{13,15},{14,10},{15,... | collective-permute-start | bytes 1572872 | tf_op jit(solution)/shard_map/ppermute | solution.py:326
  274.4 24.1 %collective-permute-start.48 = (bf16[64,2048]{1,0:T(8,128)(2,1)S(1)}, bf16[64,2048]{1,0:T(8,128)(2,1)S(1)}, u32[]{:S(2)}, u32[]{:S(2)}) collective-permute-start(bf16[64,2048]{1,0:T(8,128)(2,1)S(1)} %slice.522), channel_id=1, source_target_pairs={{4,0},{5,1},{8,4},{9,5},{12,8},{13,9},{14,12},{15,13},{10,14},{11,... | collective-permute-start | bytes 786440 | tf_op jit(solution)/shard_map/ppermute | solution.py:329
  287.9 17.2 %collective-permute-start.45 = (bf16[128,2048]{1,0:T(8,128)(2,1)S(1)}, bf16[128,2048]{1,0:T(8,128)(2,1)S(1)}, u32[]{:S(2)}, u32[]{:S(2)}) collective-permute-start(bf16[128,2048]{1,0:T(8,128)(2,1)S(1)} %collective-permute-done.43), channel_id=1, source_target_pairs={{0,1},{1,0},{2,3},{3,2},{4,5},{5,4},{6,7},{7,6},{8,9},{9,8},{10,11... | collective-permute-start | bytes 1572872 | tf_op jit(solution)/shard_map/ppermute | solution.py:332
  298.5 110.0 %collective-permute-start.61 = (bf16[128,2048]{1,0:T(8,128)(2,1)S(1)}, bf16[128,2048]{1,0:T(8,128)(2,1)S(1)}, u32[]{:S(2)}, u32[]{:S(2)}) collective-permute-start(bf16[128,2048]{1,0:T(8,128)(2,1)S(1)} %convolution_convert_fusion.18), channel_id=1, source_target_pairs={{0,1},{1,0},{2,3},{3,2},{4,5},{5,4},{6,7},{7,6},{8,9},{9,8},{10,11... | collective-permute-start | bytes 1572872 | tf_op jit(solution)/shard_map/ppermute | solution.py:332
  305.1 30.4 %collective-permute-start.41 = (bf16[256,2048]{1,0:T(8,128)(2,1)S(1)}, bf16[256,2048]{1,0:T(8,128)(2,1)S(1)}, u32[]{:S(2)}, u32[]{:S(2)}) collective-permute-start(bf16[256,2048]{1,0:T(8,128)(2,1)S(1)} %convolution_convert_fusion.6), channel_id=1, source_target_pairs={{0,1},{1,0},{2,3},{3,2},{4,5},{5,4},{6,7},{7,6},{8,9},{9,8},{10,11... | collective-permute-start | bytes 3145736 | tf_op jit(solution)/shard_map/ppermute | solution.py:332
  308.4 25.6 %collective-permute-start.71 = (bf16[256,2048]{1,0:T(8,128)(2,1)}, bf16[256,2048]{1,0:T(8,128)(2,1)S(1)}, u32[]{:S(2)}, u32[]{:S(2)}) collective-permute-start(bf16[256,2048]{1,0:T(8,128)(2,1)} %convolution_convert_fusion.12), channel_id=1, source_target_pairs={{0,1},{1,0},{2,3},{3,2},{4,5},{5,4},{6,7},{7,6},{8,9},{9,8},{10,11... | collective-permute-start | bytes 3145736 | tf_op jit(solution)/shard_map/ppermute | solution.py:332
  310.9 26.7 %collective-permute-start.51 = (bf16[128,2048]{1,0:T(8,128)(2,1)S(1)}, bf16[128,2048]{1,0:T(8,128)(2,1)S(1)}, u32[]{:S(2)}, u32[]{:S(2)}) collective-permute-start(bf16[128,2048]{1,0:T(8,128)(2,1)S(1)} %convolution_convert_fusion.19), channel_id=1, source_target_pairs={{0,1},{1,0},{2,3},{3,2},{4,5},{5,4},{6,7},{7,6},{8,9},{9,8},{10,11... | collective-permute-start | bytes 1572872 | tf_op jit(solution)/shard_map/ppermute | solution.py:332
  337.6 94.3 %collective-permute-start.128 = (bf16[512,2048]{1,0:T(8,128)(2,1)S(1)}, bf16[512,2048]{1,0:T(8,128)(2,1)S(1)}, u32[]{:S(2)}, u32[]{:S(2)}) collective-permute-start(bf16[512,2048]{1,0:T(8,128)(2,1)S(1)} %convolution_convert_fusion.1), channel_id=1, source_target_pairs={{0,16},{16,0},{1,17},{17,1},{2,18},{18,2},{3,19},{19,3},{4,20},{20... | collective-permute-start | bytes 6291464 | tf_op jit(solution)/shard_map/ppermute | solution.py:376
  404.8 16.2 %collective-permute-start.55 = (bf16[128,2048]{1,0:T(8,128)(2,1)S(1)}, bf16[128,2048]{1,0:T(8,128)(2,1)S(1)}, u32[]{:S(2)}, u32[]{:S(2)}) collective-permute-start(bf16[128,2048]{1,0:T(8,128)(2,1)S(1)} %get-tuple-element.78), channel_id=1, source_target_pairs={{4,0},{5,1},{8,4},{9,5},{12,8},{13,9},{14,12},{15,13},{10,14},{11,... | collective-permute-start | bytes 1572872 | tf_op jit(solution)/shard_map/ppermute | solution.py:329
  406.0 16.1 %collective-permute-start.59 = (bf16[128,2048]{1,0:T(8,128)(2,1)S(1)}, bf16[128,2048]{1,0:T(8,128)(2,1)S(1)}, u32[]{:S(2)}, u32[]{:S(2)}) collective-permute-start(bf16[128,2048]{1,0:T(8,128)(2,1)S(1)} %get-tuple-element.79), channel_id=1, source_target_pairs={{0,4},{1,5},{4,8},{5,9},{8,12},{9,13},{12,14},{13,15},{14,10},{15,... | collective-permute-start | bytes 1572872 | tf_op jit(solution)/shard_map/ppermute | solution.py:326
  407.2 18.5 %collective-permute-start.85 = (bf16[128,2048]{1,0:T(8,128)(2,1)S(1)}, bf16[128,2048]{1,0:T(8,128)(2,1)S(1)}, u32[]{:S(2)}, u32[]{:S(2)}) collective-permute-start(bf16[128,2048]{1,0:T(8,128)(2,1)S(1)} %get-tuple-element.72), channel_id=1, source_target_pairs={{4,0},{5,1},{8,4},{9,5},{12,8},{13,9},{14,12},{15,13},{10,14},{11,... | collective-permute-start | bytes 1572872 | tf_op jit(solution)/shard_map/ppermute | solution.py:329
  408.4 18.3 %collective-permute-start.89 = (bf16[128,2048]{1,0:T(8,128)(2,1)S(1)}, bf16[128,2048]{1,0:T(8,128)(2,1)S(1)}, u32[]{:S(2)}, u32[]{:S(2)}) collective-permute-start(bf16[128,2048]{1,0:T(8,128)(2,1)S(1)} %get-tuple-element.73), channel_id=1, source_target_pairs={{0,4},{1,5},{4,8},{5,9},{8,12},{9,13},{12,14},{13,15},{14,10},{15,... | collective-permute-start | bytes 1572872 | tf_op jit(solution)/shard_map/ppermute | solution.py:326
  421.0 86.1 %collective-permute-start.127 = (bf16[1024,2048]{1,0:T(8,128)(2,1)S(1)}, bf16[1024,2048]{1,0:T(8,128)(2,1)}, u32[]{:S(2)}, u32[]{:S(2)}) collective-permute-start(bf16[1024,2048]{1,0:T(8,128)(2,1)S(1)} %convolution_convert_fusion), channel_id=1, source_target_pairs={{0,16},{16,0},{1,17},{17,1},{2,18},{18,2},{3,19},{19,3},{4,20},{20... | collective-permute-start | bytes 12582920 | tf_op jit(solution)/shard_map/ppermute | solution.py:376
  442.1 14.7 %collective-permute-start.94 = (bf16[128,2048]{1,0:T(8,128)(2,1)S(1)}, bf16[128,2048]{1,0:T(8,128)(2,1)S(1)}, u32[]{:S(2)}, u32[]{:S(2)}) collective-permute-start(bf16[128,2048]{1,0:T(8,128)(2,1)S(1)} %collective-permute-done.92), channel_id=1, source_target_pairs={{0,1},{1,0},{2,3},{3,2},{4,5},{5,4},{6,7},{7,6},{8,9},{9,8},{10,11... | collective-permute-start | bytes 1572872 | tf_op jit(solution)/shard_map/ppermute | solution.py:332
  442.2 14.3 %collective-permute-start.95 = (bf16[128,2048]{1,0:T(8,128)(2,1)S(1)}, bf16[128,2048]{1,0:T(8,128)(2,1)S(1)}, u32[]{:S(2)}, u32[]{:S(2)}) collective-permute-start(bf16[128,2048]{1,0:T(8,128)(2,1)S(1)} %collective-permute-done.91), channel_id=1, source_target_pairs={{0,4},{1,5},{4,8},{5,9},{8,12},{9,13},{12,14},{13,15},{14,10},{15,... | collective-permute-start | bytes 1572872 | tf_op jit(solution)/shard_map/ppermute | solution.py:326
  442.2 14.3 %collective-permute-start.93 = (bf16[128,2048]{1,0:T(8,128)(2,1)S(1)}, bf16[128,2048]{1,0:T(8,128)(2,1)S(1)}, u32[]{:S(2)}, u32[]{:S(2)}) collective-permute-start(bf16[128,2048]{1,0:T(8,128)(2,1)S(1)} %collective-permute-done.91), channel_id=1, source_target_pairs={{0,1},{1,0},{2,3},{3,2},{4,5},{5,4},{6,7},{7,6},{8,9},{9,8},{10,11... | collective-permute-start | bytes 1572872 | tf_op jit(solution)/shard_map/ppermute | solution.py:332
  452.2 64.3 %collective-permute-start.100 = (bf16[128,2048]{1,0:T(8,128)(2,1)S(1)}, bf16[128,2048]{1,0:T(8,128)(2,1)S(1)}, u32[]{:S(2)}, u32[]{:S(2)}) collective-permute-start(bf16[128,2048]{1,0:T(8,128)(2,1)S(1)} %collective-permute-done.96), channel_id=1, source_target_pairs={{4,0},{5,1},{8,4},{9,5},{12,8},{13,9},{14,12},{15,13},{10,14},{11,... | collective-permute-start | bytes 1572872 | tf_op jit(solution)/shard_map/ppermute | solution.py:329
  456.5 63.8 %collective-permute-start.98 = (bf16[128,2048]{1,0:T(8,128)(2,1)S(1)}, bf16[128,2048]{1,0:T(8,128)(2,1)S(1)}, u32[]{:S(2)}, u32[]{:S(2)}) collective-permute-start(bf16[128,2048]{1,0:T(8,128)(2,1)S(1)} %collective-permute-done.96), channel_id=1, source_target_pairs={{0,1},{1,0},{2,3},{3,2},{4,5},{5,4},{6,7},{7,6},{8,9},{9,8},{10,11... | collective-permute-start | bytes 1572872 | tf_op jit(solution)/shard_map/ppermute | solution.py:332
  456.5 61.8 %collective-permute-start.99 = (bf16[128,2048]{1,0:T(8,128)(2,1)S(1)}, bf16[128,2048]{1,0:T(8,128)(2,1)S(1)}, u32[]{:S(2)}, u32[]{:S(2)}) collective-permute-start(bf16[128,2048]{1,0:T(8,128)(2,1)S(1)} %collective-permute-done.95), channel_id=1, source_target_pairs={{0,4},{1,5},{4,8},{5,9},{8,12},{9,13},{12,14},{13,15},{14,10},{15,... | collective-permute-start | bytes 1572872 | tf_op jit(solution)/shard_map/ppermute | solution.py:326
  456.8 61.8 %collective-permute-start.97 = (bf16[128,2048]{1,0:T(8,128)(2,1)S(1)}, bf16[128,2048]{1,0:T(8,128)(2,1)}, u32[]{:S(2)}, u32[]{:S(2)}) collective-permute-start(bf16[128,2048]{1,0:T(8,128)(2,1)S(1)} %collective-permute-done.95), channel_id=1, source_target_pairs={{0,1},{1,0},{2,3},{3,2},{4,5},{5,4},{6,7},{7,6},{8,9},{9,8},{10,11... | collective-permute-start | bytes 1572872 | tf_op jit(solution)/shard_map/ppermute | solution.py:332
  567.6 13.6 %collective-permute-start.111 = (bf16[128,2048]{1,0:T(8,128)(2,1)S(1)}, bf16[128,2048]{1,0:T(8,128)(2,1)S(1)}, u32[]{:S(2)}, u32[]{:S(2)}) collective-permute-start(bf16[128,2048]{1,0:T(8,128)(2,1)S(1)} %convolution_convert_fusion.15), channel_id=1, source_target_pairs={{0,1},{1,0},{2,3},{3,2},{4,5},{5,4},{6,7},{7,6},{8,9},{9,8},{10,11... | collective-permute-start | bytes 1572872 | tf_op jit(solution)/shard_map/ppermute | solution.py:332
  571.3 24.8 %collective-permute-start.109 = (bf16[256,2048]{1,0:T(8,128)(2,1)S(1)}, bf16[256,2048]{1,0:T(8,128)(2,1)S(1)}, u32[]{:S(2)}, u32[]{:S(2)}) collective-permute-start(bf16[256,2048]{1,0:T(8,128)(2,1)S(1)} %convolution_convert_fusion.3), channel_id=1, source_target_pairs={{0,1},{1,0},{2,3},{3,2},{4,5},{5,4},{6,7},{7,6},{8,9},{9,8},{10,11... | collective-permute-start | bytes 3145736 | tf_op jit(solution)/shard_map/ppermute | solution.py:332
  575.9 37.3 %collective-permute-start.125 = (bf16[2048,384]{0,1:T(8,128)(2,1)S(1)}, bf16[2048,384]{0,1:T(8,128)(2,1)S(1)}, u32[]{:S(2)}, u32[]{:S(2)}) collective-permute-start(bf16[2048,384]{0,1:T(8,128)(2,1)S(1)} %get-tuple-element.58), channel_id=1, source_target_pairs={{0,16},{16,0},{1,17},{17,1},{2,18},{18,2},{3,19},{19,3},{4,20},{20... | collective-permute-start | bytes 4718600 | tf_op jit(solution)/shard_map/ppermute | solution.py:376
  580.7 15.4 %collective-permute-start.124 = (f32[2,2048]{1,0:T(2,128)S(1)}, f32[2,2048]{1,0:T(2,128)S(1)}, u32[]{:S(2)}, u32[]{:S(2)}) collective-permute-start(f32[2,2048]{1,0:T(2,128)S(1)} %add.341), channel_id=1, source_target_pairs={{0,8},{1,9},{2,10},{3,11},{4,12},{5,13},{6,14},{7,15},{8,0},{9,1},... | collective-permute-start | bytes 49160 | tf_op jit(solution)/shard_map/ppermute | solution.py:369
  596.1 40.4 %collective-permute-start.107 = (bf16[128,2048]{1,0:T(8,128)(2,1)}, bf16[128,2048]{1,0:T(8,128)(2,1)}, u32[]{:S(2)}, u32[]{:S(2)}) collective-permute-start(bf16[128,2048]{1,0:T(8,128)(2,1)} %convolution_convert_fusion.16), channel_id=1, source_target_pairs={{0,1},{1,0},{2,3},{3,2},{4,5},{5,4},{6,7},{7,6},{8,9},{9,8},{10,11... | collective-permute-start | bytes 1572872 | tf_op jit(solution)/shard_map/ppermute | solution.py:332
  596.1 24.4 %collective-permute-start.108 = (bf16[256,2048]{1,0:T(8,128)(2,1)}, bf16[256,2048]{1,0:T(8,128)(2,1)}, u32[]{:S(2)}, u32[]{:S(2)}) collective-permute-start(bf16[256,2048]{1,0:T(8,128)(2,1)} %convolution_convert_fusion.4), channel_id=1, source_target_pairs={{0,1},{1,0},{2,3},{3,2},{4,5},{5,4},{6,7},{7,6},{8,9},{9,8},{10,11... | collective-permute-start | bytes 3145736 | tf_op jit(solution)/shard_map/ppermute | solution.py:332
  603.9 30.4 %collective-permute-start.126 = (bf16[128,2048]{1,0:T(8,128)(2,1)S(1)}, bf16[128,2048]{1,0:T(8,128)(2,1)}, u32[]{:S(2)}, u32[]{:S(2)}) collective-permute-start(bf16[128,2048]{1,0:T(8,128)(2,1)S(1)} %convolution_convert_fusion.14), channel_id=1, source_target_pairs={{0,16},{16,0},{1,17},{17,1},{2,18},{18,2},{3,19},{19,3},{4,20},{20... | collective-permute-start | bytes 1572872 | tf_op jit(solution)/shard_map/ppermute | solution.py:376
  606.8 16.3 %collective-permute-start.114 = (bf16[128,2048]{1,0:T(8,128)(2,1)}, bf16[128,2048]{1,0:T(8,128)(2,1)}, u32[]{:S(2)}, u32[]{:S(2)}) collective-permute-start(bf16[128,2048]{1,0:T(8,128)(2,1)} %get-tuple-element.68), channel_id=1, source_target_pairs={{4,0},{5,1},{8,4},{9,5},{12,8},{13,9},{14,12},{15,13},{10,14},{11,... | collective-permute-start | bytes 1572872 | tf_op jit(solution)/shard_map/ppermute | solution.py:329
  613.1 16.9 %collective-permute-start.118 = (bf16[128,2048]{1,0:T(8,128)(2,1)}, bf16[128,2048]{1,0:T(8,128)(2,1)}, u32[]{:S(2)}, u32[]{:S(2)}) collective-permute-start(bf16[128,2048]{1,0:T(8,128)(2,1)} %get-tuple-element.69), channel_id=1, source_target_pairs={{0,4},{1,5},{4,8},{5,9},{8,12},{9,13},{12,14},{13,15},{14,10},{15,... | collective-permute-start | bytes 1572872 | tf_op jit(solution)/shard_map/ppermute | solution.py:326
  615.9 50.7 %all-to-all-start.1 = ((bf16[16,128,384]{1,2,0:T(8,128)(2,1)}), bf16[16,128,384]{1,2,0:T(8,128)(2,1)}, u32[]{:S(2)}, u32[]{:S(2)}) async-start(bf16[16,128,384]{1,2,0:T(8,128)(2,1)} %copy_bitcast_fusion), calls=%async_computation.1 | async-start | bytes 3145728 | tf_op jit(solution)/shard_map/all_to_all | solution.py:518
  631.5 28.6 %collective-permute-start.115 = (bf16[128,2048]{1,0:T(8,128)(2,1)S(1)}, bf16[128,2048]{1,0:T(8,128)(2,1)S(1)}, u32[]{:S(2)}, u32[]{:S(2)}) collective-permute-start(bf16[128,2048]{1,0:T(8,128)(2,1)S(1)} %get-tuple-element.66), channel_id=1, source_target_pairs={{4,0},{5,1},{8,4},{9,5},{12,8},{13,9},{14,12},{15,13},{10,14},{11,... | collective-permute-start | bytes 1572872 | tf_op jit(solution)/shard_map/ppermute | solution.py:329
  632.9 28.8 %collective-permute-start.119 = (bf16[128,2048]{1,0:T(8,128)(2,1)S(1)}, bf16[128,2048]{1,0:T(8,128)(2,1)S(1)}, u32[]{:S(2)}, u32[]{:S(2)}) collective-permute-start(bf16[128,2048]{1,0:T(8,128)(2,1)S(1)} %get-tuple-element.67), channel_id=1, source_target_pairs={{0,4},{1,5},{4,8},{5,9},{8,12},{9,13},{12,14},{13,15},{14,10},{15,... | collective-permute-start | bytes 1572872 | tf_op jit(solution)/shard_map/ppermute | solution.py:326
  (132 other events, 1426.8 us)

commit v2 on v1

--- a/solution.py
+++ b/solution.py
@@ -4,6 +4,7 @@
 from jax import lax
 from jax.experimental import pallas as pl
 from jax.experimental.pallas import tpu as pltpu
+import math
 import numpy as np
 from jax.sharding import PartitionSpec as P
 
@@ -64,7 +65,7 @@
         value_ref[target, :] = value_lin.astype(jnp.bfloat16)
         turned[:, target] = value_lin.T.astype(jnp.bfloat16)
 
-    block_q = min(256, rows)
+    block_q = min(512, rows)
     block_k = min(512, rows)
 
     @pl.loop(0, rows // block_q)
@@ -170,7 +171,7 @@
             )
         key_t[:, target] = key_ref[target, :].astype(jnp.float32).T.astype(jnp.bfloat16)
 
-    block_q = min(256, rows)
+    block_q = min(512, rows)
     block_k = min(512, rows)
 
     @pl.loop(0, rows // block_q)
@@ -271,10 +272,10 @@
 
 def rotary_tables(row_count, width):
     half_dim = HEAD_DIM // 2
-    frequency = THETA ** (-jnp.arange(half_dim, dtype=jnp.float32) * 2.0 / HEAD_DIM)
+    feature = (jnp.arange(width, dtype=jnp.int32) % half_dim).astype(jnp.float32)
+    frequency = THETA ** (-feature * 2.0 / HEAD_DIM)
     angles = jnp.arange(row_count, dtype=jnp.float32)[:, None] * frequency[None, :]
-    copies = width // half_dim
-    return (jnp.tile(jnp.cos(angles), (1, copies)), jnp.tile(jnp.sin(angles), (1, copies)))
+    return (jnp.cos(angles), jnp.sin(angles))
 
 
 def rms_factor(matrix):
@@ -291,6 +292,177 @@
     gate_back = hidden_back * up_proj * sigmoid_gate * (1.0 + gate_proj * (1.0 - sigmoid_gate))
     up_back = hidden_back * jax.nn.silu(gate_proj)
     return (gate_back.astype(jnp.bfloat16), up_back.astype(jnp.bfloat16))
+
+
+SMALL = pl.CostEstimate(flops=1024, bytes_accessed=1024, transcendentals=0)
+
+
+def dot_tn(a, b):
+    return lax.dot_general(a, b, (((0,), (0,)), ((), ())), preferred_element_type=jnp.float32)
+
+
+def fitting(tile, extent):
+    return math.gcd(tile, extent)
+
+
+def call_kernel(body, name, grid, ins, outs, args):
+    return pl.pallas_call(
+        body,
+        grid=grid,
+        in_specs=[pl.BlockSpec(*spec) for spec in ins],
+        out_specs=[pl.BlockSpec(block, index) for block, index, _, _ in outs],
+        out_shape=[jax.ShapeDtypeStruct(shape, dtype) for _, _, shape, dtype in outs],
+        compiler_params=pltpu.CompilerParams(vmem_limit_bytes=VMEM_LIMIT),
+        cost_estimate=SMALL,
+        name=name,
+    )(*args)
+
+
+def first(i):
+    return (0, 0)
+
+
+def along(i):
+    return (0, i)
+
+
+def down_rows(i):
+    return (i, 0)
+
+
+def fill(target_ref, piece_refs):
+    start = 0
+    for piece_ref in piece_refs:
+        count = piece_ref.shape[0]
+        target_ref[start : start + count, :] = piece_ref[...]
+        start += count
+
+
+def grads_kernel(lefts, rights, *refs):
+    out_refs, (left_ref, right_ref) = refs[lefts + rights : -2], refs[-2:]
+
+    @pl.when(pl.program_id(0) == 0)
+    def _():
+        fill(left_ref, refs[:lefts])
+
+    fill(right_ref, refs[lefts : lefts + rights])
+    total = dot_tn(left_ref[...], right_ref[...]).astype(jnp.bfloat16)
+    rows = out_refs[0].shape[0]
+    for piece, out_ref in enumerate(out_refs):
+        out_ref[...] = total[piece * rows : (piece + 1) * rows]
+
+
+def weight_grads(lefts, rights, rows):
+    count = sum(piece.shape[0] for piece in lefts)
+    wide = lefts[0].shape[1]
+    width = rights[0].shape[1]
+    tile = fitting(512, width)
+    return pl.pallas_call(
+        functools.partial(grads_kernel, len(lefts), len(rights)),
+        grid=(width // tile,),
+        in_specs=[pl.BlockSpec(piece.shape, first) for piece in lefts]
+        + [pl.BlockSpec((piece.shape[0], tile), along) for piece in rights],
+        out_specs=[pl.BlockSpec((rows, tile), along)] * (wide // rows),
+        out_shape=[jax.ShapeDtypeStruct((rows, width), jnp.bfloat16)] * (wide // rows),
+        scratch_shapes=[
+            pltpu.VMEM((count, wide), jnp.bfloat16),
+            pltpu.VMEM((count, tile), jnp.bfloat16),
+        ],
+        compiler_params=pltpu.CompilerParams(vmem_limit_bytes=VMEM_LIMIT),
+        cost_estimate=SMALL,
+        name="weight_grads",
+    )(*lefts, *rights)
+
+
+def heads_kernel(upper_ref, left_ref, right_ref, weight_ref, keep_ref, give_ref, gain_ref):
+    total = dot_tn(left_ref[...], right_ref[...])
+    count, half, width = keep_ref.shape
+    sums = jnp.sum(total * weight_ref[...].astype(jnp.float32), axis=1, keepdims=True)
+    gain_ref[...] = jnp.broadcast_to(sums, (total.shape[0], 128)).T[:1]
+    blocks = total.astype(jnp.bfloat16).reshape(count, 2, half, width)
+    upper = upper_ref[0] == 1
+    keep_ref[...] = jnp.where(upper, blocks[:, 1], blocks[:, 0])
+    give_ref[...] = jnp.where(upper, blocks[:, 0], blocks[:, 1])
+
+
+def heads_grads(left, right, weight, upper, rows):
+    count, wide = left.shape
+    width = right.shape[1]
+    tile = fitting(512, wide)
+    half = ((tile // rows, rows // 2, width), lambda i: (i, 0, 0))
+    whole = ((wide // rows, rows // 2, width), jnp.bfloat16)
+    return pl.pallas_call(
+        heads_kernel,
+        grid=(wide // tile,),
+        in_specs=[
+            pl.BlockSpec(memory_space=pltpu.SMEM),
+            pl.BlockSpec((count, tile), along),
+            pl.BlockSpec((count, width), first),
+            pl.BlockSpec((tile, width), down_rows),
+        ],
+        out_specs=[pl.BlockSpec(*half), pl.BlockSpec(*half), pl.BlockSpec((1, tile), along)],
+        out_shape=[
+            jax.ShapeDtypeStruct(*whole),
+            jax.ShapeDtypeStruct(*whole),
+            jax.ShapeDtypeStruct((1, wide), jnp.float32),
+        ],
+        compiler_params=pltpu.CompilerParams(vmem_limit_bytes=VMEM_LIMIT),
+        cost_estimate=SMALL,
+        name="heads_grads",
+    )(upper, left, right, weight)
+
+
+def assemble_kernel(side_ref, near_ref, far_ref, *out_refs):
+    half, width = near_ref.shape[1:]
+    columns = width // len(out_refs)
+    upper = side_ref[0] == 1
+    low = jnp.where(upper, far_ref[...], near_ref[...]).astype(jnp.float32)
+    high = jnp.where(upper, near_ref[...], far_ref[...]).astype(jnp.float32)
+    for piece, out_ref in enumerate(out_refs):
+        for source in range(near_ref.shape[0]):
+            place = slice(source * columns, (source + 1) * columns)
+            taken = slice(piece * columns, (piece + 1) * columns)
+            out_ref[:half, place] = low[source, :, taken]
+            out_ref[half:, place] = high[source, :, taken]
+
+
+def assemble(near, far, side, count):
+    size, half, width = near.shape
+    shape = (2 * half, size * width // count)
+    vmem = pl.BlockSpec(memory_space=pltpu.VMEM)
+    return pl.pallas_call(
+        assemble_kernel,
+        in_specs=[pl.BlockSpec(memory_space=pltpu.SMEM), vmem, vmem],
+        out_specs=[vmem] * count,
+        out_shape=[jax.ShapeDtypeStruct(shape, jnp.float32)] * count,
+        compiler_params=pltpu.CompilerParams(vmem_limit_bytes=VMEM_LIMIT),
+        cost_estimate=SMALL,
+        name="assemble",
+    )(side, near, far)
+
+
+def sums_kernel(*refs):
+    out_ref = refs[-1]
+    count = (len(refs) - 1) // 2
+    rows = refs[0].shape[0]
+    for piece in range(count):
+        out_ref[piece * rows : (piece + 1) * rows, :] = refs[piece][...].astype(
+            jnp.float32
+        ) + refs[count + piece][...].astype(jnp.float32)
+
+
+def sum_pieces(parts, others):
+    rows, width = parts[0].shape
+    tile = fitting(512, width)
+    total = rows * len(parts)
+    return call_kernel(
+        sums_kernel,
+        "sum_pieces",
+        (width // tile,),
+        [((rows, tile), along)] * (2 * len(parts)),
+        [((total, tile), along, (total, width), jnp.float32)],
+        (*parts, *others),
+    )
 
 
 class Ring:
@@ -331,22 +503,21 @@
     def twin(self, array):
         return lax.ppermute(array, "wide", self.across)
 
-    def gather(self, rows):
-        groups = [[rows, self.twin(rows)]]
+    def gather(self, rows, groups):
+        groups.append([rows, self.twin(rows)])
         ahead = behind = rows
         middle = rows.shape[0] // 2
         for step in range(1, self.reach + 1):
             if step == self.reach:
                 ahead, behind = ahead[:middle], behind[middle:]
-            ahead, behind = self.forward(ahead), self.backward(behind)
+            (ahead, behind), _ = yield ((self.forward, ahead), (self.backward, behind)), ()
             groups.append([ahead, behind, self.twin(ahead), self.twin(behind)])
-        return [jnp.concatenate(group, axis=0) for group in groups]
 
     def scatter(self, make):
-        sums = [None] * (self.reach + 1)
         down = up = None
+        held = ()
         for step in range(self.reach, -1, -1):
-            mine, other = make(step)
+            mine, other = make(step, *held)
             total = mine + self.twin(other.astype(jnp.bfloat16)).astype(jnp.float32)
             count = total.shape[0] // 2
             if step == 0:
@@ -359,23 +530,97 @@
             elif step < self.reach - 1:
                 low = low + down.astype(jnp.float32)
                 high = high + up.astype(jnp.float32)
-            down = self.backward(low.astype(jnp.bfloat16))
-            up = self.forward(high.astype(jnp.bfloat16))
+            held = (low.astype(jnp.bfloat16), high.astype(jnp.bfloat16))
+            (down, up), _ = yield ((self.backward, held[0]), (self.forward, held[1])), ()
 
     def total(self, array):
-        array = array + lax.ppermute(array, "narrow", [(0, 1), (1, 0)])
         bit = 1
         while bit < self.size:
-            array = array + lax.ppermute(array, "wide", [(i, i ^ bit) for i in range(self.size)])
+            pairs = [(i, i ^ bit) for i in range(self.size)]
+            send = functools.partial(lax.ppermute, axis_name="wide", perm=pairs)
+            ((other,), _) = yield ((send, array),), ()
+            array = array + other
             bit *= 2
-        return array
-
-
-def both_sequences(part):
-    part = lax.optimization_barrier(part.astype(jnp.bfloat16))
-    return part.astype(jnp.float32) + lax.ppermute(part, "narrow", [(0, 1), (1, 0)]).astype(
-        jnp.float32
-    )
+        ((other,), _) = yield ((swapped, array),), ()
+        return array + other
+
+
+class Stream:
+    def __init__(self, hops):
+        self.hops = hops
+        self.asked, self.beside = next(hops)
+        self.result = None
+
+    def post(self):
+        return [send(array) for send, array in self.asked]
+
+    def land(self, arrived, beside):
+        try:
+            self.asked, self.beside = self.hops.send((arrived, beside))
+        except StopIteration as end:
+            self.asked, self.beside = None, ()
+            self.result = end.value
+
+
+class Swaps:
+    def __init__(self):
+        self.waiting = []
+        self.done = {}
+        self.parts = {}
+
+    def add(self, name, parts):
+        self.parts[name] = list(parts)
+        self.done[name] = []
+        self.waiting += [(name, index) for index in range(len(parts))]
+
+    def sums(self, name):
+        return (self.parts[name], self.done[name])
+
+
+def joined(*lists):
+    held = list(lax.optimization_barrier(tuple(array for part in lists for array in part)))
+    result = []
+    for part in lists:
+        result.append(held[: len(part)])
+        held = held[len(part) :]
+    return result
+
+
+def hop(streams, swaps=None, count=1, beside=(), work=None, given=()):
+    streams = [stream for stream in streams if stream.asked is not None]
+    ready = []
+    if swaps is not None:
+        ready, swaps.waiting = swaps.waiting[:count], swaps.waiting[count:]
+    if work is not None:
+        flat, tree = jax.tree.flatten(given)
+        *sent, flat = joined(*[[array for _, array in s.asked] for s in streams], flat)
+        for stream, arrays in zip(streams, sent):
+            stream.asked = [(send, array) for (send, _), array in zip(stream.asked, arrays)]
+        beside = work(*jax.tree.unflatten(tree, flat))
+    lists = [stream.post() for stream in streams]
+    lists += [stream.beside for stream in streams]
+    lists.append([swapped(swaps.parts[name][index]) for name, index in ready])
+    lists.append(beside)
+    *lists, moved, beside = joined(*lists)
+    for (name, _), piece in zip(ready, moved):
+        swaps.done[name].append(piece)
+    for place, stream in enumerate(streams):
+        stream.land(lists[place], lists[len(streams) + place])
+    return beside
+
+
+def travel(stream, swaps=None, count=1):
+    while stream.asked is not None:
+        hop([stream], swaps, count)
+    return stream.result
+
+
+def swapped(part):
+    return lax.ppermute(part, "narrow", [(0, 1), (1, 0)])
+
+
+def after(array, *others):
+    return lax.optimization_barrier((array,) + others)[0]
 
 
 def halves(array):
@@ -430,99 +675,178 @@
         [w.reshape(own_width, -1, width) for w in (w_query, w_key, w_value)], axis=-1
     ).transpose(1, 0, 2)
     blocks = jnp.repeat(blocks, sharing, axis=0)
-    w_heads = lax.all_to_all(blocks, "wide", 0, 0, tiled=True).reshape(model_width, 3 * width)
+    half_rows = own_width // 2
+    upper = lax.axis_index("narrow") == 1
     w_out_heads = w_out
     if sharing > 1:
         near = [list(range(a, a + sharing)) for a in range(0, size, sharing)]
         w_out_heads = lax.all_gather(w_out, "wide", axis=0, tiled=True, axis_index_groups=near)
-
+    units = w_gate.shape[0]
+    w_both = jnp.concatenate([w_gate, w_up], axis=0)
     factor_one = rms_factor(inputs)
     normed_one = inputs * factor_one
     norm_one = (normed_one * gain_one).astype(jnp.bfloat16)
-    group_one = ring.gather(norm_one)
-    lin = jnp.concatenate([dot_nn(rows, w_heads) for rows in group_one], axis=0)
-    heads_attention, query, key, value, logs = attention_forward(
-        slot_of, lengths, lin, cosine, sine
-    )
-    attention = own_columns(heads_attention)
+    sent = jnp.where(upper, blocks[:, half_rows:], blocks[:, :half_rows])
+    near_half = lax.all_to_all(after(sent, norm_one), "wide", 0, 0, tiled=True)
+    group_one = []
+    one = Stream(ring.gather(norm_one, group_one))
+    hop([one])
+    cosine, sine = hop([one], beside=(cosine, sine))
+    travel(one)
+    far_half = swapped(near_half)
+    w_heads = jnp.stack(
+        [jnp.where(upper, far_half, near_half), jnp.where(upper, near_half, far_half)], axis=1
+    ).reshape(model_width, 3 * width)
+    all_one = jnp.concatenate(sum(group_one, []), axis=0)
+    lin = dot_nn(all_one, w_heads)
     starts = [0]
     for rows in group_one:
-        starts.append(starts[-1] + rows.shape[0])
+        starts.append(starts[-1] + sum(piece.shape[0] for piece in rows))
 
     def group_of(array, step):
         return array[starts[step] : starts[step + 1]]
 
-    def residual_part(step):
+    group_back = []
+    back = Stream(ring.gather(after(mlp_back, lin), group_back))
+    heads_attention, query, key, value, logs = hop(
+        [back], beside=attention_forward(slot_of, lengths, lin, cosine, sine)
+    )
+    attention = own_columns(heads_attention)
+
+    def residual_part(step, *held):
         mine, other = halves(group_of(attention, step))
         return dot_nn(mine, w_out), dot_nn(other, w_out)
 
-    residual = inputs + ring.scatter(residual_part)
+    mixed = Stream(ring.scatter(residual_part))
+    while mixed.asked is not None:
+        hop([mixed, back])
+    residual = inputs + mixed.result
     factor_two = rms_factor(residual)
     normed_two = residual * factor_two
     norm_two = (normed_two * gain_two).astype(jnp.bfloat16)
-    group_back = ring.gather(mlp_back)
-    group_two = ring.gather(norm_two)
-    w_both = jnp.concatenate([w_gate, w_up], axis=0)
-    units = w_gate.shape[0]
+    group_two = []
+    two = Stream(ring.gather(norm_two, group_two))
     hidden = []
     both_back = []
-    for rows, back in zip(group_two, group_back):
-        both = dot_nt(rows, w_both)
+
+    def feed(step):
+        both = dot_nt(jnp.concatenate(group_two[step], axis=0), w_both)
         gate_proj, up_proj = both[:, :units], both[:, units:]
-        hidden.append((jax.nn.silu(gate_proj) * up_proj).astype(jnp.bfloat16))
-        both_back.append(
-            jnp.concatenate(swiglu_back(dot_nt(back, w_down), gate_proj, up_proj), axis=1)
+        hidden_back = dot_nt(jnp.concatenate(group_back[step], axis=0), w_down)
+        return (
+            (jax.nn.silu(gate_proj) * up_proj).astype(jnp.bfloat16),
+            jnp.concatenate(swiglu_back(hidden_back, gate_proj, up_proj), axis=1),
         )
 
-    def pull_part(step):
-        mine, other = halves(both_back[step])
+    hop([two])
+    for step in range(1, ring.reach):
+        fed = hop([two], beside=feed(step - 1))
+        hidden.append(fed[0])
+        both_back.append(fed[1])
+    for step in (ring.reach - 1, ring.reach):
+        fed = feed(step)
+        hidden.append(fed[0])
+        both_back.append(fed[1])
+
+    def pull_part(step, *held):
+        mine, other = halves(after(both_back[step], *held))
         return dot_nn(mine, w_both), dot_nn(other, w_both)
 
-    def mlp_part(step):
-        mine, other = halves(hidden[step])
+    def mlp_part(step, *held):
+        mine, other = halves(after(hidden[step], *held))
         return dot_nn(mine, w_down), dot_nn(other, w_down)
 
-    norm_two_back = ring.scatter(pull_part)
+    swaps = Swaps()
+    grads = functools.partial(weight_grads, rows=local_rows)
+    pull = Stream(ring.scatter(pull_part))
+    hop([pull])
+    down_parts = hop([pull], work=grads, given=(hidden, sum(group_back, [])))
+    swaps.add("down", down_parts)
+    norm_two_back = travel(pull, swaps)
     residual_back = y_back + norm_back(norm_two_back, normed_two, gain_two, factor_two)
     gain_two_term = jnp.sum(norm_two_back * normed_two, axis=0)
     branch_back = residual_back.astype(jnp.bfloat16)
-    group_branch = ring.gather(branch_back)
+    mlp = Stream(ring.scatter(mlp_part))
+    group_branch = []
+    branch = Stream(ring.gather(branch_back, group_branch))
+    pieces_two = sum(group_two, [])
+    for name, place in (("gate", slice(None, units)), ("up", slice(units, None))):
+        parts = hop(
+            [branch, mlp],
+            swaps,
+            2,
+            work=grads,
+            given=([both[:, place] for both in both_back], pieces_two),
+        )
+        swaps.add(name, parts)
+    (down_sum,) = hop([branch], swaps, work=sum_pieces, given=swaps.sums("down"))
+    while branch.asked is not None:
+        hop([branch], swaps)
     upstream = jnp.concatenate(
-        [dot_nt(rows, w_out_heads).astype(jnp.bfloat16) for rows in group_branch], axis=0
-    )
-    mlp_out = ring.scatter(mlp_part)
-    block_output = (residual + mlp_out).astype(jnp.bfloat16)
-
-    all_two = jnp.concatenate(group_two, axis=0)
-    both_sum = both_sequences(contract_rows(jnp.concatenate(both_back, axis=0), all_two))
-    down_sum = both_sequences(
-        contract_rows(jnp.concatenate(hidden, axis=0), jnp.concatenate(group_back, axis=0))
-    )
-    out_sum = both_sequences(contract_rows(attention, jnp.concatenate(group_branch, axis=0)))
-
-    lin_back = own_columns(
-        attention_backward(
-            slot_of, lengths, query, key, value, heads_attention, upstream, logs, cosine, sine
-        )
-    )
+        [
+            dot_nt(jnp.concatenate(rows, axis=0), w_out_heads).astype(jnp.bfloat16)
+            for rows in group_branch
+        ],
+        axis=0,
+    )
+    (lin_back,) = hop(
+        [mlp],
+        swaps,
+        2,
+        beside=(
+            attention_backward(
+                slot_of, lengths, query, key, value, heads_attention, upstream, logs, cosine, sine
+            ),
+        ),
+    )
+    lin_back = own_columns(lin_back)
     w_own = own_columns(w_heads)
 
-    def input_part(step):
-        mine, other = halves(group_of(lin_back, step))
+    def input_part(step, *held):
+        mine, other = halves(after(group_of(lin_back, step), *held))
         return dot_nt(mine, w_own), dot_nt(other, w_own)
 
-    heads_part = contract_rows(jnp.concatenate(group_one, axis=0), lin_back)
-    gain_one_term = jnp.sum(heads_part * w_own.astype(jnp.float32), axis=1) / gain_one
-    gain_totals = ring.total(jnp.stack([gain_one_term, gain_two_term]))
-    heads_sum = both_sequences(heads_part).astype(jnp.bfloat16).reshape(size, own_width, 3 * own_width)
-    heads_sum = lax.all_to_all(heads_sum, "wide", 0, 0, tiled=True).astype(jnp.float32)
-    attention_sums = [
-        heads_sum[:, :, piece * own_width : (piece + 1) * own_width]
-        .transpose(1, 0, 2)
-        .reshape(own_width, model_width)
-        for piece in range(3)
-    ]
-    norm_one_back = ring.scatter(input_part)
+    pulled = Stream(ring.scatter(input_part))
+    side = lax.axis_index("narrow").reshape(1)
+    keep, give, gain_one_sum = hop(
+        [mlp],
+        swaps,
+        work=functools.partial(heads_grads, rows=own_width),
+        given=(all_one, lin_back, w_own, side),
+    )
+    while mlp.asked is not None:
+        hop([mlp], swaps)
+    block_output = (residual + mlp.result).astype(jnp.bfloat16)
+    totals = Stream(ring.total(jnp.stack([gain_one_sum[0] / gain_one, gain_two_term])))
+    hop([totals])
+
+    def before(piece, parts, others):
+        return (swapped(piece), *sum_pieces(parts, others))
+
+    given, gate_sum = hop([pulled, totals], work=before, given=(give, *swaps.sums("gate")))
+    heads_sum = lax.all_to_all(
+        (keep.astype(jnp.float32) + given.astype(jnp.float32)).astype(jnp.bfloat16),
+        "wide",
+        0,
+        0,
+        tiled=True,
+    )
+    out_parts = hop(
+        [pulled, totals],
+        swaps,
+        work=functools.partial(weight_grads, rows=own_width),
+        given=([attention], sum(group_branch, [])),
+    )
+    while swaps.waiting:
+        hop([], swaps)
+    swaps.add("out", out_parts)
+    (up_sum,) = hop([pulled, totals], swaps, work=sum_pieces, given=swaps.sums("up"))
+    far, out_sum = hop([pulled, totals], work=before, given=(heads_sum, *swaps.sums("out")))
+    while pulled.asked is not None or totals.asked is not None:
+        hop([pulled, totals])
+    norm_one_back = pulled.result
+    gain_totals = totals.result
+    attention_sums = assemble(heads_sum, far, side, 3)
     input_back = residual_back + norm_back(norm_one_back, normed_one, gain_one, factor_one)
     return (
         block_output[None],
@@ -533,8 +857,8 @@
         attention_sums[2],
         out_sum,
         gain_totals[1],
-        both_sum[:units],
-        both_sum[units:],
+        gate_sum,
+        up_sum,
         down_sum,
     )
 

time: 692 us -> 610 us (0.88)
  local copies, waits for them, and re-layouts: 96.4 us -> 40 us
  Pallas kernels: 54.5 us -> 108 us
  waiting for transfers between devices: 243 us -> 203 us
  matrix products: 115 us -> 88.9 us
  starting transfers between devices: 127 us -> 116 us
    ppermute x32, waiting for transfers between devices: 119 us -> 52.8 us  [backward(): return lax.ppermute(array, 'wide', self.behind)]
    pallas_call x0 -> x10, Pallas kernels: none -> 63 us  [the longest x4 32.1 us: weight_grads(): pl.pallas_call(functools.partial(grads_kernel, len(lefts), len(rights)),...]
    unnamed x201 -> x261, local copies, waits for them, and re-layouts: 72.6 us -> 26.4 us
    dot_general x4 -> x0, matrix products: 29.6 us -> none  [contract_rows(): lax.dot_general(left_side, right_side, (((0,), (0,)), ((), ())), preferre...]
    ppermute x32, waiting for transfers between devices: 67.4 us -> 92.5 us  [forward(): return lax.ppermute(array, 'wide', self.ahead)]
    ppermute x32, starting transfers between devices: 55.4 us -> 39.6 us  [forward(): return lax.ppermute(array, 'wide', self.ahead)]
    ppermute x9 -> x21, starting transfers between devices: 8.34 us -> 23.3 us  [the longest x17 18.4 us: swapped(): return lax.ppermute(part, 'narrow', [(0, 1), (1, 0)])]
    convert_element_type x8 -> x12, other arithmetic: 4.64 us -> 15.4 us  [the longest x8 10.6 us: scatter(): held = (low.astype(jnp.bfloat16), high.astype(jnp.bfloat16))]
  transfers between devices with their start and end apart: 131 -> 143, of which waited for: 41 -> 53; matrix products, arithmetic and copies ran while one was open for 32% -> 21% of each run, Pallas kernels for 4% -> 17%
where the time goes in v2:
time: 610 us; the launch traced here: 599 us
  waiting for transfers between devices  203 us (33%)
  starting transfers between devices  116 us (19%)
  Pallas kernels  108 us (18%)
  matrix products  88.9 us (15%)
  other arithmetic  40.5 us (7%)
  local copies, waits for them, and re-layouts  40 us (7%)
    ppermute x32, waiting for transfers between devices, forward(): return lax.ppermute(array, 'wide', self.ahead)  92.5 us
    ppermute x32, waiting for transfers between devices, backward(): return lax.ppermute(array, 'wide', self.behind)  52.8 us
    dot_general x25, matrix products, dot_nt(): lax.dot_general(a, b, (((1,), (1,)), ((), ())), preferred_element_type=jn...  48.1 us
    dot_general x31, matrix products, dot_nn(): lax.dot_general(a, b, (((1,), (0,)), ((), ())), preferred_element_type=jn...  40.8 us
    ppermute x32, starting transfers between devices, forward(): return lax.ppermute(array, 'wide', self.ahead)  39.6 us
    ppermute x17, waiting for transfers between devices, swapped(): return lax.ppermute(part, 'narrow', [(0, 1), (1, 0)])  36.8 us
    ppermute x32, starting transfers between devices, backward(): return lax.ppermute(array, 'wide', self.behind)  32.7 us
    pallas_call x4, Pallas kernels, weight_grads(): pl.pallas_call(functools.partial(grads_kernel, len(lefts), len(rights)),...  32.1 us
  transfers between devices with their start and end apart: 143, of which 53 were waited for; matrix products, arithmetic and copies ran while one was open for 21% of the time, Pallas kernels for 17%

profile of v2, /device:TPU:0, one launch (start us, length us, event | category | flops | bytes accessed | tf_op | source)
XLA Modules:
  0.0 599.5 jit_solution(16537556680384129115)
XLA Ops:
  2.8 2.2 constant_dynamic-update-slice_fusion.17
  5.0 3.0 collective-permute-start.1
  10.9 6.5 %all-to-all-start = ((bf16[16,64,384]{2,1,0:T(8,128)(2,1)}), bf16[16,64,384]{2,1,0:T(8,128)(2,1)S(1)}, u32[]{:S(2)}, u32[]{:S(2)}) async-start(bf16[16,64,384]{2,1,0:T(8,128)(2,1)} %slice_select_fusion), calls=%async_computation | async-start | bytes 1572864 | tf_op jit(solution)/shard_map/all_to_all | solution.py:690
  19.0 4.7 fusion.161
  24.9 2.6 collective-permute-start.5
  33.4 10.0 %collective-permute-done.5 = bf16[128,2048]{1,0:T(8,128)(2,1)} collective-permute-done((bf16[128,2048]{1,0:T(8,128)(2,1)}, bf16[128,2048]{1,0:T(8,128)(2,1)}, u32[]{:S(2)}, u32[]{:S(2)}) %collective-permute-start.5) | collective-permute-done | bytes 524320 | tf_op jit(solution)/shard_map/ppermute | solution.py:498
  43.4 2.2 collective-permute-done.6
  46.1 5.7 collective-permute-start.9
  58.9 5.3 collective-permute-done.10
  74.8 3.0 collective-permute-done.14
  83.3 9.2 %fusion.294.lin_ref = f32[2048,384]{1,0:T(8,128)} fusion(bf16[2048,2048]{1,0:T(8,128)(2,1)} %constant_dynamic-update-slice_fusion.left_ref, bf16[2048,384]{1,0:T(8,128)(2,1)S(1)} %bitcast.108), kind=kOutput, calls=%fused_computation.401 | convolution fusion | flops 3221225472 | bytes 13107200 | tf_op jit(solution)/shard_map/dot_general | solution.py:21
  95.7 20.1 %attention_forward.1 = (bf16[2048,128]{1,0:T(8,128)(2,1)}, bf16[2048,128]{1,0:T(8,128)(2,1)}, bf16[2048,128]{1,0:T(8,128)(2,1)}, bf16[2048,128]{1,0:T(8,128)(2,1)}, f32[8,2048]{1,0:T(8,128)}) custom-call(s32[16]{0:T(128)} %dynamic-slice_bitcast_fusion.slot_ref, s32[1]{0:T(128)} %copy.65.length_ref, f32[2048,384]{1,0:T(8,128)} %fusion.294.lin_ref, ...), custom_call_target="tpu_custom_call" | custom-call | flops 2147483648 | bytes 6291456 | tf_op jit(solution)/shard_map/attention_forward/pallas_call | solution.py:129
  123.9 9.9 %collective-permute-done.27.refs_11_ = bf16[128,2048]{1,0:T(8,128)(2,1)S(1)} collective-permute-done((bf16[128,2048]{1,0:T(8,128)(2,1)S(1)}, bf16[128,2048]{1,0:T(8,128)(2,1)S(1)}, u32[]{:S(2)}, u32[]{:S(2)}) %collective-permute-start.27) | collective-permute-done | bytes 524320 | tf_op jit(solution)/shard_map/ppermute | solution.py:498
  135.8 4.4 collective-permute-done.25
  146.4 9.0 %collective-permute-done.31.refs_15_ = bf16[128,2048]{1,0:T(8,128)(2,1)S(1)} collective-permute-done((bf16[128,2048]{1,0:T(8,128)(2,1)S(1)}, bf16[128,2048]{1,0:T(8,128)(2,1)S(1)}, u32[]{:S(2)}, u32[]{:S(2)}) %collective-permute-start.31) | collective-permute-done | bytes 524320 | tf_op jit(solution)/shard_map/ppermute | solution.py:498
  155.8 8.8 %collective-permute-done.30 = bf16[128,2048]{1,0:T(8,128)(2,1)S(1)} collective-permute-done((bf16[128,2048]{1,0:T(8,128)(2,1)S(1)}, bf16[128,2048]{1,0:T(8,128)(2,1)S(1)}, u32[]{:S(2)}, u32[]{:S(2)}) %collective-permute-start.30) | collective-permute-done | bytes 524320 | tf_op jit(solution)/shard_map/ppermute | solution.py:498
  169.7 14.0 %collective-permute-done.35.refs_19_ = bf16[64,2048]{1,0:T(8,128)(2,1)S(1)} collective-permute-done((bf16[64,2048]{1,0:T(8,128)(2,1)S(1)}, bf16[64,2048]{1,0:T(8,128)(2,1)S(1)}, u32[]{:S(2)}, u32[]{:S(2)}) %collective-permute-start.35) | collective-permute-done | bytes 262176 | tf_op jit(solution)/shard_map/ppermute | solution.py:498
  186.6 7.7 %collective-permute-done.37 = bf16[128,2048]{1,0:T(8,128)(2,1)S(1)} collective-permute-done((bf16[128,2048]{1,0:T(8,128)(2,1)S(1)}, bf16[128,2048]{1,0:T(8,128)(2,1)S(1)}, u32[]{:S(2)}, u32[]{:S(2)}) %collective-permute-start.37) | collective-permute-done | bytes 524320 | tf_op jit(solution)/shard_map/ppermute | solution.py:501
  198.2 11.8 %collective-permute-done.39.refs_7_ = bf16[128,2048]{1,0:T(8,128)(2,1)S(1)} collective-permute-done((bf16[128,2048]{1,0:T(8,128)(2,1)S(1)}, bf16[128,2048]{1,0:T(8,128)(2,1)S(1)}, u32[]{:S(2)}, u32[]{:S(2)}) %collective-permute-start.39) | collective-permute-done | bytes 524320 | tf_op jit(solution)/shard_map/ppermute | solution.py:498
  216.6 7.6 %collective-permute-done.41.refs_11_ = bf16[128,2048]{1,0:T(8,128)(2,1)S(1)} collective-permute-done((bf16[128,2048]{1,0:T(8,128)(2,1)S(1)}, bf16[128,2048]{1,0:T(8,128)(2,1)S(1)}, u32[]{:S(2)}, u32[]{:S(2)}) %collective-permute-start.41) | collective-permute-done | bytes 524320 | tf_op jit(solution)/shard_map/ppermute | solution.py:498
  227.2 2.4 fusion.4
  231.2 3.5 multiply_convert_fusion.7
  235.8 4.7 collective-permute-done.45.refs_15_
  240.5 3.5 collective-permute-done.46.refs_16_
  246.2 2.4 fusion.20
  248.7 4.1 multiply_convert_fusion.4
  259.4 2.4 fusion.36
  261.9 3.9 multiply_convert_fusion.1
  270.8 6.2 %collective-permute-done.69 = bf16[64,2048]{1,0:T(8,128)(2,1)S(1)} collective-permute-done((bf16[64,2048]{1,0:T(8,128)(2,1)S(1)}, bf16[64,2048]{1,0:T(8,128)(2,1)S(1)}, u32[]{:S(2)}, u32[]{:S(2)}) %collective-permute-start.69) | collective-permute-done | bytes 262176 | tf_op jit(solution)/shard_map/ppermute | solution.py:501
  281.3 2.2 convolution_convert_fusion.10
  287.7 8.7 %weight_grads.4 = (bf16[128,2048]{1,0:T(8,128)(2,1)}, bf16[128,2048]{1,0:T(8,128)(2,1)}, bf16[128,2048]{1,0:T(8,128)(2,1)}, bf16[128,2048]{1,0:T(8,128)(2,1)}) custom-call(bf16[256,512]{1,0:T(8,128)(2,1)} %get-tuple-element.507.refs_0_, bf16[512,512]{1,0:T(8,128)(2,1)} %get-tuple-element.476.refs_1_, bf16[512,512]{1,0:T(8,128)(2,1)} %get-tuple-element.438.refs_2_, ...), custom_call_target="tpu_custom_call" | custom-call | flops 1024 | bytes 1024 | tf_op jit(solution)/shard_map/weight_grads/pallas_call | solution.py:360
  299.2 2.6 convert_add_fusion.6
  313.8 8.4 %collective-permute-done.77.refs_4_ = bf16[128,2048]{1,0:T(8,128)(2,1)S(1)} collective-permute-done((bf16[128,2048]{1,0:T(8,128)(2,1)S(1)}, bf16[128,2048]{1,0:T(8,128)(2,1)S(1)}, u32[]{:S(2)}, u32[]{:S(2)}) %collective-permute-start.77) | collective-permute-done | bytes 524320 | tf_op jit(solution)/shard_map/ppermute | solution.py:619
  329.6 2.9 collective-permute-done.81.refs_5_
  334.1 3.1 collective-permute-done.79
  344.4 3.0 collective-permute-done.86.refs_6_
  349.0 8.7 %weight_grads.5 = (bf16[128,2048]{1,0:T(8,128)(2,1)}, bf16[128,2048]{1,0:T(8,128)(2,1)}, bf16[128,2048]{1,0:T(8,128)(2,1)}, bf16[128,2048]{1,0:T(8,128)(2,1)}) custom-call(bf16[256,512]{1,0:T(8,128)(2,1)} %get-tuple-element.409.refs_0_, bf16[512,512]{1,0:T(8,128)(2,1)} %get-tuple-element.410.refs_1_, bf16[512,512]{1,0:T(8,128)(2,1)} %get-tuple-element.411.refs_2_, ...), custom_call_target="tpu_custom_call" | custom-call | flops 1024 | bytes 1024 | tf_op jit(solution)/shard_map/weight_grads/pallas_call | solution.py:360
  365.7 9.6 %collective-permute-done.89.refs_7_ = bf16[128,2048]{1,0:T(8,128)(2,1)} collective-permute-done((bf16[128,2048]{1,0:T(8,128)(2,1)}, bf16[128,2048]{1,0:T(8,128)(2,1)}, u32[]{:S(2)}, u32[]{:S(2)}) %collective-permute-start.89) | collective-permute-done | bytes 524320 | tf_op jit(solution)/shard_map/ppermute | solution.py:498
  376.4 6.8 %collective-permute-done.91 = bf16[128,2048]{1,0:T(8,128)(2,1)S(1)} collective-permute-done((bf16[128,2048]{1,0:T(8,128)(2,1)S(1)}, bf16[128,2048]{1,0:T(8,128)(2,1)S(1)}, u32[]{:S(2)}, u32[]{:S(2)}) %collective-permute-start.91) | collective-permute-done | bytes 524320 | tf_op jit(solution)/shard_map/ppermute | solution.py:501
  387.7 8.7 %weight_grads.6 = (bf16[128,2048]{1,0:T(8,128)(2,1)}, bf16[128,2048]{1,0:T(8,128)(2,1)}, bf16[128,2048]{1,0:T(8,128)(2,1)}, bf16[128,2048]{1,0:T(8,128)(2,1)}) custom-call(bf16[256,512]{1,0:T(8,128)(2,1)} %get-tuple-element.447.refs_0_, bf16[512,512]{1,0:T(8,128)(2,1)} %get-tuple-element.448.refs_1_, bf16[512,512]{1,0:T(8,128)(2,1)} %get-tuple-element.449.refs_2_, ...), custom_call_target="tpu_custom_call" | custom-call | flops 1024 | bytes 1024 | tf_op jit(solution)/shard_map/weight_grads/pallas_call | solution.py:360
  401.4 4.8 sum_pieces.4
  407.5 2.9 fusion.88
  413.6 2.3 fusion.112
  418.0 2.4 fusion.91
  430.4 24.7 %attention_backward.1.right_ref = bf16[2048,384]{1,0:T(8,128)(2,1)} custom-call(s32[16]{0:T(128)} %dynamic-slice_bitcast_fusion.slot_ref, s32[1]{0:T(128)} %copy.65.length_ref, bf16[2048,128]{1,0:T(8,128)(2,1)} %get-tuple-element.479.query_ref, bf16[2048,128]{1,0:T(8,128)(2,1)} %get-tuple-element.480.key_ref, ...), custom_call_target="tpu_custom_call" | custom-call | flops 5368709120 | bytes 9437184 | tf_op jit(solution)/shard_map/attention_backward/pallas_call | solution.py:242
  462.1 2.3 fusion.110
  468.8 9.6 %heads_grads.1 = (bf16[16,64,384]{2,1,0:T(8,128)(2,1)}, bf16[16,64,384]{2,1,0:T(8,128)(2,1)}, f32[1,2048]{1,0:T(1,128)}) custom-call(s32[1]{0:T(128)} %bitcast.10.upper_ref.side_ref, bf16[2048,2048]{1,0:T(8,128)(2,1)} %constant_dynamic-update-slice_fusion.left_ref, bf16[2048,384]{1,0:T(8,128)(2,1)} %attention_backward.1.right_ref, bf16[2048,384]{1,0:T(8,128)(2,1)} %bitcast.109), custom_call_target="tpu_custom_call" | custom-call | flops 1024 | bytes 1024 | tf_op jit(solution)/shard_map/heads_grads/pallas_call | solution.py:394
  485.6 4.8 sum_pieces.5
  492.6 9.0 %collective-permute-done.125 = bf16[16,64,384]{2,1,0:T(8,128)(2,1)} collective-permute-done((bf16[16,64,384]{2,1,0:T(8,128)(2,1)}, bf16[16,64,384]{2,1,0:T(8,128)(2,1)}, u32[]{:S(2)}, u32[]{:S(2)}) %collective-permute-start.125) | collective-permute-done | bytes 786464 | tf_op jit(solution)/shard_map/ppermute | solution.py:619
  509.1 5.9 weight_grads.7.refs_0_
  514.9 4.7 collective-permute-done.130.refs_7_
  523.6 2.3 fusion.108
  527.6 2.2 add_convert_fusion
  529.8 4.3 all-to-all-start.1
  538.0 2.3 fusion.233
  540.3 2.7 collective-permute-start.134
  544.3 4.9 sum_pieces.6
  549.4 17.5 %collective-permute-done.134 = f32[2,2048]{1,0:T(2,128)S(1)} collective-permute-done((f32[2,2048]{1,0:T(2,128)S(1)}, f32[2,2048]{1,0:T(2,128)S(1)}, u32[]{:S(2)}, u32[]{:S(2)}) %collective-permute-start.134) | collective-permute-done | bytes 16416 | tf_op jit(solution)/shard_map/ppermute | solution.py:555
  576.4 2.2 fusion.163
  578.7 3.6 sum_pieces.7
  582.3 7.3 %collective-permute-done.139 = f32[2,2048]{1,0:T(2,128)S(1)} collective-permute-done((f32[2,2048]{1,0:T(2,128)S(1)}, f32[2,2048]{1,0:T(2,128)S(1)}, u32[]{:S(2)}, u32[]{:S(2)}) %collective-permute-start.139) | collective-permute-done | bytes 16416 | tf_op jit(solution)/shard_map/ppermute | solution.py:619
  591.4 2.1 fusion.100
  593.5 3.2 assemble.1
  596.7 2.5 fusion.104
  (632 shorter events, 219.5 us)
Async XLA Ops:
  5.0 18.7 %collective-permute-start.1 = (bf16[128,2048]{1,0:T(8,128)(2,1)}, bf16[128,2048]{1,0:T(8,128)(2,1)}, u32[]{:S(2)}, u32[]{:S(2)}) collective-permute-start(bf16[128,2048]{1,0:T(8,128)(2,1)} %get-tuple-element.617), channel_id=1, source_target_pairs={{0,4},{1,5},{4,8},{5,9},{8,12},{9,13},{12,14},{13,15},{14,10},{15,... | collective-permute-start | bytes 1572872 | tf_op jit(solution)/shard_map/ppermute | solution.py:498
  8.0 16.9 %collective-permute-start.2 = (bf16[128,2048]{1,0:T(8,128)(2,1)}, bf16[128,2048]{1,0:T(8,128)(2,1)}, u32[]{:S(2)}, u32[]{:S(2)}) collective-permute-start(bf16[128,2048]{1,0:T(8,128)(2,1)} %get-tuple-element.617), channel_id=1, source_target_pairs={{4,0},{5,1},{8,4},{9,5},{12,8},{13,9},{14,12},{15,13},{10,14},{11,... | collective-permute-start | bytes 1572872 | tf_op jit(solution)/shard_map/ppermute | solution.py:501
  8.0 19.7 %collective-permute-start = (bf16[128,2048]{1,0:T(8,128)(2,1)}, bf16[128,2048]{1,0:T(8,128)(2,1)}, u32[]{:S(2)}, u32[]{:S(2)}) collective-permute-start(bf16[128,2048]{1,0:T(8,128)(2,1)} %get-tuple-element.617), channel_id=1, source_target_pairs={{0,1},{1,0},{2,3},{3,2},{4,5},{5,4},{6,7},{7,6},{8,9},{9,8},{10,11... | collective-permute-start | bytes 1572872 | tf_op jit(solution)/shard_map/ppermute | solution.py:504
  10.9 46.5 %all-to-all-start = ((bf16[16,64,384]{2,1,0:T(8,128)(2,1)}), bf16[16,64,384]{2,1,0:T(8,128)(2,1)S(1)}, u32[]{:S(2)}, u32[]{:S(2)}) async-start(bf16[16,64,384]{2,1,0:T(8,128)(2,1)} %slice_select_fusion), calls=%async_computation | async-start | bytes 1572864 | tf_op jit(solution)/shard_map/all_to_all | solution.py:690
  24.9 21.3 %collective-permute-start.3 = (bf16[128,2048]{1,0:T(8,128)(2,1)}, bf16[128,2048]{1,0:T(8,128)(2,1)S(1)}, u32[]{:S(2)}, u32[]{:S(2)}) collective-permute-start(bf16[128,2048]{1,0:T(8,128)(2,1)} %collective-permute-done.1), channel_id=1, source_target_pairs={{0,1},{1,0},{2,3},{3,2},{4,5},{5,4},{6,7},{7,6},{8,9},{9,8},{10,11... | collective-permute-start | bytes 1572872 | tf_op jit(solution)/shard_map/ppermute | solution.py:504
  24.9 18.5 %collective-permute-start.5 = (bf16[128,2048]{1,0:T(8,128)(2,1)}, bf16[128,2048]{1,0:T(8,128)(2,1)}, u32[]{:S(2)}, u32[]{:S(2)}) collective-permute-start(bf16[128,2048]{1,0:T(8,128)(2,1)} %collective-permute-done.1), channel_id=1, source_target_pairs={{0,4},{1,5},{4,8},{5,9},{8,12},{9,13},{12,14},{13,15},{14,10},{15,... | collective-permute-start | bytes 1572872 | tf_op jit(solution)/shard_map/ppermute | solution.py:498
  27.5 25.2 %collective-permute-start.4 = (bf16[128,2048]{1,0:T(8,128)(2,1)}, bf16[128,2048]{1,0:T(8,128)(2,1)S(1)}, u32[]{:S(2)}, u32[]{:S(2)}) collective-permute-start(bf16[128,2048]{1,0:T(8,128)(2,1)} %collective-permute-done.2), channel_id=1, source_target_pairs={{0,1},{1,0},{2,3},{3,2},{4,5},{5,4},{6,7},{7,6},{8,9},{9,8},{10,11... | collective-permute-start | bytes 1572872 | tf_op jit(solution)/shard_map/ppermute | solution.py:504
  27.7 17.9 %collective-permute-start.6 = (bf16[128,2048]{1,0:T(8,128)(2,1)}, bf16[128,2048]{1,0:T(8,128)(2,1)}, u32[]{:S(2)}, u32[]{:S(2)}) collective-permute-start(bf16[128,2048]{1,0:T(8,128)(2,1)} %collective-permute-done.2), channel_id=1, source_target_pairs={{4,0},{5,1},{8,4},{9,5},{12,8},{13,9},{14,12},{15,13},{10,14},{11,... | collective-permute-start | bytes 1572872 | tf_op jit(solution)/shard_map/ppermute | solution.py:501
  45.6 24.0 %collective-permute-start.8 = (bf16[128,2048]{1,0:T(8,128)(2,1)}, bf16[128,2048]{1,0:T(8,128)(2,1)}, u32[]{:S(2)}, u32[]{:S(2)}) collective-permute-start(bf16[128,2048]{1,0:T(8,128)(2,1)} %collective-permute-done.6), channel_id=1, source_target_pairs={{0,1},{1,0},{2,3},{3,2},{4,5},{5,4},{6,7},{7,6},{8,9},{9,8},{10,11... | collective-permute-start | bytes 1572872 | tf_op jit(solution)/shard_map/ppermute | solution.py:504
  45.6 18.5 %collective-permute-start.10 = (bf16[128,2048]{1,0:T(8,128)(2,1)}, bf16[128,2048]{1,0:T(8,128)(2,1)S(1)}, u32[]{:S(2)}, u32[]{:S(2)}) collective-permute-start(bf16[128,2048]{1,0:T(8,128)(2,1)} %collective-permute-done.6), channel_id=1, source_target_pairs={{4,0},{5,1},{8,4},{9,5},{12,8},{13,9},{14,12},{15,13},{10,14},{11,... | collective-permute-start | bytes 1572872 | tf_op jit(solution)/shard_map/ppermute | solution.py:501
  45.9 20.3 %collective-permute-start.7 = (bf16[128,2048]{1,0:T(8,128)(2,1)}, bf16[128,2048]{1,0:T(8,128)(2,1)}, u32[]{:S(2)}, u32[]{:S(2)}) collective-permute-start(bf16[128,2048]{1,0:T(8,128)(2,1)} %collective-permute-done.5), channel_id=1, source_target_pairs={{0,1},{1,0},{2,3},{3,2},{4,5},{5,4},{6,7},{7,6},{8,9},{9,8},{10,11... | collective-permute-start | bytes 1572872 | tf_op jit(solution)/shard_map/ppermute | solution.py:504
  46.1 18.5 %collective-permute-start.9 = (bf16[128,2048]{1,0:T(8,128)(2,1)}, bf16[128,2048]{1,0:T(8,128)(2,1)}, u32[]{:S(2)}, u32[]{:S(2)}) collective-permute-start(bf16[128,2048]{1,0:T(8,128)(2,1)} %collective-permute-done.5), channel_id=1, source_target_pairs={{0,4},{1,5},{4,8},{5,9},{8,12},{9,13},{12,14},{13,15},{14,10},{15,... | collective-permute-start | bytes 1572872 | tf_op jit(solution)/shard_map/ppermute | solution.py:498
  57.4 25.6 %collective-permute-start.17 = (bf16[16,64,384]{2,1,0:T(8,128)(2,1)S(1)}, bf16[16,64,384]{2,1,0:T(8,128)(2,1)S(1)}, u32[]{:S(2)}, u32[]{:S(2)}) collective-permute-start(bf16[16,64,384]{2,1,0:T(8,128)(2,1)S(1)} %all-to-all-done), channel_id=1, source_target_pairs={{0,16},{16,0},{1,17},{17,1},{2,18},{18,2},{3,19},{19,3},{4,20},{20... | collective-permute-start | bytes 2359304 | tf_op jit(solution)/shard_map/ppermute | solution.py:619
  92.5 23.4 %collective-permute-start.18 = (bf16[128,2048]{1,0:T(8,128)(2,1)S(1)}, bf16[128,2048]{1,0:T(8,128)(2,1)S(1)}, u32[]{:S(2)}, u32[]{:S(2)}) collective-permute-start(bf16[128,2048]{1,0:T(8,128)(2,1)S(1)} %copy-done.35), channel_id=1, source_target_pairs={{0,4},{1,5},{4,8},{5,9},{8,12},{9,13},{12,14},{13,15},{14,10},{15,... | collective-permute-start | bytes 1572872 | tf_op jit(solution)/shard_map/ppermute | solution.py:498
  94.2 21.7 %collective-permute-start.19 = (bf16[128,2048]{1,0:T(8,128)(2,1)S(1)}, bf16[128,2048]{1,0:T(8,128)(2,1)}, u32[]{:S(2)}, u32[]{:S(2)}) collective-permute-start(bf16[128,2048]{1,0:T(8,128)(2,1)S(1)} %copy-done.35), channel_id=1, source_target_pairs={{4,0},{5,1},{8,4},{9,5},{12,8},{13,9},{14,12},{15,13},{10,14},{11,... | collective-permute-start | bytes 1572872 | tf_op jit(solution)/shard_map/ppermute | solution.py:501
  118.4 24.2 %collective-permute-start.23 = (bf16[256,2048]{1,0:T(8,128)(2,1)S(1)}, bf16[256,2048]{1,0:T(8,128)(2,1)S(1)}, u32[]{:S(2)}, u32[]{:S(2)}) collective-permute-start(bf16[256,2048]{1,0:T(8,128)(2,1)S(1)} %convolution_convert_fusion.6), channel_id=1, source_target_pairs={{0,1},{1,0},{2,3},{3,2},{4,5},{5,4},{6,7},{7,6},{8,9},{9,8},{10,11... | collective-permute-start | bytes 3145736 | tf_op jit(solution)/shard_map/ppermute | solution.py:504
  121.4 18.8 %collective-permute-start.25 = (bf16[64,2048]{1,0:T(8,128)(2,1)S(1)}, bf16[64,2048]{1,0:T(8,128)(2,1)S(1)}, u32[]{:S(2)}, u32[]{:S(2)}) collective-permute-start(bf16[64,2048]{1,0:T(8,128)(2,1)S(1)} %get-tuple-element.685), channel_id=1, source_target_pairs={{4,0},{5,1},{8,4},{9,5},{12,8},{13,9},{14,12},{15,13},{10,14},{11,... | collective-permute-start | bytes 786440 | tf_op jit(solution)/shard_map/ppermute | solution.py:501
  121.8 18.4 %collective-permute-start.26 = (bf16[64,2048]{1,0:T(8,128)(2,1)S(1)}, bf16[64,2048]{1,0:T(8,128)(2,1)S(1)}, u32[]{:S(2)}, u32[]{:S(2)}) collective-permute-start(bf16[64,2048]{1,0:T(8,128)(2,1)S(1)} %get-tuple-element.684), channel_id=1, source_target_pairs={{0,4},{1,5},{4,8},{5,9},{8,12},{9,13},{12,14},{13,15},{14,10},{15,... | collective-permute-start | bytes 786440 | tf_op jit(solution)/shard_map/ppermute | solution.py:498
  143.3 21.3 %collective-permute-start.30 = (bf16[128,2048]{1,0:T(8,128)(2,1)S(1)}, bf16[128,2048]{1,0:T(8,128)(2,1)S(1)}, u32[]{:S(2)}, u32[]{:S(2)}) collective-permute-start(bf16[128,2048]{1,0:T(8,128)(2,1)S(1)} %pad_maximum_fusion.5), channel_id=1, source_target_pairs={{0,4},{1,5},{4,8},{5,9},{8,12},{9,13},{12,14},{13,15},{14,10},{15,... | collective-permute-start | bytes 1572872 | tf_op jit(solution)/shard_map/ppermute | solution.py:498
  143.7 21.0 %collective-permute-start.29 = (bf16[128,2048]{1,0:T(8,128)(2,1)S(1)}, bf16[128,2048]{1,0:T(8,128)(2,1)S(1)}, u32[]{:S(2)}, u32[]{:S(2)}) collective-permute-start(bf16[128,2048]{1,0:T(8,128)(2,1)S(1)} %pad_maximum_fusion.4), channel_id=1, source_target_pairs={{4,0},{5,1},{8,4},{9,5},{12,8},{13,9},{14,12},{15,13},{10,14},{11,... | collective-permute-start | bytes 1572872 | tf_op jit(solution)/shard_map/ppermute | solution.py:501
  145.9 23.4 %collective-permute-start.21 = (bf16[256,2048]{1,0:T(8,128)(2,1)S(1)}, bf16[256,2048]{1,0:T(8,128)(2,1)S(1)}, u32[]{:S(2)}, u32[]{:S(2)}) collective-permute-start(bf16[256,2048]{1,0:T(8,128)(2,1)S(1)} %convolution_convert_fusion.8), channel_id=1, source_target_pairs={{0,1},{1,0},{2,3},{3,2},{4,5},{5,4},{6,7},{7,6},{8,9},{9,8},{10,11... | collective-permute-start | bytes 3145736 | tf_op jit(solution)/shard_map/ppermute | solution.py:504
  165.0 18.7 %collective-permute-start.33 = (bf16[128,2048]{1,0:T(8,128)(2,1)S(1)}, bf16[128,2048]{1,0:T(8,128)(2,1)S(1)}, u32[]{:S(2)}, u32[]{:S(2)}) collective-permute-start(bf16[128,2048]{1,0:T(8,128)(2,1)S(1)} %get-tuple-element.648), channel_id=1, source_target_pairs={{4,0},{5,1},{8,4},{9,5},{12,8},{13,9},{14,12},{15,13},{10,14},{11,... | collective-permute-start | bytes 1572872 | tf_op jit(solution)/shard_map/ppermute | solution.py:501
  166.7 17.1 %collective-permute-start.34 = (bf16[128,2048]{1,0:T(8,128)(2,1)S(1)}, bf16[128,2048]{1,0:T(8,128)(2,1)S(1)}, u32[]{:S(2)}, u32[]{:S(2)}) collective-permute-start(bf16[128,2048]{1,0:T(8,128)(2,1)S(1)} %get-tuple-element.647), channel_id=1, source_target_pairs={{0,4},{1,5},{4,8},{5,9},{8,12},{9,13},{12,14},{13,15},{14,10},{15,... | collective-permute-start | bytes 1572872 | tf_op jit(solution)/shard_map/ppermute | solution.py:498
  167.1 16.6 %collective-permute-start.35 = (bf16[64,2048]{1,0:T(8,128)(2,1)S(1)}, bf16[64,2048]{1,0:T(8,128)(2,1)S(1)}, u32[]{:S(2)}, u32[]{:S(2)}) collective-permute-start(bf16[64,2048]{1,0:T(8,128)(2,1)S(1)} %slice.417), channel_id=1, source_target_pairs={{0,4},{1,5},{4,8},{5,9},{8,12},{9,13},{12,14},{13,15},{14,10},{15,... | collective-permute-start | bytes 786440 | tf_op jit(solution)/shard_map/ppermute | solution.py:498
  167.5 16.2 %collective-permute-start.36 = (bf16[64,2048]{1,0:T(8,128)(2,1)S(1)}, bf16[64,2048]{1,0:T(8,128)(2,1)S(1)}, u32[]{:S(2)}, u32[]{:S(2)}) collective-permute-start(bf16[64,2048]{1,0:T(8,128)(2,1)S(1)} %slice.418), channel_id=1, source_target_pairs={{4,0},{5,1},{8,4},{9,5},{12,8},{13,9},{14,12},{15,13},{10,14},{11,... | collective-permute-start | bytes 786440 | tf_op jit(solution)/shard_map/ppermute | solution.py:501
  195.6 17.4 %collective-permute-start.43 = (bf16[128,2048]{1,0:T(8,128)(2,1)S(1)}, bf16[128,2048]{1,0:T(8,128)(2,1)S(1)}, u32[]{:S(2)}, u32[]{:S(2)}) collective-permute-start(bf16[128,2048]{1,0:T(8,128)(2,1)S(1)} %multiply_convert_fusion.9.refs_5_), channel_id=1, source_target_pairs={{0,1},{1,0},{2,3},{3,2},{4,5},{5,4},{6,7},{7,6},{8,9},{9,8},{10,11... | collective-permute-start | bytes 1572872 | tf_op jit(solution)/shard_map/ppermute | solution.py:504
  197.9 16.6 %collective-permute-start.44 = (bf16[128,2048]{1,0:T(8,128)(2,1)S(1)}, bf16[128,2048]{1,0:T(8,128)(2,1)S(1)}, u32[]{:S(2)}, u32[]{:S(2)}) collective-permute-start(bf16[128,2048]{1,0:T(8,128)(2,1)S(1)} %copy-done.36), channel_id=1, source_target_pairs={{0,1},{1,0},{2,3},{3,2},{4,5},{5,4},{6,7},{7,6},{8,9},{9,8},{10,11... | collective-permute-start | bytes 1572872 | tf_op jit(solution)/shard_map/ppermute | solution.py:504
  226.0 22.6 %collective-permute-start.55 = (bf16[128,2048]{1,0:T(8,128)(2,1)S(1)}, bf16[128,2048]{1,0:T(8,128)(2,1)S(1)}, u32[]{:S(2)}, u32[]{:S(2)}) collective-permute-start(bf16[128,2048]{1,0:T(8,128)(2,1)S(1)} %collective-permute-done.27.refs_11_), channel_id=1, source_target_pairs={{0,1},{1,0},{2,3},{3,2},{4,5},{5,4},{6,7},{7,6},{8,9},{9,8},{10,11... | collective-permute-start | bytes 1572872 | tf_op jit(solution)/shard_map/ppermute | solution.py:504
  226.1 19.5 %collective-permute-start.53 = (bf16[128,2048]{1,0:T(8,128)(2,1)S(1)}, bf16[128,2048]{1,0:T(8,128)(2,1)S(1)}, u32[]{:S(2)}, u32[]{:S(2)}) collective-permute-start(bf16[128,2048]{1,0:T(8,128)(2,1)S(1)} %collective-permute-done.41.refs_11_), channel_id=1, source_target_pairs={{0,1},{1,0},{2,3},{3,2},{4,5},{5,4},{6,7},{7,6},{8,9},{9,8},{10,11... | collective-permute-start | bytes 1572872 | tf_op jit(solution)/shard_map/ppermute | solution.py:504
  229.6 16.6 %collective-permute-start.54 = (bf16[128,2048]{1,0:T(8,128)(2,1)S(1)}, bf16[128,2048]{1,0:T(8,128)(2,1)S(1)}, u32[]{:S(2)}, u32[]{:S(2)}) collective-permute-start(bf16[128,2048]{1,0:T(8,128)(2,1)S(1)} %collective-permute-done.42.refs_12_), channel_id=1, source_target_pairs={{0,1},{1,0},{2,3},{3,2},{4,5},{5,4},{6,7},{7,6},{8,9},{9,8},{10,11... | collective-permute-start | bytes 1572872 | tf_op jit(solution)/shard_map/ppermute | solution.py:504
  283.5 15.7 %collective-permute-start.71 = (bf16[256,2048]{1,0:T(8,128)(2,1)}, bf16[256,2048]{1,0:T(8,128)(2,1)}, u32[]{:S(2)}, u32[]{:S(2)}) collective-permute-start(bf16[256,2048]{1,0:T(8,128)(2,1)} %convolution_convert_fusion.10), channel_id=1, source_target_pairs={{0,1},{1,0},{2,3},{3,2},{4,5},{5,4},{6,7},{7,6},{8,9},{9,8},{10,11... | collective-permute-start | bytes 3145736 | tf_op jit(solution)/shard_map/ppermute | solution.py:504
  287.7 23.2 %collective-permute-start.61 = (bf16[128,2048]{1,0:T(8,128)(2,1)}, bf16[128,2048]{1,0:T(8,128)(2,1)}, u32[]{:S(2)}, u32[]{:S(2)}) collective-permute-start(bf16[128,2048]{1,0:T(8,128)(2,1)} %convolution_convert_fusion.17), channel_id=1, source_target_pairs={{0,1},{1,0},{2,3},{3,2},{4,5},{5,4},{6,7},{7,6},{8,9},{9,8},{10,11... | collective-permute-start | bytes 1572872 | tf_op jit(solution)/shard_map/ppermute | solution.py:504
  304.8 18.3 %collective-permute-start.74 = (bf16[256,2048]{1,0:T(8,128)(2,1)S(1)}, bf16[256,2048]{1,0:T(8,128)(2,1)S(1)}, u32[]{:S(2)}, u32[]{:S(2)}) collective-permute-start(bf16[256,2048]{1,0:T(8,128)(2,1)S(1)} %convolution_convert_fusion.9), channel_id=1, source_target_pairs={{0,1},{1,0},{2,3},{3,2},{4,5},{5,4},{6,7},{7,6},{8,9},{9,8},{10,11... | collective-permute-start | bytes 3145736 | tf_op jit(solution)/shard_map/ppermute | solution.py:504
  313.3 19.3 %collective-permute-start.81 = (bf16[128,2048]{1,0:T(8,128)(2,1)S(1)}, bf16[128,2048]{1,0:T(8,128)(2,1)S(1)}, u32[]{:S(2)}, u32[]{:S(2)}) collective-permute-start(bf16[128,2048]{1,0:T(8,128)(2,1)S(1)} %copy-done.75), channel_id=1, source_target_pairs={{0,16},{16,0},{1,17},{17,1},{2,18},{18,2},{3,19},{19,3},{4,20},{20... | collective-permute-start | bytes 1572872 | tf_op jit(solution)/shard_map/ppermute | solution.py:619
  337.2 20.6 %collective-permute-start.87 = (bf16[128,2048]{1,0:T(8,128)(2,1)}, bf16[128,2048]{1,0:T(8,128)(2,1)}, u32[]{:S(2)}, u32[]{:S(2)}) collective-permute-start(bf16[128,2048]{1,0:T(8,128)(2,1)} %get-tuple-element.494.refs_3_), channel_id=1, source_target_pairs={{0,16},{16,0},{1,17},{17,1},{2,18},{18,2},{3,19},{19,3},{4,20},{20... | collective-permute-start | bytes 1572872 | tf_op jit(solution)/shard_map/ppermute | solution.py:619
  340.3 17.6 %collective-permute-start.82 = (bf16[128,2048]{1,0:T(8,128)(2,1)S(1)}, bf16[128,2048]{1,0:T(8,128)(2,1)}, u32[]{:S(2)}, u32[]{:S(2)}) collective-permute-start(bf16[128,2048]{1,0:T(8,128)(2,1)S(1)} %get-tuple-element.549.refs_1_), channel_id=1, source_target_pairs={{0,4},{1,5},{4,8},{5,9},{8,12},{9,13},{12,14},{13,15},{14,10},{15,... | collective-permute-start | bytes 1572872 | tf_op jit(solution)/shard_map/ppermute | solution.py:498
  341.1 16.9 %collective-permute-start.83 = (bf16[128,2048]{1,0:T(8,128)(2,1)S(1)}, bf16[128,2048]{1,0:T(8,128)(2,1)}, u32[]{:S(2)}, u32[]{:S(2)}) collective-permute-start(bf16[128,2048]{1,0:T(8,128)(2,1)S(1)} %get-tuple-element.549.refs_1_), channel_id=1, source_target_pairs={{4,0},{5,1},{8,4},{9,5},{12,8},{13,9},{14,12},{15,13},{10,14},{11,... | collective-permute-start | bytes 1572872 | tf_op jit(solution)/shard_map/ppermute | solution.py:501
  362.1 21.1 %collective-permute-start.91 = (bf16[128,2048]{1,0:T(8,128)(2,1)S(1)}, bf16[128,2048]{1,0:T(8,128)(2,1)S(1)}, u32[]{:S(2)}, u32[]{:S(2)}) collective-permute-start(bf16[128,2048]{1,0:T(8,128)(2,1)S(1)} %pad_maximum_fusion.10), channel_id=1, source_target_pairs={{4,0},{5,1},{8,4},{9,5},{12,8},{13,9},{14,12},{15,13},{10,14},{11,... | collective-permute-start | bytes 1572872 | tf_op jit(solution)/shard_map/ppermute | solution.py:501
  363.4 22.9 %collective-permute-start.92 = (bf16[128,2048]{1,0:T(8,128)(2,1)S(1)}, bf16[128,2048]{1,0:T(8,128)(2,1)}, u32[]{:S(2)}, u32[]{:S(2)}) collective-permute-start(bf16[128,2048]{1,0:T(8,128)(2,1)S(1)} %pad_maximum_fusion.11), channel_id=1, source_target_pairs={{0,4},{1,5},{4,8},{5,9},{8,12},{9,13},{12,14},{13,15},{14,10},{15,... | collective-permute-start | bytes 1572872 | tf_op jit(solution)/shard_map/ppermute | solution.py:498
  364.2 22.2 %collective-permute-start.93 = (bf16[128,2048]{1,0:T(8,128)(2,1)S(1)}, bf16[128,2048]{1,0:T(8,128)(2,1)S(1)}, u32[]{:S(2)}, u32[]{:S(2)}) collective-permute-start(bf16[128,2048]{1,0:T(8,128)(2,1)S(1)} %copy-done.73), channel_id=1, source_target_pairs={{0,16},{16,0},{1,17},{17,1},{2,18},{18,2},{3,19},{19,3},{4,20},{20... | collective-permute-start | bytes 1572872 | tf_op jit(solution)/shard_map/ppermute | solution.py:619
  375.3 22.0 %collective-permute-start.100 = (bf16[128,2048]{1,0:T(8,128)(2,1)S(1)}, bf16[128,2048]{1,0:T(8,128)(2,1)}, u32[]{:S(2)}, u32[]{:S(2)}) collective-permute-start(bf16[128,2048]{1,0:T(8,128)(2,1)S(1)} %get-tuple-element.549.refs_1_), channel_id=1, source_target_pairs={{0,1},{1,0},{2,3},{3,2},{4,5},{5,4},{6,7},{7,6},{8,9},{9,8},{10,11... | collective-permute-start | bytes 1572872 | tf_op jit(solution)/shard_map/ppermute | solution.py:504
  376.4 21.6 %collective-permute-start.101 = (bf16[128,2048]{1,0:T(8,128)(2,1)}, bf16[128,2048]{1,0:T(8,128)(2,1)}, u32[]{:S(2)}, u32[]{:S(2)}) collective-permute-start(bf16[128,2048]{1,0:T(8,128)(2,1)} %collective-permute-done.82.refs_3_), channel_id=1, source_target_pairs={{0,1},{1,0},{2,3},{3,2},{4,5},{5,4},{6,7},{7,6},{8,9},{9,8},{10,11... | collective-permute-start | bytes 1572872 | tf_op jit(solution)/shard_map/ppermute | solution.py:504
  386.3 26.0 %collective-permute-start.88 = (bf16[256,2048]{1,0:T(8,128)(2,1)S(1)}, bf16[256,2048]{1,0:T(8,128)(2,1)S(1)}, u32[]{:S(2)}, u32[]{:S(2)}) collective-permute-start(bf16[256,2048]{1,0:T(8,128)(2,1)S(1)} %convolution_convert_fusion.4), channel_id=1, source_target_pairs={{0,1},{1,0},{2,3},{3,2},{4,5},{5,4},{6,7},{7,6},{8,9},{9,8},{10,11... | collective-permute-start | bytes 3145736 | tf_op jit(solution)/shard_map/ppermute | solution.py:504
  387.2 19.0 %collective-permute-start.102 = (bf16[128,2048]{1,0:T(8,128)(2,1)}, bf16[128,2048]{1,0:T(8,128)(2,1)}, u32[]{:S(2)}, u32[]{:S(2)}) collective-permute-start(bf16[128,2048]{1,0:T(8,128)(2,1)} %collective-permute-done.83.refs_4_), channel_id=1, source_target_pairs={{0,1},{1,0},{2,3},{3,2},{4,5},{5,4},{6,7},{7,6},{8,9},{9,8},{10,11... | collective-permute-start | bytes 1572872 | tf_op jit(solution)/shard_map/ppermute | solution.py:504
  406.2 15.9 %collective-permute-start.112 = (bf16[128,2048]{1,0:T(8,128)(2,1)}, bf16[128,2048]{1,0:T(8,128)(2,1)S(1)}, u32[]{:S(2)}, u32[]{:S(2)}) collective-permute-start(bf16[128,2048]{1,0:T(8,128)(2,1)} %get-tuple-element.535.refs_3_), channel_id=1, source_target_pairs={{0,16},{16,0},{1,17},{17,1},{2,18},{18,2},{3,19},{19,3},{4,20},{20... | collective-permute-start | bytes 1572872 | tf_op jit(solution)/shard_map/ppermute | solution.py:619
  422.2 32.9 %collective-permute-start.98 = (bf16[128,2048]{1,0:T(8,128)(2,1)S(1)}, bf16[128,2048]{1,0:T(8,128)(2,1)}, u32[]{:S(2)}, u32[]{:S(2)}) collective-permute-start(bf16[128,2048]{1,0:T(8,128)(2,1)S(1)} %copy-done.69), channel_id=1, source_target_pairs={{0,16},{16,0},{1,17},{17,1},{2,18},{18,2},{3,19},{19,3},{4,20},{20... | collective-permute-start | bytes 1572872 | tf_op jit(solution)/shard_map/ppermute | solution.py:619
  424.4 32.0 %collective-permute-start.99 = (bf16[128,2048]{1,0:T(8,128)(2,1)}, bf16[128,2048]{1,0:T(8,128)(2,1)}, u32[]{:S(2)}, u32[]{:S(2)}) collective-permute-start(bf16[128,2048]{1,0:T(8,128)(2,1)} %get-tuple-element.580.refs_1_), channel_id=1, source_target_pairs={{0,16},{16,0},{1,17},{17,1},{2,18},{18,2},{3,19},{19,3},{4,20},{20... | collective-permute-start | bytes 1572872 | tf_op jit(solution)/shard_map/ppermute | solution.py:619
  425.1 31.4 %collective-permute-start.96 = (bf16[128,2048]{1,0:T(8,128)(2,1)}, bf16[128,2048]{1,0:T(8,128)(2,1)}, u32[]{:S(2)}, u32[]{:S(2)}) collective-permute-start(bf16[128,2048]{1,0:T(8,128)(2,1)} %get-tuple-element.633), channel_id=1, source_target_pairs={{4,0},{5,1},{8,4},{9,5},{12,8},{13,9},{14,12},{15,13},{10,14},{11,... | collective-permute-start | bytes 1572872 | tf_op jit(solution)/shard_map/ppermute | solution.py:501
  428.3 28.2 %collective-permute-start.97 = (bf16[128,2048]{1,0:T(8,128)(2,1)}, bf16[128,2048]{1,0:T(8,128)(2,1)}, u32[]{:S(2)}, u32[]{:S(2)}) collective-permute-start(bf16[128,2048]{1,0:T(8,128)(2,1)} %get-tuple-element.632), channel_id=1, source_target_pairs={{0,4},{1,5},{4,8},{5,9},{8,12},{9,13},{12,14},{13,15},{14,10},{15,... | collective-permute-start | bytes 1572872 | tf_op jit(solution)/shard_map/ppermute | solution.py:498
  429.3 30.8 %collective-permute-start.95 = (bf16[256,2048]{1,0:T(8,128)(2,1)}, bf16[256,2048]{1,0:T(8,128)(2,1)}, u32[]{:S(2)}, u32[]{:S(2)}) collective-permute-start(bf16[256,2048]{1,0:T(8,128)(2,1)} %convolution_convert_fusion.3), channel_id=1, source_target_pairs={{0,1},{1,0},{2,3},{3,2},{4,5},{5,4},{6,7},{7,6},{8,9},{9,8},{10,11... | collective-permute-start | bytes 3145736 | tf_op jit(solution)/shard_map/ppermute | solution.py:504
  455.1 23.3 %collective-permute-start.118 = (bf16[128,2048]{1,0:T(8,128)(2,1)}, bf16[128,2048]{1,0:T(8,128)(2,1)}, u32[]{:S(2)}, u32[]{:S(2)}) collective-permute-start(bf16[128,2048]{1,0:T(8,128)(2,1)} %get-tuple-element.581.refs_2_), channel_id=1, source_target_pairs={{0,16},{16,0},{1,17},{17,1},{2,18},{18,2},{3,19},{19,3},{4,20},{20... | collective-permute-start | bytes 1572872 | tf_op jit(solution)/shard_map/ppermute | solution.py:619
  468.7 21.7 %collective-permute-start.120 = (bf16[256,2048]{1,0:T(8,128)(2,1)S(1)}, bf16[256,2048]{1,0:T(8,128)(2,1)}, u32[]{:S(2)}, u32[]{:S(2)}) collective-permute-start(bf16[256,2048]{1,0:T(8,128)(2,1)S(1)} %convolution_convert_fusion.2), channel_id=1, source_target_pairs={{0,1},{1,0},{2,3},{3,2},{4,5},{5,4},{6,7},{7,6},{8,9},{9,8},{10,11... | collective-permute-start | bytes 3145736 | tf_op jit(solution)/shard_map/ppermute | solution.py:504
  481.6 20.0 %collective-permute-start.125 = (bf16[16,64,384]{2,1,0:T(8,128)(2,1)}, bf16[16,64,384]{2,1,0:T(8,128)(2,1)}, u32[]{:S(2)}, u32[]{:S(2)}) collective-permute-start(bf16[16,64,384]{2,1,0:T(8,128)(2,1)} %get-tuple-element.531), channel_id=1, source_target_pairs={{0,16},{16,0},{1,17},{17,1},{2,18},{18,2},{3,19},{19,3},{4,20},{20... | collective-permute-start | bytes 2359304 | tf_op jit(solution)/shard_map/ppermute | solution.py:619
  505.2 16.3 %collective-permute-start.126 = (bf16[256,2048]{1,0:T(8,128)(2,1)S(1)}, bf16[256,2048]{1,0:T(8,128)(2,1)}, u32[]{:S(2)}, u32[]{:S(2)}) collective-permute-start(bf16[256,2048]{1,0:T(8,128)(2,1)S(1)} %convolution_convert_fusion.1), channel_id=1, source_target_pairs={{0,1},{1,0},{2,3},{3,2},{4,5},{5,4},{6,7},{7,6},{8,9},{9,8},{10,11... | collective-permute-start | bytes 3145736 | tf_op jit(solution)/shard_map/ppermute | solution.py:504
  527.6 39.4 %collective-permute-start.131 = (bf16[256,2048]{1,0:T(8,128)(2,1)}, bf16[256,2048]{1,0:T(8,128)(2,1)}, u32[]{:S(2)}, u32[]{:S(2)}) collective-permute-start(bf16[256,2048]{1,0:T(8,128)(2,1)} %convolution_convert_fusion), channel_id=1, source_target_pairs={{0,1},{1,0},{2,3},{3,2},{4,5},{5,4},{6,7},{7,6},{8,9},{9,8},{10,11... | collective-permute-start | bytes 3145736 | tf_op jit(solution)/shard_map/ppermute | solution.py:504
  529.8 40.4 %all-to-all-start.1 = ((bf16[16,64,384]{2,1,0:T(8,128)(2,1)}), bf16[16,64,384]{2,1,0:T(8,128)(2,1)}, u32[]{:S(2)}, u32[]{:S(2)}) async-start(bf16[16,64,384]{2,1,0:T(8,128)(2,1)} %add_convert_fusion), calls=%async_computation.1 | async-start | bytes 1572864 | tf_op jit(solution)/shard_map/all_to_all | solution.py:827
  536.0 30.9 %collective-permute-start.132 = (bf16[128,2048]{1,0:T(8,128)(2,1)}, bf16[128,2048]{1,0:T(8,128)(2,1)S(1)}, u32[]{:S(2)}, u32[]{:S(2)}) collective-permute-start(bf16[128,2048]{1,0:T(8,128)(2,1)} %get-tuple-element.575), channel_id=1, source_target_pairs={{4,0},{5,1},{8,4},{9,5},{12,8},{13,9},{14,12},{15,13},{10,14},{11,... | collective-permute-start | bytes 1572872 | tf_op jit(solution)/shard_map/ppermute | solution.py:501
  537.8 29.1 %collective-permute-start.133 = (bf16[128,2048]{1,0:T(8,128)(2,1)}, bf16[128,2048]{1,0:T(8,128)(2,1)S(1)}, u32[]{:S(2)}, u32[]{:S(2)}) collective-permute-start(bf16[128,2048]{1,0:T(8,128)(2,1)} %get-tuple-element.576), channel_id=1, source_target_pairs={{0,4},{1,5},{4,8},{5,9},{8,12},{9,13},{12,14},{13,15},{14,10},{15,... | collective-permute-start | bytes 1572872 | tf_op jit(solution)/shard_map/ppermute | solution.py:498
  540.3 26.5 %collective-permute-start.134 = (f32[2,2048]{1,0:T(2,128)S(1)}, f32[2,2048]{1,0:T(2,128)S(1)}, u32[]{:S(2)}, u32[]{:S(2)}) collective-permute-start(f32[2,2048]{1,0:T(2,128)S(1)} %add.338), channel_id=1, source_target_pairs={{0,8},{1,9},{2,10},{3,11},{4,12},{5,13},{6,14},{7,15},{8,0},{9,1},... | collective-permute-start | bytes 49160 | tf_op jit(solution)/shard_map/ppermute | solution.py:555
  549.4 26.9 %collective-permute-start.115 = (bf16[128,2048]{1,0:T(8,128)(2,1)}, bf16[128,2048]{1,0:T(8,128)(2,1)}, u32[]{:S(2)}, u32[]{:S(2)}) collective-permute-start(bf16[128,2048]{1,0:T(8,128)(2,1)} %convolution_convert_fusion.14), channel_id=1, source_target_pairs={{0,1},{1,0},{2,3},{3,2},{4,5},{5,4},{6,7},{7,6},{8,9},{9,8},{10,11... | collective-permute-start | bytes 1572872 | tf_op jit(solution)/shard_map/ppermute | solution.py:504
  570.2 19.4 %collective-permute-start.140 = (bf16[16,64,384]{2,1,0:T(8,128)(2,1)}, bf16[16,64,384]{2,1,0:T(8,128)(2,1)S(1)}, u32[]{:S(2)}, u32[]{:S(2)}) collective-permute-start(bf16[16,64,384]{2,1,0:T(8,128)(2,1)} %all-to-all-done.1.near_ref), channel_id=1, source_target_pairs={{0,16},{16,0},{1,17},{17,1},{2,18},{18,2},{3,19},{19,3},{4,20},{20... | collective-permute-start | bytes 2359304 | tf_op jit(solution)/shard_map/ppermute | solution.py:619
  571.3 18.3 %collective-permute-start.137 = (bf16[128,2048]{1,0:T(8,128)(2,1)}, bf16[128,2048]{1,0:T(8,128)(2,1)S(1)}, u32[]{:S(2)}, u32[]{:S(2)}) collective-permute-start(bf16[128,2048]{1,0:T(8,128)(2,1)} %get-tuple-element.594), channel_id=1, source_target_pairs={{4,0},{5,1},{8,4},{9,5},{12,8},{13,9},{14,12},{15,13},{10,14},{11,... | collective-permute-start | bytes 1572872 | tf_op jit(solution)/shard_map/ppermute | solution.py:501
  572.8 16.8 %collective-permute-start.138 = (bf16[128,2048]{1,0:T(8,128)(2,1)}, bf16[128,2048]{1,0:T(8,128)(2,1)S(1)}, u32[]{:S(2)}, u32[]{:S(2)}) collective-permute-start(bf16[128,2048]{1,0:T(8,128)(2,1)} %get-tuple-element.595), channel_id=1, source_target_pairs={{0,4},{1,5},{4,8},{5,9},{8,12},{9,13},{12,14},{13,15},{14,10},{15,... | collective-permute-start | bytes 1572872 | tf_op jit(solution)/shard_map/ppermute | solution.py:498
  573.3 16.3 %collective-permute-start.139 = (f32[2,2048]{1,0:T(2,128)S(1)}, f32[2,2048]{1,0:T(2,128)S(1)}, u32[]{:S(2)}, u32[]{:S(2)}) collective-permute-start(f32[2,2048]{1,0:T(2,128)S(1)} %add.342), channel_id=1, source_target_pairs={{0,16},{16,0},{1,17},{17,1},{2,18},{18,2},{3,19},{19,3},{4,20},{20... | collective-permute-start | bytes 49160 | tf_op jit(solution)/shard_map/ppermute | solution.py:619
  (201 other events, 2560.1 us)

commit v3 on v2

--- a/solution.py
+++ b/solution.py
@@ -50,7 +50,7 @@
     length = length_ref[0]
     scale = HEAD_DIM ** (-0.5)
 
-    @pl.loop(0, slots)
+    @pl.loop(0, slots, unroll=4)
     def _(place):
         source = pl.ds(pl.multiple_of(slot_ref[place] * shard, shard), shard)
         target = pl.ds(pl.multiple_of(place * shard, shard), shard)
@@ -65,7 +65,7 @@
         value_ref[target, :] = value_lin.astype(jnp.bfloat16)
         turned[:, target] = value_lin.T.astype(jnp.bfloat16)
 
-    block_q = min(512, rows)
+    block_q = min(1024, rows)
     block_k = min(512, rows)
 
     @pl.loop(0, rows // block_q)
@@ -114,7 +114,7 @@
         joined = jnp.concatenate([state[3 * h + 2] / state[3 * h + 1] for h in range(heads)], axis=0)
         attn_nat[pl.ds(q_first, block_q), :] = joined.T.astype(jnp.bfloat16)
 
-    @pl.loop(0, slots)
+    @pl.loop(0, slots, unroll=4)
     def _(place):
         source = pl.ds(pl.multiple_of(slot_ref[place] * shard, shard), shard)
         target = pl.ds(pl.multiple_of(place * shard, shard), shard)
@@ -158,7 +158,7 @@
     key_acc[...] = jnp.zeros_like(key_acc)
     value_acc[...] = jnp.zeros_like(value_acc)
 
-    @pl.loop(0, slots)
+    @pl.loop(0, slots, unroll=4)
     def _(place):
         source = pl.ds(pl.multiple_of(slot_ref[place] * shard, shard), shard)
         target = pl.ds(pl.multiple_of(place * shard, shard), shard)
@@ -221,7 +221,7 @@
         state = lax.fori_loop(full, stop, functools.partial(step, masked=True), state)
         query_acc[here, :] = (jnp.concatenate(state, axis=0) * scale).T
 
-    @pl.loop(0, slots)
+    @pl.loop(0, slots, unroll=4)
     def _(place):
         source = pl.ds(pl.multiple_of(slot_ref[place] * shard, shard), shard)
         target = pl.ds(pl.multiple_of(place * shard, shard), shard)
@@ -241,9 +241,9 @@
     smem = pl.BlockSpec(memory_space=pltpu.SMEM)
     return pl.pallas_call(
         backward_kernel,
-        out_shape=jax.ShapeDtypeStruct((rows, 3 * width), jnp.bfloat16),
+        out_shape=[jax.ShapeDtypeStruct((rows, 3 * width), jnp.bfloat16)],
         in_specs=[smem, smem] + [vmem] * 8,
-        out_specs=vmem,
+        out_specs=[vmem],
         scratch_shapes=[
             pltpu.VMEM((width, rows), jnp.bfloat16),
             pltpu.VMEM((rows, width), jnp.bfloat16),
@@ -305,19 +305,6 @@
     return math.gcd(tile, extent)
 
 
-def call_kernel(body, name, grid, ins, outs, args):
-    return pl.pallas_call(
-        body,
-        grid=grid,
-        in_specs=[pl.BlockSpec(*spec) for spec in ins],
-        out_specs=[pl.BlockSpec(block, index) for block, index, _, _ in outs],
-        out_shape=[jax.ShapeDtypeStruct(shape, dtype) for _, _, shape, dtype in outs],
-        compiler_params=pltpu.CompilerParams(vmem_limit_bytes=VMEM_LIMIT),
-        cost_estimate=SMALL,
-        name=name,
-    )(*args)
-
-
 def first(i):
     return (0, 0)
 
@@ -346,24 +333,26 @@
         fill(left_ref, refs[:lefts])
 
     fill(right_ref, refs[lefts : lefts + rights])
-    total = dot_tn(left_ref[...], right_ref[...]).astype(jnp.bfloat16)
-    rows = out_refs[0].shape[0]
-    for piece, out_ref in enumerate(out_refs):
-        out_ref[...] = total[piece * rows : (piece + 1) * rows]
-
-
-def weight_grads(lefts, rights, rows):
+    total = dot_tn(left_ref[...], right_ref[...])
+    start = 0
+    for out_ref in out_refs:
+        rows = out_ref.shape[0]
+        out_ref[...] = total[start : start + rows].astype(jnp.bfloat16)
+        start += rows
+
+
+def weight_grads(lefts, rights, cuts, place=0):
     count = sum(piece.shape[0] for piece in lefts)
-    wide = lefts[0].shape[1]
+    wide = sum(cuts)
     width = rights[0].shape[1]
     tile = fitting(512, width)
     return pl.pallas_call(
         functools.partial(grads_kernel, len(lefts), len(rights)),
         grid=(width // tile,),
-        in_specs=[pl.BlockSpec(piece.shape, first) for piece in lefts]
+        in_specs=[pl.BlockSpec((piece.shape[0], wide), lambda i: (0, place)) for piece in lefts]
         + [pl.BlockSpec((piece.shape[0], tile), along) for piece in rights],
-        out_specs=[pl.BlockSpec((rows, tile), along)] * (wide // rows),
-        out_shape=[jax.ShapeDtypeStruct((rows, width), jnp.bfloat16)] * (wide // rows),
+        out_specs=[pl.BlockSpec((rows, tile), along) for rows in cuts],
+        out_shape=[jax.ShapeDtypeStruct((rows, width), jnp.bfloat16) for rows in cuts],
         scratch_shapes=[
             pltpu.VMEM((count, wide), jnp.bfloat16),
             pltpu.VMEM((count, tile), jnp.bfloat16),
@@ -374,7 +363,9 @@
     )(*lefts, *rights)
 
 
-def heads_kernel(upper_ref, left_ref, right_ref, weight_ref, keep_ref, give_ref, gain_ref):
+def heads_kernel(upper_ref, right_ref, weight_ref, *refs):
+    *piece_refs, keep_ref, give_ref, gain_ref, left_ref = refs
+    fill(left_ref, piece_refs)
     total = dot_tn(left_ref[...], right_ref[...])
     count, half, width = keep_ref.shape
     sums = jnp.sum(total * weight_ref[...].astype(jnp.float32), axis=1, keepdims=True)
@@ -385,9 +376,9 @@
     give_ref[...] = jnp.where(upper, blocks[:, 0], blocks[:, 1])
 
 
-def heads_grads(left, right, weight, upper, rows):
-    count, wide = left.shape
-    width = right.shape[1]
+def heads_grads(lefts, right, weight, upper, rows):
+    count, width = right.shape
+    wide = weight.shape[0]
     tile = fitting(512, wide)
     half = ((tile // rows, rows // 2, width), lambda i: (i, 0, 0))
     whole = ((wide // rows, rows // 2, width), jnp.bfloat16)
@@ -396,73 +387,81 @@
         grid=(wide // tile,),
         in_specs=[
             pl.BlockSpec(memory_space=pltpu.SMEM),
-            pl.BlockSpec((count, tile), along),
             pl.BlockSpec((count, width), first),
             pl.BlockSpec((tile, width), down_rows),
-        ],
+        ]
+        + [pl.BlockSpec((piece.shape[0], tile), along) for piece in lefts],
         out_specs=[pl.BlockSpec(*half), pl.BlockSpec(*half), pl.BlockSpec((1, tile), along)],
         out_shape=[
             jax.ShapeDtypeStruct(*whole),
             jax.ShapeDtypeStruct(*whole),
             jax.ShapeDtypeStruct((1, wide), jnp.float32),
         ],
+        scratch_shapes=[pltpu.VMEM((count, tile), jnp.bfloat16)],
         compiler_params=pltpu.CompilerParams(vmem_limit_bytes=VMEM_LIMIT),
         cost_estimate=SMALL,
         name="heads_grads",
-    )(upper, left, right, weight)
-
-
-def assemble_kernel(side_ref, near_ref, far_ref, *out_refs):
-    half, width = near_ref.shape[1:]
-    columns = width // len(out_refs)
+    )(upper, right, weight, *lefts)
+
+
+def assemble_kernel(side_ref, *refs):
+    out_refs = refs[-3:]
+    given = (len(refs) - 3) // 2
+    size, part, width = refs[0].shape
+    columns = width // 3
     upper = side_ref[0] == 1
-    low = jnp.where(upper, far_ref[...], near_ref[...]).astype(jnp.float32)
-    high = jnp.where(upper, near_ref[...], far_ref[...]).astype(jnp.float32)
-    for piece, out_ref in enumerate(out_refs):
-        for source in range(near_ref.shape[0]):
-            place = slice(source * columns, (source + 1) * columns)
-            taken = slice(piece * columns, (piece + 1) * columns)
-            out_ref[:half, place] = low[source, :, taken]
-            out_ref[half:, place] = high[source, :, taken]
-
-
-def assemble(near, far, side, count):
-    size, half, width = near.shape
-    shape = (2 * half, size * width // count)
+    for index, (near_ref, far_ref) in enumerate(zip(refs[:given], refs[given:-3])):
+        low = jnp.where(upper, far_ref[...], near_ref[...]).astype(jnp.float32)
+        high = jnp.where(upper, near_ref[...], far_ref[...]).astype(jnp.float32)
+        for piece, out_ref in enumerate(out_refs):
+            for source in range(size):
+                place = slice(source * columns, (source + 1) * columns)
+                taken = slice(piece * columns, (piece + 1) * columns)
+                for start, block in ((index, low), (given + index, high)):
+                    out_ref[start * part : (start + 1) * part, place] = block[source, :, taken]
+
+
+def assemble(near, far, side):
+    size, part, width = near[0].shape
+    shape = (2 * len(near) * part, size * width // 3)
     vmem = pl.BlockSpec(memory_space=pltpu.VMEM)
     return pl.pallas_call(
         assemble_kernel,
-        in_specs=[pl.BlockSpec(memory_space=pltpu.SMEM), vmem, vmem],
-        out_specs=[vmem] * count,
-        out_shape=[jax.ShapeDtypeStruct(shape, jnp.float32)] * count,
+        in_specs=[pl.BlockSpec(memory_space=pltpu.SMEM)] + [vmem] * (2 * len(near)),
+        out_specs=[vmem] * 3,
+        out_shape=[jax.ShapeDtypeStruct(shape, jnp.float32)] * 3,
         compiler_params=pltpu.CompilerParams(vmem_limit_bytes=VMEM_LIMIT),
         cost_estimate=SMALL,
         name="assemble",
-    )(side, near, far)
+    )(side, *near, *far)
 
 
 def sums_kernel(*refs):
     out_ref = refs[-1]
     count = (len(refs) - 1) // 2
-    rows = refs[0].shape[0]
-    for piece in range(count):
-        out_ref[piece * rows : (piece + 1) * rows, :] = refs[piece][...].astype(
-            jnp.float32
-        ) + refs[count + piece][...].astype(jnp.float32)
+    start = 0
+    for part_ref, other_ref in zip(refs[:count], refs[count:-1]):
+        rows = part_ref.shape[0]
+        out_ref[start : start + rows, :] = part_ref[...].astype(jnp.float32) + other_ref[
+            ...
+        ].astype(jnp.float32)
+        start += rows
 
 
 def sum_pieces(parts, others):
-    rows, width = parts[0].shape
+    width = parts[0].shape[1]
     tile = fitting(512, width)
-    total = rows * len(parts)
-    return call_kernel(
+    total = sum(piece.shape[0] for piece in parts)
+    return pl.pallas_call(
         sums_kernel,
-        "sum_pieces",
-        (width // tile,),
-        [((rows, tile), along)] * (2 * len(parts)),
-        [((total, tile), along, (total, width), jnp.float32)],
-        (*parts, *others),
-    )
+        grid=(width // tile,),
+        in_specs=[pl.BlockSpec((piece.shape[0], tile), along) for piece in (*parts, *others)],
+        out_specs=[pl.BlockSpec((total, tile), along)],
+        out_shape=[jax.ShapeDtypeStruct((total, width), jnp.float32)],
+        compiler_params=pltpu.CompilerParams(vmem_limit_bytes=VMEM_LIMIT),
+        cost_estimate=SMALL,
+        name="sum_pieces",
+    )(*parts, *others)
 
 
 class Ring:
@@ -514,35 +513,48 @@
             groups.append([ahead, behind, self.twin(ahead), self.twin(behind)])
 
     def scatter(self, make):
-        down = up = None
-        held = ()
-        for step in range(self.reach, -1, -1):
+        def pair_sum(step, *held):
             mine, other = make(step, *held)
-            total = mine + self.twin(other.astype(jnp.bfloat16)).astype(jnp.float32)
+            return mine + self.twin(other.astype(jnp.bfloat16)).astype(jnp.float32)
+
+        total = pair_sum(self.reach)
+        middle = total.shape[0] // 2
+        low, high = total[:middle], total[middle:]
+        for step in range(self.reach - 1, -1, -1):
+            held = (low.astype(jnp.bfloat16), high.astype(jnp.bfloat16))
+            (down, up), (total,) = (
+                yield (
+                    ((self.backward, held[0]), (self.forward, held[1])),
+                    (pair_sum(step, *held),),
+                )
+            )
+            down, up = down.astype(jnp.float32), up.astype(jnp.float32)
+            if step == 0:
+                return total + down + up
             count = total.shape[0] // 2
-            if step == 0:
-                return total + down.astype(jnp.float32) + up.astype(jnp.float32)
             low, high = total[:count], total[count:]
             if step == self.reach - 1:
-                middle = count // 2
-                low = jnp.concatenate([low[:middle] + down.astype(jnp.float32), low[middle:]], axis=0)
-                high = jnp.concatenate([high[:middle], high[middle:] + up.astype(jnp.float32)], axis=0)
-            elif step < self.reach - 1:
-                low = low + down.astype(jnp.float32)
-                high = high + up.astype(jnp.float32)
-            held = (low.astype(jnp.bfloat16), high.astype(jnp.bfloat16))
-            (down, up), _ = yield ((self.backward, held[0]), (self.forward, held[1])), ()
+                low = jnp.concatenate([low[:middle] + down, low[middle:]], axis=0)
+                high = jnp.concatenate([high[:middle], high[middle:] + up], axis=0)
+            else:
+                low, high = low + down, high + up
 
     def total(self, array):
-        bit = 1
+        def flip(bit):
+            pairs = [(i, i ^ bit) for i in range(self.size)]
+            return functools.partial(lax.ppermute, axis_name="wide", perm=pairs)
+
+        ways = [swapped]
+        bit = 4
         while bit < self.size:
-            pairs = [(i, i ^ bit) for i in range(self.size)]
-            send = functools.partial(lax.ppermute, axis_name="wide", perm=pairs)
-            ((other,), _) = yield ((send, array),), ()
+            ways.insert(0 if bit > 4 else 1, flip(bit))
+            bit *= 2
+        for way in ways:
+            ((other,), _) = yield ((way, array),), ()
             array = array + other
-            bit *= 2
-        ((other,), _) = yield ((swapped, array),), ()
-        return array + other
+        for bit in (2, 1):
+            array = array + flip(bit)(array)
+        return array
 
 
 class Stream:
@@ -591,15 +603,14 @@
     ready = []
     if swaps is not None:
         ready, swaps.waiting = swaps.waiting[:count], swaps.waiting[count:]
+    asked = [array for stream in streams for _, array in stream.asked]
     if work is not None:
         flat, tree = jax.tree.flatten(given)
-        *sent, flat = joined(*[[array for _, array in s.asked] for s in streams], flat)
-        for stream, arrays in zip(streams, sent):
-            stream.asked = [(send, array) for (send, _), array in zip(stream.asked, arrays)]
-        beside = work(*jax.tree.unflatten(tree, flat))
+        beside = work(*jax.tree.unflatten(tree, joined(asked, flat)[1]))
+    pieces = joined(asked, [swaps.parts[name][index] for name, index in ready])[1]
     lists = [stream.post() for stream in streams]
     lists += [stream.beside for stream in streams]
-    lists.append([swapped(swaps.parts[name][index]) for name, index in ready])
+    lists.append([swapped(piece) for piece in pieces])
     lists.append(beside)
     *lists, moved, beside = joined(*lists)
     for (name, _), piece in zip(ready, moved):
@@ -692,13 +703,14 @@
     one = Stream(ring.gather(norm_one, group_one))
     hop([one])
     cosine, sine = hop([one], beside=(cosine, sine))
-    travel(one)
+    while one.asked is not None:
+        hop([one])
     far_half = swapped(near_half)
     w_heads = jnp.stack(
         [jnp.where(upper, far_half, near_half), jnp.where(upper, near_half, far_half)], axis=1
     ).reshape(model_width, 3 * width)
-    all_one = jnp.concatenate(sum(group_one, []), axis=0)
-    lin = dot_nn(all_one, w_heads)
+    pieces_one = sum(group_one, [])
+    lin = dot_nn(jnp.concatenate(pieces_one, axis=0), w_heads)
     starts = [0]
     for rows in group_one:
         starts.append(starts[-1] + sum(piece.shape[0] for piece in rows))
@@ -738,30 +750,34 @@
             jnp.concatenate(swiglu_back(hidden_back, gate_proj, up_proj), axis=1),
         )
 
-    hop([two])
-    for step in range(1, ring.reach):
-        fed = hop([two], beside=feed(step - 1))
+    for step in range(ring.reach):
+        fed = hop([two], beside=feed(step))
         hidden.append(fed[0])
         both_back.append(fed[1])
-    for step in (ring.reach - 1, ring.reach):
-        fed = feed(step)
-        hidden.append(fed[0])
-        both_back.append(fed[1])
+    fed = feed(ring.reach)
+    hidden.append(fed[0])
+    both_back.append(fed[1])
 
     def pull_part(step, *held):
         mine, other = halves(after(both_back[step], *held))
         return dot_nn(mine, w_both), dot_nn(other, w_both)
 
     def mlp_part(step, *held):
-        mine, other = halves(after(hidden[step], *held))
+        mine, other = halves(after(hidden[step], *(held or (branch_back,))))
         return dot_nn(mine, w_down), dot_nn(other, w_down)
 
     swaps = Swaps()
-    grads = functools.partial(weight_grads, rows=local_rows)
+    cuts = [[units // 16 * count for count in row] for row in ((4, 4, 8), (8, 8), (2, 8, 6))]
     pull = Stream(ring.scatter(pull_part))
     hop([pull])
-    down_parts = hop([pull], work=grads, given=(hidden, sum(group_back, [])))
-    swaps.add("down", down_parts)
+    swaps.add(
+        "down",
+        hop(
+            [pull],
+            work=functools.partial(weight_grads, cuts=cuts[0]),
+            given=(hidden, sum(group_back, [])),
+        ),
+    )
     norm_two_back = travel(pull, swaps)
     residual_back = y_back + norm_back(norm_two_back, normed_two, gain_two, factor_two)
     gain_two_term = jnp.sum(norm_two_back * normed_two, axis=0)
@@ -770,16 +786,17 @@
     group_branch = []
     branch = Stream(ring.gather(branch_back, group_branch))
     pieces_two = sum(group_two, [])
-    for name, place in (("gate", slice(None, units)), ("up", slice(units, None))):
+    for place, name in enumerate(("gate", "up")):
         parts = hop(
             [branch, mlp],
             swaps,
-            2,
-            work=grads,
-            given=([both[:, place] for both in both_back], pieces_two),
+            work=functools.partial(
+                weight_grads, cuts=cuts[1 + place], place=place
+            ),
+            given=(both_back, pieces_two),
         )
         swaps.add(name, parts)
-    (down_sum,) = hop([branch], swaps, work=sum_pieces, given=swaps.sums("down"))
+    (down_sum,) = hop([branch, mlp], swaps, work=sum_pieces, given=swaps.sums("down"))
     while branch.asked is not None:
         hop([branch], swaps)
     upstream = jnp.concatenate(
@@ -792,11 +809,8 @@
     (lin_back,) = hop(
         [mlp],
         swaps,
-        2,
-        beside=(
-            attention_backward(
-                slot_of, lengths, query, key, value, heads_attention, upstream, logs, cosine, sine
-            ),
+        beside=attention_backward(
+            slot_of, lengths, query, key, value, heads_attention, upstream, logs, cosine, sine
         ),
     )
     lin_back = own_columns(lin_back)
@@ -809,21 +823,27 @@
     pulled = Stream(ring.scatter(input_part))
     side = lax.axis_index("narrow").reshape(1)
     keep, give, gain_one_sum = hop(
-        [mlp],
+        [pulled],
         swaps,
         work=functools.partial(heads_grads, rows=own_width),
-        given=(all_one, lin_back, w_own, side),
+        given=(pieces_one, lin_back, w_own, side),
     )
     while mlp.asked is not None:
-        hop([mlp], swaps)
-    block_output = (residual + mlp.result).astype(jnp.bfloat16)
+        hop([mlp])
     totals = Stream(ring.total(jnp.stack([gain_one_sum[0] / gain_one, gain_two_term])))
-    hop([totals])
-
-    def before(piece, parts, others):
-        return (swapped(piece), *sum_pieces(parts, others))
-
-    given, gate_sum = hop([pulled, totals], work=before, given=(give, *swaps.sums("gate")))
+
+    def before(piece, left, rights, parts, others):
+        return (
+            swapped(piece),
+            *weight_grads([left], rights, (own_width,)),
+            *sum_pieces(parts, others),
+        )
+
+    given, out_part, gate_sum = hop(
+        [pulled, totals],
+        work=before,
+        given=(give, attention, sum(group_branch, []), *swaps.sums("gate")),
+    )
     heads_sum = lax.all_to_all(
         (keep.astype(jnp.float32) + given.astype(jnp.float32)).astype(jnp.bfloat16),
         "wide",
@@ -831,22 +851,17 @@
         0,
         tiled=True,
     )
-    out_parts = hop(
-        [pulled, totals],
-        swaps,
-        work=functools.partial(weight_grads, rows=own_width),
-        given=([attention], sum(group_branch, [])),
-    )
-    while swaps.waiting:
-        hop([], swaps)
-    swaps.add("out", out_parts)
-    (up_sum,) = hop([pulled, totals], swaps, work=sum_pieces, given=swaps.sums("up"))
-    far, out_sum = hop([pulled, totals], work=before, given=(heads_sum, *swaps.sums("out")))
+    swaps.add("out", [out_part])
+    hop([pulled, totals], swaps)
+    (up_sum,) = hop([pulled, totals], work=sum_pieces, given=swaps.sums("up"))
     while pulled.asked is not None or totals.asked is not None:
         hop([pulled, totals])
     norm_one_back = pulled.result
+    block_output = (residual + after(mlp.result, norm_one_back)).astype(jnp.bfloat16)
     gain_totals = totals.result
-    attention_sums = assemble(heads_sum, far, side, 3)
+    far = swapped(heads_sum)
+    (out_sum,) = sum_pieces(*swaps.sums("out"))
+    attention_sums = assemble([heads_sum], [far], side)
     input_back = residual_back + norm_back(norm_one_back, normed_one, gain_one, factor_one)
     return (
         block_output[None],

time: 610 us -> 593 us (0.972)
  other arithmetic: 40.5 us -> 47.9 us
  matrix products: 88.9 us -> 82.1 us
    ppermute x4 -> x2, waiting for transfers between devices: 19.6 us -> 2.02 us  [post(): return [send(array) for send, array in self.asked]]
    ppermute x17 -> x13, waiting for transfers between devices: 36.8 us -> 48.7 us  [swapped(): return lax.ppermute(part, 'narrow', [(0, 1), (1, 0)])]
    ppermute x56, waiting for transfers between devices: 1.52 us -> 8.08 us  [twin(): return lax.ppermute(array, 'wide', self.across)]
    dot_general x31, matrix products: 40.8 us -> 34.5 us  [dot_nn(): lax.dot_general(a, b, (((1,), (0,)), ((), ())), preferred_element_type=jn...]
    ppermute x17 -> x13, starting transfers between devices: 18.4 us -> 13.1 us  [swapped(): return lax.ppermute(part, 'narrow', [(0, 1), (1, 0)])]
    unnamed x261 -> x239, local copies, waits for them, and re-layouts: 26.4 us -> 25.3 us
  transfers between devices with their start and end apart: 143 -> 139, of which waited for: 53 -> 60; matrix products, arithmetic and copies ran while one was open for 21% -> 19% of each run, Pallas kernels for 17% -> 17%
where the time goes in v3:
time: 593 us; the launch traced here: 585 us
  waiting for transfers between devices  202 us (34%)
  starting transfers between devices  112 us (19%)
  Pallas kernels  103 us (17%)
  matrix products  82.1 us (14%)
  other arithmetic  47.9 us (8%)
  local copies, waits for them, and re-layouts  34.7 us (6%)
    ppermute x32, waiting for transfers between devices, forward(): return lax.ppermute(array, 'wide', self.ahead)  93.5 us
    ppermute x13, waiting for transfers between devices, swapped(): return lax.ppermute(part, 'narrow', [(0, 1), (1, 0)])  48.7 us
    ppermute x32, waiting for transfers between devices, backward(): return lax.ppermute(array, 'wide', self.behind)  48.3 us
    dot_general x25, matrix products, dot_nt(): lax.dot_general(a, b, (((1,), (1,)), ((), ())), preferred_element_type=jn...  47.6 us
    ppermute x32, starting transfers between devices, forward(): return lax.ppermute(array, 'wide', self.ahead)  38.7 us
    dot_general x31, matrix products, dot_nn(): lax.dot_general(a, b, (((1,), (0,)), ((), ())), preferred_element_type=jn...  34.5 us
    ppermute x32, starting transfers between devices, backward(): return lax.ppermute(array, 'wide', self.behind)  34.1 us
    pallas_call x4, Pallas kernels, weight_grads(): pl.pallas_call(functools.partial(grads_kernel, len(lefts), len(rights)),...  32.2 us
  transfers between devices with their start and end apart: 139, of which 60 were waited for; matrix products, arithmetic and copies ran while one was open for 19% of the time, Pallas kernels for 17%

profile of v3, /device:TPU:0, one launch (start us, length us, event | category | flops | bytes accessed | tf_op | source)
XLA Modules:
  0.0 585.0 jit_solution(12413903109205087402)
XLA Ops:
  2.7 2.0 constant_dynamic-update-slice_fusion.17
  4.8 2.9 collective-permute-start.2
  12.6 6.5 %all-to-all-start = ((bf16[16,64,384]{2,1,0:T(8,128)(2,1)}), bf16[16,64,384]{2,1,0:T(8,128)(2,1)}, u32[]{:S(2)}, u32[]{:S(2)}) async-start(bf16[16,64,384]{2,1,0:T(8,128)(2,1)} %slice_select_fusion), calls=%async_computation | async-start | bytes 1572864 | tf_op jit(solution)/shard_map/all_to_all | solution.py:701
  19.8 2.0 fusion.138.refs_5_
  21.8 4.7 fusion.142
  33.7 10.7 %collective-permute-done.5.refs_6_ = bf16[128,2048]{1,0:T(8,128)(2,1)} collective-permute-done((bf16[128,2048]{1,0:T(8,128)(2,1)}, bf16[128,2048]{1,0:T(8,128)(2,1)}, u32[]{:S(2)}, u32[]{:S(2)}) %collective-permute-start.5) | collective-permute-done | bytes 524320 | tf_op jit(solution)/shard_map/ppermute | solution.py:497
  46.2 5.8 collective-permute-start.9
  60.5 2.7 collective-permute-done.9.refs_10_
  63.2 3.2 collective-permute-done.10.refs_11_
  84.2 9.1 %fusion.266.lin_ref = f32[2048,384]{1,0:T(8,128)} fusion(bf16[2048,2048]{1,0:T(8,128)(2,1)} %constant_dynamic-update-slice_fusion, bf16[2048,384]{1,0:T(8,128)(2,1)S(1)} %bitcast.109), kind=kOutput, calls=%fused_computation.372 | convolution fusion | flops 3221225472 | bytes 13107200 | tf_op jit(solution)/shard_map/dot_general | solution.py:21
  97.0 18.0 %attention_forward.1 = (bf16[2048,128]{1,0:T(8,128)(2,1)}, bf16[2048,128]{1,0:T(8,128)(2,1)}, bf16[2048,128]{1,0:T(8,128)(2,1)}, bf16[2048,128]{1,0:T(8,128)(2,1)}, f32[8,2048]{1,0:T(8,128)}) custom-call(s32[16]{0:T(128)} %dynamic-slice_bitcast_fusion.slot_ref, s32[1]{0:T(128)} %copy.65.length_ref, f32[2048,384]{1,0:T(8,128)} %fusion.266.lin_ref, ...), custom_call_target="tpu_custom_call" | custom-call | flops 2147483648 | bytes 6291456 | tf_op jit(solution)/shard_map/attention_forward/pallas_call | solution.py:129
  123.6 9.6 %collective-permute-done.23.refs_11_ = bf16[128,2048]{1,0:T(8,128)(2,1)S(1)} collective-permute-done((bf16[128,2048]{1,0:T(8,128)(2,1)}, bf16[128,2048]{1,0:T(8,128)(2,1)S(1)}, u32[]{:S(2)}, u32[]{:S(2)}) %collective-permute-start.23) | collective-permute-done | bytes 524320 | tf_op jit(solution)/shard_map/ppermute | solution.py:497
  134.8 3.2 collective-permute-done.22
  144.7 9.8 %collective-permute-done.26 = bf16[128,2048]{1,0:T(8,128)(2,1)S(1)} collective-permute-done((bf16[128,2048]{1,0:T(8,128)(2,1)S(1)}, bf16[128,2048]{1,0:T(8,128)(2,1)S(1)}, u32[]{:S(2)}, u32[]{:S(2)}) %collective-permute-start.26) | collective-permute-done | bytes 524320 | tf_op jit(solution)/shard_map/ppermute | solution.py:500
  154.8 9.1 %collective-permute-done.28.refs_15_ = bf16[128,2048]{1,0:T(8,128)(2,1)S(1)} collective-permute-done((bf16[128,2048]{1,0:T(8,128)(2,1)S(1)}, bf16[128,2048]{1,0:T(8,128)(2,1)S(1)}, u32[]{:S(2)}, u32[]{:S(2)}) %collective-permute-start.28) | collective-permute-done | bytes 524320 | tf_op jit(solution)/shard_map/ppermute | solution.py:497
  169.3 13.4 %collective-permute-done.34.refs_20_ = bf16[64,2048]{1,0:T(8,128)(2,1)S(1)} collective-permute-done((bf16[64,2048]{1,0:T(8,128)(2,1)S(1)}, bf16[64,2048]{1,0:T(8,128)(2,1)S(1)}, u32[]{:S(2)}, u32[]{:S(2)}) %collective-permute-start.34) | collective-permute-done | bytes 262176 | tf_op jit(solution)/shard_map/ppermute | solution.py:500
  185.4 8.0 %collective-permute-done.37 = bf16[128,2048]{1,0:T(8,128)(2,1)S(1)} collective-permute-done((bf16[128,2048]{1,0:T(8,128)(2,1)S(1)}, bf16[128,2048]{1,0:T(8,128)(2,1)S(1)}, u32[]{:S(2)}, u32[]{:S(2)}) %collective-permute-start.37) | collective-permute-done | bytes 524320 | tf_op jit(solution)/shard_map/ppermute | solution.py:497
  203.1 7.6 %collective-permute-done.42.refs_8_ = bf16[128,2048]{1,0:T(8,128)(2,1)S(1)} collective-permute-done((bf16[128,2048]{1,0:T(8,128)(2,1)S(1)}, bf16[128,2048]{1,0:T(8,128)(2,1)S(1)}, u32[]{:S(2)}, u32[]{:S(2)}) %collective-permute-start.42) | collective-permute-done | bytes 524320 | tf_op jit(solution)/shard_map/ppermute | solution.py:500
  214.8 2.4 fusion.1
  217.2 3.9 multiply_convert_fusion.7
  222.2 4.0 collective-permute-done.45.refs_11_
  230.6 2.4 fusion.17
  233.1 3.9 multiply_convert_fusion.4
  237.1 5.0 collective-permute-done.51.refs_15_
  246.5 2.4 fusion.33
  248.9 3.9 multiply_convert_fusion.1
  267.5 4.8 collective-permute-done.67
  275.1 2.2 convolution_convert_fusion.10
  279.7 8.7 %weight_grads.4 = (bf16[128,2048]{1,0:T(8,128)(2,1)}, bf16[128,2048]{1,0:T(8,128)(2,1)}, bf16[256,2048]{1,0:T(8,128)(2,1)}) custom-call(bf16[256,512]{1,0:T(8,128)(2,1)} %get-tuple-element.488.refs_0_, bf16[512,512]{1,0:T(8,128)(2,1)} %get-tuple-element.473.refs_1_, bf16[512,512]{1,0:T(8,128)(2,1)} %get-tuple-element.439.refs_2_, ...), custom_call_target="tpu_custom_call" | custom-call | flops 1024 | bytes 1024 | tf_op jit(solution)/shard_map/weight_grads/pallas_call | solution.py:349
  288.5 2.6 convert_add_fusion.7
  300.1 10.4 %collective-permute-done.75.refs_3_ = bf16[128,2048]{1,0:T(8,128)(2,1)S(1)} collective-permute-done((bf16[128,2048]{1,0:T(8,128)(2,1)S(1)}, bf16[128,2048]{1,0:T(8,128)(2,1)S(1)}, u32[]{:S(2)}, u32[]{:S(2)}) %collective-permute-start.75) | collective-permute-done | bytes 524320 | tf_op jit(solution)/shard_map/ppermute | solution.py:630
  317.1 9.6 %collective-permute-done.79.refs_4_ = bf16[128,2048]{1,0:T(8,128)(2,1)S(1)} collective-permute-done((bf16[128,2048]{1,0:T(8,128)(2,1)S(1)}, bf16[128,2048]{1,0:T(8,128)(2,1)S(1)}, u32[]{:S(2)}, u32[]{:S(2)}) %collective-permute-start.79) | collective-permute-done | bytes 524320 | tf_op jit(solution)/shard_map/ppermute | solution.py:630
  337.7 8.8 %weight_grads.5 = (bf16[256,2048]{1,0:T(8,128)(2,1)}, bf16[256,2048]{1,0:T(8,128)(2,1)}) custom-call(bf16[256,1024]{1,0:T(8,128)(2,1)} %pad_maximum_fusion.6.refs_0_, bf16[512,1024]{1,0:T(8,128)(2,1)} %pad_maximum_fusion.1.refs_1_, bf16[512,1024]{1,0:T(8,128)(2,1)} %copy-done.9, bf16[512,1024]{1,0:T(8,128)(2,1)} %copy-done.10, bf16[256,1024]{1,0:T(8,128)(2,1)} %copy-done.12, ...), custom_call_target="tpu_custom_call" | custom-call | flops 1024 | bytes 1024 | tf_op jit(solution)/shard_map/weight_grads/pallas_call | solution.py:349
  348.9 2.0 collective-permute-done.80.refs_3_
  350.9 4.3 collective-permute-done.84
  355.3 5.0 collective-permute-done.86.refs_5_
  367.5 8.8 %weight_grads.6 = (bf16[64,2048]{1,0:T(8,128)(2,1)}, bf16[256,2048]{1,0:T(8,128)(2,1)}, bf16[192,2048]{1,0:T(8,128)(2,1)}) custom-call(bf16[256,1024]{1,0:T(8,128)(2,1)} %pad_maximum_fusion.6.refs_0_, bf16[512,1024]{1,0:T(8,128)(2,1)} %pad_maximum_fusion.1.refs_1_, bf16[512,1024]{1,0:T(8,128)(2,1)} %copy-done.9, bf16[512,1024]{1,0:T(8,128)(2,1)} %copy-done.10, ...), custom_call_target="tpu_custom_call" | custom-call | flops 1024 | bytes 1024 | tf_op jit(solution)/shard_map/weight_grads/pallas_call | solution.py:349
  379.8 10.1 %collective-permute-done.87.refs_7_ = bf16[128,2048]{1,0:T(8,128)(2,1)} collective-permute-done((bf16[128,2048]{1,0:T(8,128)(2,1)}, bf16[128,2048]{1,0:T(8,128)(2,1)}, u32[]{:S(2)}, u32[]{:S(2)}) %collective-permute-start.87) | collective-permute-done | bytes 524320 | tf_op jit(solution)/shard_map/ppermute | solution.py:497
  389.9 2.6 add_convert_fusion.9
  402.6 2.6 fusion.85
  405.1 4.8 sum_pieces.4
  410.7 2.9 collective-permute-done.96
  414.5 9.5 %collective-permute-done.93.refs_11_ = bf16[128,2048]{1,0:T(8,128)(2,1)S(1)} collective-permute-done((bf16[128,2048]{1,0:T(8,128)(2,1)}, bf16[128,2048]{1,0:T(8,128)(2,1)S(1)}, u32[]{:S(2)}, u32[]{:S(2)}) %collective-permute-start.93) | collective-permute-done | bytes 524320 | tf_op jit(solution)/shard_map/ppermute | solution.py:497
  425.2 2.5 add_convert_fusion.7
  432.0 4.1 collective-permute-done.112.refs_3_
  436.1 2.6 fusion.88
  448.6 22.7 %attention_backward.1.right_ref = bf16[2048,384]{1,0:T(8,128)(2,1)} custom-call(s32[16]{0:T(128)} %dynamic-slice_bitcast_fusion.slot_ref, s32[1]{0:T(128)} %copy.65.length_ref, bf16[2048,128]{1,0:T(8,128)(2,1)} %get-tuple-element.491.query_ref, bf16[2048,128]{1,0:T(8,128)(2,1)} %get-tuple-element.492.key_ref, ...), custom_call_target="tpu_custom_call" | custom-call | flops 5368709120 | bytes 9437184 | tf_op jit(solution)/shard_map/attention_backward/pallas_call | solution.py:242
  479.5 9.1 %heads_grads.1 = (bf16[16,64,384]{2,1,0:T(8,128)(2,1)}, bf16[16,64,384]{2,1,0:T(8,128)(2,1)}, f32[1,2048]{1,0:T(1,128)}) custom-call(s32[1]{0:T(128)} %bitcast.10.upper_ref.side_ref, bf16[2048,384]{1,0:T(8,128)(2,1)} %attention_backward.1.right_ref, bf16[2048,384]{1,0:T(8,128)(2,1)} %bitcast.110, bf16[128,2048]{1,0:T(8,128)(2,1)} %copy-done.35, ...), custom_call_target="tpu_custom_call" | custom-call | flops 1024 | bytes 1024 | tf_op jit(solution)/shard_map/heads_grads/pallas_call | solution.py:385
  490.6 6.9 %collective-permute-done.119.refs_5_ = bf16[192,2048]{1,0:T(8,128)(2,1)} collective-permute-done((bf16[192,2048]{1,0:T(8,128)(2,1)}, bf16[192,2048]{1,0:T(8,128)(2,1)}, u32[]{:S(2)}, u32[]{:S(2)}) %collective-permute-start.119) | collective-permute-done | bytes 786464 | tf_op jit(solution)/shard_map/ppermute | solution.py:630
  505.9 4.7 sum_pieces.5
  510.7 5.9 %weight_grads.7.refs_0_ = bf16[128,2048]{1,0:T(8,128)(2,1)} custom-call(bf16[2048,128]{1,0:T(8,128)(2,1)} %get-tuple-element.541.att_ref.refs_0_, bf16[128,2048]{1,0:T(8,128)(2,1)} %copy-done.28, bf16[128,2048]{1,0:T(8,128)(2,1)} %copy-done.77, bf16[128,2048]{1,0:T(8,128)(2,1)} %collective-permute-done.80.refs_3_, ...), custom_call_target="tpu_custom_call" | custom-call | flops 1024 | bytes 1024 | tf_op jit(solution)/shard_map/weight_grads/pallas_call | solution.py:349
  518.5 3.3 collective-permute-done.124
  521.9 2.3 add_convert_fusion.4
  530.6 2.2 add_convert_fusion
  532.8 4.7 all-to-all-start.1
  537.5 2.4 convert_add_fusion
  539.9 3.0 collective-permute-done.129.refs_1_
  543.0 2.5 add_convert_fusion.2
  546.9 2.4 convert_add_fusion.12
  553.0 3.4 sum_pieces.7
  556.4 4.8 sum_pieces.6
  562.7 2.1 convert_add_fusion.11
  574.3 6.4 %collective-permute-done.136.refs_1_ = bf16[16,64,384]{2,1,0:T(8,128)(2,1)S(1)} collective-permute-done((bf16[16,64,384]{2,1,0:T(8,128)(2,1)}, bf16[16,64,384]{2,1,0:T(8,128)(2,1)S(1)}, u32[]{:S(2)}, u32[]{:S(2)}) %collective-permute-start.136) | collective-permute-done | bytes 786464 | tf_op jit(solution)/shard_map/ppermute | solution.py:630
  581.5 3.2 assemble.1
  (606 shorter events, 224.2 us)
Async XLA Ops:
  4.8 21.7 %collective-permute-start.2 = (bf16[128,2048]{1,0:T(8,128)(2,1)S(1)}, bf16[128,2048]{1,0:T(8,128)(2,1)}, u32[]{:S(2)}, u32[]{:S(2)}) collective-permute-start(bf16[128,2048]{1,0:T(8,128)(2,1)S(1)} %get-tuple-element.511.refs_0_), channel_id=1, source_target_pairs={{4,0},{5,1},{8,4},{9,5},{12,8},{13,9},{14,12},{15,13},{10,14},{11,... | collective-permute-start | bytes 1572872 | tf_op jit(solution)/shard_map/ppermute | solution.py:500
  7.7 18.8 %collective-permute-start.1 = (bf16[128,2048]{1,0:T(8,128)(2,1)S(1)}, bf16[128,2048]{1,0:T(8,128)(2,1)}, u32[]{:S(2)}, u32[]{:S(2)}) collective-permute-start(bf16[128,2048]{1,0:T(8,128)(2,1)S(1)} %get-tuple-element.511.refs_0_), channel_id=1, source_target_pairs={{0,4},{1,5},{4,8},{5,9},{8,12},{9,13},{12,14},{13,15},{14,10},{15,... | collective-permute-start | bytes 1572872 | tf_op jit(solution)/shard_map/ppermute | solution.py:497
  7.9 21.1 %collective-permute-start = (bf16[128,2048]{1,0:T(8,128)(2,1)S(1)}, bf16[128,2048]{1,0:T(8,128)(2,1)S(1)}, u32[]{:S(2)}, u32[]{:S(2)}) collective-permute-start(bf16[128,2048]{1,0:T(8,128)(2,1)S(1)} %get-tuple-element.511.refs_0_), channel_id=1, source_target_pairs={{0,1},{1,0},{2,3},{3,2},{4,5},{5,4},{6,7},{7,6},{8,9},{9,8},{10,11... | collective-permute-start | bytes 1572872 | tf_op jit(solution)/shard_map/ppermute | solution.py:503
  12.6 46.4 %all-to-all-start = ((bf16[16,64,384]{2,1,0:T(8,128)(2,1)}), bf16[16,64,384]{2,1,0:T(8,128)(2,1)}, u32[]{:S(2)}, u32[]{:S(2)}) async-start(bf16[16,64,384]{2,1,0:T(8,128)(2,1)} %slice_select_fusion), calls=%async_computation | async-start | bytes 1572864 | tf_op jit(solution)/shard_map/all_to_all | solution.py:701
  26.5 17.8 %collective-permute-start.5 = (bf16[128,2048]{1,0:T(8,128)(2,1)}, bf16[128,2048]{1,0:T(8,128)(2,1)}, u32[]{:S(2)}, u32[]{:S(2)}) collective-permute-start(bf16[128,2048]{1,0:T(8,128)(2,1)} %collective-permute-done.1.refs_2_), channel_id=1, source_target_pairs={{0,4},{1,5},{4,8},{5,9},{8,12},{9,13},{12,14},{13,15},{14,10},{15,... | collective-permute-start | bytes 1572872 | tf_op jit(solution)/shard_map/ppermute | solution.py:497
  28.5 23.5 %collective-permute-start.3 = (bf16[128,2048]{1,0:T(8,128)(2,1)}, bf16[128,2048]{1,0:T(8,128)(2,1)S(1)}, u32[]{:S(2)}, u32[]{:S(2)}) collective-permute-start(bf16[128,2048]{1,0:T(8,128)(2,1)} %collective-permute-done.1.refs_2_), channel_id=1, source_target_pairs={{0,1},{1,0},{2,3},{3,2},{4,5},{5,4},{6,7},{7,6},{8,9},{9,8},{10,11... | collective-permute-start | bytes 1572872 | tf_op jit(solution)/shard_map/ppermute | solution.py:503
  28.5 17.7 %collective-permute-start.6 = (bf16[128,2048]{1,0:T(8,128)(2,1)}, bf16[128,2048]{1,0:T(8,128)(2,1)}, u32[]{:S(2)}, u32[]{:S(2)}) collective-permute-start(bf16[128,2048]{1,0:T(8,128)(2,1)} %collective-permute-done.2.refs_3_), channel_id=1, source_target_pairs={{4,0},{5,1},{8,4},{9,5},{12,8},{13,9},{14,12},{15,13},{10,14},{11,... | collective-permute-start | bytes 1572872 | tf_op jit(solution)/shard_map/ppermute | solution.py:500
  28.7 24.9 %collective-permute-start.4 = (bf16[128,2048]{1,0:T(8,128)(2,1)}, bf16[128,2048]{1,0:T(8,128)(2,1)S(1)}, u32[]{:S(2)}, u32[]{:S(2)}) collective-permute-start(bf16[128,2048]{1,0:T(8,128)(2,1)} %collective-permute-done.2.refs_3_), channel_id=1, source_target_pairs={{0,1},{1,0},{2,3},{3,2},{4,5},{5,4},{6,7},{7,6},{8,9},{9,8},{10,11... | collective-permute-start | bytes 1572872 | tf_op jit(solution)/shard_map/ppermute | solution.py:503
  46.2 17.1 %collective-permute-start.9 = (bf16[128,2048]{1,0:T(8,128)(2,1)}, bf16[128,2048]{1,0:T(8,128)(2,1)S(1)}, u32[]{:S(2)}, u32[]{:S(2)}) collective-permute-start(bf16[128,2048]{1,0:T(8,128)(2,1)} %collective-permute-done.5.refs_6_), channel_id=1, source_target_pairs={{0,4},{1,5},{4,8},{5,9},{8,12},{9,13},{12,14},{13,15},{14,10},{15,... | collective-permute-start | bytes 1572872 | tf_op jit(solution)/shard_map/ppermute | solution.py:497
  51.9 15.2 %collective-permute-start.7 = (bf16[128,2048]{1,0:T(8,128)(2,1)}, bf16[128,2048]{1,0:T(8,128)(2,1)}, u32[]{:S(2)}, u32[]{:S(2)}) collective-permute-start(bf16[128,2048]{1,0:T(8,128)(2,1)} %collective-permute-done.5.refs_6_), channel_id=1, source_target_pairs={{0,1},{1,0},{2,3},{3,2},{4,5},{5,4},{6,7},{7,6},{8,9},{9,8},{10,11... | collective-permute-start | bytes 1572872 | tf_op jit(solution)/shard_map/ppermute | solution.py:503
  51.9 14.5 %collective-permute-start.10 = (bf16[128,2048]{1,0:T(8,128)(2,1)}, bf16[128,2048]{1,0:T(8,128)(2,1)S(1)}, u32[]{:S(2)}, u32[]{:S(2)}) collective-permute-start(bf16[128,2048]{1,0:T(8,128)(2,1)} %collective-permute-done.6.refs_7_), channel_id=1, source_target_pairs={{4,0},{5,1},{8,4},{9,5},{12,8},{13,9},{14,12},{15,13},{10,14},{11,... | collective-permute-start | bytes 1572872 | tf_op jit(solution)/shard_map/ppermute | solution.py:500
  52.0 17.4 %collective-permute-start.8 = (bf16[128,2048]{1,0:T(8,128)(2,1)}, bf16[128,2048]{1,0:T(8,128)(2,1)}, u32[]{:S(2)}, u32[]{:S(2)}) collective-permute-start(bf16[128,2048]{1,0:T(8,128)(2,1)} %collective-permute-done.6.refs_7_), channel_id=1, source_target_pairs={{0,1},{1,0},{2,3},{3,2},{4,5},{5,4},{6,7},{7,6},{8,9},{9,8},{10,11... | collective-permute-start | bytes 1572872 | tf_op jit(solution)/shard_map/ppermute | solution.py:503
  59.0 23.7 %collective-permute-start.17 = (bf16[16,64,384]{2,1,0:T(8,128)(2,1)}, bf16[16,64,384]{2,1,0:T(8,128)(2,1)S(1)}, u32[]{:S(2)}, u32[]{:S(2)}) collective-permute-start(bf16[16,64,384]{2,1,0:T(8,128)(2,1)} %all-to-all-done), channel_id=1, source_target_pairs={{0,16},{16,0},{1,17},{17,1},{2,18},{18,2},{3,19},{19,3},{4,20},{20... | collective-permute-start | bytes 2359304 | tf_op jit(solution)/shard_map/ppermute | solution.py:630
  93.4 21.7 %collective-permute-start.19 = (bf16[128,2048]{1,0:T(8,128)(2,1)S(1)}, bf16[128,2048]{1,0:T(8,128)(2,1)S(1)}, u32[]{:S(2)}, u32[]{:S(2)}) collective-permute-start(bf16[128,2048]{1,0:T(8,128)(2,1)S(1)} %copy-done.42), channel_id=1, source_target_pairs={{4,0},{5,1},{8,4},{9,5},{12,8},{13,9},{14,12},{15,13},{10,14},{11,... | collective-permute-start | bytes 1572872 | tf_op jit(solution)/shard_map/ppermute | solution.py:500
  94.8 20.3 %collective-permute-start.18 = (bf16[128,2048]{1,0:T(8,128)(2,1)S(1)}, bf16[128,2048]{1,0:T(8,128)(2,1)}, u32[]{:S(2)}, u32[]{:S(2)}) collective-permute-start(bf16[128,2048]{1,0:T(8,128)(2,1)S(1)} %copy-done.42), channel_id=1, source_target_pairs={{0,4},{1,5},{4,8},{5,9},{8,12},{9,13},{12,14},{13,15},{14,10},{15,... | collective-permute-start | bytes 1572872 | tf_op jit(solution)/shard_map/ppermute | solution.py:497
  118.2 15.0 %collective-permute-start.23 = (bf16[128,2048]{1,0:T(8,128)(2,1)}, bf16[128,2048]{1,0:T(8,128)(2,1)S(1)}, u32[]{:S(2)}, u32[]{:S(2)}) collective-permute-start(bf16[128,2048]{1,0:T(8,128)(2,1)} %collective-permute-done.18.refs_7_), channel_id=1, source_target_pairs={{0,4},{1,5},{4,8},{5,9},{8,12},{9,13},{12,14},{13,15},{14,10},{15,... | collective-permute-start | bytes 1572872 | tf_op jit(solution)/shard_map/ppermute | solution.py:497
  120.0 14.8 %collective-permute-start.24 = (bf16[128,2048]{1,0:T(8,128)(2,1)S(1)}, bf16[128,2048]{1,0:T(8,128)(2,1)S(1)}, u32[]{:S(2)}, u32[]{:S(2)}) collective-permute-start(bf16[128,2048]{1,0:T(8,128)(2,1)S(1)} %collective-permute-done.19.refs_8_), channel_id=1, source_target_pairs={{4,0},{5,1},{8,4},{9,5},{12,8},{13,9},{14,12},{15,13},{10,14},{11,... | collective-permute-start | bytes 1572872 | tf_op jit(solution)/shard_map/ppermute | solution.py:500
  120.7 23.5 %collective-permute-start.30 = (bf16[256,2048]{1,0:T(8,128)(2,1)S(1)}, bf16[256,2048]{1,0:T(8,128)(2,1)S(1)}, u32[]{:S(2)}, u32[]{:S(2)}) collective-permute-start(bf16[256,2048]{1,0:T(8,128)(2,1)S(1)} %convolution_convert_fusion.7), channel_id=1, source_target_pairs={{0,1},{1,0},{2,3},{3,2},{4,5},{5,4},{6,7},{7,6},{8,9},{9,8},{10,11... | collective-permute-start | bytes 3145736 | tf_op jit(solution)/shard_map/ppermute | solution.py:503
  121.1 16.8 %collective-permute-start.22 = (bf16[64,2048]{1,0:T(8,128)(2,1)S(1)}, bf16[64,2048]{1,0:T(8,128)(2,1)S(1)}, u32[]{:S(2)}, u32[]{:S(2)}) collective-permute-start(bf16[64,2048]{1,0:T(8,128)(2,1)S(1)} %get-tuple-element.669), channel_id=1, source_target_pairs={{0,4},{1,5},{4,8},{5,9},{8,12},{9,13},{12,14},{13,15},{14,10},{15,... | collective-permute-start | bytes 786440 | tf_op jit(solution)/shard_map/ppermute | solution.py:497
  122.9 16.3 %collective-permute-start.21 = (bf16[64,2048]{1,0:T(8,128)(2,1)S(1)}, bf16[64,2048]{1,0:T(8,128)(2,1)S(1)}, u32[]{:S(2)}, u32[]{:S(2)}) collective-permute-start(bf16[64,2048]{1,0:T(8,128)(2,1)S(1)} %get-tuple-element.670), channel_id=1, source_target_pairs={{4,0},{5,1},{8,4},{9,5},{12,8},{13,9},{14,12},{15,13},{10,14},{11,... | collective-permute-start | bytes 786440 | tf_op jit(solution)/shard_map/ppermute | solution.py:500
  139.5 14.9 %collective-permute-start.26 = (bf16[128,2048]{1,0:T(8,128)(2,1)S(1)}, bf16[128,2048]{1,0:T(8,128)(2,1)S(1)}, u32[]{:S(2)}, u32[]{:S(2)}) collective-permute-start(bf16[128,2048]{1,0:T(8,128)(2,1)S(1)} %pad_maximum_fusion.4), channel_id=1, source_target_pairs={{4,0},{5,1},{8,4},{9,5},{12,8},{13,9},{14,12},{15,13},{10,14},{11,... | collective-permute-start | bytes 1572872 | tf_op jit(solution)/shard_map/ppermute | solution.py:500
  139.9 14.9 %collective-permute-start.27 = (bf16[128,2048]{1,0:T(8,128)(2,1)S(1)}, bf16[128,2048]{1,0:T(8,128)(2,1)S(1)}, u32[]{:S(2)}, u32[]{:S(2)}) collective-permute-start(bf16[128,2048]{1,0:T(8,128)(2,1)S(1)} %pad_maximum_fusion.5), channel_id=1, source_target_pairs={{0,4},{1,5},{4,8},{5,9},{8,12},{9,13},{12,14},{13,15},{14,10},{15,... | collective-permute-start | bytes 1572872 | tf_op jit(solution)/shard_map/ppermute | solution.py:497
  141.7 22.2 %collective-permute-start.28 = (bf16[128,2048]{1,0:T(8,128)(2,1)S(1)}, bf16[128,2048]{1,0:T(8,128)(2,1)S(1)}, u32[]{:S(2)}, u32[]{:S(2)}) collective-permute-start(bf16[128,2048]{1,0:T(8,128)(2,1)S(1)} %collective-permute-done.23.refs_11_), channel_id=1, source_target_pairs={{0,4},{1,5},{4,8},{5,9},{8,12},{9,13},{12,14},{13,15},{14,10},{15,... | collective-permute-start | bytes 1572872 | tf_op jit(solution)/shard_map/ppermute | solution.py:497
  142.3 21.6 %collective-permute-start.29 = (bf16[128,2048]{1,0:T(8,128)(2,1)S(1)}, bf16[128,2048]{1,0:T(8,128)(2,1)S(1)}, u32[]{:S(2)}, u32[]{:S(2)}) collective-permute-start(bf16[128,2048]{1,0:T(8,128)(2,1)S(1)} %collective-permute-done.24.refs_12_), channel_id=1, source_target_pairs={{4,0},{5,1},{8,4},{9,5},{12,8},{13,9},{14,12},{15,13},{10,14},{11,... | collective-permute-start | bytes 1572872 | tf_op jit(solution)/shard_map/ppermute | solution.py:500
  144.2 24.4 %collective-permute-start.35 = (bf16[256,2048]{1,0:T(8,128)(2,1)S(1)}, bf16[256,2048]{1,0:T(8,128)(2,1)S(1)}, u32[]{:S(2)}, u32[]{:S(2)}) collective-permute-start(bf16[256,2048]{1,0:T(8,128)(2,1)S(1)} %convolution_convert_fusion.6), channel_id=1, source_target_pairs={{0,1},{1,0},{2,3},{3,2},{4,5},{5,4},{6,7},{7,6},{8,9},{9,8},{10,11... | collective-permute-start | bytes 3145736 | tf_op jit(solution)/shard_map/ppermute | solution.py:503
  164.2 18.4 %collective-permute-start.32 = (bf16[128,2048]{1,0:T(8,128)(2,1)S(1)}, bf16[128,2048]{1,0:T(8,128)(2,1)S(1)}, u32[]{:S(2)}, u32[]{:S(2)}) collective-permute-start(bf16[128,2048]{1,0:T(8,128)(2,1)S(1)} %get-tuple-element.638), channel_id=1, source_target_pairs={{0,4},{1,5},{4,8},{5,9},{8,12},{9,13},{12,14},{13,15},{14,10},{15,... | collective-permute-start | bytes 1572872 | tf_op jit(solution)/shard_map/ppermute | solution.py:497
  165.8 16.9 %collective-permute-start.31 = (bf16[128,2048]{1,0:T(8,128)(2,1)S(1)}, bf16[128,2048]{1,0:T(8,128)(2,1)S(1)}, u32[]{:S(2)}, u32[]{:S(2)}) collective-permute-start(bf16[128,2048]{1,0:T(8,128)(2,1)S(1)} %get-tuple-element.639), channel_id=1, source_target_pairs={{4,0},{5,1},{8,4},{9,5},{12,8},{13,9},{14,12},{15,13},{10,14},{11,... | collective-permute-start | bytes 1572872 | tf_op jit(solution)/shard_map/ppermute | solution.py:500
  166.6 18.5 %collective-permute-start.38 = (bf16[128,2048]{1,0:T(8,128)(2,1)S(1)}, bf16[128,2048]{1,0:T(8,128)(2,1)S(1)}, u32[]{:S(2)}, u32[]{:S(2)}) collective-permute-start(bf16[128,2048]{1,0:T(8,128)(2,1)S(1)} %convolution_convert_fusion.18), channel_id=1, source_target_pairs={{0,1},{1,0},{2,3},{3,2},{4,5},{5,4},{6,7},{7,6},{8,9},{9,8},{10,11... | collective-permute-start | bytes 1572872 | tf_op jit(solution)/shard_map/ppermute | solution.py:503
  166.7 15.9 %collective-permute-start.34 = (bf16[64,2048]{1,0:T(8,128)(2,1)S(1)}, bf16[64,2048]{1,0:T(8,128)(2,1)S(1)}, u32[]{:S(2)}, u32[]{:S(2)}) collective-permute-start(bf16[64,2048]{1,0:T(8,128)(2,1)S(1)} %slice.395), channel_id=1, source_target_pairs={{4,0},{5,1},{8,4},{9,5},{12,8},{13,9},{14,12},{15,13},{10,14},{11,... | collective-permute-start | bytes 786440 | tf_op jit(solution)/shard_map/ppermute | solution.py:500
  277.3 14.7 %collective-permute-start.69 = (bf16[128,2048]{1,0:T(8,128)(2,1)}, bf16[128,2048]{1,0:T(8,128)(2,1)}, u32[]{:S(2)}, u32[]{:S(2)}) collective-permute-start(bf16[128,2048]{1,0:T(8,128)(2,1)} %pad_maximum_fusion.8), channel_id=1, source_target_pairs={{4,0},{5,1},{8,4},{9,5},{12,8},{13,9},{14,12},{15,13},{10,14},{11,... | collective-permute-start | bytes 1572872 | tf_op jit(solution)/shard_map/ppermute | solution.py:500
  278.4 14.8 %collective-permute-start.70 = (bf16[128,2048]{1,0:T(8,128)(2,1)}, bf16[128,2048]{1,0:T(8,128)(2,1)}, u32[]{:S(2)}, u32[]{:S(2)}) collective-permute-start(bf16[128,2048]{1,0:T(8,128)(2,1)} %pad_maximum_fusion.9), channel_id=1, source_target_pairs={{0,4},{1,5},{4,8},{5,9},{8,12},{9,13},{12,14},{13,15},{14,10},{15,... | collective-permute-start | bytes 1572872 | tf_op jit(solution)/shard_map/ppermute | solution.py:497
  334.5 25.8 %collective-permute-start.86 = (bf16[256,2048]{1,0:T(8,128)(2,1)}, bf16[256,2048]{1,0:T(8,128)(2,1)}, u32[]{:S(2)}, u32[]{:S(2)}) collective-permute-start(bf16[256,2048]{1,0:T(8,128)(2,1)} %get-tuple-element.481.refs_2_), channel_id=1, source_target_pairs={{0,16},{16,0},{1,17},{17,1},{2,18},{18,2},{3,19},{19,3},{4,20},{20... | collective-permute-start | bytes 3145736 | tf_op jit(solution)/shard_map/ppermute | solution.py:630
  336.0 14.9 %collective-permute-start.80 = (bf16[128,2048]{1,0:T(8,128)(2,1)S(1)}, bf16[128,2048]{1,0:T(8,128)(2,1)}, u32[]{:S(2)}, u32[]{:S(2)}) collective-permute-start(bf16[128,2048]{1,0:T(8,128)(2,1)S(1)} %get-tuple-element.542.refs_1_), channel_id=1, source_target_pairs={{0,4},{1,5},{4,8},{5,9},{8,12},{9,13},{12,14},{13,15},{14,10},{15,... | collective-permute-start | bytes 1572872 | tf_op jit(solution)/shard_map/ppermute | solution.py:497
  336.9 18.4 %collective-permute-start.84 = (bf16[64,2048]{1,0:T(8,128)(2,1)S(1)}, bf16[64,2048]{1,0:T(8,128)(2,1)S(1)}, u32[]{:S(2)}, u32[]{:S(2)}) collective-permute-start(bf16[64,2048]{1,0:T(8,128)(2,1)S(1)} %get-tuple-element.665), channel_id=1, source_target_pairs={{0,4},{1,5},{4,8},{5,9},{8,12},{9,13},{12,14},{13,15},{14,10},{15,... | collective-permute-start | bytes 786440 | tf_op jit(solution)/shard_map/ppermute | solution.py:497
  363.1 26.8 %collective-permute-start.92 = (bf16[256,2048]{1,0:T(8,128)(2,1)S(1)}, bf16[256,2048]{1,0:T(8,128)(2,1)}, u32[]{:S(2)}, u32[]{:S(2)}) collective-permute-start(bf16[256,2048]{1,0:T(8,128)(2,1)S(1)} %copy-done.65), channel_id=1, source_target_pairs={{0,16},{16,0},{1,17},{17,1},{2,18},{18,2},{3,19},{19,3},{4,20},{20... | collective-permute-start | bytes 3145736 | tf_op jit(solution)/shard_map/ppermute | solution.py:630
  363.5 15.1 %collective-permute-start.89 = (bf16[128,2048]{1,0:T(8,128)(2,1)}, bf16[128,2048]{1,0:T(8,128)(2,1)}, u32[]{:S(2)}, u32[]{:S(2)}) collective-permute-start(bf16[128,2048]{1,0:T(8,128)(2,1)} %pad_maximum_fusion.10), channel_id=1, source_target_pairs={{4,0},{5,1},{8,4},{9,5},{12,8},{13,9},{14,12},{15,13},{10,14},{11,... | collective-permute-start | bytes 1572872 | tf_op jit(solution)/shard_map/ppermute | solution.py:500
  364.7 15.1 %collective-permute-start.90 = (bf16[128,2048]{1,0:T(8,128)(2,1)}, bf16[128,2048]{1,0:T(8,128)(2,1)}, u32[]{:S(2)}, u32[]{:S(2)}) collective-permute-start(bf16[128,2048]{1,0:T(8,128)(2,1)} %pad_maximum_fusion.11), channel_id=1, source_target_pairs={{0,4},{1,5},{4,8},{5,9},{8,12},{9,13},{12,14},{13,15},{14,10},{15,... | collective-permute-start | bytes 1572872 | tf_op jit(solution)/shard_map/ppermute | solution.py:497
  365.5 24.4 %collective-permute-start.87 = (bf16[128,2048]{1,0:T(8,128)(2,1)}, bf16[128,2048]{1,0:T(8,128)(2,1)}, u32[]{:S(2)}, u32[]{:S(2)}) collective-permute-start(bf16[128,2048]{1,0:T(8,128)(2,1)} %collective-permute-done.80.refs_3_), channel_id=1, source_target_pairs={{0,4},{1,5},{4,8},{5,9},{8,12},{9,13},{12,14},{13,15},{14,10},{15,... | collective-permute-start | bytes 1572872 | tf_op jit(solution)/shard_map/ppermute | solution.py:497
  366.4 23.6 %collective-permute-start.88 = (bf16[128,2048]{1,0:T(8,128)(2,1)}, bf16[128,2048]{1,0:T(8,128)(2,1)}, u32[]{:S(2)}, u32[]{:S(2)}) collective-permute-start(bf16[128,2048]{1,0:T(8,128)(2,1)} %collective-permute-done.81.refs_4_), channel_id=1, source_target_pairs={{4,0},{5,1},{8,4},{9,5},{12,8},{13,9},{14,12},{15,13},{10,14},{11,... | collective-permute-start | bytes 1572872 | tf_op jit(solution)/shard_map/ppermute | solution.py:500
  394.3 30.2 %collective-permute-start.98 = (bf16[256,2048]{1,0:T(8,128)(2,1)S(1)}, bf16[256,2048]{1,0:T(8,128)(2,1)}, u32[]{:S(2)}, u32[]{:S(2)}) collective-permute-start(bf16[256,2048]{1,0:T(8,128)(2,1)S(1)} %copy-done.66), channel_id=1, source_target_pairs={{0,16},{16,0},{1,17},{17,1},{2,18},{18,2},{3,19},{19,3},{4,20},{20... | collective-permute-start | bytes 3145736 | tf_op jit(solution)/shard_map/ppermute | solution.py:630
  398.5 15.1 %collective-permute-start.96 = (bf16[128,2048]{1,0:T(8,128)(2,1)}, bf16[128,2048]{1,0:T(8,128)(2,1)}, u32[]{:S(2)}, u32[]{:S(2)}) collective-permute-start(bf16[128,2048]{1,0:T(8,128)(2,1)} %get-tuple-element.623), channel_id=1, source_target_pairs={{0,4},{1,5},{4,8},{5,9},{8,12},{9,13},{12,14},{13,15},{14,10},{15,... | collective-permute-start | bytes 1572872 | tf_op jit(solution)/shard_map/ppermute | solution.py:497
  399.3 15.1 %collective-permute-start.95 = (bf16[128,2048]{1,0:T(8,128)(2,1)}, bf16[128,2048]{1,0:T(8,128)(2,1)}, u32[]{:S(2)}, u32[]{:S(2)}) collective-permute-start(bf16[128,2048]{1,0:T(8,128)(2,1)} %get-tuple-element.624), channel_id=1, source_target_pairs={{4,0},{5,1},{8,4},{9,5},{12,8},{13,9},{14,12},{15,13},{10,14},{11,... | collective-permute-start | bytes 1572872 | tf_op jit(solution)/shard_map/ppermute | solution.py:500
  400.5 23.4 %collective-permute-start.93 = (bf16[128,2048]{1,0:T(8,128)(2,1)}, bf16[128,2048]{1,0:T(8,128)(2,1)S(1)}, u32[]{:S(2)}, u32[]{:S(2)}) collective-permute-start(bf16[128,2048]{1,0:T(8,128)(2,1)} %collective-permute-done.87.refs_7_), channel_id=1, source_target_pairs={{0,4},{1,5},{4,8},{5,9},{8,12},{9,13},{12,14},{13,15},{14,10},{15,... | collective-permute-start | bytes 1572872 | tf_op jit(solution)/shard_map/ppermute | solution.py:497
  401.4 23.1 %collective-permute-start.94 = (bf16[128,2048]{1,0:T(8,128)(2,1)}, bf16[128,2048]{1,0:T(8,128)(2,1)S(1)}, u32[]{:S(2)}, u32[]{:S(2)}) collective-permute-start(bf16[128,2048]{1,0:T(8,128)(2,1)} %collective-permute-done.88.refs_8_), channel_id=1, source_target_pairs={{4,0},{5,1},{8,4},{9,5},{12,8},{13,9},{14,12},{15,13},{10,14},{11,... | collective-permute-start | bytes 1572872 | tf_op jit(solution)/shard_map/ppermute | solution.py:500
  413.6 16.3 %collective-permute-start.106 = (bf16[128,2048]{1,0:T(8,128)(2,1)}, bf16[128,2048]{1,0:T(8,128)(2,1)S(1)}, u32[]{:S(2)}, u32[]{:S(2)}) collective-permute-start(bf16[128,2048]{1,0:T(8,128)(2,1)} %collective-permute-done.87.refs_7_), channel_id=1, source_target_pairs={{0,1},{1,0},{2,3},{3,2},{4,5},{5,4},{6,7},{7,6},{8,9},{9,8},{10,11... | collective-permute-start | bytes 1572872 | tf_op jit(solution)/shard_map/ppermute | solution.py:503
  414.4 16.7 %collective-permute-start.107 = (bf16[128,2048]{1,0:T(8,128)(2,1)}, bf16[128,2048]{1,0:T(8,128)(2,1)S(1)}, u32[]{:S(2)}, u32[]{:S(2)}) collective-permute-start(bf16[128,2048]{1,0:T(8,128)(2,1)} %collective-permute-done.88.refs_8_), channel_id=1, source_target_pairs={{0,1},{1,0},{2,3},{3,2},{4,5},{5,4},{6,7},{7,6},{8,9},{9,8},{10,11... | collective-permute-start | bytes 1572872 | tf_op jit(solution)/shard_map/ppermute | solution.py:503
  424.5 16.4 %collective-permute-start.108 = (bf16[128,2048]{1,0:T(8,128)(2,1)S(1)}, bf16[128,2048]{1,0:T(8,128)(2,1)S(1)}, u32[]{:S(2)}, u32[]{:S(2)}) collective-permute-start(bf16[128,2048]{1,0:T(8,128)(2,1)S(1)} %collective-permute-done.93.refs_11_), channel_id=1, source_target_pairs={{0,1},{1,0},{2,3},{3,2},{4,5},{5,4},{6,7},{7,6},{8,9},{9,8},{10,11... | collective-permute-start | bytes 1572872 | tf_op jit(solution)/shard_map/ppermute | solution.py:503
  424.6 18.1 %collective-permute-start.109 = (bf16[128,2048]{1,0:T(8,128)(2,1)S(1)}, bf16[128,2048]{1,0:T(8,128)(2,1)S(1)}, u32[]{:S(2)}, u32[]{:S(2)}) collective-permute-start(bf16[128,2048]{1,0:T(8,128)(2,1)S(1)} %collective-permute-done.94.refs_12_), channel_id=1, source_target_pairs={{0,1},{1,0},{2,3},{3,2},{4,5},{5,4},{6,7},{7,6},{8,9},{9,8},{10,11... | collective-permute-start | bytes 1572872 | tf_op jit(solution)/shard_map/ppermute | solution.py:503
  438.7 32.7 %collective-permute-start.100 = (bf16[128,2048]{1,0:T(8,128)(2,1)}, bf16[128,2048]{1,0:T(8,128)(2,1)}, u32[]{:S(2)}, u32[]{:S(2)}) collective-permute-start(bf16[128,2048]{1,0:T(8,128)(2,1)} %get-tuple-element.621), channel_id=1, source_target_pairs={{0,4},{1,5},{4,8},{5,9},{8,12},{9,13},{12,14},{13,15},{14,10},{15,... | collective-permute-start | bytes 1572872 | tf_op jit(solution)/shard_map/ppermute | solution.py:497
  439.6 31.8 %collective-permute-start.99 = (bf16[128,2048]{1,0:T(8,128)(2,1)}, bf16[128,2048]{1,0:T(8,128)(2,1)}, u32[]{:S(2)}, u32[]{:S(2)}) collective-permute-start(bf16[128,2048]{1,0:T(8,128)(2,1)} %get-tuple-element.622), channel_id=1, source_target_pairs={{4,0},{5,1},{8,4},{9,5},{12,8},{13,9},{14,12},{15,13},{10,14},{11,... | collective-permute-start | bytes 1572872 | tf_op jit(solution)/shard_map/ppermute | solution.py:500
  440.9 30.4 %collective-permute-start.102 = (bf16[256,2048]{1,0:T(8,128)(2,1)S(1)}, bf16[256,2048]{1,0:T(8,128)(2,1)}, u32[]{:S(2)}, u32[]{:S(2)}) collective-permute-start(bf16[256,2048]{1,0:T(8,128)(2,1)S(1)} %copy-done.64), channel_id=1, source_target_pairs={{0,16},{16,0},{1,17},{17,1},{2,18},{18,2},{3,19},{19,3},{4,20},{20... | collective-permute-start | bytes 3145736 | tf_op jit(solution)/shard_map/ppermute | solution.py:630
  477.4 20.1 %collective-permute-start.119 = (bf16[192,2048]{1,0:T(8,128)(2,1)}, bf16[192,2048]{1,0:T(8,128)(2,1)}, u32[]{:S(2)}, u32[]{:S(2)}) collective-permute-start(bf16[192,2048]{1,0:T(8,128)(2,1)} %get-tuple-element.581.refs_2_), channel_id=1, source_target_pairs={{0,16},{16,0},{1,17},{17,1},{2,18},{18,2},{3,19},{19,3},{4,20},{20... | collective-permute-start | bytes 2359304 | tf_op jit(solution)/shard_map/ppermute | solution.py:630
  501.4 15.1 %collective-permute-start.123 = (bf16[256,2048]{1,0:T(8,128)(2,1)S(1)}, bf16[256,2048]{1,0:T(8,128)(2,1)}, u32[]{:S(2)}, u32[]{:S(2)}) collective-permute-start(bf16[256,2048]{1,0:T(8,128)(2,1)S(1)} %convolution_convert_fusion.1), channel_id=1, source_target_pairs={{0,1},{1,0},{2,3},{3,2},{4,5},{5,4},{6,7},{7,6},{8,9},{9,8},{10,11... | collective-permute-start | bytes 3145736 | tf_op jit(solution)/shard_map/ppermute | solution.py:503
  501.6 20.3 %collective-permute-start.124 = (bf16[16,64,384]{2,1,0:T(8,128)(2,1)}, bf16[16,64,384]{2,1,0:T(8,128)(2,1)}, u32[]{:S(2)}, u32[]{:S(2)}) collective-permute-start(bf16[16,64,384]{2,1,0:T(8,128)(2,1)} %get-tuple-element.540), channel_id=1, source_target_pairs={{0,16},{16,0},{1,17},{17,1},{2,18},{18,2},{3,19},{19,3},{4,20},{20... | collective-permute-start | bytes 2359304 | tf_op jit(solution)/shard_map/ppermute | solution.py:630
  501.9 16.6 %collective-permute-start.120 = (bf16[128,2048]{1,0:T(8,128)(2,1)}, bf16[128,2048]{1,0:T(8,128)(2,1)S(1)}, u32[]{:S(2)}, u32[]{:S(2)}) collective-permute-start(bf16[128,2048]{1,0:T(8,128)(2,1)} %pad_maximum_fusion.12), channel_id=1, source_target_pairs={{4,0},{5,1},{8,4},{9,5},{12,8},{13,9},{14,12},{15,13},{10,14},{11,... | collective-permute-start | bytes 1572872 | tf_op jit(solution)/shard_map/ppermute | solution.py:500
  503.1 15.4 %collective-permute-start.121 = (bf16[128,2048]{1,0:T(8,128)(2,1)}, bf16[128,2048]{1,0:T(8,128)(2,1)}, u32[]{:S(2)}, u32[]{:S(2)}) collective-permute-start(bf16[128,2048]{1,0:T(8,128)(2,1)} %pad_maximum_fusion.13), channel_id=1, source_target_pairs={{0,4},{1,5},{4,8},{5,9},{8,12},{9,13},{12,14},{13,15},{14,10},{15,... | collective-permute-start | bytes 1572872 | tf_op jit(solution)/shard_map/ppermute | solution.py:497
  525.9 17.1 %collective-permute-start.126 = (bf16[128,2048]{1,0:T(8,128)(2,1)}, bf16[128,2048]{1,0:T(8,128)(2,1)}, u32[]{:S(2)}, u32[]{:S(2)}) collective-permute-start(bf16[128,2048]{1,0:T(8,128)(2,1)} %get-tuple-element.617), channel_id=1, source_target_pairs={{0,4},{1,5},{4,8},{5,9},{8,12},{9,13},{12,14},{13,15},{14,10},{15,... | collective-permute-start | bytes 1572872 | tf_op jit(solution)/shard_map/ppermute | solution.py:497
  526.7 16.2 %collective-permute-start.125 = (bf16[128,2048]{1,0:T(8,128)(2,1)}, bf16[128,2048]{1,0:T(8,128)(2,1)}, u32[]{:S(2)}, u32[]{:S(2)}) collective-permute-start(bf16[128,2048]{1,0:T(8,128)(2,1)} %get-tuple-element.618), channel_id=1, source_target_pairs={{4,0},{5,1},{8,4},{9,5},{12,8},{13,9},{14,12},{15,13},{10,14},{11,... | collective-permute-start | bytes 1572872 | tf_op jit(solution)/shard_map/ppermute | solution.py:500
  532.8 28.4 %all-to-all-start.1 = ((bf16[16,64,384]{2,1,0:T(8,128)(2,1)}), bf16[16,64,384]{2,1,0:T(8,128)(2,1)}, u32[]{:S(2)}, u32[]{:S(2)}) async-start(bf16[16,64,384]{2,1,0:T(8,128)(2,1)} %add_convert_fusion), calls=%async_computation.1 | async-start | bytes 1572864 | tf_op jit(solution)/shard_map/all_to_all | solution.py:847
  546.9 15.8 %collective-permute-start.133 = (bf16[128,2048]{1,0:T(8,128)(2,1)}, bf16[128,2048]{1,0:T(8,128)(2,1)}, u32[]{:S(2)}, u32[]{:S(2)}) collective-permute-start(bf16[128,2048]{1,0:T(8,128)(2,1)} %convolution_convert_fusion.12), channel_id=1, source_target_pairs={{0,1},{1,0},{2,3},{3,2},{4,5},{5,4},{6,7},{7,6},{8,9},{9,8},{10,11... | collective-permute-start | bytes 1572872 | tf_op jit(solution)/shard_map/ppermute | solution.py:503
  549.3 17.6 %collective-permute-start.131 = (bf16[128,2048]{1,0:T(8,128)(2,1)}, bf16[128,2048]{1,0:T(8,128)(2,1)}, u32[]{:S(2)}, u32[]{:S(2)}) collective-permute-start(bf16[128,2048]{1,0:T(8,128)(2,1)} %get-tuple-element.615), channel_id=1, source_target_pairs={{0,4},{1,5},{4,8},{5,9},{8,12},{9,13},{12,14},{13,15},{14,10},{15,... | collective-permute-start | bytes 1572872 | tf_op jit(solution)/shard_map/ppermute | solution.py:497
  550.1 16.7 %collective-permute-start.130 = (bf16[128,2048]{1,0:T(8,128)(2,1)}, bf16[128,2048]{1,0:T(8,128)(2,1)}, u32[]{:S(2)}, u32[]{:S(2)}) collective-permute-start(bf16[128,2048]{1,0:T(8,128)(2,1)} %get-tuple-element.616), channel_id=1, source_target_pairs={{4,0},{5,1},{8,4},{9,5},{12,8},{13,9},{14,12},{15,13},{10,14},{11,... | collective-permute-start | bytes 1572872 | tf_op jit(solution)/shard_map/ppermute | solution.py:500
  552.1 14.8 %collective-permute-start.132 = (f32[2,2048]{1,0:T(2,128)S(1)}, f32[2,2048]{1,0:T(2,128)S(1)}, u32[]{:S(2)}, u32[]{:S(2)}) collective-permute-start(f32[2,2048]{1,0:T(2,128)S(1)} %fusion.324), channel_id=1, source_target_pairs={{0,4},{1,5},{2,6},{3,7},{4,0},{5,1},{6,2},{7,3},{8,12},{9,13},{10,... | collective-permute-start | bytes 49160 | tf_op jit(solution)/shard_map/ppermute | solution.py:567
  561.2 19.4 %collective-permute-start.136 = (bf16[16,64,384]{2,1,0:T(8,128)(2,1)}, bf16[16,64,384]{2,1,0:T(8,128)(2,1)S(1)}, u32[]{:S(2)}, u32[]{:S(2)}) collective-permute-start(bf16[16,64,384]{2,1,0:T(8,128)(2,1)} %all-to-all-done.1.refs_0_), channel_id=1, source_target_pairs={{0,16},{16,0},{1,17},{17,1},{2,18},{18,2},{3,19},{19,3},{4,20},{20... | collective-permute-start | bytes 2359304 | tf_op jit(solution)/shard_map/ppermute | solution.py:630
  (186 other events, 1948.4 us)

commit v4 on v3

--- a/solution.py
+++ b/solution.py
@@ -145,9 +145,9 @@
 
 def backward_kernel(
     slot_ref, length_ref, query_ref, key_ref, value_ref, att_ref, up_ref, log_ref, cos_ref, sin_ref,
-    out_ref,
-    key_t, up_nat, delta, key_acc, value_acc, query_acc,
+    *refs,
 ):
+    *out_refs, out_ref, key_t, up_nat, delta, key_acc, value_acc, query_acc = refs
     rows = query_ref.shape[0]
     width = query_ref.shape[1]
     heads = width // HEAD_DIM
@@ -234,17 +234,28 @@
             ).astype(jnp.bfloat16)
         out_ref[source, 2 * width : 3 * width] = value_acc[target, :].astype(jnp.bfloat16)
 
-
-def attention_backward(slot_of, length, query, key, value, att, upstream, logs, cosine, sine):
+    start = 0
+    for group_ref in out_refs:
+        count = group_ref.shape[0]
+        group_ref[...] = out_ref[start : start + count, :]
+        start += count
+
+
+def attention_backward(
+    slot_of, length, query, key, value, att, upstream, logs, cosine, sine, group_rows
+):
     rows, width = query.shape
     vmem = pl.BlockSpec(memory_space=pltpu.VMEM)
     smem = pl.BlockSpec(memory_space=pltpu.SMEM)
     return pl.pallas_call(
         backward_kernel,
-        out_shape=[jax.ShapeDtypeStruct((rows, 3 * width), jnp.bfloat16)],
+        out_shape=[
+            jax.ShapeDtypeStruct((count, 3 * width), jnp.bfloat16) for count in group_rows
+        ],
         in_specs=[smem, smem] + [vmem] * 8,
-        out_specs=[vmem],
+        out_specs=[vmem] * len(group_rows),
         scratch_shapes=[
+            pltpu.VMEM((rows, 3 * width), jnp.bfloat16),
             pltpu.VMEM((width, rows), jnp.bfloat16),
             pltpu.VMEM((rows, width), jnp.bfloat16),
             pltpu.VMEM((8, rows), jnp.float32),
@@ -363,9 +374,14 @@
     )(*lefts, *rights)
 
 
-def heads_kernel(upper_ref, right_ref, weight_ref, *refs):
-    *piece_refs, keep_ref, give_ref, gain_ref, left_ref = refs
-    fill(left_ref, piece_refs)
+def heads_kernel(rights, upper_ref, weight_ref, *refs):
+    *piece_refs, keep_ref, give_ref, gain_ref, left_ref, right_ref = refs
+
+    @pl.when(pl.program_id(0) == 0)
+    def _():
+        fill(right_ref, piece_refs[:rights])
+
+    fill(left_ref, piece_refs[rights:])
     total = dot_tn(left_ref[...], right_ref[...])
     count, half, width = keep_ref.shape
     sums = jnp.sum(total * weight_ref[...].astype(jnp.float32), axis=1, keepdims=True)
@@ -376,20 +392,20 @@
     give_ref[...] = jnp.where(upper, blocks[:, 0], blocks[:, 1])
 
 
-def heads_grads(lefts, right, weight, upper, rows):
-    count, width = right.shape
-    wide = weight.shape[0]
+def heads_grads(lefts, rights, weight, upper, rows):
+    count = sum(piece.shape[0] for piece in rights)
+    wide, width = weight.shape
     tile = fitting(512, wide)
     half = ((tile // rows, rows // 2, width), lambda i: (i, 0, 0))
     whole = ((wide // rows, rows // 2, width), jnp.bfloat16)
     return pl.pallas_call(
-        heads_kernel,
+        functools.partial(heads_kernel, len(rights)),
         grid=(wide // tile,),
         in_specs=[
             pl.BlockSpec(memory_space=pltpu.SMEM),
-            pl.BlockSpec((count, width), first),
             pl.BlockSpec((tile, width), down_rows),
         ]
+        + [pl.BlockSpec(piece.shape, first) for piece in rights]
         + [pl.BlockSpec((piece.shape[0], tile), along) for piece in lefts],
         out_specs=[pl.BlockSpec(*half), pl.BlockSpec(*half), pl.BlockSpec((1, tile), along)],
         out_shape=[
@@ -397,11 +413,14 @@
             jax.ShapeDtypeStruct(*whole),
             jax.ShapeDtypeStruct((1, wide), jnp.float32),
         ],
-        scratch_shapes=[pltpu.VMEM((count, tile), jnp.bfloat16)],
+        scratch_shapes=[
+            pltpu.VMEM((count, tile), jnp.bfloat16),
+            pltpu.VMEM((count, width), jnp.bfloat16),
+        ],
         compiler_params=pltpu.CompilerParams(vmem_limit_bytes=VMEM_LIMIT),
         cost_estimate=SMALL,
         name="heads_grads",
-    )(upper, right, weight, *lefts)
+    )(upper, weight, *rights, *lefts)
 
 
 def assemble_kernel(side_ref, *refs):
@@ -767,7 +786,7 @@
         return dot_nn(mine, w_down), dot_nn(other, w_down)
 
     swaps = Swaps()
-    cuts = [[units // 16 * count for count in row] for row in ((4, 4, 8), (8, 8), (2, 8, 6))]
+    cuts = [[units // 16 * count for count in row] for row in ((4, 4, 8), (8, 8), (2, 8, 4, 2))]
     pull = Stream(ring.scatter(pull_part))
     hop([pull])
     swaps.add(
@@ -806,18 +825,29 @@
         ],
         axis=0,
     )
-    (lin_back,) = hop(
+    group_rows = [stop - start for start, stop in zip(starts, starts[1:])]
+    lin_back = hop(
         [mlp],
         swaps,
         beside=attention_backward(
-            slot_of, lengths, query, key, value, heads_attention, upstream, logs, cosine, sine
+            slot_of,
+            lengths,
+            query,
+            key,
+            value,
+            heads_attention,
+            upstream,
+            logs,
+            cosine,
+            sine,
+            group_rows,
         ),
     )
-    lin_back = own_columns(lin_back)
+    lin_back = [own_columns(rows) for rows in lin_back]
     w_own = own_columns(w_heads)
 
     def input_part(step, *held):
-        mine, other = halves(after(group_of(lin_back, step), *held))
+        mine, other = halves(after(lin_back[step], *held))
         return dot_nt(mine, w_own), dot_nt(other, w_own)
 
     pulled = Stream(ring.scatter(input_part))
@@ -853,7 +883,7 @@
     )
     swaps.add("out", [out_part])
     hop([pulled, totals], swaps)
-    (up_sum,) = hop([pulled, totals], work=sum_pieces, given=swaps.sums("up"))
+    (up_sum,) = hop([pulled, totals], swaps, work=sum_pieces, given=swaps.sums("up"))
     while pulled.asked is not None or totals.asked is not None:
         hop([pulled, totals])
     norm_one_back = pulled.result

time: 593 us -> 590 us (level)
  starting transfers between devices: 112 us -> 118 us
    ppermute x13 -> x14, starting transfers between devices: 13.1 us -> 18.4 us  [swapped(): return lax.ppermute(part, 'narrow', [(0, 1), (1, 0)])]
    ppermute x13 -> x14, waiting for transfers between devices: 48.7 us -> 43.6 us  [swapped(): return lax.ppermute(part, 'narrow', [(0, 1), (1, 0)])]
    unnamed x239 -> x253, local copies, waits for them, and re-layouts: 25.3 us -> 25.6 us
  transfers between devices with their start and end apart: 139 -> 140, of which waited for: 60 -> 58; matrix products, arithmetic and copies ran while one was open for 19% -> 19% of each run, Pallas kernels for 17% -> 17%
where the time goes in v4:
time: 590 us; the launch traced here: 582 us
  waiting for transfers between devices  197 us (33%)
  starting transfers between devices  118 us (20%)
  Pallas kernels  99.6 us (17%)
  matrix products  83.5 us (14%)
  other arithmetic  47.5 us (8%)
  local copies, waits for them, and re-layouts  33 us (6%)
    ppermute x32, waiting for transfers between devices, forward(): return lax.ppermute(array, 'wide', self.ahead)  93.2 us
    dot_general x25, matrix products, dot_nt(): lax.dot_general(a, b, (((1,), (1,)), ((), ())), preferred_element_type=jn...  49 us
    ppermute x32, waiting for transfers between devices, backward(): return lax.ppermute(array, 'wide', self.behind)  48.5 us
    ppermute x14, waiting for transfers between devices, swapped(): return lax.ppermute(part, 'narrow', [(0, 1), (1, 0)])  43.6 us
    ppermute x32, starting transfers between devices, forward(): return lax.ppermute(array, 'wide', self.ahead)  39.5 us
    dot_general x31, matrix products, dot_nn(): lax.dot_general(a, b, (((1,), (0,)), ((), ())), preferred_element_type=jn...  34.5 us
    ppermute x32, starting transfers between devices, backward(): return lax.ppermute(array, 'wide', self.behind)  33.2 us
    pallas_call x4, Pallas kernels, weight_grads(): pl.pallas_call(functools.partial(grads_kernel, len(lefts), len(rights)),...  32.2 us
  transfers between devices with their start and end apart: 140, of which 58 were waited for; matrix products, arithmetic and copies ran while one was open for 19% of the time, Pallas kernels for 17%

profile of v4, /device:TPU:0, one launch (start us, length us, event | category | flops | bytes accessed | tf_op | source)
XLA Modules:
  0.0 582.1 jit_solution(5518811595057998501)
XLA Ops:
  2.7 2.1 constant_dynamic-update-slice_fusion.17
  4.8 2.9 collective-permute-start.2
  12.6 6.5 %all-to-all-start = ((bf16[16,64,384]{2,1,0:T(8,128)(2,1)}), bf16[16,64,384]{2,1,0:T(8,128)(2,1)}, u32[]{:S(2)}, u32[]{:S(2)}) async-start(bf16[16,64,384]{2,1,0:T(8,128)(2,1)} %slice_select_fusion), calls=%async_computation | async-start | bytes 1572864 | tf_op jit(solution)/shard_map/all_to_all | solution.py:720
  21.8 4.7 fusion.142
  33.7 10.6 %collective-permute-done.5.refs_11_ = bf16[128,2048]{1,0:T(8,128)(2,1)} collective-permute-done((bf16[128,2048]{1,0:T(8,128)(2,1)}, bf16[128,2048]{1,0:T(8,128)(2,1)}, u32[]{:S(2)}, u32[]{:S(2)}) %collective-permute-start.5) | collective-permute-done | bytes 524320 | tf_op jit(solution)/shard_map/ppermute | solution.py:516
  46.2 5.8 collective-permute-start.9
  60.6 2.6 collective-permute-done.9.refs_15_
  63.3 3.2 collective-permute-done.10.refs_16_
  84.4 9.2 %fusion.264.lin_ref = f32[2048,384]{1,0:T(8,128)} fusion(bf16[2048,2048]{1,0:T(8,128)(2,1)} %constant_dynamic-update-slice_fusion, bf16[2048,384]{1,0:T(8,128)(2,1)S(1)} %bitcast.109), kind=kOutput, calls=%fused_computation.370 | convolution fusion | flops 3221225472 | bytes 13107200 | tf_op jit(solution)/shard_map/dot_general | solution.py:21
  97.2 16.0 %attention_forward.1 = (bf16[2048,128]{1,0:T(8,128)(2,1)}, bf16[2048,128]{1,0:T(8,128)(2,1)}, bf16[2048,128]{1,0:T(8,128)(2,1)}, bf16[2048,128]{1,0:T(8,128)(2,1)}, f32[8,2048]{1,0:T(8,128)}) custom-call(s32[16]{0:T(128)} %dynamic-slice_bitcast_fusion.slot_ref, s32[1]{0:T(128)} %copy.65.length_ref, f32[2048,384]{1,0:T(8,128)} %fusion.264.lin_ref, ...), custom_call_target="tpu_custom_call" | custom-call | flops 2147483648 | bytes 6291456 | tf_op jit(solution)/shard_map/attention_forward/pallas_call | solution.py:129
  121.8 9.6 %collective-permute-done.23.refs_11_ = bf16[128,2048]{1,0:T(8,128)(2,1)S(1)} collective-permute-done((bf16[128,2048]{1,0:T(8,128)(2,1)}, bf16[128,2048]{1,0:T(8,128)(2,1)S(1)}, u32[]{:S(2)}, u32[]{:S(2)}) %collective-permute-start.23) | collective-permute-done | bytes 524320 | tf_op jit(solution)/shard_map/ppermute | solution.py:516
  132.9 3.2 collective-permute-done.22
  142.9 9.8 %collective-permute-done.26 = bf16[128,2048]{1,0:T(8,128)(2,1)S(1)} collective-permute-done((bf16[128,2048]{1,0:T(8,128)(2,1)S(1)}, bf16[128,2048]{1,0:T(8,128)(2,1)S(1)}, u32[]{:S(2)}, u32[]{:S(2)}) %collective-permute-start.26) | collective-permute-done | bytes 524320 | tf_op jit(solution)/shard_map/ppermute | solution.py:519
  153.0 9.1 %collective-permute-done.28.refs_15_ = bf16[128,2048]{1,0:T(8,128)(2,1)S(1)} collective-permute-done((bf16[128,2048]{1,0:T(8,128)(2,1)S(1)}, bf16[128,2048]{1,0:T(8,128)(2,1)S(1)}, u32[]{:S(2)}, u32[]{:S(2)}) %collective-permute-start.28) | collective-permute-done | bytes 524320 | tf_op jit(solution)/shard_map/ppermute | solution.py:516
  167.4 13.4 %collective-permute-done.34.refs_20_ = bf16[64,2048]{1,0:T(8,128)(2,1)S(1)} collective-permute-done((bf16[64,2048]{1,0:T(8,128)(2,1)S(1)}, bf16[64,2048]{1,0:T(8,128)(2,1)S(1)}, u32[]{:S(2)}, u32[]{:S(2)}) %collective-permute-start.34) | collective-permute-done | bytes 262176 | tf_op jit(solution)/shard_map/ppermute | solution.py:519
  183.5 8.0 %collective-permute-done.37 = bf16[128,2048]{1,0:T(8,128)(2,1)S(1)} collective-permute-done((bf16[128,2048]{1,0:T(8,128)(2,1)S(1)}, bf16[128,2048]{1,0:T(8,128)(2,1)S(1)}, u32[]{:S(2)}, u32[]{:S(2)}) %collective-permute-start.37) | collective-permute-done | bytes 524320 | tf_op jit(solution)/shard_map/ppermute | solution.py:516
  201.3 7.6 %collective-permute-done.42.refs_8_ = bf16[128,2048]{1,0:T(8,128)(2,1)S(1)} collective-permute-done((bf16[128,2048]{1,0:T(8,128)(2,1)S(1)}, bf16[128,2048]{1,0:T(8,128)(2,1)S(1)}, u32[]{:S(2)}, u32[]{:S(2)}) %collective-permute-start.42) | collective-permute-done | bytes 524320 | tf_op jit(solution)/shard_map/ppermute | solution.py:519
  212.9 2.4 fusion.1
  215.4 4.0 multiply_convert_fusion.7
  220.5 3.9 collective-permute-done.45.refs_11_
  228.8 2.4 fusion.17
  231.2 3.9 multiply_convert_fusion.4
  235.3 4.9 collective-permute-done.51.refs_15_
  244.7 2.4 fusion.33
  247.1 3.9 multiply_convert_fusion.1
  265.7 4.8 collective-permute-done.67
  273.3 2.2 convolution_convert_fusion.10
  277.9 8.7 %weight_grads.4 = (bf16[128,2048]{1,0:T(8,128)(2,1)}, bf16[128,2048]{1,0:T(8,128)(2,1)}, bf16[256,2048]{1,0:T(8,128)(2,1)}) custom-call(bf16[256,512]{1,0:T(8,128)(2,1)} %get-tuple-element.508.refs_0_, bf16[512,512]{1,0:T(8,128)(2,1)} %get-tuple-element.493.refs_1_, bf16[512,512]{1,0:T(8,128)(2,1)} %get-tuple-element.458.refs_2_, ...), custom_call_target="tpu_custom_call" | custom-call | flops 1024 | bytes 1024 | tf_op jit(solution)/shard_map/weight_grads/pallas_call | solution.py:360
  286.7 2.6 convert_add_fusion.7
  294.3 3.5 collective-permute-start.75
  301.2 9.2 %collective-permute-done.75.refs_3_ = bf16[128,2048]{1,0:T(8,128)(2,1)S(1)} collective-permute-done((bf16[128,2048]{1,0:T(8,128)(2,1)S(1)}, bf16[128,2048]{1,0:T(8,128)(2,1)S(1)}, u32[]{:S(2)}, u32[]{:S(2)}) %collective-permute-start.75) | collective-permute-done | bytes 524320 | tf_op jit(solution)/shard_map/ppermute | solution.py:649
  317.0 11.0 %collective-permute-done.79.refs_4_ = bf16[128,2048]{1,0:T(8,128)(2,1)S(1)} collective-permute-done((bf16[128,2048]{1,0:T(8,128)(2,1)S(1)}, bf16[128,2048]{1,0:T(8,128)(2,1)S(1)}, u32[]{:S(2)}, u32[]{:S(2)}) %collective-permute-start.79) | collective-permute-done | bytes 524320 | tf_op jit(solution)/shard_map/ppermute | solution.py:649
  339.1 8.8 %weight_grads.5 = (bf16[256,2048]{1,0:T(8,128)(2,1)}, bf16[256,2048]{1,0:T(8,128)(2,1)}) custom-call(bf16[256,1024]{1,0:T(8,128)(2,1)} %pad_maximum_fusion.6.refs_0_, bf16[512,1024]{1,0:T(8,128)(2,1)} %pad_maximum_fusion.1.refs_1_, bf16[512,1024]{1,0:T(8,128)(2,1)} %copy-done.9, bf16[512,1024]{1,0:T(8,128)(2,1)} %copy-done.10, bf16[256,1024]{1,0:T(8,128)(2,1)} %copy-done.12, ...), custom_call_target="tpu_custom_call" | custom-call | flops 1024 | bytes 1024 | tf_op jit(solution)/shard_map/weight_grads/pallas_call | solution.py:360
  352.4 4.3 collective-permute-done.84
  356.7 3.5 collective-permute-done.86.refs_5_
  368.9 8.8 %weight_grads.6 = (bf16[64,2048]{1,0:T(8,128)(2,1)}, bf16[256,2048]{1,0:T(8,128)(2,1)}, bf16[128,2048]{1,0:T(8,128)(2,1)}, bf16[64,2048]{1,0:T(8,128)(2,1)}) custom-call(bf16[256,1024]{1,0:T(8,128)(2,1)} %pad_maximum_fusion.6.refs_0_, bf16[512,1024]{1,0:T(8,128)(2,1)} %pad_maximum_fusion.1.refs_1_, bf16[512,1024]{1,0:T(8,128)(2,1)} %copy-done.9, ...), custom_call_target="tpu_custom_call" | custom-call | flops 1024 | bytes 1024 | tf_op jit(solution)/shard_map/weight_grads/pallas_call | solution.py:360
  381.2 10.1 %collective-permute-done.87.refs_7_ = bf16[128,2048]{1,0:T(8,128)(2,1)} collective-permute-done((bf16[128,2048]{1,0:T(8,128)(2,1)}, bf16[128,2048]{1,0:T(8,128)(2,1)}, u32[]{:S(2)}, u32[]{:S(2)}) %collective-permute-start.87) | collective-permute-done | bytes 524320 | tf_op jit(solution)/shard_map/ppermute | solution.py:516
  391.4 2.6 add_convert_fusion.9
  396.0 2.9 collective-permute-done.103.refs_2_
  404.0 2.6 fusion.85
  406.6 4.8 sum_pieces.4
  412.1 2.9 collective-permute-done.96
  415.9 9.5 %collective-permute-done.93.refs_11_ = bf16[128,2048]{1,0:T(8,128)(2,1)S(1)} collective-permute-done((bf16[128,2048]{1,0:T(8,128)(2,1)}, bf16[128,2048]{1,0:T(8,128)(2,1)S(1)}, u32[]{:S(2)}, u32[]{:S(2)}) %collective-permute-start.93) | collective-permute-done | bytes 524320 | tf_op jit(solution)/shard_map/ppermute | solution.py:516
  426.6 2.5 add_convert_fusion.7
  431.9 5.4 collective-permute-done.112.refs_4_
  437.4 2.7 fusion.88
  448.6 21.2 %attention_backward.1 = (bf16[256,384]{1,0:T(8,128)(2,1)}, bf16[512,384]{1,0:T(8,128)(2,1)}, bf16[512,384]{1,0:T(8,128)(2,1)}, bf16[512,384]{1,0:T(8,128)(2,1)}, bf16[256,384]{1,0:T(8,128)(2,1)}) custom-call(s32[16]{0:T(128)} %dynamic-slice_bitcast_fusion.slot_ref, s32[1]{0:T(128)} %copy.65.length_ref, bf16[2048,128]{1,0:T(8,128)(2,1)} %get-tuple-element.511.query_ref, ...), custom_call_target="tpu_custom_call" | custom-call | flops 5368709120 | bytes 9437184 | tf_op jit(solution)/shard_map/attention_backward/pallas_call | solution.py:250
  476.0 3.3 collective-permute-start.119
  481.4 9.2 %heads_grads.1 = (bf16[16,64,384]{2,1,0:T(8,128)(2,1)}, bf16[16,64,384]{2,1,0:T(8,128)(2,1)}, f32[1,2048]{1,0:T(1,128)}) custom-call(s32[1]{0:T(128)} %bitcast.10.upper_ref.side_ref, bf16[2048,384]{1,0:T(8,128)(2,1)} %bitcast.110, bf16[256,384]{1,0:T(8,128)(2,1)} %get-tuple-element.608.refs_0_, bf16[512,384]{1,0:T(8,128)(2,1)} %get-tuple-element.601.refs_1_, ...), custom_call_target="tpu_custom_call" | custom-call | flops 1024 | bytes 1024 | tf_op jit(solution)/shard_map/heads_grads/pallas_call | solution.py:401
  501.7 4.7 sum_pieces.5
  506.4 5.9 %weight_grads.7.refs_0_ = bf16[128,2048]{1,0:T(8,128)(2,1)} custom-call(bf16[2048,128]{1,0:T(8,128)(2,1)} %get-tuple-element.574.att_ref.refs_0_, bf16[128,2048]{1,0:T(8,128)(2,1)} %copy-done.27, bf16[128,2048]{1,0:T(8,128)(2,1)} %copy-done.82, bf16[128,2048]{1,0:T(8,128)(2,1)} %collective-permute-done.80.refs_3_, ...), custom_call_target="tpu_custom_call" | custom-call | flops 1024 | bytes 1024 | tf_op jit(solution)/shard_map/weight_grads/pallas_call | solution.py:360
  514.3 2.6 collective-permute-done.124
  516.9 2.3 add_convert_fusion.4
  523.0 2.2 add_convert_fusion
  525.2 4.6 all-to-all-start.1
  532.7 2.4 convert_add_fusion
  535.2 5.0 collective-permute-done.129.refs_7_
  540.2 2.6 add_convert_fusion.2
  547.3 2.4 convert_add_fusion.12
  551.4 4.7 sum_pieces.6
  557.2 2.1 convert_add_fusion.11
  567.9 3.4 sum_pieces.7
  571.9 5.8 collective-permute-done.137.refs_1_
  578.6 3.2 assemble.1
  (620 shorter events, 225.1 us)
Async XLA Ops:
  4.8 21.7 %collective-permute-start.2 = (bf16[128,2048]{1,0:T(8,128)(2,1)S(1)}, bf16[128,2048]{1,0:T(8,128)(2,1)}, u32[]{:S(2)}, u32[]{:S(2)}) collective-permute-start(bf16[128,2048]{1,0:T(8,128)(2,1)S(1)} %get-tuple-element.544.refs_5_), channel_id=1, source_target_pairs={{4,0},{5,1},{8,4},{9,5},{12,8},{13,9},{14,12},{15,13},{10,14},{11,... | collective-permute-start | bytes 1572872 | tf_op jit(solution)/shard_map/ppermute | solution.py:519
  7.7 18.8 %collective-permute-start.1 = (bf16[128,2048]{1,0:T(8,128)(2,1)S(1)}, bf16[128,2048]{1,0:T(8,128)(2,1)}, u32[]{:S(2)}, u32[]{:S(2)}) collective-permute-start(bf16[128,2048]{1,0:T(8,128)(2,1)S(1)} %get-tuple-element.544.refs_5_), channel_id=1, source_target_pairs={{0,4},{1,5},{4,8},{5,9},{8,12},{9,13},{12,14},{13,15},{14,10},{15,... | collective-permute-start | bytes 1572872 | tf_op jit(solution)/shard_map/ppermute | solution.py:516
  7.9 21.1 %collective-permute-start = (bf16[128,2048]{1,0:T(8,128)(2,1)S(1)}, bf16[128,2048]{1,0:T(8,128)(2,1)S(1)}, u32[]{:S(2)}, u32[]{:S(2)}) collective-permute-start(bf16[128,2048]{1,0:T(8,128)(2,1)S(1)} %get-tuple-element.544.refs_5_), channel_id=1, source_target_pairs={{0,1},{1,0},{2,3},{3,2},{4,5},{5,4},{6,7},{7,6},{8,9},{9,8},{10,11... | collective-permute-start | bytes 1572872 | tf_op jit(solution)/shard_map/ppermute | solution.py:522
  12.6 46.5 %all-to-all-start = ((bf16[16,64,384]{2,1,0:T(8,128)(2,1)}), bf16[16,64,384]{2,1,0:T(8,128)(2,1)}, u32[]{:S(2)}, u32[]{:S(2)}) async-start(bf16[16,64,384]{2,1,0:T(8,128)(2,1)} %slice_select_fusion), calls=%async_computation | async-start | bytes 1572864 | tf_op jit(solution)/shard_map/all_to_all | solution.py:720
  26.5 17.8 %collective-permute-start.5 = (bf16[128,2048]{1,0:T(8,128)(2,1)}, bf16[128,2048]{1,0:T(8,128)(2,1)}, u32[]{:S(2)}, u32[]{:S(2)}) collective-permute-start(bf16[128,2048]{1,0:T(8,128)(2,1)} %collective-permute-done.1.refs_7_), channel_id=1, source_target_pairs={{0,4},{1,5},{4,8},{5,9},{8,12},{9,13},{12,14},{13,15},{14,10},{15,... | collective-permute-start | bytes 1572872 | tf_op jit(solution)/shard_map/ppermute | solution.py:516
  28.5 23.5 %collective-permute-start.3 = (bf16[128,2048]{1,0:T(8,128)(2,1)}, bf16[128,2048]{1,0:T(8,128)(2,1)S(1)}, u32[]{:S(2)}, u32[]{:S(2)}) collective-permute-start(bf16[128,2048]{1,0:T(8,128)(2,1)} %collective-permute-done.1.refs_7_), channel_id=1, source_target_pairs={{0,1},{1,0},{2,3},{3,2},{4,5},{5,4},{6,7},{7,6},{8,9},{9,8},{10,11... | collective-permute-start | bytes 1572872 | tf_op jit(solution)/shard_map/ppermute | solution.py:522
  28.5 17.7 %collective-permute-start.6 = (bf16[128,2048]{1,0:T(8,128)(2,1)}, bf16[128,2048]{1,0:T(8,128)(2,1)}, u32[]{:S(2)}, u32[]{:S(2)}) collective-permute-start(bf16[128,2048]{1,0:T(8,128)(2,1)} %collective-permute-done.2.refs_8_), channel_id=1, source_target_pairs={{4,0},{5,1},{8,4},{9,5},{12,8},{13,9},{14,12},{15,13},{10,14},{11,... | collective-permute-start | bytes 1572872 | tf_op jit(solution)/shard_map/ppermute | solution.py:519
  28.7 24.9 %collective-permute-start.4 = (bf16[128,2048]{1,0:T(8,128)(2,1)}, bf16[128,2048]{1,0:T(8,128)(2,1)S(1)}, u32[]{:S(2)}, u32[]{:S(2)}) collective-permute-start(bf16[128,2048]{1,0:T(8,128)(2,1)} %collective-permute-done.2.refs_8_), channel_id=1, source_target_pairs={{0,1},{1,0},{2,3},{3,2},{4,5},{5,4},{6,7},{7,6},{8,9},{9,8},{10,11... | collective-permute-start | bytes 1572872 | tf_op jit(solution)/shard_map/ppermute | solution.py:522
  46.2 17.1 %collective-permute-start.9 = (bf16[128,2048]{1,0:T(8,128)(2,1)}, bf16[128,2048]{1,0:T(8,128)(2,1)S(1)}, u32[]{:S(2)}, u32[]{:S(2)}) collective-permute-start(bf16[128,2048]{1,0:T(8,128)(2,1)} %collective-permute-done.5.refs_11_), channel_id=1, source_target_pairs={{0,4},{1,5},{4,8},{5,9},{8,12},{9,13},{12,14},{13,15},{14,10},{15,... | collective-permute-start | bytes 1572872 | tf_op jit(solution)/shard_map/ppermute | solution.py:516
  52.0 15.2 %collective-permute-start.7 = (bf16[128,2048]{1,0:T(8,128)(2,1)}, bf16[128,2048]{1,0:T(8,128)(2,1)}, u32[]{:S(2)}, u32[]{:S(2)}) collective-permute-start(bf16[128,2048]{1,0:T(8,128)(2,1)} %collective-permute-done.5.refs_11_), channel_id=1, source_target_pairs={{0,1},{1,0},{2,3},{3,2},{4,5},{5,4},{6,7},{7,6},{8,9},{9,8},{10,11... | collective-permute-start | bytes 1572872 | tf_op jit(solution)/shard_map/ppermute | solution.py:522
  52.0 17.5 %collective-permute-start.8 = (bf16[128,2048]{1,0:T(8,128)(2,1)}, bf16[128,2048]{1,0:T(8,128)(2,1)}, u32[]{:S(2)}, u32[]{:S(2)}) collective-permute-start(bf16[128,2048]{1,0:T(8,128)(2,1)} %collective-permute-done.6.refs_12_), channel_id=1, source_target_pairs={{0,1},{1,0},{2,3},{3,2},{4,5},{5,4},{6,7},{7,6},{8,9},{9,8},{10,11... | collective-permute-start | bytes 1572872 | tf_op jit(solution)/shard_map/ppermute | solution.py:522
  59.1 23.7 %collective-permute-start.17 = (bf16[16,64,384]{2,1,0:T(8,128)(2,1)}, bf16[16,64,384]{2,1,0:T(8,128)(2,1)S(1)}, u32[]{:S(2)}, u32[]{:S(2)}) collective-permute-start(bf16[16,64,384]{2,1,0:T(8,128)(2,1)} %all-to-all-done), channel_id=1, source_target_pairs={{0,16},{16,0},{1,17},{17,1},{2,18},{18,2},{3,19},{19,3},{4,20},{20... | collective-permute-start | bytes 2359304 | tf_op jit(solution)/shard_map/ppermute | solution.py:649
  93.5 19.7 %collective-permute-start.19 = (bf16[128,2048]{1,0:T(8,128)(2,1)S(1)}, bf16[128,2048]{1,0:T(8,128)(2,1)S(1)}, u32[]{:S(2)}, u32[]{:S(2)}) collective-permute-start(bf16[128,2048]{1,0:T(8,128)(2,1)S(1)} %copy-done.41), channel_id=1, source_target_pairs={{4,0},{5,1},{8,4},{9,5},{12,8},{13,9},{14,12},{15,13},{10,14},{11,... | collective-permute-start | bytes 1572872 | tf_op jit(solution)/shard_map/ppermute | solution.py:519
  95.0 18.3 %collective-permute-start.18 = (bf16[128,2048]{1,0:T(8,128)(2,1)S(1)}, bf16[128,2048]{1,0:T(8,128)(2,1)}, u32[]{:S(2)}, u32[]{:S(2)}) collective-permute-start(bf16[128,2048]{1,0:T(8,128)(2,1)S(1)} %copy-done.41), channel_id=1, source_target_pairs={{0,4},{1,5},{4,8},{5,9},{8,12},{9,13},{12,14},{13,15},{14,10},{15,... | collective-permute-start | bytes 1572872 | tf_op jit(solution)/shard_map/ppermute | solution.py:516
  116.4 15.0 %collective-permute-start.23 = (bf16[128,2048]{1,0:T(8,128)(2,1)}, bf16[128,2048]{1,0:T(8,128)(2,1)S(1)}, u32[]{:S(2)}, u32[]{:S(2)}) collective-permute-start(bf16[128,2048]{1,0:T(8,128)(2,1)} %collective-permute-done.18.refs_7_), channel_id=1, source_target_pairs={{0,4},{1,5},{4,8},{5,9},{8,12},{9,13},{12,14},{13,15},{14,10},{15,... | collective-permute-start | bytes 1572872 | tf_op jit(solution)/shard_map/ppermute | solution.py:516
  118.1 14.8 %collective-permute-start.24 = (bf16[128,2048]{1,0:T(8,128)(2,1)S(1)}, bf16[128,2048]{1,0:T(8,128)(2,1)S(1)}, u32[]{:S(2)}, u32[]{:S(2)}) collective-permute-start(bf16[128,2048]{1,0:T(8,128)(2,1)S(1)} %collective-permute-done.19.refs_8_), channel_id=1, source_target_pairs={{4,0},{5,1},{8,4},{9,5},{12,8},{13,9},{14,12},{15,13},{10,14},{11,... | collective-permute-start | bytes 1572872 | tf_op jit(solution)/shard_map/ppermute | solution.py:519
  118.9 23.5 %collective-permute-start.30 = (bf16[256,2048]{1,0:T(8,128)(2,1)S(1)}, bf16[256,2048]{1,0:T(8,128)(2,1)S(1)}, u32[]{:S(2)}, u32[]{:S(2)}) collective-permute-start(bf16[256,2048]{1,0:T(8,128)(2,1)S(1)} %convolution_convert_fusion.7), channel_id=1, source_target_pairs={{0,1},{1,0},{2,3},{3,2},{4,5},{5,4},{6,7},{7,6},{8,9},{9,8},{10,11... | collective-permute-start | bytes 3145736 | tf_op jit(solution)/shard_map/ppermute | solution.py:522
  119.3 16.8 %collective-permute-start.22 = (bf16[64,2048]{1,0:T(8,128)(2,1)S(1)}, bf16[64,2048]{1,0:T(8,128)(2,1)S(1)}, u32[]{:S(2)}, u32[]{:S(2)}) collective-permute-start(bf16[64,2048]{1,0:T(8,128)(2,1)S(1)} %get-tuple-element.702), channel_id=1, source_target_pairs={{0,4},{1,5},{4,8},{5,9},{8,12},{9,13},{12,14},{13,15},{14,10},{15,... | collective-permute-start | bytes 786440 | tf_op jit(solution)/shard_map/ppermute | solution.py:516
  121.1 16.3 %collective-permute-start.21 = (bf16[64,2048]{1,0:T(8,128)(2,1)S(1)}, bf16[64,2048]{1,0:T(8,128)(2,1)S(1)}, u32[]{:S(2)}, u32[]{:S(2)}) collective-permute-start(bf16[64,2048]{1,0:T(8,128)(2,1)S(1)} %get-tuple-element.703), channel_id=1, source_target_pairs={{4,0},{5,1},{8,4},{9,5},{12,8},{13,9},{14,12},{15,13},{10,14},{11,... | collective-permute-start | bytes 786440 | tf_op jit(solution)/shard_map/ppermute | solution.py:519
  137.7 14.9 %collective-permute-start.26 = (bf16[128,2048]{1,0:T(8,128)(2,1)S(1)}, bf16[128,2048]{1,0:T(8,128)(2,1)S(1)}, u32[]{:S(2)}, u32[]{:S(2)}) collective-permute-start(bf16[128,2048]{1,0:T(8,128)(2,1)S(1)} %pad_maximum_fusion.4), channel_id=1, source_target_pairs={{4,0},{5,1},{8,4},{9,5},{12,8},{13,9},{14,12},{15,13},{10,14},{11,... | collective-permute-start | bytes 1572872 | tf_op jit(solution)/shard_map/ppermute | solution.py:519
  138.1 14.9 %collective-permute-start.27 = (bf16[128,2048]{1,0:T(8,128)(2,1)S(1)}, bf16[128,2048]{1,0:T(8,128)(2,1)S(1)}, u32[]{:S(2)}, u32[]{:S(2)}) collective-permute-start(bf16[128,2048]{1,0:T(8,128)(2,1)S(1)} %pad_maximum_fusion.5), channel_id=1, source_target_pairs={{0,4},{1,5},{4,8},{5,9},{8,12},{9,13},{12,14},{13,15},{14,10},{15,... | collective-permute-start | bytes 1572872 | tf_op jit(solution)/shard_map/ppermute | solution.py:516
  139.9 22.2 %collective-permute-start.28 = (bf16[128,2048]{1,0:T(8,128)(2,1)S(1)}, bf16[128,2048]{1,0:T(8,128)(2,1)S(1)}, u32[]{:S(2)}, u32[]{:S(2)}) collective-permute-start(bf16[128,2048]{1,0:T(8,128)(2,1)S(1)} %collective-permute-done.23.refs_11_), channel_id=1, source_target_pairs={{0,4},{1,5},{4,8},{5,9},{8,12},{9,13},{12,14},{13,15},{14,10},{15,... | collective-permute-start | bytes 1572872 | tf_op jit(solution)/shard_map/ppermute | solution.py:516
  140.5 21.6 %collective-permute-start.29 = (bf16[128,2048]{1,0:T(8,128)(2,1)S(1)}, bf16[128,2048]{1,0:T(8,128)(2,1)S(1)}, u32[]{:S(2)}, u32[]{:S(2)}) collective-permute-start(bf16[128,2048]{1,0:T(8,128)(2,1)S(1)} %collective-permute-done.24.refs_12_), channel_id=1, source_target_pairs={{4,0},{5,1},{8,4},{9,5},{12,8},{13,9},{14,12},{15,13},{10,14},{11,... | collective-permute-start | bytes 1572872 | tf_op jit(solution)/shard_map/ppermute | solution.py:519
  142.3 24.4 %collective-permute-start.35 = (bf16[256,2048]{1,0:T(8,128)(2,1)S(1)}, bf16[256,2048]{1,0:T(8,128)(2,1)S(1)}, u32[]{:S(2)}, u32[]{:S(2)}) collective-permute-start(bf16[256,2048]{1,0:T(8,128)(2,1)S(1)} %convolution_convert_fusion.6), channel_id=1, source_target_pairs={{0,1},{1,0},{2,3},{3,2},{4,5},{5,4},{6,7},{7,6},{8,9},{9,8},{10,11... | collective-permute-start | bytes 3145736 | tf_op jit(solution)/shard_map/ppermute | solution.py:522
  162.4 18.4 %collective-permute-start.32 = (bf16[128,2048]{1,0:T(8,128)(2,1)S(1)}, bf16[128,2048]{1,0:T(8,128)(2,1)S(1)}, u32[]{:S(2)}, u32[]{:S(2)}) collective-permute-start(bf16[128,2048]{1,0:T(8,128)(2,1)S(1)} %get-tuple-element.676), channel_id=1, source_target_pairs={{0,4},{1,5},{4,8},{5,9},{8,12},{9,13},{12,14},{13,15},{14,10},{15,... | collective-permute-start | bytes 1572872 | tf_op jit(solution)/shard_map/ppermute | solution.py:516
  163.9 16.9 %collective-permute-start.31 = (bf16[128,2048]{1,0:T(8,128)(2,1)S(1)}, bf16[128,2048]{1,0:T(8,128)(2,1)S(1)}, u32[]{:S(2)}, u32[]{:S(2)}) collective-permute-start(bf16[128,2048]{1,0:T(8,128)(2,1)S(1)} %get-tuple-element.677), channel_id=1, source_target_pairs={{4,0},{5,1},{8,4},{9,5},{12,8},{13,9},{14,12},{15,13},{10,14},{11,... | collective-permute-start | bytes 1572872 | tf_op jit(solution)/shard_map/ppermute | solution.py:519
  164.8 18.5 %collective-permute-start.38 = (bf16[128,2048]{1,0:T(8,128)(2,1)S(1)}, bf16[128,2048]{1,0:T(8,128)(2,1)S(1)}, u32[]{:S(2)}, u32[]{:S(2)}) collective-permute-start(bf16[128,2048]{1,0:T(8,128)(2,1)S(1)} %convolution_convert_fusion.18), channel_id=1, source_target_pairs={{0,1},{1,0},{2,3},{3,2},{4,5},{5,4},{6,7},{7,6},{8,9},{9,8},{10,11... | collective-permute-start | bytes 1572872 | tf_op jit(solution)/shard_map/ppermute | solution.py:522
  164.9 15.9 %collective-permute-start.34 = (bf16[64,2048]{1,0:T(8,128)(2,1)S(1)}, bf16[64,2048]{1,0:T(8,128)(2,1)S(1)}, u32[]{:S(2)}, u32[]{:S(2)}) collective-permute-start(bf16[64,2048]{1,0:T(8,128)(2,1)S(1)} %slice.380), channel_id=1, source_target_pairs={{4,0},{5,1},{8,4},{9,5},{12,8},{13,9},{14,12},{15,13},{10,14},{11,... | collective-permute-start | bytes 786440 | tf_op jit(solution)/shard_map/ppermute | solution.py:519
  275.5 14.7 %collective-permute-start.69 = (bf16[128,2048]{1,0:T(8,128)(2,1)}, bf16[128,2048]{1,0:T(8,128)(2,1)}, u32[]{:S(2)}, u32[]{:S(2)}) collective-permute-start(bf16[128,2048]{1,0:T(8,128)(2,1)} %pad_maximum_fusion.8), channel_id=1, source_target_pairs={{4,0},{5,1},{8,4},{9,5},{12,8},{13,9},{14,12},{15,13},{10,14},{11,... | collective-permute-start | bytes 1572872 | tf_op jit(solution)/shard_map/ppermute | solution.py:519
  276.5 14.8 %collective-permute-start.70 = (bf16[128,2048]{1,0:T(8,128)(2,1)}, bf16[128,2048]{1,0:T(8,128)(2,1)}, u32[]{:S(2)}, u32[]{:S(2)}) collective-permute-start(bf16[128,2048]{1,0:T(8,128)(2,1)} %pad_maximum_fusion.9), channel_id=1, source_target_pairs={{0,4},{1,5},{4,8},{5,9},{8,12},{9,13},{12,14},{13,15},{14,10},{15,... | collective-permute-start | bytes 1572872 | tf_op jit(solution)/shard_map/ppermute | solution.py:516
  294.3 16.1 %collective-permute-start.75 = (bf16[128,2048]{1,0:T(8,128)(2,1)S(1)}, bf16[128,2048]{1,0:T(8,128)(2,1)S(1)}, u32[]{:S(2)}, u32[]{:S(2)}) collective-permute-start(bf16[128,2048]{1,0:T(8,128)(2,1)S(1)} %copy-done.80), channel_id=1, source_target_pairs={{0,16},{16,0},{1,17},{17,1},{2,18},{18,2},{3,19},{19,3},{4,20},{20... | collective-permute-start | bytes 1572872 | tf_op jit(solution)/shard_map/ppermute | solution.py:649
  334.5 25.8 %collective-permute-start.86 = (bf16[256,2048]{1,0:T(8,128)(2,1)}, bf16[256,2048]{1,0:T(8,128)(2,1)}, u32[]{:S(2)}, u32[]{:S(2)}) collective-permute-start(bf16[256,2048]{1,0:T(8,128)(2,1)} %get-tuple-element.501.refs_2_), channel_id=1, source_target_pairs={{0,16},{16,0},{1,17},{17,1},{2,18},{18,2},{3,19},{19,3},{4,20},{20... | collective-permute-start | bytes 3145736 | tf_op jit(solution)/shard_map/ppermute | solution.py:649
  337.4 14.9 %collective-permute-start.80 = (bf16[128,2048]{1,0:T(8,128)(2,1)S(1)}, bf16[128,2048]{1,0:T(8,128)(2,1)}, u32[]{:S(2)}, u32[]{:S(2)}) collective-permute-start(bf16[128,2048]{1,0:T(8,128)(2,1)S(1)} %get-tuple-element.575.refs_1_), channel_id=1, source_target_pairs={{0,4},{1,5},{4,8},{5,9},{8,12},{9,13},{12,14},{13,15},{14,10},{15,... | collective-permute-start | bytes 1572872 | tf_op jit(solution)/shard_map/ppermute | solution.py:516
  338.3 18.4 %collective-permute-start.84 = (bf16[64,2048]{1,0:T(8,128)(2,1)S(1)}, bf16[64,2048]{1,0:T(8,128)(2,1)S(1)}, u32[]{:S(2)}, u32[]{:S(2)}) collective-permute-start(bf16[64,2048]{1,0:T(8,128)(2,1)S(1)} %get-tuple-element.698), channel_id=1, source_target_pairs={{0,4},{1,5},{4,8},{5,9},{8,12},{9,13},{12,14},{13,15},{14,10},{15,... | collective-permute-start | bytes 786440 | tf_op jit(solution)/shard_map/ppermute | solution.py:516
  363.1 28.3 %collective-permute-start.92 = (bf16[256,2048]{1,0:T(8,128)(2,1)S(1)}, bf16[256,2048]{1,0:T(8,128)(2,1)}, u32[]{:S(2)}, u32[]{:S(2)}) collective-permute-start(bf16[256,2048]{1,0:T(8,128)(2,1)S(1)} %copy-done.67), channel_id=1, source_target_pairs={{0,16},{16,0},{1,17},{17,1},{2,18},{18,2},{3,19},{19,3},{4,20},{20... | collective-permute-start | bytes 3145736 | tf_op jit(solution)/shard_map/ppermute | solution.py:649
  364.9 15.1 %collective-permute-start.89 = (bf16[128,2048]{1,0:T(8,128)(2,1)}, bf16[128,2048]{1,0:T(8,128)(2,1)}, u32[]{:S(2)}, u32[]{:S(2)}) collective-permute-start(bf16[128,2048]{1,0:T(8,128)(2,1)} %pad_maximum_fusion.10), channel_id=1, source_target_pairs={{4,0},{5,1},{8,4},{9,5},{12,8},{13,9},{14,12},{15,13},{10,14},{11,... | collective-permute-start | bytes 1572872 | tf_op jit(solution)/shard_map/ppermute | solution.py:519
  366.1 15.1 %collective-permute-start.90 = (bf16[128,2048]{1,0:T(8,128)(2,1)}, bf16[128,2048]{1,0:T(8,128)(2,1)}, u32[]{:S(2)}, u32[]{:S(2)}) collective-permute-start(bf16[128,2048]{1,0:T(8,128)(2,1)} %pad_maximum_fusion.11), channel_id=1, source_target_pairs={{0,4},{1,5},{4,8},{5,9},{8,12},{9,13},{12,14},{13,15},{14,10},{15,... | collective-permute-start | bytes 1572872 | tf_op jit(solution)/shard_map/ppermute | solution.py:516
  366.9 24.4 %collective-permute-start.87 = (bf16[128,2048]{1,0:T(8,128)(2,1)}, bf16[128,2048]{1,0:T(8,128)(2,1)}, u32[]{:S(2)}, u32[]{:S(2)}) collective-permute-start(bf16[128,2048]{1,0:T(8,128)(2,1)} %collective-permute-done.80.refs_3_), channel_id=1, source_target_pairs={{0,4},{1,5},{4,8},{5,9},{8,12},{9,13},{12,14},{13,15},{14,10},{15,... | collective-permute-start | bytes 1572872 | tf_op jit(solution)/shard_map/ppermute | solution.py:516
  367.8 23.6 %collective-permute-start.88 = (bf16[128,2048]{1,0:T(8,128)(2,1)}, bf16[128,2048]{1,0:T(8,128)(2,1)}, u32[]{:S(2)}, u32[]{:S(2)}) collective-permute-start(bf16[128,2048]{1,0:T(8,128)(2,1)} %collective-permute-done.81.refs_4_), channel_id=1, source_target_pairs={{4,0},{5,1},{8,4},{9,5},{12,8},{13,9},{14,12},{15,13},{10,14},{11,... | collective-permute-start | bytes 1572872 | tf_op jit(solution)/shard_map/ppermute | solution.py:519
  395.7 30.2 %collective-permute-start.98 = (bf16[256,2048]{1,0:T(8,128)(2,1)S(1)}, bf16[256,2048]{1,0:T(8,128)(2,1)}, u32[]{:S(2)}, u32[]{:S(2)}) collective-permute-start(bf16[256,2048]{1,0:T(8,128)(2,1)S(1)} %copy-done.68), channel_id=1, source_target_pairs={{0,16},{16,0},{1,17},{17,1},{2,18},{18,2},{3,19},{19,3},{4,20},{20... | collective-permute-start | bytes 3145736 | tf_op jit(solution)/shard_map/ppermute | solution.py:649
  399.9 15.1 %collective-permute-start.96 = (bf16[128,2048]{1,0:T(8,128)(2,1)}, bf16[128,2048]{1,0:T(8,128)(2,1)}, u32[]{:S(2)}, u32[]{:S(2)}) collective-permute-start(bf16[128,2048]{1,0:T(8,128)(2,1)} %get-tuple-element.661), channel_id=1, source_target_pairs={{0,4},{1,5},{4,8},{5,9},{8,12},{9,13},{12,14},{13,15},{14,10},{15,... | collective-permute-start | bytes 1572872 | tf_op jit(solution)/shard_map/ppermute | solution.py:516
  400.8 15.1 %collective-permute-start.95 = (bf16[128,2048]{1,0:T(8,128)(2,1)}, bf16[128,2048]{1,0:T(8,128)(2,1)}, u32[]{:S(2)}, u32[]{:S(2)}) collective-permute-start(bf16[128,2048]{1,0:T(8,128)(2,1)} %get-tuple-element.662), channel_id=1, source_target_pairs={{4,0},{5,1},{8,4},{9,5},{12,8},{13,9},{14,12},{15,13},{10,14},{11,... | collective-permute-start | bytes 1572872 | tf_op jit(solution)/shard_map/ppermute | solution.py:519
  402.0 23.4 %collective-permute-start.93 = (bf16[128,2048]{1,0:T(8,128)(2,1)}, bf16[128,2048]{1,0:T(8,128)(2,1)S(1)}, u32[]{:S(2)}, u32[]{:S(2)}) collective-permute-start(bf16[128,2048]{1,0:T(8,128)(2,1)} %collective-permute-done.87.refs_7_), channel_id=1, source_target_pairs={{0,4},{1,5},{4,8},{5,9},{8,12},{9,13},{12,14},{13,15},{14,10},{15,... | collective-permute-start | bytes 1572872 | tf_op jit(solution)/shard_map/ppermute | solution.py:516
  402.8 23.1 %collective-permute-start.94 = (bf16[128,2048]{1,0:T(8,128)(2,1)}, bf16[128,2048]{1,0:T(8,128)(2,1)S(1)}, u32[]{:S(2)}, u32[]{:S(2)}) collective-permute-start(bf16[128,2048]{1,0:T(8,128)(2,1)} %collective-permute-done.88.refs_8_), channel_id=1, source_target_pairs={{4,0},{5,1},{8,4},{9,5},{12,8},{13,9},{14,12},{15,13},{10,14},{11,... | collective-permute-start | bytes 1572872 | tf_op jit(solution)/shard_map/ppermute | solution.py:519
  415.0 14.8 %collective-permute-start.106 = (bf16[128,2048]{1,0:T(8,128)(2,1)}, bf16[128,2048]{1,0:T(8,128)(2,1)S(1)}, u32[]{:S(2)}, u32[]{:S(2)}) collective-permute-start(bf16[128,2048]{1,0:T(8,128)(2,1)} %collective-permute-done.87.refs_7_), channel_id=1, source_target_pairs={{0,1},{1,0},{2,3},{3,2},{4,5},{5,4},{6,7},{7,6},{8,9},{9,8},{10,11... | collective-permute-start | bytes 1572872 | tf_op jit(solution)/shard_map/ppermute | solution.py:522
  415.9 15.2 %collective-permute-start.107 = (bf16[128,2048]{1,0:T(8,128)(2,1)}, bf16[128,2048]{1,0:T(8,128)(2,1)S(1)}, u32[]{:S(2)}, u32[]{:S(2)}) collective-permute-start(bf16[128,2048]{1,0:T(8,128)(2,1)} %collective-permute-done.88.refs_8_), channel_id=1, source_target_pairs={{0,1},{1,0},{2,3},{3,2},{4,5},{5,4},{6,7},{7,6},{8,9},{9,8},{10,11... | collective-permute-start | bytes 1572872 | tf_op jit(solution)/shard_map/ppermute | solution.py:522
  425.9 16.4 %collective-permute-start.108 = (bf16[128,2048]{1,0:T(8,128)(2,1)S(1)}, bf16[128,2048]{1,0:T(8,128)(2,1)S(1)}, u32[]{:S(2)}, u32[]{:S(2)}) collective-permute-start(bf16[128,2048]{1,0:T(8,128)(2,1)S(1)} %collective-permute-done.93.refs_11_), channel_id=1, source_target_pairs={{0,1},{1,0},{2,3},{3,2},{4,5},{5,4},{6,7},{7,6},{8,9},{9,8},{10,11... | collective-permute-start | bytes 1572872 | tf_op jit(solution)/shard_map/ppermute | solution.py:522
  426.0 16.7 %collective-permute-start.109 = (bf16[128,2048]{1,0:T(8,128)(2,1)S(1)}, bf16[128,2048]{1,0:T(8,128)(2,1)S(1)}, u32[]{:S(2)}, u32[]{:S(2)}) collective-permute-start(bf16[128,2048]{1,0:T(8,128)(2,1)S(1)} %collective-permute-done.94.refs_12_), channel_id=1, source_target_pairs={{0,1},{1,0},{2,3},{3,2},{4,5},{5,4},{6,7},{7,6},{8,9},{9,8},{10,11... | collective-permute-start | bytes 1572872 | tf_op jit(solution)/shard_map/ppermute | solution.py:522
  440.1 29.8 %collective-permute-start.100 = (bf16[128,2048]{1,0:T(8,128)(2,1)}, bf16[128,2048]{1,0:T(8,128)(2,1)}, u32[]{:S(2)}, u32[]{:S(2)}) collective-permute-start(bf16[128,2048]{1,0:T(8,128)(2,1)} %get-tuple-element.659), channel_id=1, source_target_pairs={{0,4},{1,5},{4,8},{5,9},{8,12},{9,13},{12,14},{13,15},{14,10},{15,... | collective-permute-start | bytes 1572872 | tf_op jit(solution)/shard_map/ppermute | solution.py:516
  441.0 28.9 %collective-permute-start.99 = (bf16[128,2048]{1,0:T(8,128)(2,1)}, bf16[128,2048]{1,0:T(8,128)(2,1)}, u32[]{:S(2)}, u32[]{:S(2)}) collective-permute-start(bf16[128,2048]{1,0:T(8,128)(2,1)} %get-tuple-element.660), channel_id=1, source_target_pairs={{4,0},{5,1},{8,4},{9,5},{12,8},{13,9},{14,12},{15,13},{10,14},{11,... | collective-permute-start | bytes 1572872 | tf_op jit(solution)/shard_map/ppermute | solution.py:519
  442.4 27.5 %collective-permute-start.102 = (bf16[256,2048]{1,0:T(8,128)(2,1)S(1)}, bf16[256,2048]{1,0:T(8,128)(2,1)S(1)}, u32[]{:S(2)}, u32[]{:S(2)}) collective-permute-start(bf16[256,2048]{1,0:T(8,128)(2,1)S(1)} %copy-done.66), channel_id=1, source_target_pairs={{0,16},{16,0},{1,17},{17,1},{2,18},{18,2},{3,19},{19,3},{4,20},{20... | collective-permute-start | bytes 3145736 | tf_op jit(solution)/shard_map/ppermute | solution.py:649
  475.8 14.7 %collective-permute-start.118 = (bf16[256,2048]{1,0:T(8,128)(2,1)S(1)}, bf16[256,2048]{1,0:T(8,128)(2,1)}, u32[]{:S(2)}, u32[]{:S(2)}) collective-permute-start(bf16[256,2048]{1,0:T(8,128)(2,1)S(1)} %convolution_convert_fusion.2), channel_id=1, source_target_pairs={{0,1},{1,0},{2,3},{3,2},{4,5},{5,4},{6,7},{7,6},{8,9},{9,8},{10,11... | collective-permute-start | bytes 3145736 | tf_op jit(solution)/shard_map/ppermute | solution.py:522
  476.0 16.6 %collective-permute-start.119 = (bf16[128,2048]{1,0:T(8,128)(2,1)S(1)}, bf16[128,2048]{1,0:T(8,128)(2,1)}, u32[]{:S(2)}, u32[]{:S(2)}) collective-permute-start(bf16[128,2048]{1,0:T(8,128)(2,1)S(1)} %copy-done.77), channel_id=1, source_target_pairs={{0,16},{16,0},{1,17},{17,1},{2,18},{18,2},{3,19},{19,3},{4,20},{20... | collective-permute-start | bytes 1572872 | tf_op jit(solution)/shard_map/ppermute | solution.py:649
  496.5 15.8 %collective-permute-start.123 = (bf16[256,2048]{1,0:T(8,128)(2,1)S(1)}, bf16[256,2048]{1,0:T(8,128)(2,1)}, u32[]{:S(2)}, u32[]{:S(2)}) collective-permute-start(bf16[256,2048]{1,0:T(8,128)(2,1)S(1)} %convolution_convert_fusion.1), channel_id=1, source_target_pairs={{0,1},{1,0},{2,3},{3,2},{4,5},{5,4},{6,7},{7,6},{8,9},{9,8},{10,11... | collective-permute-start | bytes 3145736 | tf_op jit(solution)/shard_map/ppermute | solution.py:522
  496.6 20.3 %collective-permute-start.124 = (bf16[16,64,384]{2,1,0:T(8,128)(2,1)}, bf16[16,64,384]{2,1,0:T(8,128)(2,1)}, u32[]{:S(2)}, u32[]{:S(2)}) collective-permute-start(bf16[16,64,384]{2,1,0:T(8,128)(2,1)} %get-tuple-element.573), channel_id=1, source_target_pairs={{0,16},{16,0},{1,17},{17,1},{2,18},{18,2},{3,19},{19,3},{4,20},{20... | collective-permute-start | bytes 2359304 | tf_op jit(solution)/shard_map/ppermute | solution.py:649
  497.7 16.6 %collective-permute-start.120 = (bf16[128,2048]{1,0:T(8,128)(2,1)}, bf16[128,2048]{1,0:T(8,128)(2,1)S(1)}, u32[]{:S(2)}, u32[]{:S(2)}) collective-permute-start(bf16[128,2048]{1,0:T(8,128)(2,1)} %pad_maximum_fusion.12), channel_id=1, source_target_pairs={{4,0},{5,1},{8,4},{9,5},{12,8},{13,9},{14,12},{15,13},{10,14},{11,... | collective-permute-start | bytes 1572872 | tf_op jit(solution)/shard_map/ppermute | solution.py:519
  498.9 15.4 %collective-permute-start.121 = (bf16[128,2048]{1,0:T(8,128)(2,1)}, bf16[128,2048]{1,0:T(8,128)(2,1)}, u32[]{:S(2)}, u32[]{:S(2)}) collective-permute-start(bf16[128,2048]{1,0:T(8,128)(2,1)} %pad_maximum_fusion.13), channel_id=1, source_target_pairs={{0,4},{1,5},{4,8},{5,9},{8,12},{9,13},{12,14},{13,15},{14,10},{15,... | collective-permute-start | bytes 1572872 | tf_op jit(solution)/shard_map/ppermute | solution.py:516
  520.9 19.2 %collective-permute-start.126 = (bf16[128,2048]{1,0:T(8,128)(2,1)}, bf16[128,2048]{1,0:T(8,128)(2,1)}, u32[]{:S(2)}, u32[]{:S(2)}) collective-permute-start(bf16[128,2048]{1,0:T(8,128)(2,1)} %get-tuple-element.655), channel_id=1, source_target_pairs={{0,4},{1,5},{4,8},{5,9},{8,12},{9,13},{12,14},{13,15},{14,10},{15,... | collective-permute-start | bytes 1572872 | tf_op jit(solution)/shard_map/ppermute | solution.py:516
  521.8 18.4 %collective-permute-start.125 = (bf16[128,2048]{1,0:T(8,128)(2,1)}, bf16[128,2048]{1,0:T(8,128)(2,1)}, u32[]{:S(2)}, u32[]{:S(2)}) collective-permute-start(bf16[128,2048]{1,0:T(8,128)(2,1)} %get-tuple-element.656), channel_id=1, source_target_pairs={{4,0},{5,1},{8,4},{9,5},{12,8},{13,9},{14,12},{15,13},{10,14},{11,... | collective-permute-start | bytes 1572872 | tf_op jit(solution)/shard_map/ppermute | solution.py:519
  525.2 30.9 %all-to-all-start.1 = ((bf16[16,64,384]{2,1,0:T(8,128)(2,1)}), bf16[16,64,384]{2,1,0:T(8,128)(2,1)}, u32[]{:S(2)}, u32[]{:S(2)}) async-start(bf16[16,64,384]{2,1,0:T(8,128)(2,1)} %add_convert_fusion), calls=%async_computation.1 | async-start | bytes 1572864 | tf_op jit(solution)/shard_map/all_to_all | solution.py:877
  542.8 18.6 %collective-permute-start.131 = (bf16[128,2048]{1,0:T(8,128)(2,1)}, bf16[128,2048]{1,0:T(8,128)(2,1)}, u32[]{:S(2)}, u32[]{:S(2)}) collective-permute-start(bf16[128,2048]{1,0:T(8,128)(2,1)} %get-tuple-element.653), channel_id=1, source_target_pairs={{0,4},{1,5},{4,8},{5,9},{8,12},{9,13},{12,14},{13,15},{14,10},{15,... | collective-permute-start | bytes 1572872 | tf_op jit(solution)/shard_map/ppermute | solution.py:516
  544.5 16.8 %collective-permute-start.130 = (bf16[128,2048]{1,0:T(8,128)(2,1)}, bf16[128,2048]{1,0:T(8,128)(2,1)}, u32[]{:S(2)}, u32[]{:S(2)}) collective-permute-start(bf16[128,2048]{1,0:T(8,128)(2,1)} %get-tuple-element.654), channel_id=1, source_target_pairs={{4,0},{5,1},{8,4},{9,5},{12,8},{13,9},{14,12},{15,13},{10,14},{11,... | collective-permute-start | bytes 1572872 | tf_op jit(solution)/shard_map/ppermute | solution.py:519
  546.3 15.0 %collective-permute-start.134 = (bf16[128,2048]{1,0:T(8,128)(2,1)}, bf16[128,2048]{1,0:T(8,128)(2,1)}, u32[]{:S(2)}, u32[]{:S(2)}) collective-permute-start(bf16[128,2048]{1,0:T(8,128)(2,1)} %weight_grads.7.refs_0_), channel_id=1, source_target_pairs={{0,16},{16,0},{1,17},{17,1},{2,18},{18,2},{3,19},{19,3},{4,20},{20... | collective-permute-start | bytes 1572872 | tf_op jit(solution)/shard_map/ppermute | solution.py:649
  556.1 21.6 %collective-permute-start.137 = (bf16[16,64,384]{2,1,0:T(8,128)(2,1)}, bf16[16,64,384]{2,1,0:T(8,128)(2,1)S(1)}, u32[]{:S(2)}, u32[]{:S(2)}) collective-permute-start(bf16[16,64,384]{2,1,0:T(8,128)(2,1)} %all-to-all-done.1.refs_0_), channel_id=1, source_target_pairs={{0,16},{16,0},{1,17},{17,1},{2,18},{18,2},{3,19},{19,3},{4,20},{20... | collective-permute-start | bytes 2359304 | tf_op jit(solution)/shard_map/ppermute | solution.py:649
  (194 other events, 1984.3 us)

commit v5 on v4

--- a/solution.py
+++ b/solution.py
@@ -786,7 +786,7 @@
         return dot_nn(mine, w_down), dot_nn(other, w_down)
 
     swaps = Swaps()
-    cuts = [[units // 16 * count for count in row] for row in ((4, 4, 8), (8, 8), (2, 8, 4, 2))]
+    cuts = [[units // 16 * count for count in row] for row in ((4, 4, 8), (8, 8), (3, 9, 4))]
     pull = Stream(ring.scatter(pull_part))
     hop([pull])
     swaps.add(

time: 590 us -> 589 us (level)
  starting transfers between devices: 118 us -> 112 us
    ppermute x14 -> x13, starting transfers between devices: 18.4 us -> 13.3 us  [swapped(): return lax.ppermute(part, 'narrow', [(0, 1), (1, 0)])]
    ppermute x14 -> x13, waiting for transfers between devices: 43.6 us -> 38.6 us  [swapped(): return lax.ppermute(part, 'narrow', [(0, 1), (1, 0)])]
    unnamed x253 -> x251, local copies, waits for them, and re-layouts: 25.6 us -> 26.5 us
  transfers between devices with their start and end apart: 140 -> 139, of which waited for: 58 -> 61; matrix products, arithmetic and copies ran while one was open for 19% -> 19% of each run, Pallas kernels for 17% -> 17%
where the time goes in v5:
time: 589 us; the launch traced here: 581 us
  waiting for transfers between devices  197 us (33%)
  starting transfers between devices  112 us (19%)
  Pallas kernels  103 us (17%)
  matrix products  83.1 us (14%)
  other arithmetic  47.9 us (8%)
  local copies, waits for them, and re-layouts  33.8 us (6%)
    ppermute x32, waiting for transfers between devices, forward(): return lax.ppermute(array, 'wide', self.ahead)  93.6 us
    ppermute x32, waiting for transfers between devices, backward(): return lax.ppermute(array, 'wide', self.behind)  52.4 us
    dot_general x25, matrix products, dot_nt(): lax.dot_general(a, b, (((1,), (1,)), ((), ())), preferred_element_type=jn...  48.6 us
    ppermute x32, starting transfers between devices, forward(): return lax.ppermute(array, 'wide', self.ahead)  38.9 us
    ppermute x13, waiting for transfers between devices, swapped(): return lax.ppermute(part, 'narrow', [(0, 1), (1, 0)])  38.6 us
    dot_general x31, matrix products, dot_nn(): lax.dot_general(a, b, (((1,), (0,)), ((), ())), preferred_element_type=jn...  34.5 us
    ppermute x32, starting transfers between devices, backward(): return lax.ppermute(array, 'wide', self.behind)  33.8 us
    pallas_call x4, Pallas kernels, weight_grads(): pl.pallas_call(functools.partial(grads_kernel, len(lefts), len(rights)),...  32.2 us
  transfers between devices with their start and end apart: 139, of which 61 were waited for; matrix products, arithmetic and copies ran while one was open for 19% of the time, Pallas kernels for 17%

profile of v5, /device:TPU:0, one launch (start us, length us, event | category | flops | bytes accessed | tf_op | source)
XLA Modules:
  0.0 580.8 jit_solution(12408347098283066188)
XLA Ops:
  2.7 2.0 constant_dynamic-update-slice_fusion.17
  4.8 2.9 collective-permute-start.2
  12.6 6.5 %all-to-all-start = ((bf16[16,64,384]{2,1,0:T(8,128)(2,1)}), bf16[16,64,384]{2,1,0:T(8,128)(2,1)}, u32[]{:S(2)}, u32[]{:S(2)}) async-start(bf16[16,64,384]{2,1,0:T(8,128)(2,1)} %slice_select_fusion), calls=%async_computation | async-start | bytes 1572864 | tf_op jit(solution)/shard_map/all_to_all | solution.py:720
  19.8 2.0 fusion.138.refs_5_
  21.8 4.7 fusion.142
  33.6 10.7 %collective-permute-done.5.refs_11_ = bf16[128,2048]{1,0:T(8,128)(2,1)} collective-permute-done((bf16[128,2048]{1,0:T(8,128)(2,1)}, bf16[128,2048]{1,0:T(8,128)(2,1)}, u32[]{:S(2)}, u32[]{:S(2)}) %collective-permute-start.5) | collective-permute-done | bytes 524320 | tf_op jit(solution)/shard_map/ppermute | solution.py:516
  46.2 5.8 collective-permute-start.9
  60.6 2.6 collective-permute-done.9.refs_15_
  63.2 3.2 collective-permute-done.10.refs_16_
  84.2 9.2 %fusion.264.lin_ref = f32[2048,384]{1,0:T(8,128)} fusion(bf16[2048,2048]{1,0:T(8,128)(2,1)} %constant_dynamic-update-slice_fusion, bf16[2048,384]{1,0:T(8,128)(2,1)S(1)} %bitcast.109), kind=kOutput, calls=%fused_computation.370 | convolution fusion | flops 3221225472 | bytes 13107200 | tf_op jit(solution)/shard_map/dot_general | solution.py:21
  97.0 18.0 %attention_forward.1 = (bf16[2048,128]{1,0:T(8,128)(2,1)}, bf16[2048,128]{1,0:T(8,128)(2,1)}, bf16[2048,128]{1,0:T(8,128)(2,1)}, bf16[2048,128]{1,0:T(8,128)(2,1)}, f32[8,2048]{1,0:T(8,128)}) custom-call(s32[16]{0:T(128)} %dynamic-slice_bitcast_fusion.slot_ref, s32[1]{0:T(128)} %copy.65.length_ref, f32[2048,384]{1,0:T(8,128)} %fusion.264.lin_ref, ...), custom_call_target="tpu_custom_call" | custom-call | flops 2147483648 | bytes 6291456 | tf_op jit(solution)/shard_map/attention_forward/pallas_call | solution.py:129
  123.6 9.6 %collective-permute-done.23.refs_11_ = bf16[128,2048]{1,0:T(8,128)(2,1)S(1)} collective-permute-done((bf16[128,2048]{1,0:T(8,128)(2,1)}, bf16[128,2048]{1,0:T(8,128)(2,1)S(1)}, u32[]{:S(2)}, u32[]{:S(2)}) %collective-permute-start.23) | collective-permute-done | bytes 524320 | tf_op jit(solution)/shard_map/ppermute | solution.py:516
  134.8 3.2 collective-permute-done.22
  144.7 9.8 %collective-permute-done.26 = bf16[128,2048]{1,0:T(8,128)(2,1)S(1)} collective-permute-done((bf16[128,2048]{1,0:T(8,128)(2,1)S(1)}, bf16[128,2048]{1,0:T(8,128)(2,1)S(1)}, u32[]{:S(2)}, u32[]{:S(2)}) %collective-permute-start.26) | collective-permute-done | bytes 524320 | tf_op jit(solution)/shard_map/ppermute | solution.py:519
  154.8 9.1 %collective-permute-done.28.refs_15_ = bf16[128,2048]{1,0:T(8,128)(2,1)S(1)} collective-permute-done((bf16[128,2048]{1,0:T(8,128)(2,1)S(1)}, bf16[128,2048]{1,0:T(8,128)(2,1)S(1)}, u32[]{:S(2)}, u32[]{:S(2)}) %collective-permute-start.28) | collective-permute-done | bytes 524320 | tf_op jit(solution)/shard_map/ppermute | solution.py:516
  169.3 13.4 %collective-permute-done.34.refs_20_ = bf16[64,2048]{1,0:T(8,128)(2,1)S(1)} collective-permute-done((bf16[64,2048]{1,0:T(8,128)(2,1)S(1)}, bf16[64,2048]{1,0:T(8,128)(2,1)S(1)}, u32[]{:S(2)}, u32[]{:S(2)}) %collective-permute-start.34) | collective-permute-done | bytes 262176 | tf_op jit(solution)/shard_map/ppermute | solution.py:519
  185.4 8.0 %collective-permute-done.37 = bf16[128,2048]{1,0:T(8,128)(2,1)S(1)} collective-permute-done((bf16[128,2048]{1,0:T(8,128)(2,1)S(1)}, bf16[128,2048]{1,0:T(8,128)(2,1)S(1)}, u32[]{:S(2)}, u32[]{:S(2)}) %collective-permute-start.37) | collective-permute-done | bytes 524320 | tf_op jit(solution)/shard_map/ppermute | solution.py:516
  203.1 7.6 %collective-permute-done.42.refs_8_ = bf16[128,2048]{1,0:T(8,128)(2,1)S(1)} collective-permute-done((bf16[128,2048]{1,0:T(8,128)(2,1)S(1)}, bf16[128,2048]{1,0:T(8,128)(2,1)S(1)}, u32[]{:S(2)}, u32[]{:S(2)}) %collective-permute-start.42) | collective-permute-done | bytes 524320 | tf_op jit(solution)/shard_map/ppermute | solution.py:519
  214.8 2.4 fusion.1
  217.2 3.9 multiply_convert_fusion.7
  222.2 4.0 collective-permute-done.45.refs_11_
  230.6 2.4 fusion.17
  233.1 3.9 multiply_convert_fusion.4
  237.1 5.0 collective-permute-done.51.refs_15_
  246.5 2.4 fusion.33
  248.9 3.9 multiply_convert_fusion.1
  267.5 4.8 collective-permute-done.67
  275.1 2.2 convolution_convert_fusion.10
  279.7 8.7 %weight_grads.4 = (bf16[128,2048]{1,0:T(8,128)(2,1)}, bf16[128,2048]{1,0:T(8,128)(2,1)}, bf16[256,2048]{1,0:T(8,128)(2,1)}) custom-call(bf16[256,512]{1,0:T(8,128)(2,1)} %get-tuple-element.501.refs_0_, bf16[512,512]{1,0:T(8,128)(2,1)} %get-tuple-element.486.refs_1_, bf16[512,512]{1,0:T(8,128)(2,1)} %get-tuple-element.452.refs_2_, ...), custom_call_target="tpu_custom_call" | custom-call | flops 1024 | bytes 1024 | tf_op jit(solution)/shard_map/weight_grads/pallas_call | solution.py:360
  288.5 2.6 convert_add_fusion.7
  300.1 10.4 %collective-permute-done.75.refs_3_ = bf16[128,2048]{1,0:T(8,128)(2,1)S(1)} collective-permute-done((bf16[128,2048]{1,0:T(8,128)(2,1)S(1)}, bf16[128,2048]{1,0:T(8,128)(2,1)S(1)}, u32[]{:S(2)}, u32[]{:S(2)}) %collective-permute-start.75) | collective-permute-done | bytes 524320 | tf_op jit(solution)/shard_map/ppermute | solution.py:649
  317.1 9.6 %collective-permute-done.79.refs_4_ = bf16[128,2048]{1,0:T(8,128)(2,1)S(1)} collective-permute-done((bf16[128,2048]{1,0:T(8,128)(2,1)S(1)}, bf16[128,2048]{1,0:T(8,128)(2,1)S(1)}, u32[]{:S(2)}, u32[]{:S(2)}) %collective-permute-start.79) | collective-permute-done | bytes 524320 | tf_op jit(solution)/shard_map/ppermute | solution.py:649
  337.7 8.8 %weight_grads.5 = (bf16[256,2048]{1,0:T(8,128)(2,1)}, bf16[256,2048]{1,0:T(8,128)(2,1)}) custom-call(bf16[256,1024]{1,0:T(8,128)(2,1)} %pad_maximum_fusion.6.refs_0_, bf16[512,1024]{1,0:T(8,128)(2,1)} %pad_maximum_fusion.1.refs_1_, bf16[512,1024]{1,0:T(8,128)(2,1)} %copy-done.9, bf16[512,1024]{1,0:T(8,128)(2,1)} %copy-done.10, bf16[256,1024]{1,0:T(8,128)(2,1)} %copy-done.12, ...), custom_call_target="tpu_custom_call" | custom-call | flops 1024 | bytes 1024 | tf_op jit(solution)/shard_map/weight_grads/pallas_call | solution.py:360
  348.9 2.0 collective-permute-done.80.refs_3_
  350.9 4.3 collective-permute-done.84
  355.3 5.0 collective-permute-done.86.refs_5_
  367.5 8.8 %weight_grads.6 = (bf16[96,2048]{1,0:T(8,128)(2,1)}, bf16[288,2048]{1,0:T(8,128)(2,1)}, bf16[128,2048]{1,0:T(8,128)(2,1)}) custom-call(bf16[256,1024]{1,0:T(8,128)(2,1)} %pad_maximum_fusion.6.refs_0_, bf16[512,1024]{1,0:T(8,128)(2,1)} %pad_maximum_fusion.1.refs_1_, bf16[512,1024]{1,0:T(8,128)(2,1)} %copy-done.9, bf16[512,1024]{1,0:T(8,128)(2,1)} %copy-done.10, ...), custom_call_target="tpu_custom_call" | custom-call | flops 1024 | bytes 1024 | tf_op jit(solution)/shard_map/weight_grads/pallas_call | solution.py:360
  379.8 10.1 %collective-permute-done.87.refs_7_ = bf16[128,2048]{1,0:T(8,128)(2,1)} collective-permute-done((bf16[128,2048]{1,0:T(8,128)(2,1)}, bf16[128,2048]{1,0:T(8,128)(2,1)}, u32[]{:S(2)}, u32[]{:S(2)}) %collective-permute-start.87) | collective-permute-done | bytes 524320 | tf_op jit(solution)/shard_map/ppermute | solution.py:516
  390.0 2.6 add_convert_fusion.9
  402.6 2.6 fusion.85
  405.2 4.8 sum_pieces.4
  410.7 2.9 collective-permute-done.96
  414.5 9.5 %collective-permute-done.93.refs_11_ = bf16[128,2048]{1,0:T(8,128)(2,1)S(1)} collective-permute-done((bf16[128,2048]{1,0:T(8,128)(2,1)}, bf16[128,2048]{1,0:T(8,128)(2,1)S(1)}, u32[]{:S(2)}, u32[]{:S(2)}) %collective-permute-start.93) | collective-permute-done | bytes 524320 | tf_op jit(solution)/shard_map/ppermute | solution.py:516
  425.2 2.5 add_convert_fusion.7
  432.1 3.9 collective-permute-done.111.refs_16_
  436.0 2.7 fusion.88
  448.7 22.8 %attention_backward.1 = (bf16[256,384]{1,0:T(8,128)(2,1)}, bf16[512,384]{1,0:T(8,128)(2,1)}, bf16[512,384]{1,0:T(8,128)(2,1)}, bf16[512,384]{1,0:T(8,128)(2,1)}, bf16[256,384]{1,0:T(8,128)(2,1)}) custom-call(s32[16]{0:T(128)} %dynamic-slice_bitcast_fusion.slot_ref, s32[1]{0:T(128)} %copy.65.length_ref, bf16[2048,128]{1,0:T(8,128)(2,1)} %get-tuple-element.504.query_ref, ...), custom_call_target="tpu_custom_call" | custom-call | flops 5368709120 | bytes 9437184 | tf_op jit(solution)/shard_map/attention_backward/pallas_call | solution.py:250
  480.4 9.2 %heads_grads.1 = (bf16[16,64,384]{2,1,0:T(8,128)(2,1)}, bf16[16,64,384]{2,1,0:T(8,128)(2,1)}, f32[1,2048]{1,0:T(1,128)}) custom-call(s32[1]{0:T(128)} %bitcast.10.upper_ref.side_ref, bf16[2048,384]{1,0:T(8,128)(2,1)} %bitcast.110, bf16[256,384]{1,0:T(8,128)(2,1)} %get-tuple-element.601.refs_0_, bf16[512,384]{1,0:T(8,128)(2,1)} %get-tuple-element.594.refs_1_, ...), custom_call_target="tpu_custom_call" | custom-call | flops 1024 | bytes 1024 | tf_op jit(solution)/shard_map/heads_grads/pallas_call | solution.py:401
  501.7 4.7 sum_pieces.5
  506.4 5.9 %weight_grads.7.refs_0_ = bf16[128,2048]{1,0:T(8,128)(2,1)} custom-call(bf16[2048,128]{1,0:T(8,128)(2,1)} %get-tuple-element.567.att_ref.refs_0_, bf16[128,2048]{1,0:T(8,128)(2,1)} %copy-done.27, bf16[128,2048]{1,0:T(8,128)(2,1)} %copy-done.82, bf16[128,2048]{1,0:T(8,128)(2,1)} %collective-permute-done.80.refs_3_, ...), custom_call_target="tpu_custom_call" | custom-call | flops 1024 | bytes 1024 | tf_op jit(solution)/shard_map/weight_grads/pallas_call | solution.py:360
  514.3 2.6 collective-permute-done.124
  517.0 2.3 add_convert_fusion.4
  525.7 2.2 add_convert_fusion
  527.9 4.6 all-to-all-start.1
  532.5 2.4 convert_add_fusion
  535.0 3.7 collective-permute-done.129.refs_1_
  538.6 2.5 add_convert_fusion.2
  542.6 2.4 convert_add_fusion.12
  548.8 3.4 sum_pieces.7
  552.2 4.8 sum_pieces.6
  558.1 2.1 convert_add_fusion.11
  560.3 2.4 collective-permute-done.132
  570.1 6.4 %collective-permute-done.136.refs_1_ = bf16[16,64,384]{2,1,0:T(8,128)(2,1)S(1)} collective-permute-done((bf16[16,64,384]{2,1,0:T(8,128)(2,1)}, bf16[16,64,384]{2,1,0:T(8,128)(2,1)S(1)}, u32[]{:S(2)}, u32[]{:S(2)}) %collective-permute-start.136) | collective-permute-done | bytes 786464 | tf_op jit(solution)/shard_map/ppermute | solution.py:649
  577.3 3.2 assemble.1
  (616 shorter events, 224.6 us)
Async XLA Ops:
  4.8 21.7 %collective-permute-start.2 = (bf16[128,2048]{1,0:T(8,128)(2,1)S(1)}, bf16[128,2048]{1,0:T(8,128)(2,1)}, u32[]{:S(2)}, u32[]{:S(2)}) collective-permute-start(bf16[128,2048]{1,0:T(8,128)(2,1)S(1)} %get-tuple-element.537.refs_5_), channel_id=1, source_target_pairs={{4,0},{5,1},{8,4},{9,5},{12,8},{13,9},{14,12},{15,13},{10,14},{11,... | collective-permute-start | bytes 1572872 | tf_op jit(solution)/shard_map/ppermute | solution.py:519
  7.7 18.8 %collective-permute-start.1 = (bf16[128,2048]{1,0:T(8,128)(2,1)S(1)}, bf16[128,2048]{1,0:T(8,128)(2,1)}, u32[]{:S(2)}, u32[]{:S(2)}) collective-permute-start(bf16[128,2048]{1,0:T(8,128)(2,1)S(1)} %get-tuple-element.537.refs_5_), channel_id=1, source_target_pairs={{0,4},{1,5},{4,8},{5,9},{8,12},{9,13},{12,14},{13,15},{14,10},{15,... | collective-permute-start | bytes 1572872 | tf_op jit(solution)/shard_map/ppermute | solution.py:516
  7.9 21.1 %collective-permute-start = (bf16[128,2048]{1,0:T(8,128)(2,1)S(1)}, bf16[128,2048]{1,0:T(8,128)(2,1)S(1)}, u32[]{:S(2)}, u32[]{:S(2)}) collective-permute-start(bf16[128,2048]{1,0:T(8,128)(2,1)S(1)} %get-tuple-element.537.refs_5_), channel_id=1, source_target_pairs={{0,1},{1,0},{2,3},{3,2},{4,5},{5,4},{6,7},{7,6},{8,9},{9,8},{10,11... | collective-permute-start | bytes 1572872 | tf_op jit(solution)/shard_map/ppermute | solution.py:522
  12.6 46.5 %all-to-all-start = ((bf16[16,64,384]{2,1,0:T(8,128)(2,1)}), bf16[16,64,384]{2,1,0:T(8,128)(2,1)}, u32[]{:S(2)}, u32[]{:S(2)}) async-start(bf16[16,64,384]{2,1,0:T(8,128)(2,1)} %slice_select_fusion), calls=%async_computation | async-start | bytes 1572864 | tf_op jit(solution)/shard_map/all_to_all | solution.py:720
  26.5 17.8 %collective-permute-start.5 = (bf16[128,2048]{1,0:T(8,128)(2,1)}, bf16[128,2048]{1,0:T(8,128)(2,1)}, u32[]{:S(2)}, u32[]{:S(2)}) collective-permute-start(bf16[128,2048]{1,0:T(8,128)(2,1)} %collective-permute-done.1.refs_7_), channel_id=1, source_target_pairs={{0,4},{1,5},{4,8},{5,9},{8,12},{9,13},{12,14},{13,15},{14,10},{15,... | collective-permute-start | bytes 1572872 | tf_op jit(solution)/shard_map/ppermute | solution.py:516
  28.5 23.5 %collective-permute-start.3 = (bf16[128,2048]{1,0:T(8,128)(2,1)}, bf16[128,2048]{1,0:T(8,128)(2,1)S(1)}, u32[]{:S(2)}, u32[]{:S(2)}) collective-permute-start(bf16[128,2048]{1,0:T(8,128)(2,1)} %collective-permute-done.1.refs_7_), channel_id=1, source_target_pairs={{0,1},{1,0},{2,3},{3,2},{4,5},{5,4},{6,7},{7,6},{8,9},{9,8},{10,11... | collective-permute-start | bytes 1572872 | tf_op jit(solution)/shard_map/ppermute | solution.py:522
  28.5 17.7 %collective-permute-start.6 = (bf16[128,2048]{1,0:T(8,128)(2,1)}, bf16[128,2048]{1,0:T(8,128)(2,1)}, u32[]{:S(2)}, u32[]{:S(2)}) collective-permute-start(bf16[128,2048]{1,0:T(8,128)(2,1)} %collective-permute-done.2.refs_8_), channel_id=1, source_target_pairs={{4,0},{5,1},{8,4},{9,5},{12,8},{13,9},{14,12},{15,13},{10,14},{11,... | collective-permute-start | bytes 1572872 | tf_op jit(solution)/shard_map/ppermute | solution.py:519
  28.7 24.9 %collective-permute-start.4 = (bf16[128,2048]{1,0:T(8,128)(2,1)}, bf16[128,2048]{1,0:T(8,128)(2,1)S(1)}, u32[]{:S(2)}, u32[]{:S(2)}) collective-permute-start(bf16[128,2048]{1,0:T(8,128)(2,1)} %collective-permute-done.2.refs_8_), channel_id=1, source_target_pairs={{0,1},{1,0},{2,3},{3,2},{4,5},{5,4},{6,7},{7,6},{8,9},{9,8},{10,11... | collective-permute-start | bytes 1572872 | tf_op jit(solution)/shard_map/ppermute | solution.py:522
  46.2 17.1 %collective-permute-start.9 = (bf16[128,2048]{1,0:T(8,128)(2,1)}, bf16[128,2048]{1,0:T(8,128)(2,1)S(1)}, u32[]{:S(2)}, u32[]{:S(2)}) collective-permute-start(bf16[128,2048]{1,0:T(8,128)(2,1)} %collective-permute-done.5.refs_11_), channel_id=1, source_target_pairs={{0,4},{1,5},{4,8},{5,9},{8,12},{9,13},{12,14},{13,15},{14,10},{15,... | collective-permute-start | bytes 1572872 | tf_op jit(solution)/shard_map/ppermute | solution.py:516
  51.9 15.2 %collective-permute-start.7 = (bf16[128,2048]{1,0:T(8,128)(2,1)}, bf16[128,2048]{1,0:T(8,128)(2,1)}, u32[]{:S(2)}, u32[]{:S(2)}) collective-permute-start(bf16[128,2048]{1,0:T(8,128)(2,1)} %collective-permute-done.5.refs_11_), channel_id=1, source_target_pairs={{0,1},{1,0},{2,3},{3,2},{4,5},{5,4},{6,7},{7,6},{8,9},{9,8},{10,11... | collective-permute-start | bytes 1572872 | tf_op jit(solution)/shard_map/ppermute | solution.py:522
  51.9 14.5 %collective-permute-start.10 = (bf16[128,2048]{1,0:T(8,128)(2,1)}, bf16[128,2048]{1,0:T(8,128)(2,1)S(1)}, u32[]{:S(2)}, u32[]{:S(2)}) collective-permute-start(bf16[128,2048]{1,0:T(8,128)(2,1)} %collective-permute-done.6.refs_12_), channel_id=1, source_target_pairs={{4,0},{5,1},{8,4},{9,5},{12,8},{13,9},{14,12},{15,13},{10,14},{11,... | collective-permute-start | bytes 1572872 | tf_op jit(solution)/shard_map/ppermute | solution.py:519
  52.0 17.4 %collective-permute-start.8 = (bf16[128,2048]{1,0:T(8,128)(2,1)}, bf16[128,2048]{1,0:T(8,128)(2,1)}, u32[]{:S(2)}, u32[]{:S(2)}) collective-permute-start(bf16[128,2048]{1,0:T(8,128)(2,1)} %collective-permute-done.6.refs_12_), channel_id=1, source_target_pairs={{0,1},{1,0},{2,3},{3,2},{4,5},{5,4},{6,7},{7,6},{8,9},{9,8},{10,11... | collective-permute-start | bytes 1572872 | tf_op jit(solution)/shard_map/ppermute | solution.py:522
  59.1 23.6 %collective-permute-start.17 = (bf16[16,64,384]{2,1,0:T(8,128)(2,1)}, bf16[16,64,384]{2,1,0:T(8,128)(2,1)S(1)}, u32[]{:S(2)}, u32[]{:S(2)}) collective-permute-start(bf16[16,64,384]{2,1,0:T(8,128)(2,1)} %all-to-all-done), channel_id=1, source_target_pairs={{0,16},{16,0},{1,17},{17,1},{2,18},{18,2},{3,19},{19,3},{4,20},{20... | collective-permute-start | bytes 2359304 | tf_op jit(solution)/shard_map/ppermute | solution.py:649
  93.4 21.7 %collective-permute-start.19 = (bf16[128,2048]{1,0:T(8,128)(2,1)S(1)}, bf16[128,2048]{1,0:T(8,128)(2,1)S(1)}, u32[]{:S(2)}, u32[]{:S(2)}) collective-permute-start(bf16[128,2048]{1,0:T(8,128)(2,1)S(1)} %copy-done.41), channel_id=1, source_target_pairs={{4,0},{5,1},{8,4},{9,5},{12,8},{13,9},{14,12},{15,13},{10,14},{11,... | collective-permute-start | bytes 1572872 | tf_op jit(solution)/shard_map/ppermute | solution.py:519
  94.8 20.2 %collective-permute-start.18 = (bf16[128,2048]{1,0:T(8,128)(2,1)S(1)}, bf16[128,2048]{1,0:T(8,128)(2,1)}, u32[]{:S(2)}, u32[]{:S(2)}) collective-permute-start(bf16[128,2048]{1,0:T(8,128)(2,1)S(1)} %copy-done.41), channel_id=1, source_target_pairs={{0,4},{1,5},{4,8},{5,9},{8,12},{9,13},{12,14},{13,15},{14,10},{15,... | collective-permute-start | bytes 1572872 | tf_op jit(solution)/shard_map/ppermute | solution.py:516
  118.2 15.0 %collective-permute-start.23 = (bf16[128,2048]{1,0:T(8,128)(2,1)}, bf16[128,2048]{1,0:T(8,128)(2,1)S(1)}, u32[]{:S(2)}, u32[]{:S(2)}) collective-permute-start(bf16[128,2048]{1,0:T(8,128)(2,1)} %collective-permute-done.18.refs_7_), channel_id=1, source_target_pairs={{0,4},{1,5},{4,8},{5,9},{8,12},{9,13},{12,14},{13,15},{14,10},{15,... | collective-permute-start | bytes 1572872 | tf_op jit(solution)/shard_map/ppermute | solution.py:516
  119.9 14.8 %collective-permute-start.24 = (bf16[128,2048]{1,0:T(8,128)(2,1)S(1)}, bf16[128,2048]{1,0:T(8,128)(2,1)S(1)}, u32[]{:S(2)}, u32[]{:S(2)}) collective-permute-start(bf16[128,2048]{1,0:T(8,128)(2,1)S(1)} %collective-permute-done.19.refs_8_), channel_id=1, source_target_pairs={{4,0},{5,1},{8,4},{9,5},{12,8},{13,9},{14,12},{15,13},{10,14},{11,... | collective-permute-start | bytes 1572872 | tf_op jit(solution)/shard_map/ppermute | solution.py:519
  120.7 23.5 %collective-permute-start.30 = (bf16[256,2048]{1,0:T(8,128)(2,1)S(1)}, bf16[256,2048]{1,0:T(8,128)(2,1)S(1)}, u32[]{:S(2)}, u32[]{:S(2)}) collective-permute-start(bf16[256,2048]{1,0:T(8,128)(2,1)S(1)} %convolution_convert_fusion.7), channel_id=1, source_target_pairs={{0,1},{1,0},{2,3},{3,2},{4,5},{5,4},{6,7},{7,6},{8,9},{9,8},{10,11... | collective-permute-start | bytes 3145736 | tf_op jit(solution)/shard_map/ppermute | solution.py:522
  121.1 16.8 %collective-permute-start.22 = (bf16[64,2048]{1,0:T(8,128)(2,1)S(1)}, bf16[64,2048]{1,0:T(8,128)(2,1)S(1)}, u32[]{:S(2)}, u32[]{:S(2)}) collective-permute-start(bf16[64,2048]{1,0:T(8,128)(2,1)S(1)} %get-tuple-element.690), channel_id=1, source_target_pairs={{0,4},{1,5},{4,8},{5,9},{8,12},{9,13},{12,14},{13,15},{14,10},{15,... | collective-permute-start | bytes 786440 | tf_op jit(solution)/shard_map/ppermute | solution.py:516
  122.9 16.3 %collective-permute-start.21 = (bf16[64,2048]{1,0:T(8,128)(2,1)S(1)}, bf16[64,2048]{1,0:T(8,128)(2,1)S(1)}, u32[]{:S(2)}, u32[]{:S(2)}) collective-permute-start(bf16[64,2048]{1,0:T(8,128)(2,1)S(1)} %get-tuple-element.691), channel_id=1, source_target_pairs={{4,0},{5,1},{8,4},{9,5},{12,8},{13,9},{14,12},{15,13},{10,14},{11,... | collective-permute-start | bytes 786440 | tf_op jit(solution)/shard_map/ppermute | solution.py:519
  139.5 14.9 %collective-permute-start.26 = (bf16[128,2048]{1,0:T(8,128)(2,1)S(1)}, bf16[128,2048]{1,0:T(8,128)(2,1)S(1)}, u32[]{:S(2)}, u32[]{:S(2)}) collective-permute-start(bf16[128,2048]{1,0:T(8,128)(2,1)S(1)} %pad_maximum_fusion.4), channel_id=1, source_target_pairs={{4,0},{5,1},{8,4},{9,5},{12,8},{13,9},{14,12},{15,13},{10,14},{11,... | collective-permute-start | bytes 1572872 | tf_op jit(solution)/shard_map/ppermute | solution.py:519
  139.9 14.9 %collective-permute-start.27 = (bf16[128,2048]{1,0:T(8,128)(2,1)S(1)}, bf16[128,2048]{1,0:T(8,128)(2,1)S(1)}, u32[]{:S(2)}, u32[]{:S(2)}) collective-permute-start(bf16[128,2048]{1,0:T(8,128)(2,1)S(1)} %pad_maximum_fusion.5), channel_id=1, source_target_pairs={{0,4},{1,5},{4,8},{5,9},{8,12},{9,13},{12,14},{13,15},{14,10},{15,... | collective-permute-start | bytes 1572872 | tf_op jit(solution)/shard_map/ppermute | solution.py:516
  141.7 22.2 %collective-permute-start.28 = (bf16[128,2048]{1,0:T(8,128)(2,1)S(1)}, bf16[128,2048]{1,0:T(8,128)(2,1)S(1)}, u32[]{:S(2)}, u32[]{:S(2)}) collective-permute-start(bf16[128,2048]{1,0:T(8,128)(2,1)S(1)} %collective-permute-done.23.refs_11_), channel_id=1, source_target_pairs={{0,4},{1,5},{4,8},{5,9},{8,12},{9,13},{12,14},{13,15},{14,10},{15,... | collective-permute-start | bytes 1572872 | tf_op jit(solution)/shard_map/ppermute | solution.py:516
  142.3 21.6 %collective-permute-start.29 = (bf16[128,2048]{1,0:T(8,128)(2,1)S(1)}, bf16[128,2048]{1,0:T(8,128)(2,1)S(1)}, u32[]{:S(2)}, u32[]{:S(2)}) collective-permute-start(bf16[128,2048]{1,0:T(8,128)(2,1)S(1)} %collective-permute-done.24.refs_12_), channel_id=1, source_target_pairs={{4,0},{5,1},{8,4},{9,5},{12,8},{13,9},{14,12},{15,13},{10,14},{11,... | collective-permute-start | bytes 1572872 | tf_op jit(solution)/shard_map/ppermute | solution.py:519
  144.2 24.4 %collective-permute-start.35 = (bf16[256,2048]{1,0:T(8,128)(2,1)S(1)}, bf16[256,2048]{1,0:T(8,128)(2,1)S(1)}, u32[]{:S(2)}, u32[]{:S(2)}) collective-permute-start(bf16[256,2048]{1,0:T(8,128)(2,1)S(1)} %convolution_convert_fusion.6), channel_id=1, source_target_pairs={{0,1},{1,0},{2,3},{3,2},{4,5},{5,4},{6,7},{7,6},{8,9},{9,8},{10,11... | collective-permute-start | bytes 3145736 | tf_op jit(solution)/shard_map/ppermute | solution.py:522
  164.2 18.4 %collective-permute-start.32 = (bf16[128,2048]{1,0:T(8,128)(2,1)S(1)}, bf16[128,2048]{1,0:T(8,128)(2,1)S(1)}, u32[]{:S(2)}, u32[]{:S(2)}) collective-permute-start(bf16[128,2048]{1,0:T(8,128)(2,1)S(1)} %get-tuple-element.664), channel_id=1, source_target_pairs={{0,4},{1,5},{4,8},{5,9},{8,12},{9,13},{12,14},{13,15},{14,10},{15,... | collective-permute-start | bytes 1572872 | tf_op jit(solution)/shard_map/ppermute | solution.py:516
  165.8 16.9 %collective-permute-start.31 = (bf16[128,2048]{1,0:T(8,128)(2,1)S(1)}, bf16[128,2048]{1,0:T(8,128)(2,1)S(1)}, u32[]{:S(2)}, u32[]{:S(2)}) collective-permute-start(bf16[128,2048]{1,0:T(8,128)(2,1)S(1)} %get-tuple-element.665), channel_id=1, source_target_pairs={{4,0},{5,1},{8,4},{9,5},{12,8},{13,9},{14,12},{15,13},{10,14},{11,... | collective-permute-start | bytes 1572872 | tf_op jit(solution)/shard_map/ppermute | solution.py:519
  166.6 18.5 %collective-permute-start.38 = (bf16[128,2048]{1,0:T(8,128)(2,1)S(1)}, bf16[128,2048]{1,0:T(8,128)(2,1)S(1)}, u32[]{:S(2)}, u32[]{:S(2)}) collective-permute-start(bf16[128,2048]{1,0:T(8,128)(2,1)S(1)} %convolution_convert_fusion.18), channel_id=1, source_target_pairs={{0,1},{1,0},{2,3},{3,2},{4,5},{5,4},{6,7},{7,6},{8,9},{9,8},{10,11... | collective-permute-start | bytes 1572872 | tf_op jit(solution)/shard_map/ppermute | solution.py:522
  166.7 15.9 %collective-permute-start.34 = (bf16[64,2048]{1,0:T(8,128)(2,1)S(1)}, bf16[64,2048]{1,0:T(8,128)(2,1)S(1)}, u32[]{:S(2)}, u32[]{:S(2)}) collective-permute-start(bf16[64,2048]{1,0:T(8,128)(2,1)S(1)} %slice.380), channel_id=1, source_target_pairs={{4,0},{5,1},{8,4},{9,5},{12,8},{13,9},{14,12},{15,13},{10,14},{11,... | collective-permute-start | bytes 786440 | tf_op jit(solution)/shard_map/ppermute | solution.py:519
  277.3 14.7 %collective-permute-start.69 = (bf16[128,2048]{1,0:T(8,128)(2,1)}, bf16[128,2048]{1,0:T(8,128)(2,1)}, u32[]{:S(2)}, u32[]{:S(2)}) collective-permute-start(bf16[128,2048]{1,0:T(8,128)(2,1)} %pad_maximum_fusion.8), channel_id=1, source_target_pairs={{4,0},{5,1},{8,4},{9,5},{12,8},{13,9},{14,12},{15,13},{10,14},{11,... | collective-permute-start | bytes 1572872 | tf_op jit(solution)/shard_map/ppermute | solution.py:519
  278.3 14.8 %collective-permute-start.70 = (bf16[128,2048]{1,0:T(8,128)(2,1)}, bf16[128,2048]{1,0:T(8,128)(2,1)}, u32[]{:S(2)}, u32[]{:S(2)}) collective-permute-start(bf16[128,2048]{1,0:T(8,128)(2,1)} %pad_maximum_fusion.9), channel_id=1, source_target_pairs={{0,4},{1,5},{4,8},{5,9},{8,12},{9,13},{12,14},{13,15},{14,10},{15,... | collective-permute-start | bytes 1572872 | tf_op jit(solution)/shard_map/ppermute | solution.py:516
  296.1 14.3 %collective-permute-start.75 = (bf16[128,2048]{1,0:T(8,128)(2,1)S(1)}, bf16[128,2048]{1,0:T(8,128)(2,1)S(1)}, u32[]{:S(2)}, u32[]{:S(2)}) collective-permute-start(bf16[128,2048]{1,0:T(8,128)(2,1)S(1)} %copy-done.80), channel_id=1, source_target_pairs={{0,16},{16,0},{1,17},{17,1},{2,18},{18,2},{3,19},{19,3},{4,20},{20... | collective-permute-start | bytes 1572872 | tf_op jit(solution)/shard_map/ppermute | solution.py:649
  334.5 25.8 %collective-permute-start.86 = (bf16[256,2048]{1,0:T(8,128)(2,1)}, bf16[256,2048]{1,0:T(8,128)(2,1)}, u32[]{:S(2)}, u32[]{:S(2)}) collective-permute-start(bf16[256,2048]{1,0:T(8,128)(2,1)} %get-tuple-element.494.refs_2_), channel_id=1, source_target_pairs={{0,16},{16,0},{1,17},{17,1},{2,18},{18,2},{3,19},{19,3},{4,20},{20... | collective-permute-start | bytes 3145736 | tf_op jit(solution)/shard_map/ppermute | solution.py:649
  336.0 14.9 %collective-permute-start.80 = (bf16[128,2048]{1,0:T(8,128)(2,1)S(1)}, bf16[128,2048]{1,0:T(8,128)(2,1)}, u32[]{:S(2)}, u32[]{:S(2)}) collective-permute-start(bf16[128,2048]{1,0:T(8,128)(2,1)S(1)} %get-tuple-element.568.refs_1_), channel_id=1, source_target_pairs={{0,4},{1,5},{4,8},{5,9},{8,12},{9,13},{12,14},{13,15},{14,10},{15,... | collective-permute-start | bytes 1572872 | tf_op jit(solution)/shard_map/ppermute | solution.py:516
  336.9 18.4 %collective-permute-start.84 = (bf16[64,2048]{1,0:T(8,128)(2,1)S(1)}, bf16[64,2048]{1,0:T(8,128)(2,1)S(1)}, u32[]{:S(2)}, u32[]{:S(2)}) collective-permute-start(bf16[64,2048]{1,0:T(8,128)(2,1)S(1)} %get-tuple-element.686), channel_id=1, source_target_pairs={{0,4},{1,5},{4,8},{5,9},{8,12},{9,13},{12,14},{13,15},{14,10},{15,... | collective-permute-start | bytes 786440 | tf_op jit(solution)/shard_map/ppermute | solution.py:516
  363.1 26.8 %collective-permute-start.92 = (bf16[256,2048]{1,0:T(8,128)(2,1)S(1)}, bf16[256,2048]{1,0:T(8,128)(2,1)}, u32[]{:S(2)}, u32[]{:S(2)}) collective-permute-start(bf16[256,2048]{1,0:T(8,128)(2,1)S(1)} %copy-done.68), channel_id=1, source_target_pairs={{0,16},{16,0},{1,17},{17,1},{2,18},{18,2},{3,19},{19,3},{4,20},{20... | collective-permute-start | bytes 3145736 | tf_op jit(solution)/shard_map/ppermute | solution.py:649
  363.5 15.1 %collective-permute-start.89 = (bf16[128,2048]{1,0:T(8,128)(2,1)}, bf16[128,2048]{1,0:T(8,128)(2,1)}, u32[]{:S(2)}, u32[]{:S(2)}) collective-permute-start(bf16[128,2048]{1,0:T(8,128)(2,1)} %pad_maximum_fusion.10), channel_id=1, source_target_pairs={{4,0},{5,1},{8,4},{9,5},{12,8},{13,9},{14,12},{15,13},{10,14},{11,... | collective-permute-start | bytes 1572872 | tf_op jit(solution)/shard_map/ppermute | solution.py:519
  364.7 15.1 %collective-permute-start.90 = (bf16[128,2048]{1,0:T(8,128)(2,1)}, bf16[128,2048]{1,0:T(8,128)(2,1)}, u32[]{:S(2)}, u32[]{:S(2)}) collective-permute-start(bf16[128,2048]{1,0:T(8,128)(2,1)} %pad_maximum_fusion.11), channel_id=1, source_target_pairs={{0,4},{1,5},{4,8},{5,9},{8,12},{9,13},{12,14},{13,15},{14,10},{15,... | collective-permute-start | bytes 1572872 | tf_op jit(solution)/shard_map/ppermute | solution.py:516
  365.5 24.4 %collective-permute-start.87 = (bf16[128,2048]{1,0:T(8,128)(2,1)}, bf16[128,2048]{1,0:T(8,128)(2,1)}, u32[]{:S(2)}, u32[]{:S(2)}) collective-permute-start(bf16[128,2048]{1,0:T(8,128)(2,1)} %collective-permute-done.80.refs_3_), channel_id=1, source_target_pairs={{0,4},{1,5},{4,8},{5,9},{8,12},{9,13},{12,14},{13,15},{14,10},{15,... | collective-permute-start | bytes 1572872 | tf_op jit(solution)/shard_map/ppermute | solution.py:516
  366.4 23.6 %collective-permute-start.88 = (bf16[128,2048]{1,0:T(8,128)(2,1)}, bf16[128,2048]{1,0:T(8,128)(2,1)}, u32[]{:S(2)}, u32[]{:S(2)}) collective-permute-start(bf16[128,2048]{1,0:T(8,128)(2,1)} %collective-permute-done.81.refs_4_), channel_id=1, source_target_pairs={{4,0},{5,1},{8,4},{9,5},{12,8},{13,9},{14,12},{15,13},{10,14},{11,... | collective-permute-start | bytes 1572872 | tf_op jit(solution)/shard_map/ppermute | solution.py:519
  394.3 30.2 %collective-permute-start.98 = (bf16[256,2048]{1,0:T(8,128)(2,1)S(1)}, bf16[256,2048]{1,0:T(8,128)(2,1)}, u32[]{:S(2)}, u32[]{:S(2)}) collective-permute-start(bf16[256,2048]{1,0:T(8,128)(2,1)S(1)} %copy-done.69), channel_id=1, source_target_pairs={{0,16},{16,0},{1,17},{17,1},{2,18},{18,2},{3,19},{19,3},{4,20},{20... | collective-permute-start | bytes 3145736 | tf_op jit(solution)/shard_map/ppermute | solution.py:649
  398.5 15.1 %collective-permute-start.96 = (bf16[128,2048]{1,0:T(8,128)(2,1)}, bf16[128,2048]{1,0:T(8,128)(2,1)}, u32[]{:S(2)}, u32[]{:S(2)}) collective-permute-start(bf16[128,2048]{1,0:T(8,128)(2,1)} %get-tuple-element.649), channel_id=1, source_target_pairs={{0,4},{1,5},{4,8},{5,9},{8,12},{9,13},{12,14},{13,15},{14,10},{15,... | collective-permute-start | bytes 1572872 | tf_op jit(solution)/shard_map/ppermute | solution.py:516
  399.4 15.1 %collective-permute-start.95 = (bf16[128,2048]{1,0:T(8,128)(2,1)}, bf16[128,2048]{1,0:T(8,128)(2,1)}, u32[]{:S(2)}, u32[]{:S(2)}) collective-permute-start(bf16[128,2048]{1,0:T(8,128)(2,1)} %get-tuple-element.650), channel_id=1, source_target_pairs={{4,0},{5,1},{8,4},{9,5},{12,8},{13,9},{14,12},{15,13},{10,14},{11,... | collective-permute-start | bytes 1572872 | tf_op jit(solution)/shard_map/ppermute | solution.py:519
  400.6 23.4 %collective-permute-start.93 = (bf16[128,2048]{1,0:T(8,128)(2,1)}, bf16[128,2048]{1,0:T(8,128)(2,1)S(1)}, u32[]{:S(2)}, u32[]{:S(2)}) collective-permute-start(bf16[128,2048]{1,0:T(8,128)(2,1)} %collective-permute-done.87.refs_7_), channel_id=1, source_target_pairs={{0,4},{1,5},{4,8},{5,9},{8,12},{9,13},{12,14},{13,15},{14,10},{15,... | collective-permute-start | bytes 1572872 | tf_op jit(solution)/shard_map/ppermute | solution.py:516
  401.4 23.1 %collective-permute-start.94 = (bf16[128,2048]{1,0:T(8,128)(2,1)}, bf16[128,2048]{1,0:T(8,128)(2,1)S(1)}, u32[]{:S(2)}, u32[]{:S(2)}) collective-permute-start(bf16[128,2048]{1,0:T(8,128)(2,1)} %collective-permute-done.88.refs_8_), channel_id=1, source_target_pairs={{4,0},{5,1},{8,4},{9,5},{12,8},{13,9},{14,12},{15,13},{10,14},{11,... | collective-permute-start | bytes 1572872 | tf_op jit(solution)/shard_map/ppermute | solution.py:519
  413.6 15.3 %collective-permute-start.106 = (bf16[128,2048]{1,0:T(8,128)(2,1)}, bf16[128,2048]{1,0:T(8,128)(2,1)S(1)}, u32[]{:S(2)}, u32[]{:S(2)}) collective-permute-start(bf16[128,2048]{1,0:T(8,128)(2,1)} %collective-permute-done.87.refs_7_), channel_id=1, source_target_pairs={{0,1},{1,0},{2,3},{3,2},{4,5},{5,4},{6,7},{7,6},{8,9},{9,8},{10,11... | collective-permute-start | bytes 1572872 | tf_op jit(solution)/shard_map/ppermute | solution.py:522
  414.5 16.7 %collective-permute-start.107 = (bf16[128,2048]{1,0:T(8,128)(2,1)}, bf16[128,2048]{1,0:T(8,128)(2,1)S(1)}, u32[]{:S(2)}, u32[]{:S(2)}) collective-permute-start(bf16[128,2048]{1,0:T(8,128)(2,1)} %collective-permute-done.88.refs_8_), channel_id=1, source_target_pairs={{0,1},{1,0},{2,3},{3,2},{4,5},{5,4},{6,7},{7,6},{8,9},{9,8},{10,11... | collective-permute-start | bytes 1572872 | tf_op jit(solution)/shard_map/ppermute | solution.py:522
  424.5 16.7 %collective-permute-start.108 = (bf16[128,2048]{1,0:T(8,128)(2,1)S(1)}, bf16[128,2048]{1,0:T(8,128)(2,1)S(1)}, u32[]{:S(2)}, u32[]{:S(2)}) collective-permute-start(bf16[128,2048]{1,0:T(8,128)(2,1)S(1)} %collective-permute-done.93.refs_11_), channel_id=1, source_target_pairs={{0,1},{1,0},{2,3},{3,2},{4,5},{5,4},{6,7},{7,6},{8,9},{9,8},{10,11... | collective-permute-start | bytes 1572872 | tf_op jit(solution)/shard_map/ppermute | solution.py:522
  424.6 18.2 %collective-permute-start.109 = (bf16[128,2048]{1,0:T(8,128)(2,1)S(1)}, bf16[128,2048]{1,0:T(8,128)(2,1)S(1)}, u32[]{:S(2)}, u32[]{:S(2)}) collective-permute-start(bf16[128,2048]{1,0:T(8,128)(2,1)S(1)} %collective-permute-done.94.refs_12_), channel_id=1, source_target_pairs={{0,1},{1,0},{2,3},{3,2},{4,5},{5,4},{6,7},{7,6},{8,9},{9,8},{10,11... | collective-permute-start | bytes 1572872 | tf_op jit(solution)/shard_map/ppermute | solution.py:522
  439.0 32.5 %collective-permute-start.100 = (bf16[128,2048]{1,0:T(8,128)(2,1)}, bf16[128,2048]{1,0:T(8,128)(2,1)}, u32[]{:S(2)}, u32[]{:S(2)}) collective-permute-start(bf16[128,2048]{1,0:T(8,128)(2,1)} %get-tuple-element.647), channel_id=1, source_target_pairs={{0,4},{1,5},{4,8},{5,9},{8,12},{9,13},{12,14},{13,15},{14,10},{15,... | collective-permute-start | bytes 1572872 | tf_op jit(solution)/shard_map/ppermute | solution.py:516
  439.8 31.7 %collective-permute-start.99 = (bf16[128,2048]{1,0:T(8,128)(2,1)}, bf16[128,2048]{1,0:T(8,128)(2,1)}, u32[]{:S(2)}, u32[]{:S(2)}) collective-permute-start(bf16[128,2048]{1,0:T(8,128)(2,1)} %get-tuple-element.648), channel_id=1, source_target_pairs={{4,0},{5,1},{8,4},{9,5},{12,8},{13,9},{14,12},{15,13},{10,14},{11,... | collective-permute-start | bytes 1572872 | tf_op jit(solution)/shard_map/ppermute | solution.py:519
  441.2 30.3 %collective-permute-start.102 = (bf16[288,2048]{1,0:T(8,128)(2,1)S(1)}, bf16[288,2048]{1,0:T(8,128)(2,1)S(1)}, u32[]{:S(2)}, u32[]{:S(2)}) collective-permute-start(bf16[288,2048]{1,0:T(8,128)(2,1)S(1)} %copy-done.57), channel_id=1, source_target_pairs={{0,16},{16,0},{1,17},{17,1},{2,18},{18,2},{3,19},{19,3},{4,20},{20... | collective-permute-start | bytes 3538952 | tf_op jit(solution)/shard_map/ppermute | solution.py:649
  496.5 15.8 %collective-permute-start.123 = (bf16[256,2048]{1,0:T(8,128)(2,1)S(1)}, bf16[256,2048]{1,0:T(8,128)(2,1)}, u32[]{:S(2)}, u32[]{:S(2)}) collective-permute-start(bf16[256,2048]{1,0:T(8,128)(2,1)S(1)} %convolution_convert_fusion.1), channel_id=1, source_target_pairs={{0,1},{1,0},{2,3},{3,2},{4,5},{5,4},{6,7},{7,6},{8,9},{9,8},{10,11... | collective-permute-start | bytes 3145736 | tf_op jit(solution)/shard_map/ppermute | solution.py:522
  496.7 20.3 %collective-permute-start.124 = (bf16[16,64,384]{2,1,0:T(8,128)(2,1)}, bf16[16,64,384]{2,1,0:T(8,128)(2,1)}, u32[]{:S(2)}, u32[]{:S(2)}) collective-permute-start(bf16[16,64,384]{2,1,0:T(8,128)(2,1)} %get-tuple-element.566), channel_id=1, source_target_pairs={{0,16},{16,0},{1,17},{17,1},{2,18},{18,2},{3,19},{19,3},{4,20},{20... | collective-permute-start | bytes 2359304 | tf_op jit(solution)/shard_map/ppermute | solution.py:649
  497.8 16.6 %collective-permute-start.120 = (bf16[128,2048]{1,0:T(8,128)(2,1)}, bf16[128,2048]{1,0:T(8,128)(2,1)S(1)}, u32[]{:S(2)}, u32[]{:S(2)}) collective-permute-start(bf16[128,2048]{1,0:T(8,128)(2,1)} %pad_maximum_fusion.12), channel_id=1, source_target_pairs={{4,0},{5,1},{8,4},{9,5},{12,8},{13,9},{14,12},{15,13},{10,14},{11,... | collective-permute-start | bytes 1572872 | tf_op jit(solution)/shard_map/ppermute | solution.py:519
  499.2 15.1 %collective-permute-start.121 = (bf16[128,2048]{1,0:T(8,128)(2,1)}, bf16[128,2048]{1,0:T(8,128)(2,1)}, u32[]{:S(2)}, u32[]{:S(2)}) collective-permute-start(bf16[128,2048]{1,0:T(8,128)(2,1)} %pad_maximum_fusion.13), channel_id=1, source_target_pairs={{0,4},{1,5},{4,8},{5,9},{8,12},{9,13},{12,14},{13,15},{14,10},{15,... | collective-permute-start | bytes 1572872 | tf_op jit(solution)/shard_map/ppermute | solution.py:516
  521.0 17.7 %collective-permute-start.126 = (bf16[128,2048]{1,0:T(8,128)(2,1)}, bf16[128,2048]{1,0:T(8,128)(2,1)}, u32[]{:S(2)}, u32[]{:S(2)}) collective-permute-start(bf16[128,2048]{1,0:T(8,128)(2,1)} %get-tuple-element.643), channel_id=1, source_target_pairs={{0,4},{1,5},{4,8},{5,9},{8,12},{9,13},{12,14},{13,15},{14,10},{15,... | collective-permute-start | bytes 1572872 | tf_op jit(solution)/shard_map/ppermute | solution.py:516
  522.0 16.7 %collective-permute-start.125 = (bf16[128,2048]{1,0:T(8,128)(2,1)}, bf16[128,2048]{1,0:T(8,128)(2,1)}, u32[]{:S(2)}, u32[]{:S(2)}) collective-permute-start(bf16[128,2048]{1,0:T(8,128)(2,1)} %get-tuple-element.644), channel_id=1, source_target_pairs={{4,0},{5,1},{8,4},{9,5},{12,8},{13,9},{14,12},{15,13},{10,14},{11,... | collective-permute-start | bytes 1572872 | tf_op jit(solution)/shard_map/ppermute | solution.py:519
  527.9 29.1 %all-to-all-start.1 = ((bf16[16,64,384]{2,1,0:T(8,128)(2,1)}), bf16[16,64,384]{2,1,0:T(8,128)(2,1)}, u32[]{:S(2)}, u32[]{:S(2)}) async-start(bf16[16,64,384]{2,1,0:T(8,128)(2,1)} %add_convert_fusion), calls=%async_computation.1 | async-start | bytes 1572864 | tf_op jit(solution)/shard_map/all_to_all | solution.py:877
  542.6 15.5 %collective-permute-start.133 = (bf16[128,2048]{1,0:T(8,128)(2,1)}, bf16[128,2048]{1,0:T(8,128)(2,1)}, u32[]{:S(2)}, u32[]{:S(2)}) collective-permute-start(bf16[128,2048]{1,0:T(8,128)(2,1)} %convolution_convert_fusion.12), channel_id=1, source_target_pairs={{0,1},{1,0},{2,3},{3,2},{4,5},{5,4},{6,7},{7,6},{8,9},{9,8},{10,11... | collective-permute-start | bytes 1572872 | tf_op jit(solution)/shard_map/ppermute | solution.py:522
  545.0 17.7 %collective-permute-start.131 = (bf16[128,2048]{1,0:T(8,128)(2,1)}, bf16[128,2048]{1,0:T(8,128)(2,1)}, u32[]{:S(2)}, u32[]{:S(2)}) collective-permute-start(bf16[128,2048]{1,0:T(8,128)(2,1)} %get-tuple-element.641), channel_id=1, source_target_pairs={{0,4},{1,5},{4,8},{5,9},{8,12},{9,13},{12,14},{13,15},{14,10},{15,... | collective-permute-start | bytes 1572872 | tf_op jit(solution)/shard_map/ppermute | solution.py:516
  546.0 16.7 %collective-permute-start.130 = (bf16[128,2048]{1,0:T(8,128)(2,1)}, bf16[128,2048]{1,0:T(8,128)(2,1)}, u32[]{:S(2)}, u32[]{:S(2)}) collective-permute-start(bf16[128,2048]{1,0:T(8,128)(2,1)} %get-tuple-element.642), channel_id=1, source_target_pairs={{4,0},{5,1},{8,4},{9,5},{12,8},{13,9},{14,12},{15,13},{10,14},{11,... | collective-permute-start | bytes 1572872 | tf_op jit(solution)/shard_map/ppermute | solution.py:519
  547.7 14.9 %collective-permute-start.132 = (f32[2,2048]{1,0:T(2,128)S(1)}, f32[2,2048]{1,0:T(2,128)S(1)}, u32[]{:S(2)}, u32[]{:S(2)}) collective-permute-start(f32[2,2048]{1,0:T(2,128)S(1)} %fusion.322), channel_id=1, source_target_pairs={{0,4},{1,5},{2,6},{3,7},{4,0},{5,1},{6,2},{7,3},{8,12},{9,13},{10,... | collective-permute-start | bytes 49160 | tf_op jit(solution)/shard_map/ppermute | solution.py:586
  557.1 19.4 %collective-permute-start.136 = (bf16[16,64,384]{2,1,0:T(8,128)(2,1)}, bf16[16,64,384]{2,1,0:T(8,128)(2,1)S(1)}, u32[]{:S(2)}, u32[]{:S(2)}) collective-permute-start(bf16[16,64,384]{2,1,0:T(8,128)(2,1)} %all-to-all-done.1.refs_0_), channel_id=1, source_target_pairs={{0,16},{16,0},{1,17},{17,1},{2,18},{18,2},{3,19},{19,3},{4,20},{20... | collective-permute-start | bytes 2359304 | tf_op jit(solution)/shard_map/ppermute | solution.py:649
  (192 other events, 1979.7 us)
